TPU v7x, 32 devices: a whole 2x2x4 slice. The times are simulated.
32 devices in a mesh: groups: 2 (over x), ctx: 16 (over z, y, core).
Axes of the slice: x: 2, y: 2, z: 4, core: 2. Of those that a mesh axis runs over, the one named last changes fastest.
Arguments:
- queries: bfloat16 [4096, 4096], P(('groups', 'ctx')), parts along dimension 0, may hold values from -6 to 6
- key_input: bfloat16 [4096, 4096], P(('groups', 'ctx')), parts along dimension 0, may hold values from -6 to 6
- value_input: bfloat16 [4096, 4096], P(('groups', 'ctx')), parts along dimension 0, may hold values from -6 to 6
- log_decay: float32 [4096, 32], P(('groups', 'ctx')), parts along dimension 0, may hold values from -2.5 to 0
- conv_weight: float32 [4, 4096], replicated, may hold values from -3 to 3
- norm_gain: float32 [4096], replicated, may hold values from 0.1 to 1.9
Outputs:
- mixed_out: bfloat16 [4096, 4096], P(('groups', 'ctx')), parts along dimension 0
There are 2 independent parts, one for each index of `groups`. A program takes and returns all parts, laid end to end along the dimension named above; an argument that names none is the same for every part. Nothing has to cross between parts.
All inputs are finite; a program needn't handle non-finite values.
Results may differ from a plain program's by a relative error of at most 0.0066.
Values may be sent and summed in bfloat16 or wider, within the bound.
No kernel may reach another device: no remote copies, remote signals or barrier semaphores. Data moves between devices by JAX's collectives and lax.ppermute only.
A program may use at most 320 MiB of HBM per device.

v0:
```python
import jax
import jax.numpy as jnp
from jax import lax
from jax.sharding import PartitionSpec as P


def from_behind(block, axis, distance):
    devices = range(lax.axis_size(axis))
    route = [(i - distance, i) for i in devices if i - distance in devices]
    return lax.ppermute(block, axis, route)


def join_rows(earlier, later):
    return (earlier[0] * later[0], later[0][..., None] * earlier[1] + later[1])


def block_prefix(states, rates):
    carried = lax.associative_scan(join_rows, (rates, states), axis=0)
    inclusive = carried[1]
    return jnp.concatenate([jnp.zeros_like(inclusive[:1]), inclusive[:-1]], 0)


def on_device(queries, key_input, value_input, log_decay, conv_weight, norm_gain):
    row_count, width_all = queries.shape
    head_count = log_decay.shape[1]
    head_size = width_all // head_count
    taps = conv_weight.shape[0]
    key_tail = from_behind(key_input[row_count - (taps - 1) :], "ctx", 1)
    extended = jnp.concatenate([key_tail, key_input], 0)
    conv_sum = jnp.zeros((row_count, width_all), jnp.float32)
    for offset in range(taps):
        start = taps - 1 - offset
        conv_sum = conv_sum + conv_weight[offset][None, :] * extended[
            start : start + row_count
        ].astype(jnp.float32)
    key_conv = conv_sum.astype(jnp.bfloat16).reshape(row_count, head_count, head_size)
    query_heads = queries.reshape(row_count, head_count, head_size)
    value_heads = value_input.reshape(row_count, head_count, head_size)
    cum = jnp.cumsum(log_decay, axis=0)
    total = cum[-1]
    cum_heads = cum.T
    causal = jnp.arange(row_count)[:, None] >= jnp.arange(row_count)[None, :]
    scores = jnp.einsum("thd,shd->hts", query_heads, key_conv, preferred_element_type=jnp.float32)
    spread = cum_heads[:, :, None] - cum_heads[:, None, :]
    weights = jnp.where(
        causal[None], scores * jnp.exp(jnp.where(causal[None], spread, 0.0)), 0.0
    ).astype(jnp.bfloat16)
    intra = jnp.einsum("hts,shd->thd", weights, value_heads, preferred_element_type=jnp.float32)
    weighted_keys = (
        key_conv.astype(jnp.float32) * jnp.exp(total[None, :] - cum)[:, :, None]
    ).astype(jnp.bfloat16)
    block_state = jnp.einsum(
        "shd,she->hde", weighted_keys, value_heads, preferred_element_type=jnp.float32
    )
    decay_block = jnp.exp(total)
    stacked = block_state.reshape(1, head_count * head_size, head_size)
    row_decay = jnp.repeat(decay_block, head_size).reshape(1, head_count * head_size)
    received = (
        lax.all_to_all(stacked, "ctx", split_axis=1, concat_axis=0, tiled=True),
        lax.all_to_all(row_decay, "ctx", split_axis=1, concat_axis=0, tiled=True),
    )
    shared = block_prefix(received[0], received[1])
    returned = lax.all_to_all(
        shared.astype(jnp.bfloat16), "ctx", split_axis=0, concat_axis=1, tiled=True
    ).astype(shared.dtype)
    prefix = returned.reshape(head_count, head_size, head_size)
    prefix_low = prefix.astype(jnp.bfloat16)
    inter = (
        jnp.einsum("thd,hde->the", query_heads, prefix_low, preferred_element_type=jnp.float32)
        * jnp.exp(cum)[:, :, None]
    )
    mixed = intra + inter
    scale_inv = lax.rsqrt(jnp.mean(mixed * mixed, axis=2, keepdims=True) + 1e-05)
    gain_heads = norm_gain.reshape(head_count, head_size)
    result = (mixed * scale_inv * gain_heads[None]).astype(jnp.bfloat16)
    return result.reshape(row_count, width_all)


def solution(mesh):
    return jax.shard_map(
        on_device,
        mesh=mesh,
        in_specs=(
            P(("groups", "ctx"), None),
            P(("groups", "ctx"), None),
            P(("groups", "ctx"), None),
            P(("groups", "ctx"), None),
            P(),
            P(),
        ),
        out_specs=P(("groups", "ctx"), None),
        check_vma=False,
    )
```

profile of v0, /device:TPU:1, one launch (start us, length us, event | category | flops | bytes accessed | tf_op | source)
XLA Modules:
  0.0 147.3 jit_solution(7844349312918292314)
XLA Ops:
  1.0 4.5 %collective-permute-start = (bf16[3,4096]{1,0:T(4,128)(2,1)S(1)}, bf16[3,4096]{1,0:T(4,128)(2,1)S(1)}, u32[]{:S(2)}, u32[]{:S(2)}) collective-permute-start(bf16[3,4096]{1,0:T(4,128)(2,1)S(1)} %slice.123), channel_id=1, source_target_pairs={{0,1},{1,2},{2,3},{3,4},{4,5},{5,6},{6,7},{7,8},{8,9},{9,10},{10,1... | collective-permute-start | bytes 73736 | tf_op jit(solution)/shard_map/ppermute | solution.py:10
  7.3 5.0 %all-to-all-start.1 = ((f32[1,16,256]{2,0,1:T(1,128)}), f32[1,16,256]{2,0,1:T(1,128)S(1)}, u32[]{:S(2)}, u32[]{:S(2)}) async-start(f32[1,16,256]{2,0,1:T(1,128)} %bitcast.12), calls=%async_computation.1 | async-start | bytes 32768 | tf_op jit(solution)/shard_map/all_to_all | solution.py:60
  12.3 1.1 fusion.31
  14.1 4.0 %add_convert_fusion = bf16[128,4096]{1,0:T(8,128)(2,1)S(1)} fusion(bf16[128,4096]{1,0:T(8,128)(2,1)} %param.7, bf16[3,4096]{1,0:T(4,128)(2,1)S(1)} %collective-permute-done, f32[4096]{0:T(1024)S(1)} %bitcast.86, f32[4096]{0:T(1024)S(1)} %bitcast.87, f32[4096]{0:T(1024)S(1)} %bitcast.85, f32[4096]{0:T(1024)S(1)} %bitcast.84), kind=kLoop, calls=%fused_computation.8 | loop fusion | flops 11010048 | bytes 2187264 | tf_op jit(solution)/shard_map/convert_element_type | solution.py:36
  18.8 1.8 %fusion.5 = f32[32,128,128]{2,1,0:T(8,128)} fusion(bf16[128,32,128]{0,2,1:T(8,128)(2,1)S(1)} %bitcast.77, f32[128,32]{0,1:T(8,128)S(1)} %copy.36, bf16[128,4096]{1,0:T(8,128)(2,1)S(1)} %copy-done), kind=kOutput, calls=%fused_computation.14 | convolution fusion | flops 135790592 | bytes 4210688 | tf_op jit(solution)/shard_map/shd,she->hde/dot_general | solution.py:52
  20.6 6.0 %all-to-all-start = ((f32[1,4096,128]{2,0,1:T(1,128)}), f32[1,4096,128]{2,0,1:T(1,128)S(1)}, u32[]{:S(2)}, u32[]{:S(2)}) async-start(f32[1,4096,128]{2,0,1:T(1,128)} %bitcast.75), calls=%async_computation | async-start | bytes 4194304 | tf_op jit(solution)/shard_map/all_to_all | solution.py:59
  26.8 41.3 %all-to-all-done = f32[1,4096,128]{2,0,1:T(1,128)S(1)} async-done(((f32[1,4096,128]{2,0,1:T(1,128)}), f32[1,4096,128]{2,0,1:T(1,128)S(1)}, u32[]{:S(2)}, u32[]{:S(2)}) %all-to-all-start) | async-done | bytes 2097184 | tf_op jit(solution)/shard_map/all_to_all | solution.py:59
  70.5 2.4 %pad.29 = f32[4,256,128]{2,1,0:T(8,128)} pad(f32[2,256,128]{2,1,0:T(8,128)} %pad_maximum_fusion.3, f32[]{:T(128)} %constant.4.clone.1), padding=0_1_1x0_0_0x0_0_0 | pad | bytes 786436 | tf_op jit(solution)/shard_map/pad | solution.py:18
  73.0 1.5 %pad.30 = f32[4,256,128]{2,1,0:T(8,128)} pad(f32[2,256,128]{2,1,0:T(8,128)S(1)} %pad_add_fusion, f32[]{:T(128)} %constant.4.clone.1), padding=1_0_1x0_0_0x0_0_0 | pad | bytes 786436 | tf_op jit(solution)/shard_map/pad | solution.py:18
  74.5 2.1 %add.83 = f32[4,256,128]{2,1,0:T(8,128)} add(f32[4,256,128]{2,1,0:T(8,128)} %pad.29, f32[4,256,128]{2,1,0:T(8,128)} %pad.30) | non-fusion elementwise | flops 131072 | bytes 1572864 | tf_op jit(solution)/shard_map/add | solution.py:18
  76.6 1.4 fusion.23
  78.8 4.1 %pad.31 = f32[8,256,128]{2,1,0:T(8,128)} pad(f32[4,256,128]{2,1,0:T(8,128)} %pad_maximum_fusion.2, f32[]{:T(128)} %constant.4.clone.1), padding=0_1_1x0_0_0x0_0_0 | pad | bytes 1572868 | tf_op jit(solution)/shard_map/pad | solution.py:18
  82.9 4.1 %pad.32 = f32[8,256,128]{2,1,0:T(8,128)} pad(f32[4,256,128]{2,1,0:T(8,128)} %add.83, f32[]{:T(128)} %constant.4.clone.1), padding=1_0_1x0_0_0x0_0_0 | pad | bytes 1572868 | tf_op jit(solution)/shard_map/pad | solution.py:18
  87.1 2.8 %add.85 = f32[8,256,128]{2,1,0:T(8,128)} add(f32[8,256,128]{2,1,0:T(8,128)} %pad.31, f32[8,256,128]{2,1,0:T(8,128)} %pad.32) | non-fusion elementwise | flops 262144 | bytes 3145728 | tf_op jit(solution)/shard_map/add | solution.py:18
  90.9 4.0 %pad.46 = f32[15,256,128]{2,1,0:T(8,128)} pad(f32[8,256,128]{2,1,0:T(8,128)S(1)} %pad_maximum_fusion.1, f32[]{:T(128)} %constant.4.clone.1), padding=0_0_1x0_0_0x0_0_0 | pad | bytes 3014660 | tf_op jit(solution)/shard_map/slice | solution.py:20
  94.9 3.9 %pad.81 = f32[16,256,128]{2,1,0:T(8,128)S(1)} pad(f32[8,256,128]{2,1,0:T(8,128)} %add.85, f32[]{:T(128)} %constant.4.clone.1), padding=1_0_1x0_0_0x0_0_0 | pad | bytes 3145732
  98.8 1.8 %add_convert_fusion.1 = bf16[15,256,128]{2,1,0:T(8,128)(2,1)S(1)} fusion(f32[15,256,128]{2,1,0:T(8,128)} %pad.46, f32[16,256,128]{2,1,0:T(8,128)S(1)} %pad.81), kind=kLoop, calls=%fused_computation.9 | loop fusion | flops 983040 | bytes 4915200 | tf_op jit(solution)/shard_map/convert.2
  100.5 1.1 concatenate.19
  101.6 10.9 %all-to-all-start.2 = ((bf16[16,256,128]{2,1,0:T(8,128)(2,1)}), bf16[16,256,128]{2,1,0:T(8,128)(2,1)S(1)}, u32[]{:S(2)}, u32[]{:S(2)}) async-start(bf16[16,256,128]{2,1,0:T(8,128)(2,1)} %concatenate.19), calls=%async_computation.2 | async-start | bytes 2097152 | tf_op jit(solution)/shard_map/all_to_all | solution.py:63
  112.7 23.0 %all-to-all-done.2 = bf16[16,256,128]{2,1,0:T(8,128)(2,1)S(1)} async-done(((bf16[16,256,128]{2,1,0:T(8,128)(2,1)}), bf16[16,256,128]{2,1,0:T(8,128)(2,1)S(1)}, u32[]{:S(2)}, u32[]{:S(2)}) %all-to-all-start.2) | async-done | bytes 1048608 | tf_op jit(solution)/shard_map/all_to_all | solution.py:63
  135.6 3.5 %fusion.6 = f32[32,128,128]{2,1,0:T(8,128)} fusion(bf16[32,128,128]{2,1,0:T(8,128)(2,1)S(1)} %bitcast.79, bf16[128,4096]{1,0:T(8,128)(2,1)} %param.6), kind=kOutput, calls=%fused_computation.15 | convolution fusion | flops 134217728 | bytes 4194304 | tf_op jit(solution)/shard_map/thd,hde->the/dot_general | solution.py:69
  139.2 4.9 %multiply_reduce_fusion = (f32[128,32]{0,1:T(8,128)S(1)}, f32[128,32,128]{0,2,1:T(8,128)}) fusion(f32[128,32]{0,1:T(8,128)S(1)} %copy.41, f32[32,128,128]{2,1,0:T(8,128)} %fusion.6, bf16[128,32,128]{0,2,1:T(8,128)(2,1)S(1)} %bitcast.78, f32[32,128]{1,0:T(8,128)S(1)} %copy.31, pred[128,128]{0,1:T(8,128)(4,1)S(1)} %iota_compare_fusion, ...), kind=kOutput, calls=%fused_computation.6 | convolution fusion | flops 273149952 | bytes 7405568 | tf_op jit(solution)/shard_map/hts,shd->thd/dot_general | solution.py:48
  144.1 1.9 %multiply_convert_fusion = bf16[128,32,128]{0,2,1:T(8,128)(2,1)S(1)} fusion(f32[128,32,128]{0,2,1:T(8,128)} %get-tuple-element.18, f32[32,128]{1,0:T(8,128)S(1)} %bitcast.88, f32[128,32]{0,1:T(8,128)S(1)} %add_rsqrt_fusion), kind=kLoop, calls=%fused_computation.5 | loop fusion | flops 1572864 | bytes 3178496 | tf_op jit(solution)/shard_map/convert_element_type | solution.py:75
  146.0 1.3 copy.42
  (63 shorter events, 8.7 us)
Async XLA Ops:
  0.0 18.8 %copy-start = (bf16[128,4096]{1,0:T(8,128)(2,1)S(1)}, bf16[128,4096]{1,0:T(8,128)(2,1)}, u32[]{:S(2)}) copy-start(bf16[128,4096]{1,0:T(8,128)(2,1)} %param.8) | copy-start | bytes 3145732
  1.0 13.1 %collective-permute-start = (bf16[3,4096]{1,0:T(4,128)(2,1)S(1)}, bf16[3,4096]{1,0:T(4,128)(2,1)S(1)}, u32[]{:S(2)}, u32[]{:S(2)}) collective-permute-start(bf16[3,4096]{1,0:T(4,128)(2,1)S(1)} %slice.123), channel_id=1, source_target_pairs={{0,1},{1,2},{2,3},{3,4},{4,5},{5,6},{6,7},{7,8},{8,9},{9,10},{10,1... | collective-permute-start | bytes 73736 | tf_op jit(solution)/shard_map/ppermute | solution.py:10
  6.5 7.6 %copy-start.6 = (f32[128,32]{1,0:T(8,128)}, f32[128,32]{1,0:T(8,128)S(1)}, u32[]{:S(2)}) copy-start(f32[128,32]{1,0:T(8,128)S(1)} %reduce_window_sum.11) | copy-start | bytes 49156
  7.3 13.3 %all-to-all-start.1 = ((f32[1,16,256]{2,0,1:T(1,128)}), f32[1,16,256]{2,0,1:T(1,128)S(1)}, u32[]{:S(2)}, u32[]{:S(2)}) async-start(f32[1,16,256]{2,0,1:T(1,128)} %bitcast.12), calls=%async_computation.1 | async-start | bytes 32768 | tf_op jit(solution)/shard_map/all_to_all | solution.py:60
  18.8 1.8 %copy-start.4 = (bf16[128,4096]{0,1:T(8,128)(2,1)}, bf16[128,4096]{0,1:T(8,128)(2,1)S(1)}, u32[]{:S(2)}) copy-start(bf16[128,4096]{0,1:T(8,128)(2,1)S(1)} %copy.46) | copy-start | bytes 3145732
  20.6 47.5 %all-to-all-start = ((f32[1,4096,128]{2,0,1:T(1,128)}), f32[1,4096,128]{2,0,1:T(1,128)S(1)}, u32[]{:S(2)}, u32[]{:S(2)}) async-start(f32[1,4096,128]{2,0,1:T(1,128)} %bitcast.75), calls=%async_computation | async-start | bytes 4194304 | tf_op jit(solution)/shard_map/all_to_all | solution.py:59
  68.4 1.4 copy-start.3
  73.0 5.0 %slice-start = ((f32[8,256,128]{2,1,0:T(8,128)}), f32[1,256,128]{2,1,0:T(8,128)S(1)}, s32[]{:S(2)}) async-start(f32[8,256,128]{2,1,0:T(8,128)} %copy-done.3), calls=%async_computation.3 | async-start | bytes 262144 | tf_op jit(solution)/shard_map/slice | solution.py:18
  87.0 2.8 %copy-start.1 = (f32[8,256,128]{2,1,0:T(8,128)S(1)}, f32[8,256,128]{2,1,0:T(8,128)}, u32[]{:S(2)}) copy-start(f32[8,256,128]{2,1,0:T(8,128)} %pad.31) | copy-start | bytes 3145732
  87.1 2.8 %copy-start.2 = (f32[8,256,128]{2,1,0:T(8,128)S(1)}, f32[8,256,128]{2,1,0:T(8,128)}, u32[]{:S(2)}) copy-start(f32[8,256,128]{2,1,0:T(8,128)} %pad.32) | copy-start | bytes 3145732
  89.9 0.9 copy-start.8
  100.5 12.0 %copy-start.7 = (f32[128,32]{1,0:T(8,128)S(1)}, f32[128,32]{1,0:T(8,128)}, u32[]{:S(2)}) copy-start(f32[128,32]{1,0:T(8,128)} %copy-done.6) | copy-start | bytes 49156
  100.5 12.0 %copy-start.9 = (f32[128,32]{1,0:T(8,128)S(1)}, f32[128,32]{1,0:T(8,128)}, u32[]{:S(2)}) copy-start(f32[128,32]{1,0:T(8,128)} %get-tuple-element.9) | copy-start | bytes 49156
  101.6 34.0 %all-to-all-start.2 = ((bf16[16,256,128]{2,1,0:T(8,128)(2,1)}), bf16[16,256,128]{2,1,0:T(8,128)(2,1)S(1)}, u32[]{:S(2)}, u32[]{:S(2)}) async-start(bf16[16,256,128]{2,1,0:T(8,128)(2,1)} %concatenate.19), calls=%async_computation.2 | async-start | bytes 2097152 | tf_op jit(solution)/shard_map/all_to_all | solution.py:63
  135.6 3.5 %copy-start.5 = (bf16[128,4096]{0,1:T(8,128)(2,1)S(1)}, bf16[128,4096]{0,1:T(8,128)(2,1)}, u32[]{:S(2)}) copy-start(bf16[128,4096]{0,1:T(8,128)(2,1)} %copy-done.4) | copy-start | bytes 3145732
  139.2 4.9 %copy-start.10 = (f32[4096]{0:T(1024)S(1)}, f32[4096]{0:T(1024)}, u32[]{:S(2)}) copy-start(f32[4096]{0:T(1024)} %param.11) | copy-start | bytes 49156
where the time goes:
time: 149 us; the launch traced here: 147 us
  waiting for transfers between devices  64.2 us (43%)
  local copies, waits for them, and re-layouts  28.5 us (19%)
  starting transfers between devices  26.4 us (18%)
  other arithmetic  17.8 us (12%)
  matrix products  10.2 us (7%)
    all_to_all x1, waiting for transfers between devices, on_device(): lax.all_to_all(stacked, 'ctx', split_axis=1, concat_axis=0, tiled=True)  41.3 us
    all_to_all x1, waiting for transfers between devices, on_device(): lax.all_to_all(shared.astype(jnp.bfloat16), 'ctx', split_axis=0, concat_a...  23 us
    pad x4, local copies, waits for them, and re-layouts, block_prefix(): carried = lax.associative_scan(join_rows, (rates, states), axis=0)  12.2 us
    all_to_all x1, starting transfers between devices, on_device(): lax.all_to_all(shared.astype(jnp.bfloat16), 'ctx', split_axis=0, concat_a...  10.9 us
    all_to_all x1, starting transfers between devices, on_device(): lax.all_to_all(stacked, 'ctx', split_axis=1, concat_axis=0, tiled=True)  6.02 us
    unnamed x25, local copies, waits for them, and re-layouts  5.27 us
    all_to_all x1, starting transfers between devices, on_device(): lax.all_to_all(row_decay, 'ctx', split_axis=1, concat_axis=0, tiled=True)  5 us
    dot_general x1, matrix products, on_device(): jnp.einsum('hts,shd->thd', weights, value_heads, preferred_element_type=j...  4.9 us
  transfers between devices with their start and end apart: 4, of which 2 were waited for; matrix products, arithmetic and copies ran while one was open for 7% of the time, Pallas kernels for 0%

commit v1 on v0

v1 whole, which is shorter than its diff:
```python
import functools

import jax
import jax.numpy as jnp
from jax import lax
from jax.experimental import pallas as pl
from jax.experimental.pallas import tpu as pltpu
from jax.sharding import PartitionSpec as P

F32 = jnp.float32
BF16 = jnp.bfloat16
CHIPS = 4
SPAN = 2 * CHIPS
HALO = 8


def three_parts(x):
    hi = x.astype(BF16)
    rest = x - hi.astype(F32)
    mid = rest.astype(BF16)
    low = (rest - mid.astype(F32)).astype(BF16)
    return hi, mid, low


def conv_keys(k_ref, halo_ref, w_ref, ext_ref):
    rows = k_ref.shape[0]
    ext_ref[0:HALO, :] = halo_ref[...].astype(F32)
    ext_ref[HALO : HALO + rows, :] = k_ref[...].astype(F32)
    total = None
    for j in range(w_ref.shape[0]):
        term = w_ref[j : j + 1, :] * ext_ref[HALO - j : HALO - j + rows, :]
        total = term if total is None else total + term
    return total.astype(BF16)


def put_decay(out, heads, size, decays):
    base = heads * size
    zero = jnp.zeros((16 - 3 * heads, 128), BF16)
    rows = jnp.concatenate(decays, 0)
    parts = [p.astype(F32) for p in three_parts(rows)]
    out[base : base + 16, :] = jnp.concatenate(parts + [zero.astype(F32)], 0).astype(BF16)


def get_decay(packet, heads, size):
    base = heads * size
    tail = packet[base : base + 16, :].astype(F32)
    return tail[0:heads] + tail[heads : 2 * heads] + tail[2 * heads : 3 * heads]


def state_kernel(heads, size, idx, k_ref, halo_ref, v_ref, w_ref, cum_ref, out_ref, ext_ref):
    del idx
    key_conv = conv_keys(k_ref, halo_ref, w_ref, ext_ref)
    cum = cum_ref[0, 0:heads, :]
    total = cum_ref[0, heads : 2 * heads, :]
    ending = jnp.exp(total - cum).T
    for j in range(heads):
        cols = slice(j * size, (j + 1) * size)
        weighted = (key_conv[:, cols].astype(F32) * ending[:, j : j + 1]).astype(BF16)
        state = lax.dot_general(
            weighted, v_ref[:, cols], (((0,), (0,)), ((), ())), preferred_element_type=F32
        )
        out_ref[0, j * size : (j + 1) * size, :] = state.astype(BF16)
    decay = jnp.exp(total)
    put_decay(out_ref.at[0], heads, size, [decay[j : j + 1] for j in range(heads)])


def intra_kernel(heads, size, q_ref, k_ref, halo_ref, v_ref, w_ref, cum_ref, out_ref, ext_ref):
    rows = q_ref.shape[0]
    key_conv = conv_keys(k_ref, halo_ref, w_ref, ext_ref)
    cum = cum_ref[0, 0:heads, :]
    cum_col = cum.T
    causal = lax.broadcasted_iota(jnp.int32, (rows, rows), 0) >= lax.broadcasted_iota(
        jnp.int32, (rows, rows), 1
    )
    for j in range(heads):
        cols = slice(j * size, (j + 1) * size)
        scores = lax.dot_general(
            q_ref[:, cols],
            key_conv[:, cols],
            (((1,), (1,)), ((), ())),
            preferred_element_type=F32,
        )
        spread = cum_col[:, j : j + 1] - cum[j : j + 1, :]
        weights = jnp.where(causal, scores * jnp.exp(jnp.where(causal, spread, 0.0)), 0.0)
        out_ref[:, cols] = jnp.dot(
            weights.astype(BF16), v_ref[:, cols], preferred_element_type=F32
        )


def chip_kernel(heads, size, idx, own_ref, got_ref, *out_refs):
    first = idx[0] == 0
    for g in range(CHIPS):
        own_decay = get_decay(own_ref.at[g], heads, size)
        got_decay = get_decay(got_ref.at[g], heads, size)
        own_by = jnp.where(first, got_decay, 1.0)
        got_by = jnp.where(first, 1.0, own_decay)
        for j in range(heads):
            rows = slice(j * size, (j + 1) * size)
            out_refs[g][rows, :] = (
                own_ref[g, rows, :].astype(F32) * own_by[j : j + 1]
                + got_ref[g, rows, :].astype(F32) * got_by[j : j + 1]
            ).astype(BF16)
        both = own_decay * got_decay
        put_decay(out_refs[g], heads, size, [both[j : j + 1] for j in range(heads)])


def span_kernel(heads, size, idx, *refs):
    packets, out_ref, held = refs[:CHIPS], refs[CHIPS], refs[CHIPS + 1]
    for g in range(CHIPS):
        held[idx[1] ^ g] = packets[g][...]
    decays = [get_decay(held.at[b], heads, size) for b in range(CHIPS)]
    for j in range(heads):
        rows = slice(j * size, (j + 1) * size)
        acc = held[0, rows, :].astype(F32)
        for b in range(1, CHIPS):
            acc = acc * decays[b][j : j + 1] + held[b, rows, :].astype(F32)
        out_ref[rows, :] = acc.astype(BF16)
    whole = decays[0]
    for b in range(1, CHIPS):
        whole = whole * decays[b]
    put_decay(out_ref, heads, size, [whole[j : j + 1] for j in range(heads)])


def spread_kernel(heads, size, idx, *refs):
    packets, before = refs[:CHIPS], refs[CHIPS]
    outs, held, made = refs[CHIPS + 1 : 2 * CHIPS + 1], refs[2 * CHIPS + 1], refs[2 * CHIPS + 2]
    for g in range(CHIPS):
        held[idx[1] ^ g] = packets[g][...]
    decays = [get_decay(held.at[b], heads, size) for b in range(CHIPS)]
    for j in range(heads):
        rows = slice(j * size, (j + 1) * size)
        acc = before[rows, :].astype(F32)
        made[0, rows, :] = before[rows, :]
        for b in range(1, CHIPS):
            acc = acc * decays[b - 1][j : j + 1] + held[b - 1, rows, :].astype(F32)
            made[b, rows, :] = acc.astype(BF16)
    for g in range(CHIPS):
        outs[g][...] = made[idx[1] ^ g]


def out_kernel(heads, size, idx, q_ref, intra_ref, cum_ref, gain_ref, *refs):
    prefixes, sib_ref, out_ref, held = refs[:CHIPS], refs[CHIPS], refs[-2], refs[-1]
    g = pl.program_id(0)
    for i in range(CHIPS):

        @pl.when(g == i)
        def _():
            held[...] = prefixes[i][...]

    second = idx[0] == 1
    sib_decay = get_decay(sib_ref.at[0], heads, size)
    started = jnp.exp(cum_ref[0, 0:heads, :]).T
    for j in range(heads):
        cols = slice(j * size, (j + 1) * size)
        chip_prefix = held[cols, :].astype(F32)
        prefix = jnp.where(
            second,
            chip_prefix * sib_decay[j : j + 1] + sib_ref[0, cols, :].astype(F32),
            chip_prefix,
        ).astype(BF16)
        inter = jnp.dot(q_ref[:, cols], prefix, preferred_element_type=F32)
        mixed = intra_ref[:, cols] + inter * started[:, j : j + 1]
        scale = lax.rsqrt(jnp.mean(mixed * mixed, axis=1, keepdims=True) + 1e-05)
        out_ref[:, cols] = (mixed * scale * gain_ref[0:1, cols]).astype(BF16)


def join_spans(earlier, later, heads, size):
    base = heads * size

    def decay(x):
        tail = x[base:].astype(F32)
        return tail[0:heads] + tail[heads : 2 * heads] + tail[2 * heads : 3 * heads]

    by = decay(later)
    state = (
        by[:, None, :] * earlier[:base].astype(F32).reshape(heads, size, -1)
        + later[:base].astype(F32).reshape(heads, size, -1)
    ).reshape(base, -1)
    parts = three_parts(by * decay(earlier))
    return jnp.concatenate([state.astype(BF16), *parts, later[base + 3 * heads :]], 0)


def on_device(queries, key_input, value_input, log_decay, conv_weight, norm_gain):
    rows, width = queries.shape
    head_count = log_decay.shape[1]
    size = width // head_count
    taps = conv_weight.shape[0]
    heads = head_count // SPAN
    wide = heads * size
    packet = wide + 16
    n = lax.axis_size("ctx")
    me = lax.axis_index("ctx")
    core, chip = me % 2, (me // 2) % CHIPS
    idx = jnp.stack([core, chip]).astype(jnp.int32)

    def swap(x, mask):
        return lax.ppermute(x, "ctx", [(i, i ^ mask) for i in range(n)])

    def shift(x, by):
        return lax.ppermute(x, "ctx", [(i, i + by) for i in range(n - by)])

    halo = shift(key_input[rows - HALO :], 1)
    cum = jnp.cumsum(log_decay, axis=0).T.reshape(SPAN, heads, rows)
    cum = jnp.concatenate([cum, jnp.broadcast_to(cum[:, :, -1:], cum.shape)], 1)
    gain = norm_gain.reshape(1, width)

    def states(mine):
        def at(g, s):
            half = s[0] if mine else 1 - s[0]
            return half * CHIPS + (s[1] ^ g)

        col = lambda g, s: (0, at(g, s))
        return pl.pallas_call(
            functools.partial(state_kernel, heads, size),
            out_shape=jax.ShapeDtypeStruct((CHIPS, packet, size), BF16),
            grid_spec=pltpu.PrefetchScalarGridSpec(
                num_scalar_prefetch=1,
                grid=(CHIPS,),
                in_specs=[
                    pl.BlockSpec((rows, wide), col),
                    pl.BlockSpec((HALO, wide), col),
                    pl.BlockSpec((rows, wide), col),
                    pl.BlockSpec((taps, wide), col),
                    pl.BlockSpec((1, 2 * heads, rows), lambda g, s: (at(g, s), 0, 0)),
                ],
                out_specs=pl.BlockSpec((1, packet, size), lambda g, s: (g, 0, 0)),
                scratch_shapes=[pltpu.VMEM((rows + HALO, wide), F32)],
            ),
            name="states_mine" if mine else "states_other",
        )(idx, key_input, halo, value_input, conv_weight, cum)

    theirs = states(False)
    got = swap(theirs, 1)
    mine = states(True)
    got_late = swap(mine, 1)

    whole = lambda shape: pl.BlockSpec(shape, lambda i, s: (0,) * len(shape))
    flat = jax.ShapeDtypeStruct((packet, size), BF16)
    chip_states = pl.pallas_call(
        functools.partial(chip_kernel, heads, size),
        out_shape=[flat] * CHIPS,
        grid_spec=pltpu.PrefetchScalarGridSpec(
            num_scalar_prefetch=1,
            grid=(1,),
            in_specs=[whole((CHIPS, packet, size))] * 2,
            out_specs=[whole((packet, size))] * CHIPS,
        ),
        name="chip_states",
    )(idx, mine, got)
    packets = [chip_states[0]] + [swap(chip_states[g], 2 * g) for g in range(1, CHIPS)]

    blk = lambda g: (0, g)
    intra = pl.pallas_call(
        functools.partial(intra_kernel, heads, size),
        out_shape=jax.ShapeDtypeStruct((rows, width), F32),
        grid=(SPAN,),
        in_specs=[
            pl.BlockSpec((rows, wide), blk),
            pl.BlockSpec((rows, wide), blk),
            pl.BlockSpec((HALO, wide), blk),
            pl.BlockSpec((rows, wide), blk),
            pl.BlockSpec((taps, wide), blk),
            pl.BlockSpec((1, 2 * heads, rows), lambda g: (g, 0, 0)),
        ],
        out_specs=pl.BlockSpec((rows, wide), blk),
        scratch_shapes=[pltpu.VMEM((rows + HALO, wide), F32)],
        name="intra",
    )(queries, key_input, halo, value_input, conv_weight, cum)

    span = pl.pallas_call(
        functools.partial(span_kernel, heads, size),
        out_shape=flat,
        grid_spec=pltpu.PrefetchScalarGridSpec(
            num_scalar_prefetch=1,
            grid=(1,),
            in_specs=[whole((packet, size))] * CHIPS,
            out_specs=whole((packet, size)),
            scratch_shapes=[pltpu.VMEM((CHIPS, packet, size), BF16)],
        ),
        name="span_state",
    )(idx, *packets)
    before = shift(span, SPAN)
    reach = 1
    while reach < n // SPAN - 1:
        before = join_spans(shift(before, SPAN * reach), before, heads, size)
        reach *= 2

    low = jax.ShapeDtypeStruct((wide, size), BF16)
    chip_prefix = pl.pallas_call(
        functools.partial(spread_kernel, heads, size),
        out_shape=[low] * CHIPS,
        grid_spec=pltpu.PrefetchScalarGridSpec(
            num_scalar_prefetch=1,
            grid=(1,),
            in_specs=[whole((packet, size))] * (CHIPS + 1),
            out_specs=[whole((wide, size))] * CHIPS,
            scratch_shapes=[
                pltpu.VMEM((CHIPS, packet, size), BF16),
                pltpu.VMEM((CHIPS, wide, size), BF16),
            ],
        ),
        name="chip_prefix",
    )(idx, *packets, before)
    own = [chip_prefix[0]] + [swap(chip_prefix[g], 2 * g) for g in range(1, CHIPS)]
    other = [swap(x, 1) for x in own]

    def output(mine, prefixes, sibling, result):
        def at(g, s):
            half = s[0] if mine else 1 - s[0]
            return half * CHIPS + (s[1] ^ g)

        col = lambda g, s: (0, at(g, s))
        extra = [] if result is None else [result]
        return pl.pallas_call(
            functools.partial(out_kernel, heads, size),
            out_shape=jax.ShapeDtypeStruct((rows, width), BF16),
            grid_spec=pltpu.PrefetchScalarGridSpec(
                num_scalar_prefetch=1,
                grid=(CHIPS,),
                in_specs=[
                    pl.BlockSpec((rows, wide), col),
                    pl.BlockSpec((rows, wide), col),
                    pl.BlockSpec((1, 2 * heads, rows), lambda g, s: (at(g, s), 0, 0)),
                    pl.BlockSpec((1, wide), col),
                ]
                + [pl.BlockSpec((wide, size), lambda g, s: (0, 0))] * CHIPS
                + [pl.BlockSpec((1, packet, size), lambda g, s: (g, 0, 0))]
                + [pl.BlockSpec(memory_space=pl.ANY)] * len(extra),
                out_specs=pl.BlockSpec((rows, wide), col),
                scratch_shapes=[pltpu.VMEM((wide, size), BF16)],
            ),
            input_output_aliases={} if result is None else {6 + CHIPS: 0},
            name="out_mine" if mine else "out_other",
        )(idx, queries, intra, cum, gain, *prefixes, sibling, *extra)

    result = output(True, own, got, None)
    return output(False, other, got_late, result)


def solution(mesh):
    rows = P(("groups", "ctx"), None)
    return jax.shard_map(
        on_device,
        mesh=mesh,
        in_specs=(rows, rows, rows, rows, P(), P()),
        out_specs=rows,
        check_vma=False,
    )
```

time: 149 us -> 81.2 us (0.54)
  waiting for transfers between devices: 64.2 us -> 8.8 us
  Pallas kernels: 0 us -> 38.4 us
  local copies, waits for them, and re-layouts: 28.5 us -> 6.35 us
  other arithmetic: 17.8 us -> 1.39 us
  matrix products: 10.2 us -> 0 us
    all_to_all x3 -> x0, waiting for transfers between devices: 64.2 us -> none  [the longest x1 41.3 us: on_device(): lax.all_to_all(stacked, 'ctx', split_axis=1, concat_axis=0, tiled=True)]
    pallas_call x0 -> x8, Pallas kernels: none -> 38.4 us  [the longest x2 11.1 us: output(): pl.pallas_call(functools.partial(out_kernel, heads, size), out_shape=jax....]
    all_to_all x3 -> x0, starting transfers between devices: 21.9 us -> none  [the longest x1 10.9 us: on_device(): lax.all_to_all(shared.astype(jnp.bfloat16), 'ctx', split_axis=0, concat_a...]
    ppermute x1 -> x14, starting transfers between devices: 4.54 us -> 25.3 us  [the longest x12 16.9 us: swap(): return lax.ppermute(x, 'ctx', [(i, i ^ mask) for i in range(n)])]
    pad x4 -> x0, local copies, waits for them, and re-layouts: 12.2 us -> none  [block_prefix(): carried = lax.associative_scan(join_rows, (rates, states), axis=0)]
    dot_general x3 -> x0, matrix products: 10.2 us -> none  [the longest x1 4.9 us: on_device(): jnp.einsum('hts,shd->thd', weights, value_heads, preferred_element_type=j...]
    ppermute x1 -> x14, waiting for transfers between devices: 0.01 us -> 8.8 us  [the longest x12 6.52 us: swap(): return lax.ppermute(x, 'ctx', [(i, i ^ mask) for i in range(n)])]
    add x8 -> x0, other arithmetic: 7.34 us -> none  [the longest x3 4.9 us: block_prefix(): carried = lax.associative_scan(join_rows, (rates, states), axis=0)]
  transfers between devices with their start and end apart: 4 -> 14, of which waited for: 2 -> 4; matrix products, arithmetic and copies ran while one was open for 7% -> 3% of each run, Pallas kernels for 0% -> 35%
where the time goes in v1:
time: 81.2 us; the launch traced here: 80.4 us
  Pallas kernels  38.4 us (47%)
  starting transfers between devices  25.3 us (31%)
  waiting for transfers between devices  8.8 us (11%)
  local copies, waits for them, and re-layouts  6.35 us (8%)
  other arithmetic  1.39 us (2%)
    ppermute x12, starting transfers between devices, swap(): return lax.ppermute(x, 'ctx', [(i, i ^ mask) for i in range(n)])  16.9 us
    pallas_call x2, Pallas kernels, output(): pl.pallas_call(functools.partial(out_kernel, heads, size), out_shape=jax....  11.1 us
    pallas_call x2, Pallas kernels, states(): pl.pallas_call(functools.partial(state_kernel, heads, size), out_shape=ja...  9.88 us
    pallas_call x1, Pallas kernels, on_device(): pl.pallas_call(functools.partial(intra_kernel, heads, size), out_shape=ja...  9.25 us
    ppermute x2, starting transfers between devices, shift(): return lax.ppermute(x, 'ctx', [(i, i + by) for i in range(n - by)])  8.36 us
    ppermute x12, waiting for transfers between devices, swap(): return lax.ppermute(x, 'ctx', [(i, i ^ mask) for i in range(n)])  6.52 us
    unnamed x29, local copies, waits for them, and re-layouts  5.1 us
    pallas_call x1, Pallas kernels, on_device(): pl.pallas_call(functools.partial(spread_kernel, heads, size), out_shape=[...  2.79 us
  transfers between devices with their start and end apart: 14, of which 4 were waited for; matrix products, arithmetic and copies ran while one was open for 3% of the time, Pallas kernels for 35%

profile of v1, /device:TPU:1, one launch (start us, length us, event | category | flops | bytes accessed | tf_op | source)
XLA Modules:
  0.0 80.4 jit_solution(2524092700915413166)
XLA Ops:
  0.0 0.8 %slice.6 = bf16[8,4096]{1,0:T(8,128)(2,1)S(1)} slice(bf16[128,4096]{1,0:T(8,128)(2,1)} %k_ref.5), slice={[120:128], [0:4096]} | slice | bytes 131072 | tf_op jit(solution)/shard_map/slice | solution.py:202
  0.8 4.5 %collective-permute-start = (bf16[8,4096]{1,0:T(8,128)(2,1)S(1)}, bf16[8,4096]{1,0:T(8,128)(2,1)S(1)}, u32[]{:S(2)}, u32[]{:S(2)}) collective-permute-start(bf16[8,4096]{1,0:T(8,128)(2,1)S(1)} %slice.6), channel_id=1, source_target_pairs={{0,1},{1,2},{2,3},{3,4},{4,5},{5,6},{6,7},{7,8},{8,9},{9,10},{10,1... | collective-permute-start | bytes 196616 | tf_op jit(solution)/shard_map/ppermute | solution.py:200
  5.4 0.8 %copy.8 = f32[128,32]{1,0:T(8,128)S(1)} copy(f32[128,32]{0,1:T(8,128)} %param.9) | data formatting | bytes 32768 | tf_op args[3]
  8.7 5.0 %states_other.1 = bf16[4,528,128]{2,1,0:T(8,128)(2,1)} custom-call(s32[2]{0:T(128)} %pad_add_fusion.idx, bf16[128,4096]{1,0:T(8,128)(2,1)} %k_ref.5, bf16[8,4096]{1,0:T(8,128)(2,1)} %copy-done.1, bf16[128,4096]{1,0:T(8,128)(2,1)} %v_ref.5, f32[4,4096]{1,0:T(4,128)} %w_ref.5, f32[8,8,128]{2,1,0:T(8,128)} %pad_maximum_fusion.cum_ref), custom_call_target="tpu_custom_call" | custom-call | tf_op jit(solution)/shard_map/states_other/pallas_call | solution.py:213
  13.6 4.9 %states_mine.1.own_ref = bf16[4,528,128]{2,1,0:T(8,128)(2,1)} custom-call(s32[2]{0:T(128)} %pad_add_fusion.idx, bf16[128,4096]{1,0:T(8,128)(2,1)} %k_ref.5, bf16[8,4096]{1,0:T(8,128)(2,1)} %copy-done.1, bf16[128,4096]{1,0:T(8,128)(2,1)} %v_ref.5, f32[4,4096]{1,0:T(4,128)} %w_ref.5, f32[8,8,128]{2,1,0:T(8,128)} %pad_maximum_fusion.cum_ref), custom_call_target="tpu_custom_call" | custom-call | tf_op jit(solution)/shard_map/states_mine/pallas_call | solution.py:213
  19.9 2.7 %chip_states.1 = (bf16[528,128]{1,0:T(8,128)(2,1)}, bf16[528,128]{1,0:T(8,128)(2,1)}, bf16[528,128]{1,0:T(8,128)(2,1)}, bf16[528,128]{1,0:T(8,128)(2,1)}) custom-call(s32[2]{0:T(128)} %pad_add_fusion.idx, bf16[4,528,128]{2,1,0:T(8,128)(2,1)} %states_mine.1.own_ref, bf16[4,528,128]{2,1,0:T(8,128)(2,1)} %copy-done), custom_call_target="tpu_custom_call" | custom-call | tf_op jit(solution)/shard_map/chip_states/pallas_call | solution.py:239
  22.6 1.2 %collective-permute-start.2 = (bf16[528,128]{1,0:T(8,128)(2,1)}, bf16[528,128]{1,0:T(8,128)(2,1)S(1)}, u32[]{:S(2)}, u32[]{:S(2)}) collective-permute-start(bf16[528,128]{1,0:T(8,128)(2,1)} %get-tuple-element.14), channel_id=1, source_target_pairs={{0,2},{1,3},{2,0},{3,1},{4,6},{5,7},{6,4},{7,5},{8,10},{9,11},{10,... | collective-permute-start | bytes 405512 | tf_op jit(solution)/shard_map/ppermute | solution.py:197
  23.8 1.3 %collective-permute-start.3 = (bf16[528,128]{1,0:T(8,128)(2,1)}, bf16[528,128]{1,0:T(8,128)(2,1)S(1)}, u32[]{:S(2)}, u32[]{:S(2)}) collective-permute-start(bf16[528,128]{1,0:T(8,128)(2,1)} %get-tuple-element.15), channel_id=1, source_target_pairs={{0,4},{1,5},{2,6},{3,7},{4,0},{5,1},{6,2},{7,3},{8,12},{9,13},{10,... | collective-permute-start | bytes 405512 | tf_op jit(solution)/shard_map/ppermute | solution.py:197
  25.4 2.7 %collective-permute-done.2.refs_1_ = bf16[528,128]{1,0:T(8,128)(2,1)S(1)} collective-permute-done((bf16[528,128]{1,0:T(8,128)(2,1)}, bf16[528,128]{1,0:T(8,128)(2,1)S(1)}, u32[]{:S(2)}, u32[]{:S(2)}) %collective-permute-start.2) | collective-permute-done | bytes 135200 | tf_op jit(solution)/shard_map/ppermute | solution.py:197
  28.0 0.9 %collective-permute-done.3.refs_2_ = bf16[528,128]{1,0:T(8,128)(2,1)S(1)} collective-permute-done((bf16[528,128]{1,0:T(8,128)(2,1)}, bf16[528,128]{1,0:T(8,128)(2,1)S(1)}, u32[]{:S(2)}, u32[]{:S(2)}) %collective-permute-start.3) | collective-permute-done | bytes 135200 | tf_op jit(solution)/shard_map/ppermute | solution.py:197
  28.9 2.9 %collective-permute-done.4.refs_3_ = bf16[528,128]{1,0:T(8,128)(2,1)S(1)} collective-permute-done((bf16[528,128]{1,0:T(8,128)(2,1)}, bf16[528,128]{1,0:T(8,128)(2,1)S(1)}, u32[]{:S(2)}, u32[]{:S(2)}) %collective-permute-start.4) | collective-permute-done | bytes 135200 | tf_op jit(solution)/shard_map/ppermute | solution.py:197
  32.5 2.6 %span_state.1 = bf16[528,128]{1,0:T(8,128)(2,1)} custom-call(s32[2]{0:T(128)} %pad_add_fusion.idx, bf16[528,128]{1,0:T(8,128)(2,1)} %get-tuple-element.13.refs_0_, bf16[528,128]{1,0:T(8,128)(2,1)} %copy-done.3, bf16[528,128]{1,0:T(8,128)(2,1)} %copy-done.4, bf16[528,128]{1,0:T(8,128)(2,1)} %copy-done.5), custom_call_target="tpu_custom_call" | custom-call | tf_op jit(solution)/shard_map/span_state/pallas_call | solution.py:270
  35.1 3.8 %collective-permute-start.5 = (bf16[528,128]{1,0:T(8,128)(2,1)}, bf16[528,128]{1,0:T(8,128)(2,1)S(1)}, u32[]{:S(2)}, u32[]{:S(2)}) collective-permute-start(bf16[528,128]{1,0:T(8,128)(2,1)} %span_state.1), channel_id=1, source_target_pairs={{0,8},{1,9},{2,10},{3,11},{4,12},{5,13},{6,14},{7,15},{16,24},{17,... | collective-permute-start | bytes 405512 | tf_op jit(solution)/shard_map/ppermute | solution.py:200
  38.9 2.3 %collective-permute-done.5.refs_4_ = bf16[528,128]{1,0:T(8,128)(2,1)S(1)} collective-permute-done((bf16[528,128]{1,0:T(8,128)(2,1)}, bf16[528,128]{1,0:T(8,128)(2,1)S(1)}, u32[]{:S(2)}, u32[]{:S(2)}) %collective-permute-start.5) | collective-permute-done | bytes 135200 | tf_op jit(solution)/shard_map/ppermute | solution.py:200
  41.9 2.8 %chip_prefix.1 = (bf16[512,128]{1,0:T(8,128)(2,1)}, bf16[512,128]{1,0:T(8,128)(2,1)}, bf16[512,128]{1,0:T(8,128)(2,1)}, bf16[512,128]{1,0:T(8,128)(2,1)}) custom-call(s32[2]{0:T(128)} %pad_add_fusion.idx, bf16[528,128]{1,0:T(8,128)(2,1)} %get-tuple-element.13.refs_0_, bf16[528,128]{1,0:T(8,128)(2,1)} %copy-done.3, bf16[528,128]{1,0:T(8,128)(2,1)} %copy-done.4, ...), custom_call_target="tpu_custom_call" | custom-call | tf_op jit(solution)/shard_map/chip_prefix/pallas_call | solution.py:289
  44.7 4.6 %collective-permute-start.9 = (bf16[512,128]{1,0:T(8,128)(2,1)}, bf16[512,128]{1,0:T(8,128)(2,1)S(1)}, u32[]{:S(2)}, u32[]{:S(2)}) collective-permute-start(bf16[512,128]{1,0:T(8,128)(2,1)} %get-tuple-element.19), channel_id=1, source_target_pairs={{0,4},{1,5},{2,6},{3,7},{4,0},{5,1},{6,2},{7,3},{8,12},{9,13},{10,... | collective-permute-start | bytes 393224 | tf_op jit(solution)/shard_map/ppermute | solution.py:197
  49.3 1.2 %collective-permute-start.7 = (bf16[512,128]{1,0:T(8,128)(2,1)}, bf16[512,128]{1,0:T(8,128)(2,1)S(1)}, u32[]{:S(2)}, u32[]{:S(2)}) collective-permute-start(bf16[512,128]{1,0:T(8,128)(2,1)} %get-tuple-element.18), channel_id=1, source_target_pairs={{0,2},{1,3},{2,0},{3,1},{4,6},{5,7},{6,4},{7,5},{8,10},{9,11},{10,... | collective-permute-start | bytes 393224 | tf_op jit(solution)/shard_map/ppermute | solution.py:197
  50.5 1.8 %collective-permute-start.6 = (bf16[512,128]{1,0:T(8,128)(2,1)}, bf16[512,128]{1,0:T(8,128)(2,1)S(1)}, u32[]{:S(2)}, u32[]{:S(2)}) collective-permute-start(bf16[512,128]{1,0:T(8,128)(2,1)} %get-tuple-element.17.refs_0_), channel_id=1, source_target_pairs={{0,1},{1,0},{2,3},{3,2},{4,5},{5,4},{6,7},{7,6},{8,9},{9,8},{10,11... | collective-permute-start | bytes 393224 | tf_op jit(solution)/shard_map/ppermute | solution.py:197
  52.3 3.1 %collective-permute-start.10 = (bf16[512,128]{1,0:T(8,128)(2,1)S(1)}, bf16[512,128]{1,0:T(8,128)(2,1)S(1)}, u32[]{:S(2)}, u32[]{:S(2)}) collective-permute-start(bf16[512,128]{1,0:T(8,128)(2,1)S(1)} %collective-permute-done.9.refs_2_), channel_id=1, source_target_pairs={{0,1},{1,0},{2,3},{3,2},{4,5},{5,4},{6,7},{7,6},{8,9},{9,8},{10,11... | collective-permute-start | bytes 393224 | tf_op jit(solution)/shard_map/ppermute | solution.py:197
  55.4 1.6 %collective-permute-start.12 = (bf16[512,128]{1,0:T(8,128)(2,1)S(1)}, bf16[512,128]{1,0:T(8,128)(2,1)S(1)}, u32[]{:S(2)}, u32[]{:S(2)}) collective-permute-start(bf16[512,128]{1,0:T(8,128)(2,1)S(1)} %collective-permute-done.11.refs_3_), channel_id=1, source_target_pairs={{0,1},{1,0},{2,3},{3,2},{4,5},{5,4},{6,7},{7,6},{8,9},{9,8},{10,11... | collective-permute-start | bytes 393224 | tf_op jit(solution)/shard_map/ppermute | solution.py:197
  57.0 1.3 %collective-permute-start.8 = (bf16[512,128]{1,0:T(8,128)(2,1)S(1)}, bf16[512,128]{1,0:T(8,128)(2,1)S(1)}, u32[]{:S(2)}, u32[]{:S(2)}) collective-permute-start(bf16[512,128]{1,0:T(8,128)(2,1)S(1)} %collective-permute-done.7.refs_1_), channel_id=1, source_target_pairs={{0,1},{1,0},{2,3},{3,2},{4,5},{5,4},{6,7},{7,6},{8,9},{9,8},{10,11... | collective-permute-start | bytes 393224 | tf_op jit(solution)/shard_map/ppermute | solution.py:197
  58.3 9.2 %intra.1.intra_ref = f32[128,4096]{1,0:T(8,128)} custom-call(bf16[128,4096]{1,0:T(8,128)(2,1)} %q_ref.5, bf16[128,4096]{1,0:T(8,128)(2,1)} %k_ref.5, bf16[8,4096]{1,0:T(8,128)(2,1)} %copy-done.1, bf16[128,4096]{1,0:T(8,128)(2,1)} %v_ref.5, f32[4,4096]{1,0:T(4,128)} %w_ref.5, f32[8,8,128]{2,1,0:T(8,128)} %pad_maximum_fusion.cum_ref), custom_call_target="tpu_custom_call" | custom-call | tf_op jit(solution)/shard_map/intra/pallas_call | solution.py:253
  67.6 5.6 %out_mine.1.refs_5_ = bf16[128,4096]{1,0:T(8,128)(2,1)} custom-call(s32[2]{0:T(128)} %pad_add_fusion.idx, bf16[128,4096]{1,0:T(8,128)(2,1)} %q_ref.5, f32[128,4096]{1,0:T(8,128)} %intra.1.intra_ref, f32[8,8,128]{2,1,0:T(8,128)} %pad_maximum_fusion.cum_ref, f32[1,4096]{1,0:T(1,128)} %bitcast.9, bf16[512,128]{1,0:T(8,128)(2,1)} %get-tuple-element.17.refs_0_, ...), custom_call_target="tpu_custom_call" | custom-call | tf_op jit(solution)/shard_map/out_mine/pallas_call | solution.py:314
  74.8 5.6 %out_other.1 = bf16[128,4096]{1,0:T(8,128)(2,1)} custom-call(s32[2]{0:T(128)} %pad_add_fusion.idx, bf16[128,4096]{1,0:T(8,128)(2,1)} %q_ref.5, f32[128,4096]{1,0:T(8,128)} %intra.1.intra_ref, f32[8,8,128]{2,1,0:T(8,128)} %pad_maximum_fusion.cum_ref, f32[1,4096]{1,0:T(1,128)} %bitcast.10, ...), custom_call_target="tpu_custom_call", output_to_operand_aliasing={{}: (10, {})} | custom-call | tf_op jit(solution)/shard_map/out_other/pallas_call | solution.py:314
  (50 shorter events, 6.9 us)
Async XLA Ops:
  0.8 7.2 %collective-permute-start = (bf16[8,4096]{1,0:T(8,128)(2,1)S(1)}, bf16[8,4096]{1,0:T(8,128)(2,1)S(1)}, u32[]{:S(2)}, u32[]{:S(2)}) collective-permute-start(bf16[8,4096]{1,0:T(8,128)(2,1)S(1)} %slice.6), channel_id=1, source_target_pairs={{0,1},{1,2},{2,3},{3,4},{4,5},{5,6},{6,7},{7,8},{8,9},{9,10},{10,1... | collective-permute-start | bytes 196616 | tf_op jit(solution)/shard_map/ppermute | solution.py:200
  13.6 5.4 %collective-permute-start.1 = (bf16[4,528,128]{2,1,0:T(8,128)(2,1)}, bf16[4,528,128]{2,1,0:T(8,128)(2,1)S(1)}, u32[]{:S(2)}, u32[]{:S(2)}) collective-permute-start(bf16[4,528,128]{2,1,0:T(8,128)(2,1)} %states_other.1), channel_id=1, source_target_pairs={{0,1},{1,0},{2,3},{3,2},{4,5},{5,4},{6,7},{7,6},{8,9},{9,8},{10,11... | collective-permute-start | bytes 1622024 | tf_op jit(solution)/shard_map/ppermute | solution.py:197
  18.5 54.7 %collective-permute-start.13 = (bf16[4,528,128]{2,1,0:T(8,128)(2,1)}, bf16[4,528,128]{2,1,0:T(8,128)(2,1)S(1)}, u32[]{:S(2)}, u32[]{:S(2)}) collective-permute-start(bf16[4,528,128]{2,1,0:T(8,128)(2,1)} %states_mine.1.own_ref), channel_id=1, source_target_pairs={{0,1},{1,0},{2,3},{3,2},{4,5},{5,4},{6,7},{7,6},{8,9},{9,8},{10,11... | collective-permute-start | bytes 1622024 | tf_op jit(solution)/shard_map/ppermute | solution.py:197
  19.0 0.8 %copy-start = (bf16[4,528,128]{2,1,0:T(8,128)(2,1)}, bf16[4,528,128]{2,1,0:T(8,128)(2,1)S(1)}, u32[]{:S(2)}) copy-start(bf16[4,528,128]{2,1,0:T(8,128)(2,1)S(1)} %collective-permute-done.1.got_ref.refs_4_) | copy-start | bytes 1622020
  22.6 5.4 %collective-permute-start.2 = (bf16[528,128]{1,0:T(8,128)(2,1)}, bf16[528,128]{1,0:T(8,128)(2,1)S(1)}, u32[]{:S(2)}, u32[]{:S(2)}) collective-permute-start(bf16[528,128]{1,0:T(8,128)(2,1)} %get-tuple-element.14), channel_id=1, source_target_pairs={{0,2},{1,3},{2,0},{3,1},{4,6},{5,7},{6,4},{7,5},{8,10},{9,11},{10,... | collective-permute-start | bytes 405512 | tf_op jit(solution)/shard_map/ppermute | solution.py:197
  23.8 5.1 %collective-permute-start.3 = (bf16[528,128]{1,0:T(8,128)(2,1)}, bf16[528,128]{1,0:T(8,128)(2,1)S(1)}, u32[]{:S(2)}, u32[]{:S(2)}) collective-permute-start(bf16[528,128]{1,0:T(8,128)(2,1)} %get-tuple-element.15), channel_id=1, source_target_pairs={{0,4},{1,5},{2,6},{3,7},{4,0},{5,1},{6,2},{7,3},{8,12},{9,13},{10,... | collective-permute-start | bytes 405512 | tf_op jit(solution)/shard_map/ppermute | solution.py:197
  25.1 6.7 %collective-permute-start.4 = (bf16[528,128]{1,0:T(8,128)(2,1)}, bf16[528,128]{1,0:T(8,128)(2,1)S(1)}, u32[]{:S(2)}, u32[]{:S(2)}) collective-permute-start(bf16[528,128]{1,0:T(8,128)(2,1)} %get-tuple-element.16), channel_id=1, source_target_pairs={{0,6},{1,7},{2,4},{3,5},{4,2},{5,3},{6,0},{7,1},{8,14},{9,15},{10,... | collective-permute-start | bytes 405512 | tf_op jit(solution)/shard_map/ppermute | solution.py:197
  28.0 3.8 %copy-start.3 = (bf16[528,128]{1,0:T(8,128)(2,1)}, bf16[528,128]{1,0:T(8,128)(2,1)S(1)}, u32[]{:S(2)}) copy-start(bf16[528,128]{1,0:T(8,128)(2,1)S(1)} %collective-permute-done.2.refs_1_) | copy-start | bytes 405508
  28.9 2.9 %copy-start.4 = (bf16[528,128]{1,0:T(8,128)(2,1)}, bf16[528,128]{1,0:T(8,128)(2,1)S(1)}, u32[]{:S(2)}) copy-start(bf16[528,128]{1,0:T(8,128)(2,1)S(1)} %collective-permute-done.3.refs_2_) | copy-start | bytes 405508
  35.1 6.1 %collective-permute-start.5 = (bf16[528,128]{1,0:T(8,128)(2,1)}, bf16[528,128]{1,0:T(8,128)(2,1)S(1)}, u32[]{:S(2)}, u32[]{:S(2)}) collective-permute-start(bf16[528,128]{1,0:T(8,128)(2,1)} %span_state.1), channel_id=1, source_target_pairs={{0,8},{1,9},{2,10},{3,11},{4,12},{5,13},{6,14},{7,15},{16,24},{17,... | collective-permute-start | bytes 405512 | tf_op jit(solution)/shard_map/ppermute | solution.py:200
  44.7 7.6 %collective-permute-start.9 = (bf16[512,128]{1,0:T(8,128)(2,1)}, bf16[512,128]{1,0:T(8,128)(2,1)S(1)}, u32[]{:S(2)}, u32[]{:S(2)}) collective-permute-start(bf16[512,128]{1,0:T(8,128)(2,1)} %get-tuple-element.19), channel_id=1, source_target_pairs={{0,4},{1,5},{2,6},{3,7},{4,0},{5,1},{6,2},{7,3},{8,12},{9,13},{10,... | collective-permute-start | bytes 393224 | tf_op jit(solution)/shard_map/ppermute | solution.py:197
  49.3 6.1 %collective-permute-start.11 = (bf16[512,128]{1,0:T(8,128)(2,1)}, bf16[512,128]{1,0:T(8,128)(2,1)S(1)}, u32[]{:S(2)}, u32[]{:S(2)}) collective-permute-start(bf16[512,128]{1,0:T(8,128)(2,1)} %get-tuple-element.20), channel_id=1, source_target_pairs={{0,6},{1,7},{2,4},{3,5},{4,2},{5,3},{6,0},{7,1},{8,14},{9,15},{10,... | collective-permute-start | bytes 393224 | tf_op jit(solution)/shard_map/ppermute | solution.py:197
  49.3 7.7 %collective-permute-start.7 = (bf16[512,128]{1,0:T(8,128)(2,1)}, bf16[512,128]{1,0:T(8,128)(2,1)S(1)}, u32[]{:S(2)}, u32[]{:S(2)}) collective-permute-start(bf16[512,128]{1,0:T(8,128)(2,1)} %get-tuple-element.18), channel_id=1, source_target_pairs={{0,2},{1,3},{2,0},{3,1},{4,6},{5,7},{6,4},{7,5},{8,10},{9,11},{10,... | collective-permute-start | bytes 393224 | tf_op jit(solution)/shard_map/ppermute | solution.py:197
  50.5 22.7 %collective-permute-start.6 = (bf16[512,128]{1,0:T(8,128)(2,1)}, bf16[512,128]{1,0:T(8,128)(2,1)S(1)}, u32[]{:S(2)}, u32[]{:S(2)}) collective-permute-start(bf16[512,128]{1,0:T(8,128)(2,1)} %get-tuple-element.17.refs_0_), channel_id=1, source_target_pairs={{0,1},{1,0},{2,3},{3,2},{4,5},{5,4},{6,7},{7,6},{8,9},{9,8},{10,11... | collective-permute-start | bytes 393224 | tf_op jit(solution)/shard_map/ppermute | solution.py:197
  52.3 15.3 %copy-start.8 = (bf16[512,128]{1,0:T(8,128)(2,1)}, bf16[512,128]{1,0:T(8,128)(2,1)S(1)}, u32[]{:S(2)}) copy-start(bf16[512,128]{1,0:T(8,128)(2,1)S(1)} %collective-permute-done.9.refs_2_) | copy-start | bytes 393220
  52.3 20.9 %collective-permute-start.10 = (bf16[512,128]{1,0:T(8,128)(2,1)S(1)}, bf16[512,128]{1,0:T(8,128)(2,1)S(1)}, u32[]{:S(2)}, u32[]{:S(2)}) collective-permute-start(bf16[512,128]{1,0:T(8,128)(2,1)S(1)} %collective-permute-done.9.refs_2_), channel_id=1, source_target_pairs={{0,1},{1,0},{2,3},{3,2},{4,5},{5,4},{6,7},{7,6},{8,9},{9,8},{10,11... | collective-permute-start | bytes 393224 | tf_op jit(solution)/shard_map/ppermute | solution.py:197
  55.4 12.2 %copy-start.9 = (bf16[512,128]{1,0:T(8,128)(2,1)}, bf16[512,128]{1,0:T(8,128)(2,1)S(1)}, u32[]{:S(2)}) copy-start(bf16[512,128]{1,0:T(8,128)(2,1)S(1)} %collective-permute-done.11.refs_3_) | copy-start | bytes 393220
  55.4 17.9 %collective-permute-start.12 = (bf16[512,128]{1,0:T(8,128)(2,1)S(1)}, bf16[512,128]{1,0:T(8,128)(2,1)S(1)}, u32[]{:S(2)}, u32[]{:S(2)}) collective-permute-start(bf16[512,128]{1,0:T(8,128)(2,1)S(1)} %collective-permute-done.11.refs_3_), channel_id=1, source_target_pairs={{0,1},{1,0},{2,3},{3,2},{4,5},{5,4},{6,7},{7,6},{8,9},{9,8},{10,11... | collective-permute-start | bytes 393224 | tf_op jit(solution)/shard_map/ppermute | solution.py:197
  57.0 10.6 %copy-start.10 = (bf16[512,128]{1,0:T(8,128)(2,1)}, bf16[512,128]{1,0:T(8,128)(2,1)S(1)}, u32[]{:S(2)}) copy-start(bf16[512,128]{1,0:T(8,128)(2,1)S(1)} %collective-permute-done.7.refs_1_) | copy-start | bytes 393220
  57.0 16.2 %collective-permute-start.8 = (bf16[512,128]{1,0:T(8,128)(2,1)S(1)}, bf16[512,128]{1,0:T(8,128)(2,1)S(1)}, u32[]{:S(2)}, u32[]{:S(2)}) collective-permute-start(bf16[512,128]{1,0:T(8,128)(2,1)S(1)} %collective-permute-done.7.refs_1_), channel_id=1, source_target_pairs={{0,1},{1,0},{2,3},{3,2},{4,5},{5,4},{6,7},{7,6},{8,9},{9,8},{10,11... | collective-permute-start | bytes 393224 | tf_op jit(solution)/shard_map/ppermute | solution.py:197
  73.2 0.8 %copy-start.2 = (bf16[4,528,128]{2,1,0:T(8,128)(2,1)}, bf16[4,528,128]{2,1,0:T(8,128)(2,1)S(1)}, u32[]{:S(2)}) copy-start(bf16[4,528,128]{2,1,0:T(8,128)(2,1)S(1)} %collective-permute-done.13.refs_4_) | copy-start | bytes 1622020
  73.2 0.8 %copy-start.7 = (bf16[512,128]{1,0:T(8,128)(2,1)}, bf16[512,128]{1,0:T(8,128)(2,1)S(1)}, u32[]{:S(2)}) copy-start(bf16[512,128]{1,0:T(8,128)(2,1)S(1)} %collective-permute-done.6.refs_0_) | copy-start | bytes 393220
  73.2 0.9 %copy-start.11 = (bf16[512,128]{1,0:T(8,128)(2,1)}, bf16[512,128]{1,0:T(8,128)(2,1)S(1)}, u32[]{:S(2)}) copy-start(bf16[512,128]{1,0:T(8,128)(2,1)S(1)} %collective-permute-done.10.refs_2_) | copy-start | bytes 393220
  73.3 0.9 %copy-start.12 = (bf16[512,128]{1,0:T(8,128)(2,1)}, bf16[512,128]{1,0:T(8,128)(2,1)S(1)}, u32[]{:S(2)}) copy-start(bf16[512,128]{1,0:T(8,128)(2,1)S(1)} %collective-permute-done.12.refs_3_) | copy-start | bytes 393220
  (4 other events, 2.6 us)

commit v2 on v0

v2 whole, which is shorter than its diff:
```python
import functools

import jax
import jax.numpy as jnp
from jax import lax
from jax.experimental import pallas as pl
from jax.experimental.pallas import tpu as pltpu
from jax.sharding import PartitionSpec as P

F32 = jnp.float32
BF16 = jnp.bfloat16
CHIPS = 4
SPAN = 2 * CHIPS
HALO = 8
PARTS = 16
VMEM = pl.BlockSpec(memory_space=pltpu.VMEM)
ANY = pl.BlockSpec(memory_space=pl.ANY)


def position():
    me = lax.axis_index("ctx")
    return me & 1, (me >> 1) & (CHIPS - 1)


def head_group(mine, g):
    core, chip = position()
    return (core if mine else 1 - core) * CHIPS + (chip ^ g)


def columns(block, offset, size):
    return pl.ds(pl.multiple_of(block + offset, size), size)


def call(kernel, name, out_shape, *args, scratch=(), in_specs=None, out_specs=VMEM, **options):
    if in_specs is None:
        in_specs = [VMEM] * len(args)
    args = [
        pltpu.with_memory_space_constraint(x, pltpu.VMEM) if s is VMEM else x
        for x, s in zip(args, in_specs)
    ]
    return pl.pallas_call(
        kernel,
        out_shape=out_shape,
        in_specs=in_specs,
        out_specs=out_specs,
        scratch_shapes=list(scratch),
        name=name,
        compiler_params=pltpu.CompilerParams(vmem_limit_bytes=6 << 20),
        **options,
    )(*args)


def tail_kernel(k_ref, out_ref, sem):
    rows = k_ref.shape[0]
    copy = pltpu.make_async_copy(k_ref.at[rows - HALO : rows, :], out_ref, sem)
    copy.start()
    copy.wait()


def cum_kernel(heads, decay_ref, out_ref):
    x = decay_ref[...]
    rows = x.shape[1]
    lane = lax.broadcasted_iota(jnp.int32, x.shape, 1)
    step = 1
    while step < rows:
        x = x + jnp.where(lane >= step, pltpu.roll(x, step, 1), 0.0)
        step *= 2
    total = jnp.broadcast_to(x[:, rows - 1 : rows], x.shape)
    for b in range(out_ref.shape[0]):
        these = slice(b * heads, (b + 1) * heads)
        out_ref[b, 0:heads, :] = x[these]
        out_ref[b, heads : 2 * heads, :] = total[these]


def three_parts(x):
    hi = x.astype(BF16)
    rest = x - hi.astype(F32)
    mid = rest.astype(BF16)
    low = (rest - mid.astype(F32)).astype(BF16)
    return hi, mid, low


def put_decay(out, decays, heads, size):
    base = heads * size
    parts = [p.astype(F32) for p in three_parts(decays)]
    spare = jnp.zeros((PARTS - 3 * heads, decays.shape[1]), F32)
    out[base : base + PARTS, :] = jnp.concatenate(parts + [spare], 0).astype(BF16)


def get_decay(packet, heads, size):
    base = heads * size
    tail = packet[base : base + PARTS, :].astype(F32)
    return tail[0:heads] + tail[heads : 2 * heads] + tail[2 * heads : 3 * heads]


def conv_keys(k_ref, halo_ref, w_ref, ext, cols):
    rows = k_ref.shape[0]
    ext[0:HALO, :] = halo_ref[:, cols].astype(F32)
    ext[HALO : HALO + rows, :] = k_ref[:, cols].astype(F32)
    total = None
    for j in range(w_ref.shape[0]):
        term = w_ref[j : j + 1, cols] * ext[HALO - j : HALO - j + rows, :]
        total = term if total is None else total + term
    return total.astype(BF16)


def state_kernel(mine, heads, size, k_ref, halo_ref, v_ref, w_ref, cum_ref, out_ref, ext, held):
    for g in range(CHIPS):
        b = head_group(mine, g)
        cum = cum_ref[b]
        ending = jnp.exp(cum[heads : 2 * heads] - cum[0:heads]).T
        for j in range(heads):
            cols = columns(b * heads * size, j * size, size)
            key_conv = conv_keys(k_ref, halo_ref, w_ref, ext.at[j], cols)
            held[g * heads + j] = (key_conv.astype(F32) * ending[:, j : j + 1]).astype(BF16)
    for g in range(CHIPS):
        b = head_group(mine, g)
        for j in range(heads):
            cols = columns(b * heads * size, j * size, size)
            state = lax.dot_general(
                v_ref[:, cols], held[g * heads + j], (((0,), (0,)), ((), ())),
                preferred_element_type=F32,
            )
            out_ref[g, j * size : (j + 1) * size, :] = state.astype(BF16)
        put_decay(out_ref.at[g], jnp.exp(cum_ref[b][heads : 2 * heads]), heads, size)


def intra_kernel(
    mine, heads, size, q_ref, k_ref, halo_ref, v_ref, w_ref, cum_ref, out_ref, ext, held
):
    rows = q_ref.shape[0]
    causal = lax.broadcasted_iota(jnp.int32, (rows, rows), 0) >= lax.broadcasted_iota(
        jnp.int32, (rows, rows), 1
    )
    for g in range(CHIPS):
        b = head_group(mine, g)
        cum = cum_ref[b][0:heads]
        cum_col = cum.T
        for j in range(heads):
            cols = columns(b * heads * size, j * size, size)
            key_conv = conv_keys(k_ref, halo_ref, w_ref, ext.at[j], cols)
            scores = lax.dot_general(
                q_ref[:, cols], key_conv, (((1,), (1,)), ((), ())), preferred_element_type=F32
            )
            spread = cum_col[:, j : j + 1] - cum[j : j + 1]
            weights = jnp.where(causal, scores * jnp.exp(jnp.where(causal, spread, 0.0)), 0.0)
            held[g * heads + j] = weights.astype(BF16)
    for g in range(CHIPS):
        b = head_group(mine, g)
        for j in range(heads):
            cols = columns(b * heads * size, j * size, size)
            out_ref[g * heads + j] = jnp.dot(
                held[g * heads + j], v_ref[:, cols], preferred_element_type=F32
            )


def chip_kernel(heads, size, own_ref, got_ref, out_ref):
    core, _ = position()
    first = core == 0
    for g in range(CHIPS):
        own_decay = get_decay(own_ref.at[g], heads, size)
        got_decay = get_decay(got_ref.at[g], heads, size)
        own_by = jnp.where(first, got_decay, 1.0)
        got_by = jnp.where(first, 1.0, own_decay)
        for j in range(heads):
            rows = slice(j * size, (j + 1) * size)
            out_ref[g, rows, :] = (
                own_ref[g, rows, :].astype(F32) * own_by[j : j + 1]
                + got_ref[g, rows, :].astype(F32) * got_by[j : j + 1]
            ).astype(BF16)
        put_decay(out_ref.at[g], own_decay * got_decay, heads, size)


def in_order(packets, held):
    _, chip = position()
    for g in range(CHIPS):
        held[chip ^ g] = packets[g][...]


def span_kernel(heads, size, *refs):
    packets, out_ref, held = refs[:CHIPS], refs[CHIPS], refs[CHIPS + 1]
    in_order(packets, held)
    decays = [get_decay(held.at[b], heads, size) for b in range(CHIPS)]
    for j in range(heads):
        rows = slice(j * size, (j + 1) * size)
        acc = held[0, rows, :].astype(F32)
        for b in range(1, CHIPS):
            acc = acc * decays[b][j : j + 1] + held[b, rows, :].astype(F32)
        out_ref[rows, :] = acc.astype(BF16)
    whole = decays[0]
    for b in range(1, CHIPS):
        whole = whole * decays[b]
    put_decay(out_ref, whole, heads, size)


def spread_kernel(heads, size, *refs):
    packets, before, out_ref, held = refs[:CHIPS], refs[CHIPS], refs[CHIPS + 1], refs[CHIPS + 2]
    _, chip = position()
    in_order(packets, held)
    decays = [get_decay(held.at[b], heads, size) for b in range(CHIPS)]
    for j in range(heads):
        rows = slice(j * size, (j + 1) * size)
        acc = before[rows, :].astype(F32)
        out_ref[chip, rows, :] = before[rows, :]
        for b in range(1, CHIPS):
            acc = acc * decays[b - 1][j : j + 1] + held[b - 1, rows, :].astype(F32)
            out_ref[chip ^ b, rows, :] = acc.astype(BF16)


def out_kernel(mine, heads, size, q_ref, intra_ref, cum_ref, gain_ref, sib_ref, *refs):
    prefixes, (out_ref, mixed_ref, done_ref, sems) = refs[:CHIPS], refs[-4:]
    core, _ = position()
    second = core == 1
    for g in range(CHIPS):
        b = head_group(mine, g)
        started = jnp.exp(cum_ref[b][0:heads]).T
        sib_decay = get_decay(sib_ref.at[g], heads, size)
        by = jnp.where(second, sib_decay, 1.0)
        for j in range(heads):
            cols = columns(b * heads * size, j * size, size)
            rows = slice(j * size, (j + 1) * size)
            sib = jnp.where(second, sib_ref[g, rows, :].astype(F32), 0.0)
            prefix = prefixes[g][rows, :].astype(F32) * by[j : j + 1] + sib
            inter = lax.dot_general(
                q_ref[:, cols], prefix.astype(BF16), (((1,), (1,)), ((), ())),
                preferred_element_type=F32,
            )
            mixed_ref[g * heads + j] = intra_ref[g * heads + j] + inter * started[:, j : j + 1]
    copies = []
    for g in range(CHIPS):
        b = head_group(mine, g)
        for j in range(heads):
            cols = columns(b * heads * size, j * size, size)
            mixed = mixed_ref[g * heads + j]
            scale = lax.rsqrt(jnp.mean(mixed * mixed, axis=1, keepdims=True) + 1e-05)
            done_ref[g, :, j * size : (j + 1) * size] = (
                mixed * scale * gain_ref[:, cols]
            ).astype(BF16)
        wide = columns(b * heads * size, 0, heads * size)
        copies.append(pltpu.make_async_copy(done_ref.at[g], out_ref.at[:, wide], sems.at[g]))
        copies[-1].start()
    for copy in copies:
        copy.wait()


def join_spans(earlier, later, heads, size):
    base = heads * size

    def decay(x):
        tail = x[base:].astype(F32)
        return tail[0:heads] + tail[heads : 2 * heads] + tail[2 * heads : 3 * heads]

    by = decay(later)
    state = (
        by[:, None, :] * earlier[:base].astype(F32).reshape(heads, size, -1)
        + later[:base].astype(F32).reshape(heads, size, -1)
    ).reshape(base, -1)
    parts = three_parts(by * decay(earlier))
    return jnp.concatenate([state.astype(BF16), *parts, later[base + 3 * heads :]], 0)


def on_device(queries, key_input, value_input, log_decay, conv_weight, norm_gain):
    rows, width = queries.shape
    head_count = log_decay.shape[1]
    size = width // head_count
    heads = head_count // SPAN
    half = CHIPS * heads
    packet = heads * size + PARTS
    n = lax.axis_size("ctx")

    def swap(x, mask):
        return lax.ppermute(x, "ctx", [(i, i ^ mask) for i in range(n)])

    def shift(x, by):
        return lax.ppermute(x, "ctx", [(i, i + by) for i in range(n - by)])

    tail = call(
        tail_kernel,
        "tail",
        pltpu.VMEM((HALO, width), BF16),
        key_input,
        in_specs=[ANY],
        scratch=[pltpu.SemaphoreType.DMA(())],
    )
    halo = shift(tail, 1)
    cum = call(
        functools.partial(cum_kernel, heads),
        "cum",
        pltpu.VMEM((SPAN, 2 * heads, rows), F32),
        log_decay.T,
    )
    gain = norm_gain.reshape(1, width)
    ext = pltpu.VMEM((heads, rows + HALO, size), F32)
    held = pltpu.VMEM((half, rows, size), BF16)

    def states(mine):
        return call(
            functools.partial(state_kernel, mine, heads, size),
            "states_mine" if mine else "states_other",
            pltpu.VMEM((CHIPS, packet, size), BF16),
            key_input, halo, value_input, conv_weight, cum,
            scratch=[ext, pltpu.VMEM((half, rows, size), BF16)],
        )

    def intra_part(mine, q):
        return call(
            functools.partial(intra_kernel, mine, heads, size),
            "intra_mine" if mine else "intra_other",
            pltpu.VMEM((half, rows, size), F32),
            q, key_input, halo, value_input, conv_weight, cum,
            scratch=[ext, held],
        )

    theirs = states(False)
    got = swap(theirs, 1)
    mine = states(True)
    got_late = swap(mine, 1)

    chip_states = call(
        functools.partial(chip_kernel, heads, size),
        "chip_states",
        pltpu.VMEM((CHIPS, packet, size), BF16),
        mine, got,
    )
    packets = [chip_states[0]] + [swap(chip_states[g], 2 * g) for g in range(1, CHIPS)]
    q_after, chip_states = lax.optimization_barrier((queries, chip_states))
    intra_mine = intra_part(True, q_after)
    *packets, intra_mine = lax.optimization_barrier((*packets, intra_mine))

    order = pltpu.VMEM((CHIPS, packet, size), BF16)
    span = call(
        functools.partial(span_kernel, heads, size),
        "span_state",
        pltpu.VMEM((packet, size), BF16),
        *packets,
        scratch=[order],
    )
    before = shift(span, SPAN)
    reach = 1
    while reach < n // SPAN - 1:
        before = join_spans(shift(before, SPAN * reach), before, heads, size)
        reach *= 2
    q_after, span = lax.optimization_barrier((queries, span))
    intra_other = intra_part(False, q_after)
    before, intra_other = lax.optimization_barrier((before, intra_other))

    chip_prefix = call(
        functools.partial(spread_kernel, heads, size),
        "chip_prefix",
        pltpu.VMEM((CHIPS, heads * size, size), BF16),
        *packets, before,
        scratch=[order],
    )
    own = [chip_prefix[0]] + [swap(chip_prefix[g], 2 * g) for g in range(1, CHIPS)]
    other = [swap(x, 1) for x in own]

    def output(mine, intra, sibling, prefixes, result):
        extra = [] if result is None else [result]
        return call(
            functools.partial(out_kernel, mine, heads, size),
            "out_mine" if mine else "out_other",
            jax.ShapeDtypeStruct((rows, width), BF16),
            queries, intra, cum, gain, sibling, *prefixes, *extra,
            in_specs=[VMEM] * (5 + CHIPS) + [ANY] * len(extra),
            out_specs=ANY,
            input_output_aliases={5 + CHIPS: 0} if extra else {},
            scratch=[
                pltpu.VMEM((half, rows, size), F32),
                pltpu.VMEM((CHIPS, rows, heads * size), BF16),
                pltpu.SemaphoreType.DMA((CHIPS,)),
            ],
        )

    result = output(True, intra_mine, got, own, None)
    return output(False, intra_other, got_late, other, result)


def solution(mesh):
    rows = P(("groups", "ctx"), None)
    return jax.shard_map(
        on_device,
        mesh=mesh,
        in_specs=(rows, rows, rows, rows, P(), P()),
        out_specs=rows,
        check_vma=False,
    )
```

time: 149 us -> 46.6 us (0.31)
  waiting for transfers between devices: 64.2 us -> 6.63 us
  local copies, waits for them, and re-layouts: 28.5 us -> 3.26 us
  other arithmetic: 17.8 us -> 0 us
  matrix products: 10.2 us -> 0 us
  Pallas kernels: 0 us -> 8.82 us
    all_to_all x3 -> x0, waiting for transfers between devices: 64.2 us -> none  [the longest x1 41.3 us: on_device(): lax.all_to_all(stacked, 'ctx', split_axis=1, concat_axis=0, tiled=True)]
    ppermute x1 -> x14, starting transfers between devices: 4.54 us -> 27.4 us  [the longest x12 18.6 us: swap(): return lax.ppermute(x, 'ctx', [(i, i ^ mask) for i in range(n)])]
    all_to_all x3 -> x0, starting transfers between devices: 21.9 us -> none  [the longest x1 10.9 us: on_device(): lax.all_to_all(shared.astype(jnp.bfloat16), 'ctx', split_axis=0, concat_a...]
    pad x4 -> x0, local copies, waits for them, and re-layouts: 12.2 us -> none  [block_prefix(): carried = lax.associative_scan(join_rows, (rates, states), axis=0)]
    dot_general x3 -> x0, matrix products: 10.2 us -> none  [the longest x1 4.9 us: on_device(): jnp.einsum('hts,shd->thd', weights, value_heads, preferred_element_type=j...]
    pallas_call x0 -> x11, Pallas kernels: none -> 8.82 us  [call(): pl.pallas_call(kernel, out_shape=out_shape, in_specs=in_specs, out_specs=...]
    add x8 -> x0, other arithmetic: 7.34 us -> none  [the longest x3 4.9 us: block_prefix(): carried = lax.associative_scan(join_rows, (rates, states), axis=0)]
    slice x15 -> x0, local copies, waits for them, and re-layouts: 6.96 us -> none  [the longest x1 4.02 us: block_prefix(): return jnp.concatenate([jnp.zeros_like(inclusive[:1]), inclusive[:-1]], 0)]
  transfers between devices with their start and end apart: 4 -> 14, of which waited for: 2 -> 5; matrix products, arithmetic and copies ran while one was open for 7% -> 0% of each run, Pallas kernels for 0% -> 12%
where the time goes in v2:
time: 46.6 us; the launch traced here: 46.3 us
  starting transfers between devices  27.4 us (59%)
  Pallas kernels  8.82 us (19%)
  waiting for transfers between devices  6.63 us (14%)
  local copies, waits for them, and re-layouts  3.26 us (7%)
    ppermute x12, starting transfers between devices, swap(): return lax.ppermute(x, 'ctx', [(i, i ^ mask) for i in range(n)])  18.6 us
    pallas_call x11, Pallas kernels, call(): pl.pallas_call(kernel, out_shape=out_shape, in_specs=in_specs, out_specs=...  8.82 us
    ppermute x2, starting transfers between devices, shift(): return lax.ppermute(x, 'ctx', [(i, i + by) for i in range(n - by)])  8.73 us
    ppermute x12, waiting for transfers between devices, swap(): return lax.ppermute(x, 'ctx', [(i, i ^ mask) for i in range(n)])  6.59 us
    unnamed x16, local copies, waits for them, and re-layouts  3.19 us
  transfers between devices with their start and end apart: 14, of which 5 were waited for; matrix products, arithmetic and copies ran while one was open for 0% of the time, Pallas kernels for 12%

profile of v2, /device:TPU:1, one launch (start us, length us, event | category | flops | bytes accessed | tf_op | source)
XLA Modules:
  0.0 46.3 jit_solution(14570211855751819376)
XLA Ops:
  0.0 1.2 %copy-done = bf16[128,4096]{1,0:T(8,128)(2,1)S(1)} copy-done((bf16[128,4096]{1,0:T(8,128)(2,1)S(1)}, bf16[128,4096]{1,0:T(8,128)(2,1)}, u32[]{:S(2)}) %copy-start) | copy-done | bytes 1048600
  1.3 4.7 %collective-permute-start = (bf16[8,4096]{1,0:T(8,128)(2,1)S(1)}, bf16[8,4096]{1,0:T(8,128)(2,1)S(1)}, u32[]{:S(2)}, u32[]{:S(2)}) collective-permute-start(bf16[8,4096]{1,0:T(8,128)(2,1)S(1)} %tail.1), channel_id=1, source_target_pairs={{0,1},{1,2},{2,3},{3,4},{4,5},{5,6},{6,7},{7,8},{8,9},{9,10},{10,1... | collective-permute-start | bytes 196616 | tf_op jit(solution)/shard_map/ppermute | solution.py:275
  6.0 0.7 %copy-done.7 = f32[128,32]{0,1:T(8,128)S(1)} copy-done((f32[128,32]{0,1:T(8,128)S(1)}, f32[128,32]{0,1:T(8,128)}, u32[]{:S(2)}) %copy-start.7) | copy-done | bytes 16408
  7.3 1.2 %copy-done.2 = bf16[128,4096]{1,0:T(8,128)(2,1)S(1)} copy-done((bf16[128,4096]{1,0:T(8,128)(2,1)S(1)}, bf16[128,4096]{1,0:T(8,128)(2,1)}, u32[]{:S(2)}) %copy-start.2) | copy-done | bytes 1048600
  8.5 1.0 %states_other.1 = bf16[4,528,128]{2,1,0:T(8,128)(2,1)S(1)} custom-call(bf16[128,4096]{1,0:T(8,128)(2,1)S(1)} %copy-done.1, bf16[8,4096]{1,0:T(8,128)(2,1)S(1)} %collective-permute-done.halo_ref, bf16[128,4096]{1,0:T(8,128)(2,1)S(1)} %copy-done.2, f32[4,4096]{1,0:T(4,128)S(1)} %copy-done.5, f32[8,8,128]{2,1,0:T(8,128)S(1)} %cum.1.cum_ref), custom_call_target="tpu_custom_call" | custom-call | tf_op jit(solution)/shard_map/states_other/pallas_call | solution.py:41
  9.6 1.0 %states_mine.1.own_ref = bf16[4,528,128]{2,1,0:T(8,128)(2,1)S(1)} custom-call(bf16[128,4096]{1,0:T(8,128)(2,1)S(1)} %copy-done.1, bf16[8,4096]{1,0:T(8,128)(2,1)S(1)} %collective-permute-done.halo_ref, bf16[128,4096]{1,0:T(8,128)(2,1)S(1)} %copy-done.2, f32[4,4096]{1,0:T(4,128)S(1)} %copy-done.5, f32[8,8,128]{2,1,0:T(8,128)S(1)} %cum.1.cum_ref), custom_call_target="tpu_custom_call" | custom-call | tf_op jit(solution)/shard_map/states_mine/pallas_call | solution.py:41
  10.7 0.9 %collective-permute-done.1.got_ref.sib_ref = bf16[4,528,128]{2,1,0:T(8,128)(2,1)S(1)} collective-permute-done((bf16[4,528,128]{2,1,0:T(8,128)(2,1)S(1)}, bf16[4,528,128]{2,1,0:T(8,128)(2,1)S(1)}, u32[]{:S(2)}, u32[]{:S(2)}) %collective-permute-start.1) | collective-permute-done | bytes 540704 | tf_op jit(solution)/shard_map/ppermute | solution.py:272
  11.8 2.2 %collective-permute-start.2 = (bf16[528,128]{1,0:T(8,128)(2,1)S(1)}, bf16[528,128]{1,0:T(8,128)(2,1)S(1)}, u32[]{:S(2)}, u32[]{:S(2)}) collective-permute-start(bf16[528,128]{1,0:T(8,128)(2,1)S(1)} %get-tuple-element.25), channel_id=1, source_target_pairs={{0,2},{1,3},{2,0},{3,1},{4,6},{5,7},{6,4},{7,5},{8,10},{9,11},{10,... | collective-permute-start | bytes 405512 | tf_op jit(solution)/shard_map/ppermute | solution.py:272
  14.0 1.3 %collective-permute-start.3 = (bf16[528,128]{1,0:T(8,128)(2,1)S(1)}, bf16[528,128]{1,0:T(8,128)(2,1)S(1)}, u32[]{:S(2)}, u32[]{:S(2)}) collective-permute-start(bf16[528,128]{1,0:T(8,128)(2,1)S(1)} %get-tuple-element.24), channel_id=1, source_target_pairs={{0,4},{1,5},{2,6},{3,7},{4,0},{5,1},{6,2},{7,3},{8,12},{9,13},{10,... | collective-permute-start | bytes 405512 | tf_op jit(solution)/shard_map/ppermute | solution.py:272
  15.3 0.8 %collective-permute-start.4 = (bf16[528,128]{1,0:T(8,128)(2,1)S(1)}, bf16[528,128]{1,0:T(8,128)(2,1)S(1)}, u32[]{:S(2)}, u32[]{:S(2)}) collective-permute-start(bf16[528,128]{1,0:T(8,128)(2,1)S(1)} %get-tuple-element.23), channel_id=1, source_target_pairs={{0,6},{1,7},{2,4},{3,5},{4,2},{5,3},{6,0},{7,1},{8,14},{9,15},{10,... | collective-permute-start | bytes 405512 | tf_op jit(solution)/shard_map/ppermute | solution.py:272
  16.1 1.1 %intra_mine.1.intra_ref = f32[16,128,128]{2,1,0:T(8,128)S(1)} custom-call(bf16[128,4096]{1,0:T(8,128)(2,1)S(1)} %copy-done.4, bf16[128,4096]{1,0:T(8,128)(2,1)S(1)} %copy-done.1, bf16[8,4096]{1,0:T(8,128)(2,1)S(1)} %collective-permute-done.halo_ref, bf16[128,4096]{1,0:T(8,128)(2,1)S(1)} %copy-done.3, f32[4,4096]{1,0:T(4,128)S(1)} %copy-done.5, ...), custom_call_target="tpu_custom_call" | custom-call | tf_op jit(solution)/shard_map/intra_mine/pallas_call | solution.py:41
  17.6 0.8 %collective-permute-done.3.refs_2_ = bf16[528,128]{1,0:T(8,128)(2,1)S(1)} collective-permute-done((bf16[528,128]{1,0:T(8,128)(2,1)S(1)}, bf16[528,128]{1,0:T(8,128)(2,1)S(1)}, u32[]{:S(2)}, u32[]{:S(2)}) %collective-permute-start.3) | collective-permute-done | bytes 135200 | tf_op jit(solution)/shard_map/ppermute | solution.py:272
  18.4 3.9 %collective-permute-done.4.refs_3_ = bf16[528,128]{1,0:T(8,128)(2,1)S(1)} collective-permute-done((bf16[528,128]{1,0:T(8,128)(2,1)S(1)}, bf16[528,128]{1,0:T(8,128)(2,1)S(1)}, u32[]{:S(2)}, u32[]{:S(2)}) %collective-permute-start.4) | collective-permute-done | bytes 135200 | tf_op jit(solution)/shard_map/ppermute | solution.py:272
  22.5 4.1 %collective-permute-start.5 = (bf16[528,128]{1,0:T(8,128)(2,1)S(1)}, bf16[528,128]{1,0:T(8,128)(2,1)S(1)}, u32[]{:S(2)}, u32[]{:S(2)}) collective-permute-start(bf16[528,128]{1,0:T(8,128)(2,1)S(1)} %span_state.1), channel_id=1, source_target_pairs={{0,8},{1,9},{2,10},{3,11},{4,12},{5,13},{6,14},{7,15},{16,24},{17,... | collective-permute-start | bytes 405512 | tf_op jit(solution)/shard_map/ppermute | solution.py:275
  26.6 1.9 %collective-permute-start.6 = (bf16[4,528,128]{2,1,0:T(8,128)(2,1)S(1)}, bf16[4,528,128]{2,1,0:T(8,128)(2,1)S(1)}, u32[]{:S(2)}, u32[]{:S(2)}) collective-permute-start(bf16[4,528,128]{2,1,0:T(8,128)(2,1)S(1)} %states_mine.1.own_ref), channel_id=1, source_target_pairs={{0,1},{1,0},{2,3},{3,2},{4,5},{5,4},{6,7},{7,6},{8,9},{9,8},{10,11... | collective-permute-start | bytes 1622024 | tf_op jit(solution)/shard_map/ppermute | solution.py:272
  28.4 1.1 %intra_other.1.intra_ref = f32[16,128,128]{2,1,0:T(8,128)S(1)} custom-call(bf16[128,4096]{1,0:T(8,128)(2,1)S(1)} %copy-done.4, bf16[128,4096]{1,0:T(8,128)(2,1)S(1)} %copy-done.1, bf16[8,4096]{1,0:T(8,128)(2,1)S(1)} %collective-permute-done.halo_ref, bf16[128,4096]{1,0:T(8,128)(2,1)S(1)} %copy-done.3, f32[4,4096]{1,0:T(4,128)S(1)} %copy-done.5, ...), custom_call_target="tpu_custom_call" | custom-call | tf_op jit(solution)/shard_map/intra_other/pallas_call | solution.py:41
  29.8 3.9 %collective-permute-start.10 = (bf16[512,128]{1,0:T(8,128)(2,1)S(1)}, bf16[512,128]{1,0:T(8,128)(2,1)S(1)}, u32[]{:S(2)}, u32[]{:S(2)}) collective-permute-start(bf16[512,128]{1,0:T(8,128)(2,1)S(1)} %get-tuple-element.28), channel_id=1, source_target_pairs={{0,4},{1,5},{2,6},{3,7},{4,0},{5,1},{6,2},{7,3},{8,12},{9,13},{10,... | collective-permute-start | bytes 393224 | tf_op jit(solution)/shard_map/ppermute | solution.py:272
  34.1 0.9 %collective-permute-start.8 = (bf16[512,128]{1,0:T(8,128)(2,1)S(1)}, bf16[512,128]{1,0:T(8,128)(2,1)S(1)}, u32[]{:S(2)}, u32[]{:S(2)}) collective-permute-start(bf16[512,128]{1,0:T(8,128)(2,1)S(1)} %get-tuple-element.29), channel_id=1, source_target_pairs={{0,2},{1,3},{2,0},{3,1},{4,6},{5,7},{6,4},{7,5},{8,10},{9,11},{10,... | collective-permute-start | bytes 393224 | tf_op jit(solution)/shard_map/ppermute | solution.py:272
  35.0 1.6 %collective-permute-start.7 = (bf16[512,128]{1,0:T(8,128)(2,1)S(1)}, bf16[512,128]{1,0:T(8,128)(2,1)S(1)}, u32[]{:S(2)}, u32[]{:S(2)}) collective-permute-start(bf16[512,128]{1,0:T(8,128)(2,1)S(1)} %get-tuple-element.30.refs_0_), channel_id=1, source_target_pairs={{0,1},{1,0},{2,3},{3,2},{4,5},{5,4},{6,7},{7,6},{8,9},{9,8},{10,11... | collective-permute-start | bytes 393224 | tf_op jit(solution)/shard_map/ppermute | solution.py:272
  36.6 2.7 %collective-permute-start.11 = (bf16[512,128]{1,0:T(8,128)(2,1)S(1)}, bf16[512,128]{1,0:T(8,128)(2,1)S(1)}, u32[]{:S(2)}, u32[]{:S(2)}) collective-permute-start(bf16[512,128]{1,0:T(8,128)(2,1)S(1)} %collective-permute-done.10.refs_2_), channel_id=1, source_target_pairs={{0,1},{1,0},{2,3},{3,2},{4,5},{5,4},{6,7},{7,6},{8,9},{9,8},{10,11... | collective-permute-start | bytes 393224 | tf_op jit(solution)/shard_map/ppermute | solution.py:272
  39.8 1.5 %collective-permute-start.13 = (bf16[512,128]{1,0:T(8,128)(2,1)S(1)}, bf16[512,128]{1,0:T(8,128)(2,1)S(1)}, u32[]{:S(2)}, u32[]{:S(2)}) collective-permute-start(bf16[512,128]{1,0:T(8,128)(2,1)S(1)} %collective-permute-done.12.refs_3_), channel_id=1, source_target_pairs={{0,1},{1,0},{2,3},{3,2},{4,5},{5,4},{6,7},{7,6},{8,9},{9,8},{10,11... | collective-permute-start | bytes 393224 | tf_op jit(solution)/shard_map/ppermute | solution.py:272
  41.4 1.4 %collective-permute-start.9 = (bf16[512,128]{1,0:T(8,128)(2,1)S(1)}, bf16[512,128]{1,0:T(8,128)(2,1)S(1)}, u32[]{:S(2)}, u32[]{:S(2)}) collective-permute-start(bf16[512,128]{1,0:T(8,128)(2,1)S(1)} %collective-permute-done.8.refs_1_), channel_id=1, source_target_pairs={{0,1},{1,0},{2,3},{3,2},{4,5},{5,4},{6,7},{7,6},{8,9},{9,8},{10,11... | collective-permute-start | bytes 393224 | tf_op jit(solution)/shard_map/ppermute | solution.py:272
  42.8 1.7 %out_mine.1.refs_4_ = bf16[128,4096]{1,0:T(8,128)(2,1)} custom-call(bf16[128,4096]{1,0:T(8,128)(2,1)S(1)} %copy-done.4, f32[16,128,128]{2,1,0:T(8,128)S(1)} %intra_mine.1.intra_ref, f32[8,8,128]{2,1,0:T(8,128)S(1)} %cum.1.cum_ref, f32[1,4096]{1,0:T(1,128)S(1)} %bitcast.18, bf16[4,528,128]{2,1,0:T(8,128)(2,1)S(1)} %collective-permute-done.1.got_ref.sib_ref, ...), custom_call_target="tpu_custom_call" | custom-call | tf_op jit(solution)/shard_map/out_mine/pallas_call | solution.py:41
  44.6 1.7 %out_other.1 = bf16[128,4096]{1,0:T(8,128)(2,1)} custom-call(bf16[128,4096]{1,0:T(8,128)(2,1)S(1)} %copy-done.4, f32[16,128,128]{2,1,0:T(8,128)S(1)} %intra_other.1.intra_ref, f32[8,8,128]{2,1,0:T(8,128)S(1)} %cum.1.cum_ref, f32[1,4096]{1,0:T(1,128)S(1)} %bitcast.19, ...), custom_call_target="tpu_custom_call", output_to_operand_aliasing={{}: (9, {})} | custom-call | tf_op jit(solution)/shard_map/out_other/pallas_call | solution.py:41
  (33 shorter events, 2.8 us)
Async XLA Ops:
  0.0 1.2 %copy-start = (bf16[128,4096]{1,0:T(8,128)(2,1)S(1)}, bf16[128,4096]{1,0:T(8,128)(2,1)}, u32[]{:S(2)}) copy-start(bf16[128,4096]{1,0:T(8,128)(2,1)} %k_ref.9) | copy-start | bytes 3145732
  1.2 6.1 %copy-start.1 = (bf16[128,4096]{1,0:T(8,128)(2,1)S(1)}, bf16[128,4096]{1,0:T(8,128)(2,1)}, u32[]{:S(2)}) copy-start(bf16[128,4096]{1,0:T(8,128)(2,1)} %k_ref.9) | copy-start | bytes 3145732
  1.2 6.1 %copy-start.5 = (f32[4,4096]{1,0:T(4,128)S(1)}, f32[4,4096]{1,0:T(4,128)}, u32[]{:S(2)}) copy-start(f32[4,4096]{1,0:T(4,128)} %w_ref.7) | copy-start | bytes 196612
  1.3 6.0 %collective-permute-start = (bf16[8,4096]{1,0:T(8,128)(2,1)S(1)}, bf16[8,4096]{1,0:T(8,128)(2,1)S(1)}, u32[]{:S(2)}, u32[]{:S(2)}) collective-permute-start(bf16[8,4096]{1,0:T(8,128)(2,1)S(1)} %tail.1), channel_id=1, source_target_pairs={{0,1},{1,2},{2,3},{3,4},{4,5},{5,6},{6,7},{7,8},{8,9},{9,10},{10,1... | collective-permute-start | bytes 196616 | tf_op jit(solution)/shard_map/ppermute | solution.py:275
  6.0 0.7 %copy-start.7 = (f32[128,32]{0,1:T(8,128)S(1)}, f32[128,32]{0,1:T(8,128)}, u32[]{:S(2)}) copy-start(f32[128,32]{0,1:T(8,128)} %param.9) | copy-start | bytes 49156
  7.3 1.2 %copy-start.2 = (bf16[128,4096]{1,0:T(8,128)(2,1)S(1)}, bf16[128,4096]{1,0:T(8,128)(2,1)}, u32[]{:S(2)}) copy-start(bf16[128,4096]{1,0:T(8,128)(2,1)} %v_ref.7) | copy-start | bytes 3145732
  9.5 2.0 %collective-permute-start.1 = (bf16[4,528,128]{2,1,0:T(8,128)(2,1)S(1)}, bf16[4,528,128]{2,1,0:T(8,128)(2,1)S(1)}, u32[]{:S(2)}, u32[]{:S(2)}) collective-permute-start(bf16[4,528,128]{2,1,0:T(8,128)(2,1)S(1)} %states_other.1), channel_id=1, source_target_pairs={{0,1},{1,0},{2,3},{3,2},{4,5},{5,4},{6,7},{7,6},{8,9},{9,8},{10,11... | collective-permute-start | bytes 1622024 | tf_op jit(solution)/shard_map/ppermute | solution.py:272
  10.7 5.5 %copy-start.3 = (bf16[128,4096]{1,0:T(8,128)(2,1)S(1)}, bf16[128,4096]{1,0:T(8,128)(2,1)}, u32[]{:S(2)}) copy-start(bf16[128,4096]{1,0:T(8,128)(2,1)} %v_ref.7) | copy-start | bytes 3145732
  10.7 5.5 %copy-start.4 = (bf16[128,4096]{1,0:T(8,128)(2,1)S(1)}, bf16[128,4096]{1,0:T(8,128)(2,1)}, u32[]{:S(2)}) copy-start(bf16[128,4096]{1,0:T(8,128)(2,1)} %q_ref.5) | copy-start | bytes 3145732
  11.8 5.8 %collective-permute-start.2 = (bf16[528,128]{1,0:T(8,128)(2,1)S(1)}, bf16[528,128]{1,0:T(8,128)(2,1)S(1)}, u32[]{:S(2)}, u32[]{:S(2)}) collective-permute-start(bf16[528,128]{1,0:T(8,128)(2,1)S(1)} %get-tuple-element.25), channel_id=1, source_target_pairs={{0,2},{1,3},{2,0},{3,1},{4,6},{5,7},{6,4},{7,5},{8,10},{9,11},{10,... | collective-permute-start | bytes 405512 | tf_op jit(solution)/shard_map/ppermute | solution.py:272
  14.0 4.5 %collective-permute-start.3 = (bf16[528,128]{1,0:T(8,128)(2,1)S(1)}, bf16[528,128]{1,0:T(8,128)(2,1)S(1)}, u32[]{:S(2)}, u32[]{:S(2)}) collective-permute-start(bf16[528,128]{1,0:T(8,128)(2,1)S(1)} %get-tuple-element.24), channel_id=1, source_target_pairs={{0,4},{1,5},{2,6},{3,7},{4,0},{5,1},{6,2},{7,3},{8,12},{9,13},{10,... | collective-permute-start | bytes 405512 | tf_op jit(solution)/shard_map/ppermute | solution.py:272
  15.3 7.1 %collective-permute-start.4 = (bf16[528,128]{1,0:T(8,128)(2,1)S(1)}, bf16[528,128]{1,0:T(8,128)(2,1)S(1)}, u32[]{:S(2)}, u32[]{:S(2)}) collective-permute-start(bf16[528,128]{1,0:T(8,128)(2,1)S(1)} %get-tuple-element.23), channel_id=1, source_target_pairs={{0,6},{1,7},{2,4},{3,5},{4,2},{5,3},{6,0},{7,1},{8,14},{9,15},{10,... | collective-permute-start | bytes 405512 | tf_op jit(solution)/shard_map/ppermute | solution.py:272
  22.5 7.1 %collective-permute-start.5 = (bf16[528,128]{1,0:T(8,128)(2,1)S(1)}, bf16[528,128]{1,0:T(8,128)(2,1)S(1)}, u32[]{:S(2)}, u32[]{:S(2)}) collective-permute-start(bf16[528,128]{1,0:T(8,128)(2,1)S(1)} %span_state.1), channel_id=1, source_target_pairs={{0,8},{1,9},{2,10},{3,11},{4,12},{5,13},{6,14},{7,15},{16,24},{17,... | collective-permute-start | bytes 405512 | tf_op jit(solution)/shard_map/ppermute | solution.py:275
  26.6 17.9 %collective-permute-start.6 = (bf16[4,528,128]{2,1,0:T(8,128)(2,1)S(1)}, bf16[4,528,128]{2,1,0:T(8,128)(2,1)S(1)}, u32[]{:S(2)}, u32[]{:S(2)}) collective-permute-start(bf16[4,528,128]{2,1,0:T(8,128)(2,1)S(1)} %states_mine.1.own_ref), channel_id=1, source_target_pairs={{0,1},{1,0},{2,3},{3,2},{4,5},{5,4},{6,7},{7,6},{8,9},{9,8},{10,11... | collective-permute-start | bytes 1622024 | tf_op jit(solution)/shard_map/ppermute | solution.py:272
  29.7 13.1 %copy-start.6 = (f32[4096]{0:T(1024)S(1)}, f32[4096]{0:T(1024)}, u32[]{:S(2)}) copy-start(f32[4096]{0:T(1024)} %param.11) | copy-start | bytes 49156
  29.8 6.8 %collective-permute-start.10 = (bf16[512,128]{1,0:T(8,128)(2,1)S(1)}, bf16[512,128]{1,0:T(8,128)(2,1)S(1)}, u32[]{:S(2)}, u32[]{:S(2)}) collective-permute-start(bf16[512,128]{1,0:T(8,128)(2,1)S(1)} %get-tuple-element.28), channel_id=1, source_target_pairs={{0,4},{1,5},{2,6},{3,7},{4,0},{5,1},{6,2},{7,3},{8,12},{9,13},{10,... | collective-permute-start | bytes 393224 | tf_op jit(solution)/shard_map/ppermute | solution.py:272
  33.7 6.1 %collective-permute-start.12 = (bf16[512,128]{1,0:T(8,128)(2,1)S(1)}, bf16[512,128]{1,0:T(8,128)(2,1)S(1)}, u32[]{:S(2)}, u32[]{:S(2)}) collective-permute-start(bf16[512,128]{1,0:T(8,128)(2,1)S(1)} %get-tuple-element.27), channel_id=1, source_target_pairs={{0,6},{1,7},{2,4},{3,5},{4,2},{5,3},{6,0},{7,1},{8,14},{9,15},{10,... | collective-permute-start | bytes 393224 | tf_op jit(solution)/shard_map/ppermute | solution.py:272
  34.1 7.3 %collective-permute-start.8 = (bf16[512,128]{1,0:T(8,128)(2,1)S(1)}, bf16[512,128]{1,0:T(8,128)(2,1)S(1)}, u32[]{:S(2)}, u32[]{:S(2)}) collective-permute-start(bf16[512,128]{1,0:T(8,128)(2,1)S(1)} %get-tuple-element.29), channel_id=1, source_target_pairs={{0,2},{1,3},{2,0},{3,1},{4,6},{5,7},{6,4},{7,5},{8,10},{9,11},{10,... | collective-permute-start | bytes 393224 | tf_op jit(solution)/shard_map/ppermute | solution.py:272
  35.0 9.6 %collective-permute-start.7 = (bf16[512,128]{1,0:T(8,128)(2,1)S(1)}, bf16[512,128]{1,0:T(8,128)(2,1)S(1)}, u32[]{:S(2)}, u32[]{:S(2)}) collective-permute-start(bf16[512,128]{1,0:T(8,128)(2,1)S(1)} %get-tuple-element.30.refs_0_), channel_id=1, source_target_pairs={{0,1},{1,0},{2,3},{3,2},{4,5},{5,4},{6,7},{7,6},{8,9},{9,8},{10,11... | collective-permute-start | bytes 393224 | tf_op jit(solution)/shard_map/ppermute | solution.py:272
  36.6 8.0 %collective-permute-start.11 = (bf16[512,128]{1,0:T(8,128)(2,1)S(1)}, bf16[512,128]{1,0:T(8,128)(2,1)S(1)}, u32[]{:S(2)}, u32[]{:S(2)}) collective-permute-start(bf16[512,128]{1,0:T(8,128)(2,1)S(1)} %collective-permute-done.10.refs_2_), channel_id=1, source_target_pairs={{0,1},{1,0},{2,3},{3,2},{4,5},{5,4},{6,7},{7,6},{8,9},{9,8},{10,11... | collective-permute-start | bytes 393224 | tf_op jit(solution)/shard_map/ppermute | solution.py:272
  39.8 4.7 %collective-permute-start.13 = (bf16[512,128]{1,0:T(8,128)(2,1)S(1)}, bf16[512,128]{1,0:T(8,128)(2,1)S(1)}, u32[]{:S(2)}, u32[]{:S(2)}) collective-permute-start(bf16[512,128]{1,0:T(8,128)(2,1)S(1)} %collective-permute-done.12.refs_3_), channel_id=1, source_target_pairs={{0,1},{1,0},{2,3},{3,2},{4,5},{5,4},{6,7},{7,6},{8,9},{9,8},{10,11... | collective-permute-start | bytes 393224 | tf_op jit(solution)/shard_map/ppermute | solution.py:272
  41.4 3.2 %collective-permute-start.9 = (bf16[512,128]{1,0:T(8,128)(2,1)S(1)}, bf16[512,128]{1,0:T(8,128)(2,1)S(1)}, u32[]{:S(2)}, u32[]{:S(2)}) collective-permute-start(bf16[512,128]{1,0:T(8,128)(2,1)S(1)} %collective-permute-done.8.refs_1_), channel_id=1, source_target_pairs={{0,1},{1,0},{2,3},{3,2},{4,5},{5,4},{6,7},{7,6},{8,9},{9,8},{10,11... | collective-permute-start | bytes 393224 | tf_op jit(solution)/shard_map/ppermute | solution.py:272

commit v3 on v2

--- a/solution.py
+++ b/solution.py
@@ -12,9 +12,10 @@
 CHIPS = 4
 SPAN = 2 * CHIPS
 HALO = 8
+EXCHANGE = (1, 3, 2)
 PARTS = 16
 VMEM = pl.BlockSpec(memory_space=pltpu.VMEM)
-ANY = pl.BlockSpec(memory_space=pl.ANY)
+HBM = pl.BlockSpec(memory_space=pltpu.HBM)
 
 
 def position():
@@ -35,7 +36,7 @@
     if in_specs is None:
         in_specs = [VMEM] * len(args)
     args = [
-        pltpu.with_memory_space_constraint(x, pltpu.VMEM) if s is VMEM else x
+        pltpu.with_memory_space_constraint(x, pltpu.VMEM if s is VMEM else pltpu.HBM)
         for x, s in zip(args, in_specs)
     ]
     return pl.pallas_call(
@@ -57,7 +58,8 @@
     copy.wait()
 
 
-def cum_kernel(heads, decay_ref, out_ref):
+def cum_kernel(heads, decay_ref, early_ref, out_ref):
+    del early_ref
     x = decay_ref[...]
     rows = x.shape[1]
     lane = lax.broadcasted_iota(jnp.int32, x.shape, 1)
@@ -196,48 +198,51 @@
 def spread_kernel(heads, size, *refs):
     packets, before, out_ref, held = refs[:CHIPS], refs[CHIPS], refs[CHIPS + 1], refs[CHIPS + 2]
     _, chip = position()
+    later = lax.axis_index("ctx") >= SPAN
     in_order(packets, held)
     decays = [get_decay(held.at[b], heads, size) for b in range(CHIPS)]
     for j in range(heads):
         rows = slice(j * size, (j + 1) * size)
-        acc = before[rows, :].astype(F32)
-        out_ref[chip, rows, :] = before[rows, :]
+        acc = jnp.where(later, before[rows, :].astype(F32), 0.0)
+        out_ref[chip, rows, :] = acc.astype(BF16)
         for b in range(1, CHIPS):
             acc = acc * decays[b - 1][j : j + 1] + held[b - 1, rows, :].astype(F32)
             out_ref[chip ^ b, rows, :] = acc.astype(BF16)
 
 
-def out_kernel(mine, heads, size, q_ref, intra_ref, cum_ref, gain_ref, sib_ref, *refs):
-    prefixes, (out_ref, mixed_ref, done_ref, sems) = refs[:CHIPS], refs[-4:]
+def out_kernel(items, heads, size, *refs):
+    q_ref, cum_ref, gain_ref = refs[:3]
+    per_item = [refs[3 + 3 * i : 6 + 3 * i] for i in range(len(items))]
+    out_ref, mixed_ref, done_ref, sems = refs[-4:]
     core, _ = position()
     second = core == 1
-    for g in range(CHIPS):
+    for i, (mine, g) in enumerate(items):
+        prefix_ref, intra_ref, sib_ref = per_item[i]
         b = head_group(mine, g)
         started = jnp.exp(cum_ref[b][0:heads]).T
-        sib_decay = get_decay(sib_ref.at[g], heads, size)
-        by = jnp.where(second, sib_decay, 1.0)
+        by = jnp.where(second, get_decay(sib_ref.at[g], heads, size), 1.0)
         for j in range(heads):
             cols = columns(b * heads * size, j * size, size)
             rows = slice(j * size, (j + 1) * size)
             sib = jnp.where(second, sib_ref[g, rows, :].astype(F32), 0.0)
-            prefix = prefixes[g][rows, :].astype(F32) * by[j : j + 1] + sib
+            prefix = prefix_ref[rows, :].astype(F32) * by[j : j + 1] + sib
             inter = lax.dot_general(
                 q_ref[:, cols], prefix.astype(BF16), (((1,), (1,)), ((), ())),
                 preferred_element_type=F32,
             )
-            mixed_ref[g * heads + j] = intra_ref[g * heads + j] + inter * started[:, j : j + 1]
+            mixed_ref[i * heads + j] = intra_ref[g * heads + j] + inter * started[:, j : j + 1]
     copies = []
-    for g in range(CHIPS):
-        b = head_group(mine, g)
-        for j in range(heads):
-            cols = columns(b * heads * size, j * size, size)
-            mixed = mixed_ref[g * heads + j]
+    for i, (mine, g) in enumerate(items):
+        b = head_group(mine, g)
+        for j in range(heads):
+            cols = columns(b * heads * size, j * size, size)
+            mixed = mixed_ref[i * heads + j]
             scale = lax.rsqrt(jnp.mean(mixed * mixed, axis=1, keepdims=True) + 1e-05)
-            done_ref[g, :, j * size : (j + 1) * size] = (
+            done_ref[i, :, j * size : (j + 1) * size] = (
                 mixed * scale * gain_ref[:, cols]
             ).astype(BF16)
         wide = columns(b * heads * size, 0, heads * size)
-        copies.append(pltpu.make_async_copy(done_ref.at[g], out_ref.at[:, wide], sems.at[g]))
+        copies.append(pltpu.make_async_copy(done_ref.at[i], out_ref.at[:, wide], sems.at[i]))
         copies[-1].start()
     for copy in copies:
         copy.wait()
@@ -279,7 +284,7 @@
         "tail",
         pltpu.VMEM((HALO, width), BF16),
         key_input,
-        in_specs=[ANY],
+        in_specs=[HBM],
         scratch=[pltpu.SemaphoreType.DMA(())],
     )
     halo = shift(tail, 1)
@@ -287,7 +292,7 @@
         functools.partial(cum_kernel, heads),
         "cum",
         pltpu.VMEM((SPAN, 2 * heads, rows), F32),
-        log_decay.T,
+        log_decay.T, value_input,
     )
     gain = norm_gain.reshape(1, width)
     ext = pltpu.VMEM((heads, rows + HALO, size), F32)
@@ -322,10 +327,14 @@
         pltpu.VMEM((CHIPS, packet, size), BF16),
         mine, got,
     )
-    packets = [chip_states[0]] + [swap(chip_states[g], 2 * g) for g in range(1, CHIPS)]
+    packets = {0: chip_states[0]}
+    for g in EXCHANGE:
+        packets[g] = swap(chip_states[g], 2 * g)
     q_after, chip_states = lax.optimization_barrier((queries, chip_states))
     intra_mine = intra_part(True, q_after)
-    *packets, intra_mine = lax.optimization_barrier((*packets, intra_mine))
+    *late, intra_mine = lax.optimization_barrier((*[packets[g] for g in EXCHANGE], intra_mine))
+    packets.update(zip(EXCHANGE, late))
+    packets = [packets[g] for g in range(CHIPS)]
 
     order = pltpu.VMEM((CHIPS, packet, size), BF16)
     span = call(
@@ -335,7 +344,7 @@
         *packets,
         scratch=[order],
     )
-    before = shift(span, SPAN)
+    before = swap(span, SPAN) if n == 2 * SPAN else shift(span, SPAN)
     reach = 1
     while reach < n // SPAN - 1:
         before = join_spans(shift(before, SPAN * reach), before, heads, size)
@@ -351,28 +360,41 @@
         *packets, before,
         scratch=[order],
     )
-    own = [chip_prefix[0]] + [swap(chip_prefix[g], 2 * g) for g in range(1, CHIPS)]
-    other = [swap(x, 1) for x in own]
-
-    def output(mine, intra, sibling, prefixes, result):
+    own = {0: chip_prefix[0]}
+    for g in EXCHANGE:
+        own[g] = swap(chip_prefix[g], 2 * g)
+    other = {0: swap(own[0], 1)}
+
+    def output(items, result):
+        args = [queries, cum, gain]
+        for mine, g in items:
+            args += [own[g], intra_mine, got] if mine else [other[g], intra_other, got_late]
+        count = len(args)
         extra = [] if result is None else [result]
         return call(
-            functools.partial(out_kernel, mine, heads, size),
-            "out_mine" if mine else "out_other",
+            functools.partial(out_kernel, items, heads, size),
+            "out_" + "_".join(("m" if mine else "o") + str(g) for mine, g in items),
             jax.ShapeDtypeStruct((rows, width), BF16),
-            queries, intra, cum, gain, sibling, *prefixes, *extra,
-            in_specs=[VMEM] * (5 + CHIPS) + [ANY] * len(extra),
-            out_specs=ANY,
-            input_output_aliases={5 + CHIPS: 0} if extra else {},
+            *args, *extra,
+            in_specs=[VMEM] * count + [HBM] * len(extra),
+            out_specs=HBM,
+            input_output_aliases={count: 0} if extra else {},
             scratch=[
-                pltpu.VMEM((half, rows, size), F32),
-                pltpu.VMEM((CHIPS, rows, heads * size), BF16),
-                pltpu.SemaphoreType.DMA((CHIPS,)),
+                pltpu.VMEM((len(items) * heads, rows, size), F32),
+                pltpu.VMEM((len(items), rows, heads * size), BF16),
+                pltpu.SemaphoreType.DMA((len(items),)),
             ],
         )
 
-    result = output(True, intra_mine, got, own, None)
-    return output(False, intra_other, got_late, other, result)
+    first, *last = EXCHANGE[:1] + EXCHANGE[:0:-1]
+    result = output([(True, 0), (False, 0)], None)
+    other[first] = swap(own[first], 1)
+    *late, result = lax.optimization_barrier((*[own[g] for g in last], result))
+    own.update(zip(last, late))
+    other.update({g: swap(own[g], 1) for g in last})
+    result = output([(True, first), (False, first)], result)
+    result = output([(True, g) for g in last], result)
+    return output([(False, g) for g in last], result)
 
 
 def solution(mesh):

time: 46.6 us -> 45.9 us (0.985)
  starting transfers between devices: 27.4 us -> 21 us
  waiting for transfers between devices: 6.63 us -> 11.7 us
  Pallas kernels: 8.82 us -> 11.3 us
  local copies, waits for them, and re-layouts: 3.26 us -> 1.07 us
    ppermute x12 -> x13, waiting for transfers between devices: 6.59 us -> 11.7 us  [swap(): return lax.ppermute(x, 'ctx', [(i, i ^ mask) for i in range(n)])]
    ppermute x2 -> x1, starting transfers between devices: 8.73 us -> 4.54 us  [shift(): return lax.ppermute(x, 'ctx', [(i, i + by) for i in range(n - by)])]
    pallas_call x11 -> x13, Pallas kernels: 8.82 us -> 11.3 us  [call(): pl.pallas_call(kernel, out_shape=out_shape, in_specs=in_specs, out_specs=...]
    unnamed x16 -> x12, local copies, waits for them, and re-layouts: 3.19 us -> 0.99 us
    ppermute x12 -> x13, starting transfers between devices: 18.6 us -> 16.5 us  [swap(): return lax.ppermute(x, 'ctx', [(i, i ^ mask) for i in range(n)])]
  transfers between devices with their start and end apart: 14 -> 14, of which waited for: 5 -> 6; matrix products, arithmetic and copies ran while one was open for 0% -> 0% of each run, Pallas kernels for 12% -> 17%
where the time goes in v3:
time: 45.9 us; the launch traced here: 45.2 us
  starting transfers between devices  21 us (46%)
  waiting for transfers between devices  11.7 us (25%)
  Pallas kernels  11.3 us (25%)
  local copies, waits for them, and re-layouts  1.07 us (2%)
    ppermute x13, starting transfers between devices, swap(): return lax.ppermute(x, 'ctx', [(i, i ^ mask) for i in range(n)])  16.5 us
    ppermute x13, waiting for transfers between devices, swap(): return lax.ppermute(x, 'ctx', [(i, i ^ mask) for i in range(n)])  11.7 us
    pallas_call x13, Pallas kernels, call(): pl.pallas_call(kernel, out_shape=out_shape, in_specs=in_specs, out_specs=...  11.3 us
    ppermute x1, starting transfers between devices, shift(): return lax.ppermute(x, 'ctx', [(i, i + by) for i in range(n - by)])  4.54 us
    unnamed x12, local copies, waits for them, and re-layouts  0.99 us
  transfers between devices with their start and end apart: 14, of which 6 were waited for; matrix products, arithmetic and copies ran while one was open for 0% of the time, Pallas kernels for 17%

profile of v3, /device:TPU:1, one launch (start us, length us, event | category | flops | bytes accessed | tf_op | source)
XLA Modules:
  0.0 45.2 jit_solution(6549752712214593960)
XLA Ops:
  0.0 1.0 %tail.1 = bf16[8,4096]{1,0:T(8,128)(2,1)S(1)} custom-call(bf16[128,4096]{1,0:T(8,128)(2,1)} %k_ref.9), custom_call_target="tpu_custom_call" | custom-call | tf_op jit(solution)/shard_map/tail/pallas_call | solution.py:42
  1.0 4.5 %collective-permute-start = (bf16[8,4096]{1,0:T(8,128)(2,1)S(1)}, bf16[8,4096]{1,0:T(8,128)(2,1)S(1)}, u32[]{:S(2)}, u32[]{:S(2)}) collective-permute-start(bf16[8,4096]{1,0:T(8,128)(2,1)S(1)} %tail.1), channel_id=1, source_target_pairs={{0,1},{1,2},{2,3},{3,4},{4,5},{5,6},{6,7},{7,8},{8,9},{9,10},{10,1... | collective-permute-start | bytes 196616 | tf_op jit(solution)/shard_map/ppermute | solution.py:280
  7.1 1.0 %states_other.1 = bf16[4,528,128]{2,1,0:T(8,128)(2,1)S(1)} custom-call(bf16[128,4096]{1,0:T(8,128)(2,1)S(1)} %copy-done.2, bf16[8,4096]{1,0:T(8,128)(2,1)S(1)} %collective-permute-done.halo_ref, bf16[128,4096]{1,0:T(8,128)(2,1)S(1)} %copy-done.1, f32[4,4096]{1,0:T(4,128)S(1)} %copy-done.3, f32[8,8,128]{2,1,0:T(8,128)S(1)} %cum.1.cum_ref.refs_1_), custom_call_target="tpu_custom_call" | custom-call | tf_op jit(solution)/shard_map/states_other/pallas_call | solution.py:42
  8.2 1.0 %states_mine.1.own_ref = bf16[4,528,128]{2,1,0:T(8,128)(2,1)S(1)} custom-call(bf16[128,4096]{1,0:T(8,128)(2,1)S(1)} %copy-done.2, bf16[8,4096]{1,0:T(8,128)(2,1)S(1)} %collective-permute-done.halo_ref, bf16[128,4096]{1,0:T(8,128)(2,1)S(1)} %copy-done.1, f32[4,4096]{1,0:T(4,128)S(1)} %copy-done.3, f32[8,8,128]{2,1,0:T(8,128)S(1)} %cum.1.cum_ref.refs_1_), custom_call_target="tpu_custom_call" | custom-call | tf_op jit(solution)/shard_map/states_mine/pallas_call | solution.py:42
  9.2 0.9 %collective-permute-done.1.got_ref.refs_5_.refs_8_ = bf16[4,528,128]{2,1,0:T(8,128)(2,1)S(1)} collective-permute-done((bf16[4,528,128]{2,1,0:T(8,128)(2,1)S(1)}, bf16[4,528,128]{2,1,0:T(8,128)(2,1)S(1)}, u32[]{:S(2)}, u32[]{:S(2)}) %collective-permute-start.1) | collective-permute-done | bytes 540704 | tf_op jit(solution)/shard_map/ppermute | solution.py:277
  10.4 2.9 %collective-permute-start.4 = (bf16[528,128]{1,0:T(8,128)(2,1)S(1)}, bf16[528,128]{1,0:T(8,128)(2,1)S(1)}, u32[]{:S(2)}, u32[]{:S(2)}) collective-permute-start(bf16[528,128]{1,0:T(8,128)(2,1)S(1)} %get-tuple-element.27), channel_id=1, source_target_pairs={{0,4},{1,5},{2,6},{3,7},{4,0},{5,1},{6,2},{7,3},{8,12},{9,13},{10,... | collective-permute-start | bytes 405512 | tf_op jit(solution)/shard_map/ppermute | solution.py:277
  13.5 1.0 %collective-permute-start.2 = (bf16[528,128]{1,0:T(8,128)(2,1)S(1)}, bf16[528,128]{1,0:T(8,128)(2,1)S(1)}, u32[]{:S(2)}, u32[]{:S(2)}) collective-permute-start(bf16[528,128]{1,0:T(8,128)(2,1)S(1)} %get-tuple-element.29), channel_id=1, source_target_pairs={{0,2},{1,3},{2,0},{3,1},{4,6},{5,7},{6,4},{7,5},{8,10},{9,11},{10,... | collective-permute-start | bytes 405512 | tf_op jit(solution)/shard_map/ppermute | solution.py:277
  14.5 0.9 %collective-permute-start.9 = (bf16[4,528,128]{2,1,0:T(8,128)(2,1)S(1)}, bf16[4,528,128]{2,1,0:T(8,128)(2,1)S(1)}, u32[]{:S(2)}, u32[]{:S(2)}) collective-permute-start(bf16[4,528,128]{2,1,0:T(8,128)(2,1)S(1)} %states_mine.1.own_ref), channel_id=1, source_target_pairs={{0,1},{1,0},{2,3},{3,2},{4,5},{5,4},{6,7},{7,6},{8,9},{9,8},{10,11... | collective-permute-start | bytes 1622024 | tf_op jit(solution)/shard_map/ppermute | solution.py:277
  15.5 1.1 %intra_mine.1.refs_4_.refs_7_ = f32[16,128,128]{2,1,0:T(8,128)S(1)} custom-call(bf16[128,4096]{1,0:T(8,128)(2,1)S(1)} %copy-done, bf16[128,4096]{1,0:T(8,128)(2,1)S(1)} %copy-done.2, bf16[8,4096]{1,0:T(8,128)(2,1)S(1)} %collective-permute-done.halo_ref, bf16[128,4096]{1,0:T(8,128)(2,1)S(1)} %copy-done.1, f32[4,4096]{1,0:T(4,128)S(1)} %copy-done.3, ...), custom_call_target="tpu_custom_call" | custom-call | tf_op jit(solution)/shard_map/intra_mine/pallas_call | solution.py:42
  16.9 2.9 %collective-permute-done.3.refs_3_ = bf16[528,128]{1,0:T(8,128)(2,1)S(1)} collective-permute-done((bf16[528,128]{1,0:T(8,128)(2,1)S(1)}, bf16[528,128]{1,0:T(8,128)(2,1)S(1)}, u32[]{:S(2)}, u32[]{:S(2)}) %collective-permute-start.3) | collective-permute-done | bytes 135200 | tf_op jit(solution)/shard_map/ppermute | solution.py:277
  19.8 1.0 %collective-permute-done.2.refs_1_ = bf16[528,128]{1,0:T(8,128)(2,1)S(1)} collective-permute-done((bf16[528,128]{1,0:T(8,128)(2,1)S(1)}, bf16[528,128]{1,0:T(8,128)(2,1)S(1)}, u32[]{:S(2)}, u32[]{:S(2)}) %collective-permute-start.2) | collective-permute-done | bytes 135200 | tf_op jit(solution)/shard_map/ppermute | solution.py:277
  21.0 2.4 %collective-permute-start.5 = (bf16[528,128]{1,0:T(8,128)(2,1)S(1)}, bf16[528,128]{1,0:T(8,128)(2,1)S(1)}, u32[]{:S(2)}, u32[]{:S(2)}) collective-permute-start(bf16[528,128]{1,0:T(8,128)(2,1)S(1)} %span_state.1), channel_id=1, source_target_pairs={{0,8},{1,9},{2,10},{3,11},{4,12},{5,13},{6,14},{7,15},{8,0},{9,1},... | collective-permute-start | bytes 405512 | tf_op jit(solution)/shard_map/ppermute | solution.py:277
  23.4 1.1 %intra_other.1.refs_7_.refs_4_ = f32[16,128,128]{2,1,0:T(8,128)S(1)} custom-call(bf16[128,4096]{1,0:T(8,128)(2,1)S(1)} %copy-done, bf16[128,4096]{1,0:T(8,128)(2,1)S(1)} %copy-done.2, bf16[8,4096]{1,0:T(8,128)(2,1)S(1)} %collective-permute-done.halo_ref, bf16[128,4096]{1,0:T(8,128)(2,1)S(1)} %copy-done.1, f32[4,4096]{1,0:T(4,128)S(1)} %copy-done.3, ...), custom_call_target="tpu_custom_call" | custom-call | tf_op jit(solution)/shard_map/intra_other/pallas_call | solution.py:42
  24.5 4.8 %collective-permute-done.5.refs_4_ = bf16[528,128]{1,0:T(8,128)(2,1)S(1)} collective-permute-done((bf16[528,128]{1,0:T(8,128)(2,1)S(1)}, bf16[528,128]{1,0:T(8,128)(2,1)S(1)}, u32[]{:S(2)}, u32[]{:S(2)}) %collective-permute-start.5) | collective-permute-done | bytes 135200 | tf_op jit(solution)/shard_map/ppermute | solution.py:277
  29.5 1.2 %collective-permute-start.12 = (bf16[512,128]{1,0:T(8,128)(2,1)S(1)}, bf16[512,128]{1,0:T(8,128)(2,1)S(1)}, u32[]{:S(2)}, u32[]{:S(2)}) collective-permute-start(bf16[512,128]{1,0:T(8,128)(2,1)S(1)} %get-tuple-element.31), channel_id=1, source_target_pairs={{0,2},{1,3},{2,0},{3,1},{4,6},{5,7},{6,4},{7,5},{8,10},{9,11},{10,... | collective-permute-start | bytes 393224 | tf_op jit(solution)/shard_map/ppermute | solution.py:277
  30.7 1.9 %collective-permute-start.8 = (bf16[512,128]{1,0:T(8,128)(2,1)S(1)}, bf16[512,128]{1,0:T(8,128)(2,1)S(1)}, u32[]{:S(2)}, u32[]{:S(2)}) collective-permute-start(bf16[512,128]{1,0:T(8,128)(2,1)S(1)} %get-tuple-element.32.refs_3_), channel_id=1, source_target_pairs={{0,1},{1,0},{2,3},{3,2},{4,5},{5,4},{6,7},{7,6},{8,9},{9,8},{10,11... | collective-permute-start | bytes 393224 | tf_op jit(solution)/shard_map/ppermute | solution.py:277
  33.0 1.1 %collective-permute-start.6 = (bf16[512,128]{1,0:T(8,128)(2,1)S(1)}, bf16[512,128]{1,0:T(8,128)(2,1)S(1)}, u32[]{:S(2)}, u32[]{:S(2)}) collective-permute-start(bf16[512,128]{1,0:T(8,128)(2,1)S(1)} %get-tuple-element.34), channel_id=1, source_target_pairs={{0,4},{1,5},{2,6},{3,7},{4,0},{5,1},{6,2},{7,3},{8,12},{9,13},{10,... | collective-permute-start | bytes 393224 | tf_op jit(solution)/shard_map/ppermute | solution.py:277
  34.1 3.6 %collective-permute-start.13 = (bf16[512,128]{1,0:T(8,128)(2,1)S(1)}, bf16[512,128]{1,0:T(8,128)(2,1)S(1)}, u32[]{:S(2)}, u32[]{:S(2)}) collective-permute-start(bf16[512,128]{1,0:T(8,128)(2,1)S(1)} %collective-permute-done.12.refs_3_), channel_id=1, source_target_pairs={{0,1},{1,0},{2,3},{3,2},{4,5},{5,4},{6,7},{7,6},{8,9},{9,8},{10,11... | collective-permute-start | bytes 393224 | tf_op jit(solution)/shard_map/ppermute | solution.py:277
  37.7 1.2 %out_m0_o0.1.refs_9_ = bf16[128,4096]{1,0:T(8,128)(2,1)} custom-call(bf16[128,4096]{1,0:T(8,128)(2,1)S(1)} %copy-done, f32[8,8,128]{2,1,0:T(8,128)S(1)} %cum.1.cum_ref.refs_1_, f32[1,4096]{1,0:T(1,128)S(1)} %bitcast.18, bf16[512,128]{1,0:T(8,128)(2,1)S(1)} %get-tuple-element.32.refs_3_, f32[16,128,128]{2,1,0:T(8,128)S(1)} %intra_mine.1.refs_4_.refs_7_, ...), custom_call_target="tpu_custom_call" | custom-call | tf_op jit(solution)/shard_map/out_m0_o0/pallas_call | solution.py:42
  38.9 1.7 %collective-permute-done.6.refs_3_ = bf16[512,128]{1,0:T(8,128)(2,1)S(1)} collective-permute-done((bf16[512,128]{1,0:T(8,128)(2,1)S(1)}, bf16[512,128]{1,0:T(8,128)(2,1)S(1)}, u32[]{:S(2)}, u32[]{:S(2)}) %collective-permute-start.6) | collective-permute-done | bytes 131104 | tf_op jit(solution)/shard_map/ppermute | solution.py:277
  40.6 0.8 %collective-permute-start.10 = (bf16[512,128]{1,0:T(8,128)(2,1)S(1)}, bf16[512,128]{1,0:T(8,128)(2,1)S(1)}, u32[]{:S(2)}, u32[]{:S(2)}) collective-permute-start(bf16[512,128]{1,0:T(8,128)(2,1)S(1)} %collective-permute-done.6.refs_3_), channel_id=1, source_target_pairs={{0,1},{1,0},{2,3},{3,2},{4,5},{5,4},{6,7},{7,6},{8,9},{9,8},{10,11... | collective-permute-start | bytes 393224 | tf_op jit(solution)/shard_map/ppermute | solution.py:277
  41.4 1.2 %out_m1_o1.1.refs_9_ = bf16[128,4096]{1,0:T(8,128)(2,1)} custom-call(bf16[128,4096]{1,0:T(8,128)(2,1)S(1)} %copy-done, f32[8,8,128]{2,1,0:T(8,128)S(1)} %cum.1.cum_ref.refs_1_, f32[1,4096]{1,0:T(1,128)S(1)} %bitcast.19, bf16[512,128]{1,0:T(8,128)(2,1)S(1)} %collective-permute-done.12.refs_3_, ...), custom_call_target="tpu_custom_call", output_to_operand_aliasing={{}: (9, {})} | custom-call | tf_op jit(solution)/shard_map/out_m1_o1/pallas_call | solution.py:42
  42.7 1.2 %out_m2_m3.1.refs_9_ = bf16[128,4096]{1,0:T(8,128)(2,1)} custom-call(bf16[128,4096]{1,0:T(8,128)(2,1)S(1)} %copy-done, f32[8,8,128]{2,1,0:T(8,128)S(1)} %cum.1.cum_ref.refs_1_, f32[1,4096]{1,0:T(1,128)S(1)} %bitcast.20, bf16[512,128]{1,0:T(8,128)(2,1)S(1)} %collective-permute-done.6.refs_3_, ...), custom_call_target="tpu_custom_call", output_to_operand_aliasing={{}: (9, {})} | custom-call | tf_op jit(solution)/shard_map/out_m2_m3/pallas_call | solution.py:42
  44.0 1.2 %out_o2_o3.1 = bf16[128,4096]{1,0:T(8,128)(2,1)} custom-call(bf16[128,4096]{1,0:T(8,128)(2,1)S(1)} %copy-done, f32[8,8,128]{2,1,0:T(8,128)S(1)} %cum.1.cum_ref.refs_1_, f32[1,4096]{1,0:T(1,128)S(1)} %bitcast.21, bf16[512,128]{1,0:T(8,128)(2,1)S(1)} %collective-permute-done.10.refs_3_, ...), custom_call_target="tpu_custom_call", output_to_operand_aliasing={{}: (9, {})} | custom-call | tf_op jit(solution)/shard_map/out_o2_o3/pallas_call | solution.py:42
  (31 shorter events, 3.3 us)
Async XLA Ops:
  0.0 5.6 %copy-start.1 = (bf16[128,4096]{1,0:T(8,128)(2,1)S(1)}, bf16[128,4096]{1,0:T(8,128)(2,1)}, u32[]{:S(2)}) copy-start(bf16[128,4096]{1,0:T(8,128)(2,1)} %v_ref.7) | copy-start | bytes 3145732
  0.0 6.9 %copy-start.2 = (bf16[128,4096]{1,0:T(8,128)(2,1)S(1)}, bf16[128,4096]{1,0:T(8,128)(2,1)}, u32[]{:S(2)}) copy-start(bf16[128,4096]{1,0:T(8,128)(2,1)} %k_ref.9) | copy-start | bytes 3145732
  1.0 5.9 %collective-permute-start = (bf16[8,4096]{1,0:T(8,128)(2,1)S(1)}, bf16[8,4096]{1,0:T(8,128)(2,1)S(1)}, u32[]{:S(2)}, u32[]{:S(2)}) collective-permute-start(bf16[8,4096]{1,0:T(8,128)(2,1)S(1)} %tail.1), channel_id=1, source_target_pairs={{0,1},{1,2},{2,3},{3,4},{4,5},{5,6},{6,7},{7,8},{8,9},{9,10},{10,1... | collective-permute-start | bytes 196616 | tf_op jit(solution)/shard_map/ppermute | solution.py:280
  5.6 0.7 %copy-start.5 = (f32[128,32]{0,1:T(8,128)S(1)}, f32[128,32]{0,1:T(8,128)}, u32[]{:S(2)}) copy-start(f32[128,32]{0,1:T(8,128)} %param.9) | copy-start | bytes 49156
  6.3 0.8 %copy-start.3 = (f32[4,4096]{1,0:T(4,128)S(1)}, f32[4,4096]{1,0:T(4,128)}, u32[]{:S(2)}) copy-start(f32[4,4096]{1,0:T(4,128)} %w_ref.7) | copy-start | bytes 196612
  8.1 2.0 %collective-permute-start.1 = (bf16[4,528,128]{2,1,0:T(8,128)(2,1)S(1)}, bf16[4,528,128]{2,1,0:T(8,128)(2,1)S(1)}, u32[]{:S(2)}, u32[]{:S(2)}) collective-permute-start(bf16[4,528,128]{2,1,0:T(8,128)(2,1)S(1)} %states_other.1), channel_id=1, source_target_pairs={{0,1},{1,0},{2,3},{3,2},{4,5},{5,4},{6,7},{7,6},{8,9},{9,8},{10,11... | collective-permute-start | bytes 1622024 | tf_op jit(solution)/shard_map/ppermute | solution.py:277
  9.2 6.2 %copy-start = (bf16[128,4096]{1,0:T(8,128)(2,1)S(1)}, bf16[128,4096]{1,0:T(8,128)(2,1)}, u32[]{:S(2)}) copy-start(bf16[128,4096]{1,0:T(8,128)(2,1)} %refs_0_.7) | copy-start | bytes 3145732
  10.4 6.5 %collective-permute-start.4 = (bf16[528,128]{1,0:T(8,128)(2,1)S(1)}, bf16[528,128]{1,0:T(8,128)(2,1)S(1)}, u32[]{:S(2)}, u32[]{:S(2)}) collective-permute-start(bf16[528,128]{1,0:T(8,128)(2,1)S(1)} %get-tuple-element.27), channel_id=1, source_target_pairs={{0,4},{1,5},{2,6},{3,7},{4,0},{5,1},{6,2},{7,3},{8,12},{9,13},{10,... | collective-permute-start | bytes 405512 | tf_op jit(solution)/shard_map/ppermute | solution.py:277
  13.3 6.6 %collective-permute-start.3 = (bf16[528,128]{1,0:T(8,128)(2,1)S(1)}, bf16[528,128]{1,0:T(8,128)(2,1)S(1)}, u32[]{:S(2)}, u32[]{:S(2)}) collective-permute-start(bf16[528,128]{1,0:T(8,128)(2,1)S(1)} %get-tuple-element.28), channel_id=1, source_target_pairs={{0,6},{1,7},{2,4},{3,5},{4,2},{5,3},{6,0},{7,1},{8,14},{9,15},{10,... | collective-permute-start | bytes 405512 | tf_op jit(solution)/shard_map/ppermute | solution.py:277
  13.5 7.4 %collective-permute-start.2 = (bf16[528,128]{1,0:T(8,128)(2,1)S(1)}, bf16[528,128]{1,0:T(8,128)(2,1)S(1)}, u32[]{:S(2)}, u32[]{:S(2)}) collective-permute-start(bf16[528,128]{1,0:T(8,128)(2,1)S(1)} %get-tuple-element.29), channel_id=1, source_target_pairs={{0,2},{1,3},{2,0},{3,1},{4,6},{5,7},{6,4},{7,5},{8,10},{9,11},{10,... | collective-permute-start | bytes 405512 | tf_op jit(solution)/shard_map/ppermute | solution.py:277
  14.5 23.2 %collective-permute-start.9 = (bf16[4,528,128]{2,1,0:T(8,128)(2,1)S(1)}, bf16[4,528,128]{2,1,0:T(8,128)(2,1)S(1)}, u32[]{:S(2)}, u32[]{:S(2)}) collective-permute-start(bf16[4,528,128]{2,1,0:T(8,128)(2,1)S(1)} %states_mine.1.own_ref), channel_id=1, source_target_pairs={{0,1},{1,0},{2,3},{3,2},{4,5},{5,4},{6,7},{7,6},{8,9},{9,8},{10,11... | collective-permute-start | bytes 1622024 | tf_op jit(solution)/shard_map/ppermute | solution.py:277
  21.0 8.2 %collective-permute-start.5 = (bf16[528,128]{1,0:T(8,128)(2,1)S(1)}, bf16[528,128]{1,0:T(8,128)(2,1)S(1)}, u32[]{:S(2)}, u32[]{:S(2)}) collective-permute-start(bf16[528,128]{1,0:T(8,128)(2,1)S(1)} %span_state.1), channel_id=1, source_target_pairs={{0,8},{1,9},{2,10},{3,11},{4,12},{5,13},{6,14},{7,15},{8,0},{9,1},... | collective-permute-start | bytes 405512 | tf_op jit(solution)/shard_map/ppermute | solution.py:277
  29.4 8.2 %copy-start.4 = (f32[4096]{0:T(1024)S(1)}, f32[4096]{0:T(1024)}, u32[]{:S(2)}) copy-start(f32[4096]{0:T(1024)} %param.11) | copy-start | bytes 49156
  29.5 4.6 %collective-permute-start.12 = (bf16[512,128]{1,0:T(8,128)(2,1)S(1)}, bf16[512,128]{1,0:T(8,128)(2,1)S(1)}, u32[]{:S(2)}, u32[]{:S(2)}) collective-permute-start(bf16[512,128]{1,0:T(8,128)(2,1)S(1)} %get-tuple-element.31), channel_id=1, source_target_pairs={{0,2},{1,3},{2,0},{3,1},{4,6},{5,7},{6,4},{7,5},{8,10},{9,11},{10,... | collective-permute-start | bytes 393224 | tf_op jit(solution)/shard_map/ppermute | solution.py:277
  30.7 7.0 %collective-permute-start.8 = (bf16[512,128]{1,0:T(8,128)(2,1)S(1)}, bf16[512,128]{1,0:T(8,128)(2,1)S(1)}, u32[]{:S(2)}, u32[]{:S(2)}) collective-permute-start(bf16[512,128]{1,0:T(8,128)(2,1)S(1)} %get-tuple-element.32.refs_3_), channel_id=1, source_target_pairs={{0,1},{1,0},{2,3},{3,2},{4,5},{5,4},{6,7},{7,6},{8,9},{9,8},{10,11... | collective-permute-start | bytes 393224 | tf_op jit(solution)/shard_map/ppermute | solution.py:277
  32.6 6.3 %collective-permute-start.7 = (bf16[512,128]{1,0:T(8,128)(2,1)S(1)}, bf16[512,128]{1,0:T(8,128)(2,1)S(1)}, u32[]{:S(2)}, u32[]{:S(2)}) collective-permute-start(bf16[512,128]{1,0:T(8,128)(2,1)S(1)} %get-tuple-element.33), channel_id=1, source_target_pairs={{0,6},{1,7},{2,4},{3,5},{4,2},{5,3},{6,0},{7,1},{8,14},{9,15},{10,... | collective-permute-start | bytes 393224 | tf_op jit(solution)/shard_map/ppermute | solution.py:277
  33.0 7.6 %collective-permute-start.6 = (bf16[512,128]{1,0:T(8,128)(2,1)S(1)}, bf16[512,128]{1,0:T(8,128)(2,1)S(1)}, u32[]{:S(2)}, u32[]{:S(2)}) collective-permute-start(bf16[512,128]{1,0:T(8,128)(2,1)S(1)} %get-tuple-element.34), channel_id=1, source_target_pairs={{0,4},{1,5},{2,6},{3,7},{4,0},{5,1},{6,2},{7,3},{8,12},{9,13},{10,... | collective-permute-start | bytes 393224 | tf_op jit(solution)/shard_map/ppermute | solution.py:277
  34.1 7.3 %collective-permute-start.13 = (bf16[512,128]{1,0:T(8,128)(2,1)S(1)}, bf16[512,128]{1,0:T(8,128)(2,1)S(1)}, u32[]{:S(2)}, u32[]{:S(2)}) collective-permute-start(bf16[512,128]{1,0:T(8,128)(2,1)S(1)} %collective-permute-done.12.refs_3_), channel_id=1, source_target_pairs={{0,1},{1,0},{2,3},{3,2},{4,5},{5,4},{6,7},{7,6},{8,9},{9,8},{10,11... | collective-permute-start | bytes 393224 | tf_op jit(solution)/shard_map/ppermute | solution.py:277
  40.6 3.3 %collective-permute-start.10 = (bf16[512,128]{1,0:T(8,128)(2,1)S(1)}, bf16[512,128]{1,0:T(8,128)(2,1)S(1)}, u32[]{:S(2)}, u32[]{:S(2)}) collective-permute-start(bf16[512,128]{1,0:T(8,128)(2,1)S(1)} %collective-permute-done.6.refs_3_), channel_id=1, source_target_pairs={{0,1},{1,0},{2,3},{3,2},{4,5},{5,4},{6,7},{7,6},{8,9},{9,8},{10,11... | collective-permute-start | bytes 393224 | tf_op jit(solution)/shard_map/ppermute | solution.py:277
  41.4 2.5 %collective-permute-start.11 = (bf16[512,128]{1,0:T(8,128)(2,1)S(1)}, bf16[512,128]{1,0:T(8,128)(2,1)S(1)}, u32[]{:S(2)}, u32[]{:S(2)}) collective-permute-start(bf16[512,128]{1,0:T(8,128)(2,1)S(1)} %collective-permute-done.7.refs_6_), channel_id=1, source_target_pairs={{0,1},{1,0},{2,3},{3,2},{4,5},{5,4},{6,7},{7,6},{8,9},{9,8},{10,11... | collective-permute-start | bytes 393224 | tf_op jit(solution)/shard_map/ppermute | solution.py:277

commit v4 on v3

--- a/solution.py
+++ b/solution.py
@@ -58,19 +58,19 @@
     copy.wait()
 
 
-def cum_kernel(heads, decay_ref, early_ref, out_ref):
-    del early_ref
+def cum_kernel(heads, decay_ref, out_ref):
     x = decay_ref[...]
-    rows = x.shape[1]
-    lane = lax.broadcasted_iota(jnp.int32, x.shape, 1)
-    step = 1
-    while step < rows:
-        x = x + jnp.where(lane >= step, pltpu.roll(x, step, 1), 0.0)
-        step *= 2
-    total = jnp.broadcast_to(x[:, rows - 1 : rows], x.shape)
+    count, rows = x.shape
+    upto = lax.broadcasted_iota(jnp.int32, (rows, rows), 0) <= lax.broadcasted_iota(
+        jnp.int32, (rows, rows), 1
+    )
+    parts = jnp.concatenate([p.astype(F32) for p in three_parts(x)], 0).astype(BF16)
+    sums = jnp.dot(parts, upto.astype(F32).astype(BF16), preferred_element_type=F32)
+    sums = sums[0:count] + (sums[count : 2 * count] + sums[2 * count :])
+    total = jnp.broadcast_to(sums[:, rows - 1 : rows], sums.shape)
     for b in range(out_ref.shape[0]):
         these = slice(b * heads, (b + 1) * heads)
-        out_ref[b, 0:heads, :] = x[these]
+        out_ref[b, 0:heads, :] = sums[these]
         out_ref[b, heads : 2 * heads, :] = total[these]
 
 
@@ -95,9 +95,12 @@
     return tail[0:heads] + tail[heads : 2 * heads] + tail[2 * heads : 3 * heads]
 
 
-def conv_keys(k_ref, halo_ref, w_ref, ext, cols):
+def conv_keys(k_ref, chip_halo_ref, core_halo_ref, w_ref, ext, cols):
     rows = k_ref.shape[0]
-    ext[0:HALO, :] = halo_ref[:, cols].astype(F32)
+    core, _ = position()
+    ext[0:HALO, :] = jnp.where(
+        core == 0, chip_halo_ref[:, cols].astype(F32), core_halo_ref[:, cols].astype(F32)
+    )
     ext[HALO : HALO + rows, :] = k_ref[:, cols].astype(F32)
     total = None
     for j in range(w_ref.shape[0]):
@@ -106,14 +109,15 @@
     return total.astype(BF16)
 
 
-def state_kernel(mine, heads, size, k_ref, halo_ref, v_ref, w_ref, cum_ref, out_ref, ext, held):
+def state_kernel(mine, heads, size, k_ref, chip_halo_ref, core_halo_ref, v_ref, w_ref, cum_ref, out_ref,
+    ext, held):
     for g in range(CHIPS):
         b = head_group(mine, g)
         cum = cum_ref[b]
         ending = jnp.exp(cum[heads : 2 * heads] - cum[0:heads]).T
         for j in range(heads):
             cols = columns(b * heads * size, j * size, size)
-            key_conv = conv_keys(k_ref, halo_ref, w_ref, ext.at[j], cols)
+            key_conv = conv_keys(k_ref, chip_halo_ref, core_halo_ref, w_ref, ext.at[j], cols)
             held[g * heads + j] = (key_conv.astype(F32) * ending[:, j : j + 1]).astype(BF16)
     for g in range(CHIPS):
         b = head_group(mine, g)
@@ -128,7 +132,8 @@
 
 
 def intra_kernel(
-    mine, heads, size, q_ref, k_ref, halo_ref, v_ref, w_ref, cum_ref, out_ref, ext, held
+    mine, heads, size, q_ref, k_ref, chip_halo_ref, core_halo_ref, v_ref, w_ref, cum_ref, out_ref,
+    ext, held
 ):
     rows = q_ref.shape[0]
     causal = lax.broadcasted_iota(jnp.int32, (rows, rows), 0) >= lax.broadcasted_iota(
@@ -140,7 +145,7 @@
         cum_col = cum.T
         for j in range(heads):
             cols = columns(b * heads * size, j * size, size)
-            key_conv = conv_keys(k_ref, halo_ref, w_ref, ext.at[j], cols)
+            key_conv = conv_keys(k_ref, chip_halo_ref, core_halo_ref, w_ref, ext.at[j], cols)
             scores = lax.dot_general(
                 q_ref[:, cols], key_conv, (((1,), (1,)), ((), ())), preferred_element_type=F32
             )
@@ -287,13 +292,16 @@
         in_specs=[HBM],
         scratch=[pltpu.SemaphoreType.DMA(())],
     )
-    halo = shift(tail, 1)
     cum = call(
         functools.partial(cum_kernel, heads),
         "cum",
         pltpu.VMEM((SPAN, 2 * heads, rows), F32),
-        log_decay.T, value_input,
-    )
+        log_decay.T,
+    )
+    tail, cum, keys, values = lax.optimization_barrier((tail, cum, key_input, value_input))
+    next_pairs = [(i, i + 1) for i in range(1, n - 1, 2)]
+    chip_halo = lax.ppermute(tail, "ctx", next_pairs + [(j, i) for i, j in next_pairs])
+    core_halo = swap(tail, 1)
     gain = norm_gain.reshape(1, width)
     ext = pltpu.VMEM((heads, rows + HALO, size), F32)
     held = pltpu.VMEM((half, rows, size), BF16)
@@ -303,7 +311,7 @@
             functools.partial(state_kernel, mine, heads, size),
             "states_mine" if mine else "states_other",
             pltpu.VMEM((CHIPS, packet, size), BF16),
-            key_input, halo, value_input, conv_weight, cum,
+            keys, chip_halo, core_halo, values, conv_weight, cum,
             scratch=[ext, pltpu.VMEM((half, rows, size), BF16)],
         )
 
@@ -312,7 +320,7 @@
             functools.partial(intra_kernel, mine, heads, size),
             "intra_mine" if mine else "intra_other",
             pltpu.VMEM((half, rows, size), F32),
-            q, key_input, halo, value_input, conv_weight, cum,
+            q, keys, chip_halo, core_halo, values, conv_weight, cum,
             scratch=[ext, held],
         )
 
@@ -379,6 +387,7 @@
             in_specs=[VMEM] * count + [HBM] * len(extra),
             out_specs=HBM,
             input_output_aliases={count: 0} if extra else {},
+            cost_estimate=pl.CostEstimate(flops=1, transcendentals=0, bytes_accessed=1),
             scratch=[
                 pltpu.VMEM((len(items) * heads, rows, size), F32),
                 pltpu.VMEM((len(items), rows, heads * size), BF16),
@@ -386,14 +395,15 @@
             ],
         )
 
-    first, *last = EXCHANGE[:1] + EXCHANGE[:0:-1]
+    first, *last = EXCHANGE
     result = output([(True, 0), (False, 0)], None)
+    own[first], result = lax.optimization_barrier((own[first], result))
     other[first] = swap(own[first], 1)
+    result = output([(True, first)], result)
     *late, result = lax.optimization_barrier((*[own[g] for g in last], result))
     own.update(zip(last, late))
     other.update({g: swap(own[g], 1) for g in last})
-    result = output([(True, first), (False, first)], result)
-    result = output([(True, g) for g in last], result)
+    result = output([(False, first)] + [(True, g) for g in last], result)
     return output([(False, g) for g in last], result)
 
 

time: 45.9 us -> 45.8 us (level); the launches traced: 45.2 us -> 45.6 us
  waiting for transfers between devices: 11.7 us -> 15.5 us
  starting transfers between devices: 21 us -> 17.6 us
    ppermute x13 -> x14, starting transfers between devices: 16.5 us -> 13 us  [swap(): return lax.ppermute(x, 'ctx', [(i, i ^ mask) for i in range(n)])]
    ppermute x13 -> x14, waiting for transfers between devices: 11.7 us -> 13.7 us  [swap(): return lax.ppermute(x, 'ctx', [(i, i ^ mask) for i in range(n)])]
    ppermute x1, waiting for transfers between devices: 0.02 us -> 1.86 us  [on_device(): lax.ppermute(tail, 'ctx', next_pairs + [(j, i) for i, j in next_pairs])]
    unnamed x12 -> x14, local copies, waits for them, and re-layouts: 0.99 us -> 1.25 us
  transfers between devices with their start and end apart: 14 -> 15, of which waited for: 6 -> 6; matrix products, arithmetic and copies ran while one was open for 0% -> 0% of each run, Pallas kernels for 17% -> 16%
where the time goes in v4:
time: 45.8 us; the launch traced here: 45.6 us
  starting transfers between devices  17.6 us (38%)
  waiting for transfers between devices  15.5 us (34%)
  Pallas kernels  10.9 us (24%)
  local copies, waits for them, and re-layouts  1.32 us (3%)
    ppermute x14, waiting for transfers between devices, swap(): return lax.ppermute(x, 'ctx', [(i, i ^ mask) for i in range(n)])  13.7 us
    ppermute x14, starting transfers between devices, swap(): return lax.ppermute(x, 'ctx', [(i, i ^ mask) for i in range(n)])  13 us
    pallas_call x13, Pallas kernels, call(): pl.pallas_call(kernel, out_shape=out_shape, in_specs=in_specs, out_specs=...  10.9 us
    ppermute x1, starting transfers between devices, on_device(): lax.ppermute(tail, 'ctx', next_pairs + [(j, i) for i, j in next_pairs])  4.54 us
    ppermute x1, waiting for transfers between devices, on_device(): lax.ppermute(tail, 'ctx', next_pairs + [(j, i) for i, j in next_pairs])  1.86 us
    unnamed x14, local copies, waits for them, and re-layouts  1.25 us
  transfers between devices with their start and end apart: 15, of which 6 were waited for; matrix products, arithmetic and copies ran while one was open for 0% of the time, Pallas kernels for 16%

profile of v4, /device:TPU:1, one launch (start us, length us, event | category | flops | bytes accessed | tf_op | source)
XLA Modules:
  0.0 45.6 jit_solution(9183848263312236483)
XLA Ops:
  0.0 0.9 %tail.1 = bf16[8,4096]{1,0:T(8,128)(2,1)S(1)} custom-call(bf16[128,4096]{1,0:T(8,128)(2,1)} %k_ref.5), custom_call_target="tpu_custom_call" | custom-call | tf_op jit(solution)/shard_map/tail/pallas_call | solution.py:42
  1.2 4.5 %collective-permute-start = (bf16[8,4096]{1,0:T(8,128)(2,1)S(1)}, bf16[8,4096]{1,0:T(8,128)(2,1)S(1)}, u32[]{:S(2)}, u32[]{:S(2)}) collective-permute-start(bf16[8,4096]{1,0:T(8,128)(2,1)S(1)} %tail.1), channel_id=1, source_target_pairs={{1,2},{3,4},{5,6},{7,8},{9,10},{11,12},{13,14},{2,1},{4,3},{6,5},{... | collective-permute-start | bytes 196616 | tf_op jit(solution)/shard_map/ppermute | solution.py:303
  5.8 1.9 %collective-permute-done.chip_halo_ref = bf16[8,4096]{1,0:T(8,128)(2,1)S(1)} collective-permute-done((bf16[8,4096]{1,0:T(8,128)(2,1)S(1)}, bf16[8,4096]{1,0:T(8,128)(2,1)S(1)}, u32[]{:S(2)}, u32[]{:S(2)}) %collective-permute-start) | collective-permute-done | bytes 65568 | tf_op jit(solution)/shard_map/ppermute | solution.py:303
  7.7 1.2 %copy-done.2 = bf16[128,4096]{1,0:T(8,128)(2,1)S(1)} copy-done((bf16[128,4096]{1,0:T(8,128)(2,1)S(1)}, bf16[128,4096]{1,0:T(8,128)(2,1)}, u32[]{:S(2)}) %copy-start.2) | copy-done | bytes 1048600
  8.9 1.0 %states_other.1 = bf16[4,528,128]{2,1,0:T(8,128)(2,1)S(1)} custom-call(bf16[128,4096]{1,0:T(8,128)(2,1)S(1)} %copy-done.1, bf16[8,4096]{1,0:T(8,128)(2,1)S(1)} %collective-permute-done.chip_halo_ref, bf16[8,4096]{1,0:T(8,128)(2,1)S(1)} %collective-permute-done.1.core_halo_ref, bf16[128,4096]{1,0:T(8,128)(2,1)S(1)} %copy-done.2, f32[4,4096]{1,0:T(4,128)S(1)} %copy-done.4, ...), custom_call_target="tpu_custom_call" | custom-call | tf_op jit(solution)/shard_map/states_other/pallas_call | solution.py:42
  10.0 1.0 %states_mine.1.own_ref = bf16[4,528,128]{2,1,0:T(8,128)(2,1)S(1)} custom-call(bf16[128,4096]{1,0:T(8,128)(2,1)S(1)} %copy-done.1, bf16[8,4096]{1,0:T(8,128)(2,1)S(1)} %collective-permute-done.chip_halo_ref, bf16[8,4096]{1,0:T(8,128)(2,1)S(1)} %collective-permute-done.1.core_halo_ref, bf16[128,4096]{1,0:T(8,128)(2,1)S(1)} %copy-done.2, ...), custom_call_target="tpu_custom_call" | custom-call | tf_op jit(solution)/shard_map/states_mine/pallas_call | solution.py:42
  12.2 2.1 %collective-permute-start.3 = (bf16[528,128]{1,0:T(8,128)(2,1)S(1)}, bf16[528,128]{1,0:T(8,128)(2,1)S(1)}, u32[]{:S(2)}, u32[]{:S(2)}) collective-permute-start(bf16[528,128]{1,0:T(8,128)(2,1)S(1)} %get-tuple-element.41), channel_id=1, source_target_pairs={{0,2},{1,3},{2,0},{3,1},{4,6},{5,7},{6,4},{7,5},{8,10},{9,11},{10,... | collective-permute-start | bytes 405512 | tf_op jit(solution)/shard_map/ppermute | solution.py:282
  14.3 1.5 %collective-permute-start.4 = (bf16[528,128]{1,0:T(8,128)(2,1)S(1)}, bf16[528,128]{1,0:T(8,128)(2,1)S(1)}, u32[]{:S(2)}, u32[]{:S(2)}) collective-permute-start(bf16[528,128]{1,0:T(8,128)(2,1)S(1)} %get-tuple-element.40), channel_id=1, source_target_pairs={{0,6},{1,7},{2,4},{3,5},{4,2},{5,3},{6,0},{7,1},{8,14},{9,15},{10,... | collective-permute-start | bytes 405512 | tf_op jit(solution)/shard_map/ppermute | solution.py:282
  15.8 0.9 %collective-permute-start.11 = (bf16[4,528,128]{2,1,0:T(8,128)(2,1)S(1)}, bf16[4,528,128]{2,1,0:T(8,128)(2,1)S(1)}, u32[]{:S(2)}, u32[]{:S(2)}) collective-permute-start(bf16[4,528,128]{2,1,0:T(8,128)(2,1)S(1)} %states_mine.1.own_ref), channel_id=1, source_target_pairs={{0,1},{1,0},{2,3},{3,2},{4,5},{5,4},{6,7},{7,6},{8,9},{9,8},{10,11... | collective-permute-start | bytes 1622024 | tf_op jit(solution)/shard_map/ppermute | solution.py:282
  16.8 1.1 %intra_mine.1.refs_4_.refs_7_.refs_10_ = f32[16,128,128]{2,1,0:T(8,128)S(1)} custom-call(bf16[128,4096]{1,0:T(8,128)(2,1)S(1)} %copy-done, bf16[128,4096]{1,0:T(8,128)(2,1)S(1)} %copy-done.1, bf16[8,4096]{1,0:T(8,128)(2,1)S(1)} %collective-permute-done.chip_halo_ref, bf16[8,4096]{1,0:T(8,128)(2,1)S(1)} %collective-permute-done.1.core_halo_ref, ...), custom_call_target="tpu_custom_call" | custom-call | tf_op jit(solution)/shard_map/intra_mine/pallas_call | solution.py:42
  17.9 2.4 %collective-permute-done.3.refs_1_ = bf16[528,128]{1,0:T(8,128)(2,1)S(1)} collective-permute-done((bf16[528,128]{1,0:T(8,128)(2,1)S(1)}, bf16[528,128]{1,0:T(8,128)(2,1)S(1)}, u32[]{:S(2)}, u32[]{:S(2)}) %collective-permute-start.3) | collective-permute-done | bytes 135200 | tf_op jit(solution)/shard_map/ppermute | solution.py:282
  20.3 1.8 %collective-permute-done.5.refs_2_ = bf16[528,128]{1,0:T(8,128)(2,1)S(1)} collective-permute-done((bf16[528,128]{1,0:T(8,128)(2,1)S(1)}, bf16[528,128]{1,0:T(8,128)(2,1)S(1)}, u32[]{:S(2)}, u32[]{:S(2)}) %collective-permute-start.5) | collective-permute-done | bytes 135200 | tf_op jit(solution)/shard_map/ppermute | solution.py:282
  22.3 2.3 %collective-permute-start.6 = (bf16[528,128]{1,0:T(8,128)(2,1)S(1)}, bf16[528,128]{1,0:T(8,128)(2,1)S(1)}, u32[]{:S(2)}, u32[]{:S(2)}) collective-permute-start(bf16[528,128]{1,0:T(8,128)(2,1)S(1)} %span_state.1), channel_id=1, source_target_pairs={{0,8},{1,9},{2,10},{3,11},{4,12},{5,13},{6,14},{7,15},{8,0},{9,1},... | collective-permute-start | bytes 405512 | tf_op jit(solution)/shard_map/ppermute | solution.py:282
  24.5 1.1 %intra_other.1.refs_7_.refs_4_ = f32[16,128,128]{2,1,0:T(8,128)S(1)} custom-call(bf16[128,4096]{1,0:T(8,128)(2,1)S(1)} %copy-done, bf16[128,4096]{1,0:T(8,128)(2,1)S(1)} %copy-done.1, bf16[8,4096]{1,0:T(8,128)(2,1)S(1)} %collective-permute-done.chip_halo_ref, bf16[8,4096]{1,0:T(8,128)(2,1)S(1)} %collective-permute-done.1.core_halo_ref, ...), custom_call_target="tpu_custom_call" | custom-call | tf_op jit(solution)/shard_map/intra_other/pallas_call | solution.py:42
  25.7 5.0 %collective-permute-done.6.refs_4_ = bf16[528,128]{1,0:T(8,128)(2,1)S(1)} collective-permute-done((bf16[528,128]{1,0:T(8,128)(2,1)S(1)}, bf16[528,128]{1,0:T(8,128)(2,1)S(1)}, u32[]{:S(2)}, u32[]{:S(2)}) %collective-permute-start.6) | collective-permute-done | bytes 135200 | tf_op jit(solution)/shard_map/ppermute | solution.py:282
  30.9 1.5 %collective-permute-start.10 = (bf16[512,128]{1,0:T(8,128)(2,1)S(1)}, bf16[512,128]{1,0:T(8,128)(2,1)S(1)}, u32[]{:S(2)}, u32[]{:S(2)}) collective-permute-start(bf16[512,128]{1,0:T(8,128)(2,1)S(1)} %get-tuple-element.43.refs_3_), channel_id=1, source_target_pairs={{0,1},{1,0},{2,3},{3,2},{4,5},{5,4},{6,7},{7,6},{8,9},{9,8},{10,11... | collective-permute-start | bytes 393224 | tf_op jit(solution)/shard_map/ppermute | solution.py:282
  32.4 1.0 %collective-permute-start.9 = (bf16[512,128]{1,0:T(8,128)(2,1)S(1)}, bf16[512,128]{1,0:T(8,128)(2,1)S(1)}, u32[]{:S(2)}, u32[]{:S(2)}) collective-permute-start(bf16[512,128]{1,0:T(8,128)(2,1)S(1)} %get-tuple-element.44), channel_id=1, source_target_pairs={{0,2},{1,3},{2,0},{3,1},{4,6},{5,7},{6,4},{7,5},{8,10},{9,11},{10,... | collective-permute-start | bytes 393224 | tf_op jit(solution)/shard_map/ppermute | solution.py:282
  33.9 1.2 %collective-permute-start.8 = (bf16[512,128]{1,0:T(8,128)(2,1)S(1)}, bf16[512,128]{1,0:T(8,128)(2,1)S(1)}, u32[]{:S(2)}, u32[]{:S(2)}) collective-permute-start(bf16[512,128]{1,0:T(8,128)(2,1)S(1)} %get-tuple-element.45), channel_id=1, source_target_pairs={{0,4},{1,5},{2,6},{3,7},{4,0},{5,1},{6,2},{7,3},{8,12},{9,13},{10,... | collective-permute-start | bytes 393224 | tf_op jit(solution)/shard_map/ppermute | solution.py:282
  35.1 1.2 %out_m0_o0.1.refs_6_ = bf16[128,4096]{1,0:T(8,128)(2,1)} custom-call(bf16[128,4096]{1,0:T(8,128)(2,1)S(1)} %copy-done, f32[8,8,128]{2,1,0:T(8,128)S(1)} %cum.1.cum_ref.refs_1_, f32[1,4096]{1,0:T(1,128)S(1)} %bitcast.18, bf16[512,128]{1,0:T(8,128)(2,1)S(1)} %get-tuple-element.43.refs_3_, f32[16,128,128]{2,1,0:T(8,128)S(1)} %intra_mine.1.refs_4_.refs_7_.refs_10_, ...), custom_call_target="tpu_custom_call" | custom-call | flops 1 | bytes 1 | tf_op jit(solution)/shard_map/out_m0_o0/pallas_call | solution.py:42
  36.3 3.6 %collective-permute-done.9.refs_3_ = bf16[512,128]{1,0:T(8,128)(2,1)S(1)} collective-permute-done((bf16[512,128]{1,0:T(8,128)(2,1)S(1)}, bf16[512,128]{1,0:T(8,128)(2,1)S(1)}, u32[]{:S(2)}, u32[]{:S(2)}) %collective-permute-start.9) | collective-permute-done | bytes 131104 | tf_op jit(solution)/shard_map/ppermute | solution.py:282
  39.9 1.3 %collective-permute-start.14 = (bf16[512,128]{1,0:T(8,128)(2,1)S(1)}, bf16[512,128]{1,0:T(8,128)(2,1)S(1)}, u32[]{:S(2)}, u32[]{:S(2)}) collective-permute-start(bf16[512,128]{1,0:T(8,128)(2,1)S(1)} %collective-permute-done.9.refs_3_), channel_id=1, source_target_pairs={{0,1},{1,0},{2,3},{3,2},{4,5},{5,4},{6,7},{7,6},{8,9},{9,8},{10,11... | collective-permute-start | bytes 393224 | tf_op jit(solution)/shard_map/ppermute | solution.py:282
  41.2 1.1 %out_m1.1.refs_12_ = bf16[128,4096]{1,0:T(8,128)(2,1)} custom-call(bf16[128,4096]{1,0:T(8,128)(2,1)S(1)} %copy-done, f32[8,8,128]{2,1,0:T(8,128)S(1)} %cum.1.cum_ref.refs_1_, f32[1,4096]{1,0:T(1,128)S(1)} %bitcast.19, bf16[512,128]{1,0:T(8,128)(2,1)S(1)} %collective-permute-done.9.refs_3_, ...), custom_call_target="tpu_custom_call", output_to_operand_aliasing={{}: (6, {})} | custom-call | flops 1 | bytes 1 | tf_op jit(solution)/shard_map/out_m1/pallas_call | solution.py:42
  42.8 1.5 %out_o1_m3_m2.1.refs_9_ = bf16[128,4096]{1,0:T(8,128)(2,1)} custom-call(bf16[128,4096]{1,0:T(8,128)(2,1)S(1)} %copy-done, f32[8,8,128]{2,1,0:T(8,128)S(1)} %cum.1.cum_ref.refs_1_, f32[1,4096]{1,0:T(1,128)S(1)} %bitcast.20, bf16[512,128]{1,0:T(8,128)(2,1)S(1)} %collective-permute-done.14.refs_3_, ...), custom_call_target="tpu_custom_call", output_to_operand_aliasing={{}: (12, {})} | custom-call | flops 1 | bytes 1 | tf_op jit(solution)/shard_map/out_o1_m3_m2/pallas_call | solution.py:42
  44.3 1.2 %out_o3_o2.1 = bf16[128,4096]{1,0:T(8,128)(2,1)} custom-call(bf16[128,4096]{1,0:T(8,128)(2,1)S(1)} %copy-done, f32[8,8,128]{2,1,0:T(8,128)S(1)} %cum.1.cum_ref.refs_1_, f32[1,4096]{1,0:T(1,128)S(1)} %bitcast.21, bf16[512,128]{1,0:T(8,128)(2,1)S(1)} %collective-permute-done.12.refs_3_, ...), custom_call_target="tpu_custom_call", output_to_operand_aliasing={{}: (9, {})} | custom-call | flops 1 | bytes 1 | tf_op jit(solution)/shard_map/out_o3_o2/pallas_call | solution.py:42
  (35 shorter events, 2.9 us)
Async XLA Ops:
  0.0 7.7 %copy-start.1 = (bf16[128,4096]{1,0:T(8,128)(2,1)S(1)}, bf16[128,4096]{1,0:T(8,128)(2,1)}, u32[]{:S(2)}) copy-start(bf16[128,4096]{1,0:T(8,128)(2,1)} %k_ref.5) | copy-start | bytes 3145732
  0.0 1.0 %copy-start.6 = (f32[128,32]{0,1:T(8,128)S(1)}, f32[128,32]{0,1:T(8,128)}, u32[]{:S(2)}) copy-start(f32[128,32]{0,1:T(8,128)} %param.9) | copy-start | bytes 49156
  0.0 7.7 %copy-start.4 = (f32[4,4096]{1,0:T(4,128)S(1)}, f32[4,4096]{1,0:T(4,128)}, u32[]{:S(2)}) copy-start(f32[4,4096]{1,0:T(4,128)} %w_ref.7) | copy-start | bytes 196612
  1.2 6.5 %collective-permute-start = (bf16[8,4096]{1,0:T(8,128)(2,1)S(1)}, bf16[8,4096]{1,0:T(8,128)(2,1)S(1)}, u32[]{:S(2)}, u32[]{:S(2)}) collective-permute-start(bf16[8,4096]{1,0:T(8,128)(2,1)S(1)} %tail.1), channel_id=1, source_target_pairs={{1,2},{3,4},{5,6},{7,8},{9,10},{11,12},{13,14},{2,1},{4,3},{6,5},{... | collective-permute-start | bytes 196616 | tf_op jit(solution)/shard_map/ppermute | solution.py:303
  5.7 1.9 %collective-permute-start.1 = (bf16[8,4096]{1,0:T(8,128)(2,1)S(1)}, bf16[8,4096]{1,0:T(8,128)(2,1)S(1)}, u32[]{:S(2)}, u32[]{:S(2)}) collective-permute-start(bf16[8,4096]{1,0:T(8,128)(2,1)S(1)} %tail.1), channel_id=1, source_target_pairs={{0,1},{1,0},{2,3},{3,2},{4,5},{5,4},{6,7},{7,6},{8,9},{9,8},{10,11... | collective-permute-start | bytes 196616 | tf_op jit(solution)/shard_map/ppermute | solution.py:282
  7.7 1.2 %copy-start.2 = (bf16[128,4096]{1,0:T(8,128)(2,1)S(1)}, bf16[128,4096]{1,0:T(8,128)(2,1)}, u32[]{:S(2)}) copy-start(bf16[128,4096]{1,0:T(8,128)(2,1)} %v_ref.3) | copy-start | bytes 3145732
  9.9 2.0 %collective-permute-start.2 = (bf16[4,528,128]{2,1,0:T(8,128)(2,1)S(1)}, bf16[4,528,128]{2,1,0:T(8,128)(2,1)S(1)}, u32[]{:S(2)}, u32[]{:S(2)}) collective-permute-start(bf16[4,528,128]{2,1,0:T(8,128)(2,1)S(1)} %states_other.1), channel_id=1, source_target_pairs={{0,1},{1,0},{2,3},{3,2},{4,5},{5,4},{6,7},{7,6},{8,9},{9,8},{10,11... | collective-permute-start | bytes 1622024 | tf_op jit(solution)/shard_map/ppermute | solution.py:282
  11.0 5.8 %copy-start = (bf16[128,4096]{1,0:T(8,128)(2,1)S(1)}, bf16[128,4096]{1,0:T(8,128)(2,1)}, u32[]{:S(2)}) copy-start(bf16[128,4096]{1,0:T(8,128)(2,1)} %refs_0_.7) | copy-start | bytes 3145732
  11.0 5.8 %copy-start.3 = (bf16[128,4096]{1,0:T(8,128)(2,1)S(1)}, bf16[128,4096]{1,0:T(8,128)(2,1)}, u32[]{:S(2)}) copy-start(bf16[128,4096]{1,0:T(8,128)(2,1)} %v_ref.3) | copy-start | bytes 3145732
  12.2 8.2 %collective-permute-start.3 = (bf16[528,128]{1,0:T(8,128)(2,1)S(1)}, bf16[528,128]{1,0:T(8,128)(2,1)S(1)}, u32[]{:S(2)}, u32[]{:S(2)}) collective-permute-start(bf16[528,128]{1,0:T(8,128)(2,1)S(1)} %get-tuple-element.41), channel_id=1, source_target_pairs={{0,2},{1,3},{2,0},{3,1},{4,6},{5,7},{6,4},{7,5},{8,10},{9,11},{10,... | collective-permute-start | bytes 405512 | tf_op jit(solution)/shard_map/ppermute | solution.py:282
  14.3 6.0 %collective-permute-start.4 = (bf16[528,128]{1,0:T(8,128)(2,1)S(1)}, bf16[528,128]{1,0:T(8,128)(2,1)S(1)}, u32[]{:S(2)}, u32[]{:S(2)}) collective-permute-start(bf16[528,128]{1,0:T(8,128)(2,1)S(1)} %get-tuple-element.40), channel_id=1, source_target_pairs={{0,6},{1,7},{2,4},{3,5},{4,2},{5,3},{6,0},{7,1},{8,14},{9,15},{10,... | collective-permute-start | bytes 405512 | tf_op jit(solution)/shard_map/ppermute | solution.py:282
  15.8 6.3 %collective-permute-start.5 = (bf16[528,128]{1,0:T(8,128)(2,1)S(1)}, bf16[528,128]{1,0:T(8,128)(2,1)S(1)}, u32[]{:S(2)}, u32[]{:S(2)}) collective-permute-start(bf16[528,128]{1,0:T(8,128)(2,1)S(1)} %get-tuple-element.39), channel_id=1, source_target_pairs={{0,4},{1,5},{2,6},{3,7},{4,0},{5,1},{6,2},{7,3},{8,12},{9,13},{10,... | collective-permute-start | bytes 405512 | tf_op jit(solution)/shard_map/ppermute | solution.py:282
  15.8 19.2 %collective-permute-start.11 = (bf16[4,528,128]{2,1,0:T(8,128)(2,1)S(1)}, bf16[4,528,128]{2,1,0:T(8,128)(2,1)S(1)}, u32[]{:S(2)}, u32[]{:S(2)}) collective-permute-start(bf16[4,528,128]{2,1,0:T(8,128)(2,1)S(1)} %states_mine.1.own_ref), channel_id=1, source_target_pairs={{0,1},{1,0},{2,3},{3,2},{4,5},{5,4},{6,7},{7,6},{8,9},{9,8},{10,11... | collective-permute-start | bytes 1622024 | tf_op jit(solution)/shard_map/ppermute | solution.py:282
  22.3 8.4 %collective-permute-start.6 = (bf16[528,128]{1,0:T(8,128)(2,1)S(1)}, bf16[528,128]{1,0:T(8,128)(2,1)S(1)}, u32[]{:S(2)}, u32[]{:S(2)}) collective-permute-start(bf16[528,128]{1,0:T(8,128)(2,1)S(1)} %span_state.1), channel_id=1, source_target_pairs={{0,8},{1,9},{2,10},{3,11},{4,12},{5,13},{6,14},{7,15},{8,0},{9,1},... | collective-permute-start | bytes 405512 | tf_op jit(solution)/shard_map/ppermute | solution.py:282
  30.8 4.3 %copy-start.5 = (f32[4096]{0:T(1024)S(1)}, f32[4096]{0:T(1024)}, u32[]{:S(2)}) copy-start(f32[4096]{0:T(1024)} %param.11) | copy-start | bytes 49156
  30.9 4.2 %collective-permute-start.10 = (bf16[512,128]{1,0:T(8,128)(2,1)S(1)}, bf16[512,128]{1,0:T(8,128)(2,1)S(1)}, u32[]{:S(2)}, u32[]{:S(2)}) collective-permute-start(bf16[512,128]{1,0:T(8,128)(2,1)S(1)} %get-tuple-element.43.refs_3_), channel_id=1, source_target_pairs={{0,1},{1,0},{2,3},{3,2},{4,5},{5,4},{6,7},{7,6},{8,9},{9,8},{10,11... | collective-permute-start | bytes 393224 | tf_op jit(solution)/shard_map/ppermute | solution.py:282
  32.4 7.5 %collective-permute-start.9 = (bf16[512,128]{1,0:T(8,128)(2,1)S(1)}, bf16[512,128]{1,0:T(8,128)(2,1)S(1)}, u32[]{:S(2)}, u32[]{:S(2)}) collective-permute-start(bf16[512,128]{1,0:T(8,128)(2,1)S(1)} %get-tuple-element.44), channel_id=1, source_target_pairs={{0,2},{1,3},{2,0},{3,1},{4,6},{5,7},{6,4},{7,5},{8,10},{9,11},{10,... | collective-permute-start | bytes 393224 | tf_op jit(solution)/shard_map/ppermute | solution.py:282
  33.5 8.8 %collective-permute-start.7 = (bf16[512,128]{1,0:T(8,128)(2,1)S(1)}, bf16[512,128]{1,0:T(8,128)(2,1)S(1)}, u32[]{:S(2)}, u32[]{:S(2)}) collective-permute-start(bf16[512,128]{1,0:T(8,128)(2,1)S(1)} %get-tuple-element.46), channel_id=1, source_target_pairs={{0,6},{1,7},{2,4},{3,5},{4,2},{5,3},{6,0},{7,1},{8,14},{9,15},{10,... | collective-permute-start | bytes 393224 | tf_op jit(solution)/shard_map/ppermute | solution.py:282
  33.9 8.4 %collective-permute-start.8 = (bf16[512,128]{1,0:T(8,128)(2,1)S(1)}, bf16[512,128]{1,0:T(8,128)(2,1)S(1)}, u32[]{:S(2)}, u32[]{:S(2)}) collective-permute-start(bf16[512,128]{1,0:T(8,128)(2,1)S(1)} %get-tuple-element.45), channel_id=1, source_target_pairs={{0,4},{1,5},{2,6},{3,7},{4,0},{5,1},{6,2},{7,3},{8,12},{9,13},{10,... | collective-permute-start | bytes 393224 | tf_op jit(solution)/shard_map/ppermute | solution.py:282
  39.9 2.9 %collective-permute-start.14 = (bf16[512,128]{1,0:T(8,128)(2,1)S(1)}, bf16[512,128]{1,0:T(8,128)(2,1)S(1)}, u32[]{:S(2)}, u32[]{:S(2)}) collective-permute-start(bf16[512,128]{1,0:T(8,128)(2,1)S(1)} %collective-permute-done.9.refs_3_), channel_id=1, source_target_pairs={{0,1},{1,0},{2,3},{3,2},{4,5},{5,4},{6,7},{7,6},{8,9},{9,8},{10,11... | collective-permute-start | bytes 393224 | tf_op jit(solution)/shard_map/ppermute | solution.py:282
  42.3 2.0 %collective-permute-start.12 = (bf16[512,128]{1,0:T(8,128)(2,1)S(1)}, bf16[512,128]{1,0:T(8,128)(2,1)S(1)}, u32[]{:S(2)}, u32[]{:S(2)}) collective-permute-start(bf16[512,128]{1,0:T(8,128)(2,1)S(1)} %collective-permute-done.7.refs_6_), channel_id=1, source_target_pairs={{0,1},{1,0},{2,3},{3,2},{4,5},{5,4},{6,7},{7,6},{8,9},{9,8},{10,11... | collective-permute-start | bytes 393224 | tf_op jit(solution)/shard_map/ppermute | solution.py:282
  42.4 1.9 %collective-permute-start.13 = (bf16[512,128]{1,0:T(8,128)(2,1)S(1)}, bf16[512,128]{1,0:T(8,128)(2,1)S(1)}, u32[]{:S(2)}, u32[]{:S(2)}) collective-permute-start(bf16[512,128]{1,0:T(8,128)(2,1)S(1)} %collective-permute-done.8.refs_9_), channel_id=1, source_target_pairs={{0,1},{1,0},{2,3},{3,2},{4,5},{5,4},{6,7},{7,6},{8,9},{9,8},{10,11... | collective-permute-start | bytes 393224 | tf_op jit(solution)/shard_map/ppermute | solution.py:282

commit v5 on v4

--- a/solution.py
+++ b/solution.py
@@ -51,11 +51,9 @@
     )(*args)
 
 
-def tail_kernel(k_ref, out_ref, sem):
+def tail_kernel(k_ref, out_ref):
     rows = k_ref.shape[0]
-    copy = pltpu.make_async_copy(k_ref.at[rows - HALO : rows, :], out_ref, sem)
-    copy.start()
-    copy.wait()
+    out_ref[...] = k_ref[rows - HALO : rows, :]
 
 
 def cum_kernel(heads, decay_ref, out_ref):
@@ -82,25 +80,40 @@
     return hi, mid, low
 
 
+def side(part, heads, size):
+    base = heads * size + part * PARTS
+    return slice(base, base + PARTS)
+
+
+def padded(rows):
+    rows = jnp.concatenate(rows, 0)
+    spare = jnp.zeros((PARTS - rows.shape[0], rows.shape[1]), F32)
+    return jnp.concatenate([rows, spare], 0).astype(BF16)
+
+
 def put_decay(out, decays, heads, size):
-    base = heads * size
-    parts = [p.astype(F32) for p in three_parts(decays)]
-    spare = jnp.zeros((PARTS - 3 * heads, decays.shape[1]), F32)
-    out[base : base + PARTS, :] = jnp.concatenate(parts + [spare], 0).astype(BF16)
+    out[side(0, heads, size), :] = padded([p.astype(F32) for p in three_parts(decays)])
 
 
 def get_decay(packet, heads, size):
-    base = heads * size
-    tail = packet[base : base + PARTS, :].astype(F32)
+    tail = packet[side(0, heads, size), :].astype(F32)
     return tail[0:heads] + tail[heads : 2 * heads] + tail[2 * heads : 3 * heads]
 
 
-def conv_keys(k_ref, chip_halo_ref, core_halo_ref, w_ref, ext, cols):
+def edge_states(values, edges, heads):
+    row = lax.broadcasted_iota(jnp.int32, values.shape, 0)
+    out = []
+    for j in range(heads):
+        picked = jnp.where(lax.rem(row, heads) == j, values.astype(F32), 0.0).astype(BF16)
+        out.append(
+            lax.dot_general(picked, edges, (((0,), (0,)), ((), ())), preferred_element_type=F32)
+        )
+    return out
+
+
+def conv_keys(k_ref, halo, w_ref, ext, cols):
     rows = k_ref.shape[0]
-    core, _ = position()
-    ext[0:HALO, :] = jnp.where(
-        core == 0, chip_halo_ref[:, cols].astype(F32), core_halo_ref[:, cols].astype(F32)
-    )
+    ext[0:HALO, :] = halo
     ext[HALO : HALO + rows, :] = k_ref[:, cols].astype(F32)
     total = None
     for j in range(w_ref.shape[0]):
@@ -109,33 +122,67 @@
     return total.astype(BF16)
 
 
-def state_kernel(mine, heads, size, k_ref, chip_halo_ref, core_halo_ref, v_ref, w_ref, cum_ref, out_ref,
-    ext, held):
-    for g in range(CHIPS):
-        b = head_group(mine, g)
-        cum = cum_ref[b]
+def state_kernel(
+    mine, heads, size, k_hbm, v_hbm, w_hbm, decay_hbm, out_ref,
+    k_buf, v_buf, w_buf, decay_buf, cum_ref, ext, held, sems,
+):
+    rows, wide = k_buf.shape[1:]
+    taps = w_buf.shape[1]
+    copies = [pltpu.make_async_copy(decay_hbm, decay_buf, sems.at[3 * CHIPS])]
+    copies[0].start()
+    for g in range(CHIPS):
+        cols = columns(head_group(mine, g) * wide, 0, wide)
+        for i, (source, buf) in enumerate(((k_hbm, k_buf), (w_hbm, w_buf), (v_hbm, v_buf))):
+            copies.append(
+                pltpu.make_async_copy(source.at[:, cols], buf.at[g], sems.at[3 * g + i])
+            )
+            copies[-1].start()
+    copies[0].wait()
+    cum_kernel(heads, decay_buf, cum_ref)
+    none = jnp.zeros((HALO, size), F32)
+    for g in range(CHIPS):
+        for copy in copies[1 + 3 * g : 4 + 3 * g]:
+            copy.wait()
+        cum = cum_ref[head_group(mine, g)]
         ending = jnp.exp(cum[heads : 2 * heads] - cum[0:heads]).T
-        for j in range(heads):
-            cols = columns(b * heads * size, j * size, size)
-            key_conv = conv_keys(k_ref, chip_halo_ref, core_halo_ref, w_ref, ext.at[j], cols)
+        edges, values = [], []
+        for j in range(heads):
+            cols = slice(j * size, (j + 1) * size)
+            key_conv = conv_keys(k_buf.at[g], none, w_buf.at[g], ext.at[j], cols)
             held[g * heads + j] = (key_conv.astype(F32) * ending[:, j : j + 1]).astype(BF16)
-    for g in range(CHIPS):
-        b = head_group(mine, g)
-        for j in range(heads):
-            cols = columns(b * heads * size, j * size, size)
+            last = k_buf[g, rows - HALO : rows, cols].astype(F32)
+            head_edges = []
+            for t in range(taps - 1):
+                terms = [
+                    w_buf[g, i : i + 1, cols] * last[HALO + t - i : HALO + t - i + 1]
+                    for i in range(t + 1, taps)
+                ]
+                head_edges.append(sum(terms[1:], terms[0]))
+            edges.append(head_edges)
+            values.append(v_buf[g, 0:HALO, cols].astype(F32) * ending[0:HALO, j : j + 1])
+        put_decay(out_ref.at[g], jnp.exp(cum[heads : 2 * heads]), heads, size)
+        out_ref[g, side(1, heads, size), :] = padded(
+            [edges[j][t] for t in range(taps - 1) for j in range(heads)]
+        )
+        out_ref[g, side(2, heads, size), :] = padded(
+            [values[j][t : t + 1] for t in range(taps - 1) for j in range(heads)]
+        )
+    for g in range(CHIPS):
+        for j in range(heads):
+            cols = slice(j * size, (j + 1) * size)
             state = lax.dot_general(
-                v_ref[:, cols], held[g * heads + j], (((0,), (0,)), ((), ())),
+                v_buf[g, :, cols], held[g * heads + j], (((0,), (0,)), ((), ())),
                 preferred_element_type=F32,
             )
-            out_ref[g, j * size : (j + 1) * size, :] = state.astype(BF16)
-        put_decay(out_ref.at[g], jnp.exp(cum_ref[b][heads : 2 * heads]), heads, size)
+            out_ref[g, cols, :] = state.astype(BF16)
 
 
 def intra_kernel(
     mine, heads, size, q_ref, k_ref, chip_halo_ref, core_halo_ref, v_ref, w_ref, cum_ref, out_ref,
-    ext, held
+    ext, held,
 ):
     rows = q_ref.shape[0]
+    core, _ = position()
     causal = lax.broadcasted_iota(jnp.int32, (rows, rows), 0) >= lax.broadcasted_iota(
         jnp.int32, (rows, rows), 1
     )
@@ -145,7 +192,10 @@
         cum_col = cum.T
         for j in range(heads):
             cols = columns(b * heads * size, j * size, size)
-            key_conv = conv_keys(k_ref, chip_halo_ref, core_halo_ref, w_ref, ext.at[j], cols)
+            halo = jnp.where(
+                core == 0, chip_halo_ref[:, cols].astype(F32), core_halo_ref[:, cols].astype(F32)
+            )
+            key_conv = conv_keys(k_ref, halo, w_ref, ext.at[j], cols)
             scores = lax.dot_general(
                 q_ref[:, cols], key_conv, (((1,), (1,)), ((), ())), preferred_element_type=F32
             )
@@ -169,13 +219,28 @@
         got_decay = get_decay(got_ref.at[g], heads, size)
         own_by = jnp.where(first, got_decay, 1.0)
         got_by = jnp.where(first, 1.0, own_decay)
+
+        def earlier_later(part):
+            own = own_ref[g, side(part, heads, size), :].astype(F32)
+            got = got_ref[g, side(part, heads, size), :].astype(F32)
+            return jnp.where(first, own, got), jnp.where(first, got, own)
+
+        edges, out_edges = earlier_later(1)
+        out_values, values = earlier_later(2)
+        fixes = edge_states(values.astype(BF16), edges.astype(BF16), heads)
         for j in range(heads):
             rows = slice(j * size, (j + 1) * size)
             out_ref[g, rows, :] = (
                 own_ref[g, rows, :].astype(F32) * own_by[j : j + 1]
                 + got_ref[g, rows, :].astype(F32) * got_by[j : j + 1]
+                + fixes[j]
             ).astype(BF16)
         put_decay(out_ref.at[g], own_decay * got_decay, heads, size)
+        later_by = jnp.where(first, got_decay, own_decay)
+        out_ref[g, side(1, heads, size), :] = out_edges.astype(BF16)
+        out_ref[g, side(2, heads, size), :] = padded(
+            [out_values[t * heads : (t + 1) * heads] * later_by for t in range(3)]
+        )
 
 
 def in_order(packets, held):
@@ -184,35 +249,62 @@
         held[chip ^ g] = packets[g][...]
 
 
-def span_kernel(heads, size, *refs):
+def chip_fixes(held, b, edges, heads, size):
+    return edge_states(held[b, side(2, heads, size), :], edges, heads)
+
+
+def last_edge_kernel(heads, size, *refs):
     packets, out_ref, held = refs[:CHIPS], refs[CHIPS], refs[CHIPS + 1]
     in_order(packets, held)
+    out_ref[...] = held[CHIPS - 1, side(1, heads, size), :]
+
+
+def span_kernel(heads, size, *refs):
+    packets, before, (out_ref, held) = refs[:CHIPS], refs[CHIPS:-2], refs[-2:]
+    in_order(packets, held)
     decays = [get_decay(held.at[b], heads, size) for b in range(CHIPS)]
+    fixes = [
+        chip_fixes(held, b, held[b - 1, side(1, heads, size), :], heads, size)
+        for b in range(1, CHIPS)
+    ]
+    fixes.insert(0, chip_fixes(held, 0, before[0][...], heads, size) if before else None)
     for j in range(heads):
         rows = slice(j * size, (j + 1) * size)
         acc = held[0, rows, :].astype(F32)
+        if before:
+            acc = acc + fixes[0][j]
         for b in range(1, CHIPS):
-            acc = acc * decays[b][j : j + 1] + held[b, rows, :].astype(F32)
+            acc = acc * decays[b][j : j + 1] + (held[b, rows, :].astype(F32) + fixes[b][j])
         out_ref[rows, :] = acc.astype(BF16)
     whole = decays[0]
     for b in range(1, CHIPS):
         whole = whole * decays[b]
     put_decay(out_ref, whole, heads, size)
+    out_ref[side(1, heads, size), :] = held[CHIPS - 1, side(1, heads, size), :]
+    out_ref[side(2, heads, size), :] = held[0, side(2, heads, size), :]
 
 
 def spread_kernel(heads, size, *refs):
-    packets, before, out_ref, held = refs[:CHIPS], refs[CHIPS], refs[CHIPS + 1], refs[CHIPS + 2]
+    packets, before, known, (out_ref, held) = refs[:CHIPS], refs[CHIPS], refs[CHIPS + 1 : -2], refs[-2:]
     _, chip = position()
     later = lax.axis_index("ctx") >= SPAN
     in_order(packets, held)
     decays = [get_decay(held.at[b], heads, size) for b in range(CHIPS)]
+    edges = known[0][...] if known else before[side(1, heads, size), :]
+    edges = [jnp.where(later, edges.astype(F32), 0.0).astype(BF16)]
+    edges += [held[b, side(1, heads, size), :] for b in range(CHIPS - 1)]
+    fixes = [chip_fixes(held, b, edges[b], heads, size) for b in range(CHIPS - 1)]
     for j in range(heads):
         rows = slice(j * size, (j + 1) * size)
         acc = jnp.where(later, before[rows, :].astype(F32), 0.0)
         out_ref[chip, rows, :] = acc.astype(BF16)
         for b in range(1, CHIPS):
-            acc = acc * decays[b - 1][j : j + 1] + held[b - 1, rows, :].astype(F32)
+            acc = acc * decays[b - 1][j : j + 1] + (
+                held[b - 1, rows, :].astype(F32) + fixes[b - 1][j]
+            )
             out_ref[chip ^ b, rows, :] = acc.astype(BF16)
+    for b in range(CHIPS):
+        out_ref[chip ^ b, heads * size : heads * size + PARTS, :] = edges[b]
 
 
 def out_kernel(items, heads, size, *refs):
@@ -226,10 +318,15 @@
         b = head_group(mine, g)
         started = jnp.exp(cum_ref[b][0:heads]).T
         by = jnp.where(second, get_decay(sib_ref.at[g], heads, size), 1.0)
+        fixes = edge_states(
+            sib_ref[g, side(2, heads, size), :],
+            prefix_ref[heads * size : heads * size + PARTS, :],
+            heads,
+        )
         for j in range(heads):
             cols = columns(b * heads * size, j * size, size)
             rows = slice(j * size, (j + 1) * size)
-            sib = jnp.where(second, sib_ref[g, rows, :].astype(F32), 0.0)
+            sib = jnp.where(second, sib_ref[g, rows, :].astype(F32) + fixes[j], 0.0)
             prefix = prefix_ref[rows, :].astype(F32) * by[j : j + 1] + sib
             inter = lax.dot_general(
                 q_ref[:, cols], prefix.astype(BF16), (((1,), (1,)), ((), ())),
@@ -255,9 +352,10 @@
 
 def join_spans(earlier, later, heads, size):
     base = heads * size
+    own = side(0, heads, size)
 
     def decay(x):
-        tail = x[base:].astype(F32)
+        tail = x[own].astype(F32)
         return tail[0:heads] + tail[heads : 2 * heads] + tail[2 * heads : 3 * heads]
 
     by = decay(later)
@@ -274,8 +372,9 @@
     head_count = log_decay.shape[1]
     size = width // head_count
     heads = head_count // SPAN
+    taps = conv_weight.shape[0]
     half = CHIPS * heads
-    packet = heads * size + PARTS
+    packet = heads * size + 3 * PARTS
     n = lax.axis_size("ctx")
 
     def swap(x, mask):
@@ -284,24 +383,6 @@
     def shift(x, by):
         return lax.ppermute(x, "ctx", [(i, i + by) for i in range(n - by)])
 
-    tail = call(
-        tail_kernel,
-        "tail",
-        pltpu.VMEM((HALO, width), BF16),
-        key_input,
-        in_specs=[HBM],
-        scratch=[pltpu.SemaphoreType.DMA(())],
-    )
-    cum = call(
-        functools.partial(cum_kernel, heads),
-        "cum",
-        pltpu.VMEM((SPAN, 2 * heads, rows), F32),
-        log_decay.T,
-    )
-    tail, cum, keys, values = lax.optimization_barrier((tail, cum, key_input, value_input))
-    next_pairs = [(i, i + 1) for i in range(1, n - 1, 2)]
-    chip_halo = lax.ppermute(tail, "ctx", next_pairs + [(j, i) for i, j in next_pairs])
-    core_halo = swap(tail, 1)
     gain = norm_gain.reshape(1, width)
     ext = pltpu.VMEM((heads, rows + HALO, size), F32)
     held = pltpu.VMEM((half, rows, size), BF16)
@@ -311,8 +392,18 @@
             functools.partial(state_kernel, mine, heads, size),
             "states_mine" if mine else "states_other",
             pltpu.VMEM((CHIPS, packet, size), BF16),
-            keys, chip_halo, core_halo, values, conv_weight, cum,
-            scratch=[ext, pltpu.VMEM((half, rows, size), BF16)],
+            key_input, value_input, conv_weight, log_decay.T,
+            in_specs=[HBM] * 4,
+            scratch=[
+                pltpu.VMEM((CHIPS, rows, heads * size), BF16),
+                pltpu.VMEM((CHIPS, rows, heads * size), BF16),
+                pltpu.VMEM((CHIPS, taps, heads * size), F32),
+                pltpu.VMEM((head_count, rows), F32),
+                pltpu.VMEM((SPAN, 2 * heads, rows), F32),
+                ext,
+                held,
+                pltpu.SemaphoreType.DMA((3 * CHIPS + 1,)),
+            ],
         )
 
     def intra_part(mine, q):
@@ -320,7 +411,7 @@
             functools.partial(intra_kernel, mine, heads, size),
             "intra_mine" if mine else "intra_other",
             pltpu.VMEM((half, rows, size), F32),
-            q, keys, chip_halo, core_halo, values, conv_weight, cum,
+            q, key_input, chip_halo, core_halo, value_input, conv_weight, cum,
             scratch=[ext, held],
         )
 
@@ -338,18 +429,41 @@
     packets = {0: chip_states[0]}
     for g in EXCHANGE:
         packets[g] = swap(chip_states[g], 2 * g)
-    q_after, chip_states = lax.optimization_barrier((queries, chip_states))
-    intra_mine = intra_part(True, q_after)
-    *late, intra_mine = lax.optimization_barrier((*[packets[g] for g in EXCHANGE], intra_mine))
+    keys_after, decay_after, chip_states = lax.optimization_barrier(
+        (key_input, log_decay, chip_states)
+    )
+    cum = call(
+        functools.partial(cum_kernel, heads),
+        "cum",
+        pltpu.VMEM((SPAN, 2 * heads, rows), F32),
+        decay_after.T,
+    )
+    tail = call(tail_kernel, "tail", pltpu.VMEM((HALO, width), BF16), keys_after)
+    next_pairs = [(i, i + 1) for i in range(1, n - 1, 2)]
+    chip_halo = lax.ppermute(tail, "ctx", next_pairs + [(j, i) for i, j in next_pairs])
+    core_halo = swap(tail, 1)
+    *late, chip_halo, core_halo = lax.optimization_barrier(
+        (*[packets[g] for g in EXCHANGE], chip_halo, core_halo)
+    )
     packets.update(zip(EXCHANGE, late))
     packets = [packets[g] for g in range(CHIPS)]
 
     order = pltpu.VMEM((CHIPS, packet, size), BF16)
+    known = []
+    if n > 2 * SPAN:
+        edge = call(
+            functools.partial(last_edge_kernel, heads, size),
+            "last_edge",
+            pltpu.VMEM((PARTS, size), BF16),
+            *packets,
+            scratch=[order],
+        )
+        known = [shift(edge, SPAN)]
     span = call(
         functools.partial(span_kernel, heads, size),
         "span_state",
         pltpu.VMEM((packet, size), BF16),
-        *packets,
+        *packets, *known,
         scratch=[order],
     )
     before = swap(span, SPAN) if n == 2 * SPAN else shift(span, SPAN)
@@ -358,14 +472,15 @@
         before = join_spans(shift(before, SPAN * reach), before, heads, size)
         reach *= 2
     q_after, span = lax.optimization_barrier((queries, span))
+    intra_mine = intra_part(True, q_after)
     intra_other = intra_part(False, q_after)
-    before, intra_other = lax.optimization_barrier((before, intra_other))
+    before, intra_mine, intra_other = lax.optimization_barrier((before, intra_mine, intra_other))
 
     chip_prefix = call(
         functools.partial(spread_kernel, heads, size),
         "chip_prefix",
-        pltpu.VMEM((CHIPS, heads * size, size), BF16),
-        *packets, before,
+        pltpu.VMEM((CHIPS, heads * size + PARTS, size), BF16),
+        *packets, before, *known,
         scratch=[order],
     )
     own = {0: chip_prefix[0]}
@@ -395,16 +510,12 @@
             ],
         )
 
-    first, *last = EXCHANGE
     result = output([(True, 0), (False, 0)], None)
-    own[first], result = lax.optimization_barrier((own[first], result))
-    other[first] = swap(own[first], 1)
-    result = output([(True, first)], result)
-    *late, result = lax.optimization_barrier((*[own[g] for g in last], result))
-    own.update(zip(last, late))
-    other.update({g: swap(own[g], 1) for g in last})
-    result = output([(False, first)] + [(True, g) for g in last], result)
-    return output([(False, g) for g in last], result)
+    *late, result = lax.optimization_barrier((*[own[g] for g in EXCHANGE], result))
+    own.update(zip(EXCHANGE, late))
+    other.update({g: swap(own[g], 1) for g in EXCHANGE})
+    result = output([(True, g) for g in EXCHANGE], result)
+    return output([(False, g) for g in EXCHANGE], result)
 
 
 def solution(mesh):

time: 45.8 us -> 45.1 us (0.985)
  Pallas kernels: 10.9 us -> 13.5 us
  starting transfers between devices: 17.6 us -> 16.1 us
  local copies, waits for them, and re-layouts: 1.32 us -> 0.13 us
  waiting for transfers between devices: 15.5 us -> 14.8 us
    ppermute x14, waiting for transfers between devices: 13.7 us -> 9.82 us  [swap(): return lax.ppermute(x, 'ctx', [(i, i ^ mask) for i in range(n)])]
    ppermute x1, waiting for transfers between devices: 1.86 us -> 4.96 us  [on_device(): lax.ppermute(tail, 'ctx', next_pairs + [(j, i) for i, j in next_pairs])]
    pallas_call x13 -> x12, Pallas kernels: 10.9 us -> 13.5 us  [call(): pl.pallas_call(kernel, out_shape=out_shape, in_specs=in_specs, out_specs=...]
    unnamed x14 -> x12, local copies, waits for them, and re-layouts: 1.25 us -> 0.05 us
    ppermute x1, starting transfers between devices: 4.54 us -> 3.42 us  [on_device(): lax.ppermute(tail, 'ctx', next_pairs + [(j, i) for i, j in next_pairs])]
  transfers between devices with their start and end apart: 15 -> 15, of which waited for: 6 -> 5; matrix products, arithmetic and copies ran while one was open for 0% -> 0% of each run, Pallas kernels for 16% -> 20%
where the time goes in v5:
time: 45.1 us; the launch traced here: 44.7 us
  starting transfers between devices  16.1 us (36%)
  waiting for transfers between devices  14.8 us (33%)
  Pallas kernels  13.5 us (30%)
    pallas_call x12, Pallas kernels, call(): pl.pallas_call(kernel, out_shape=out_shape, in_specs=in_specs, out_specs=...  13.5 us
    ppermute x14, starting transfers between devices, swap(): return lax.ppermute(x, 'ctx', [(i, i ^ mask) for i in range(n)])  12.6 us
    ppermute x14, waiting for transfers between devices, swap(): return lax.ppermute(x, 'ctx', [(i, i ^ mask) for i in range(n)])  9.82 us
    ppermute x1, waiting for transfers between devices, on_device(): lax.ppermute(tail, 'ctx', next_pairs + [(j, i) for i, j in next_pairs])  4.96 us
    ppermute x1, starting transfers between devices, on_device(): lax.ppermute(tail, 'ctx', next_pairs + [(j, i) for i, j in next_pairs])  3.42 us
  transfers between devices with their start and end apart: 15, of which 5 were waited for; matrix products, arithmetic and copies ran while one was open for 0% of the time, Pallas kernels for 20%

profile of v5, /device:TPU:1, one launch (start us, length us, event | category | flops | bytes accessed | tf_op | source)
XLA Modules:
  0.0 44.7 jit_solution(14973272635642891979)
XLA Ops:
  0.0 2.5 %states_other.1 = bf16[4,560,128]{2,1,0:T(8,128)(2,1)S(1)} custom-call(bf16[128,4096]{1,0:T(8,128)(2,1)} %k_ref.4, bf16[128,4096]{1,0:T(8,128)(2,1)} %v_ref.3, f32[4,4096]{1,0:T(4,128)} %w_ref.3, f32[32,128]{1,0:T(8,128)} %bitcast.22), custom_call_target="tpu_custom_call" | custom-call | tf_op jit(solution)/shard_map/states_other/pallas_call | solution.py:42
  2.6 2.5 %states_mine.1.own_ref = bf16[4,560,128]{2,1,0:T(8,128)(2,1)S(1)} custom-call(bf16[128,4096]{1,0:T(8,128)(2,1)} %k_ref.4, bf16[128,4096]{1,0:T(8,128)(2,1)} %v_ref.3, f32[4,4096]{1,0:T(4,128)} %w_ref.3, f32[32,128]{1,0:T(8,128)} %bitcast.23), custom_call_target="tpu_custom_call" | custom-call | tf_op jit(solution)/shard_map/states_mine/pallas_call | solution.py:42
  5.2 0.4 chip_states.1
  5.6 2.8 %collective-permute-start.3 = (bf16[560,128]{1,0:T(8,128)(2,1)S(1)}, bf16[560,128]{1,0:T(8,128)(2,1)S(1)}, u32[]{:S(2)}, u32[]{:S(2)}) collective-permute-start(bf16[560,128]{1,0:T(8,128)(2,1)S(1)} %get-tuple-element.35), channel_id=1, source_target_pairs={{0,4},{1,5},{2,6},{3,7},{4,0},{5,1},{6,2},{7,3},{8,12},{9,13},{10,... | collective-permute-start | bytes 430088 | tf_op jit(solution)/shard_map/ppermute | solution.py:381
  8.4 1.1 %collective-permute-start.2 = (bf16[560,128]{1,0:T(8,128)(2,1)S(1)}, bf16[560,128]{1,0:T(8,128)(2,1)S(1)}, u32[]{:S(2)}, u32[]{:S(2)}) collective-permute-start(bf16[560,128]{1,0:T(8,128)(2,1)S(1)} %get-tuple-element.36), channel_id=1, source_target_pairs={{0,6},{1,7},{2,4},{3,5},{4,2},{5,3},{6,0},{7,1},{8,14},{9,15},{10,... | collective-permute-start | bytes 430088 | tf_op jit(solution)/shard_map/ppermute | solution.py:381
  9.7 0.6 %collective-permute-start.5 = (bf16[8,4096]{1,0:T(8,128)(2,1)S(1)}, bf16[8,4096]{1,0:T(8,128)(2,1)S(1)}, u32[]{:S(2)}, u32[]{:S(2)}) collective-permute-start(bf16[8,4096]{1,0:T(8,128)(2,1)S(1)} %tail.1), channel_id=1, source_target_pairs={{0,1},{1,0},{2,3},{3,2},{4,5},{5,4},{6,7},{7,6},{8,9},{9,8},{10,11... | collective-permute-start | bytes 196616 | tf_op jit(solution)/shard_map/ppermute | solution.py:381
  10.3 3.4 %collective-permute-start.4 = (bf16[8,4096]{1,0:T(8,128)(2,1)S(1)}, bf16[8,4096]{1,0:T(8,128)(2,1)S(1)}, u32[]{:S(2)}, u32[]{:S(2)}) collective-permute-start(bf16[8,4096]{1,0:T(8,128)(2,1)S(1)} %tail.1), channel_id=1, source_target_pairs={{1,2},{3,4},{5,6},{7,8},{9,10},{11,12},{13,14},{2,1},{4,3},{6,5},{... | collective-permute-start | bytes 196616 | tf_op jit(solution)/shard_map/ppermute | solution.py:443
  13.9 5.0 %collective-permute-done.4.chip_halo_ref = bf16[8,4096]{1,0:T(8,128)(2,1)S(1)} collective-permute-done((bf16[8,4096]{1,0:T(8,128)(2,1)S(1)}, bf16[8,4096]{1,0:T(8,128)(2,1)S(1)}, u32[]{:S(2)}, u32[]{:S(2)}) %collective-permute-start.4) | collective-permute-done | bytes 65568 | tf_op jit(solution)/shard_map/ppermute | solution.py:443
  19.2 3.1 %collective-permute-start.6 = (bf16[560,128]{1,0:T(8,128)(2,1)S(1)}, bf16[560,128]{1,0:T(8,128)(2,1)S(1)}, u32[]{:S(2)}, u32[]{:S(2)}) collective-permute-start(bf16[560,128]{1,0:T(8,128)(2,1)S(1)} %span_state.1), channel_id=1, source_target_pairs={{0,8},{1,9},{2,10},{3,11},{4,12},{5,13},{6,14},{7,15},{8,0},{9,1},... | collective-permute-start | bytes 430088 | tf_op jit(solution)/shard_map/ppermute | solution.py:381
  22.5 1.1 %intra_other.1.refs_7_.refs_4_.refs_10_ = f32[16,128,128]{2,1,0:T(8,128)S(1)} custom-call(bf16[128,4096]{1,0:T(8,128)(2,1)S(1)} %copy-done, bf16[128,4096]{1,0:T(8,128)(2,1)S(1)} %copy-done.1, bf16[8,4096]{1,0:T(8,128)(2,1)S(1)} %collective-permute-done.4.chip_halo_ref, bf16[8,4096]{1,0:T(8,128)(2,1)S(1)} %collective-permute-done.5.core_halo_ref, ...), custom_call_target="tpu_custom_call" | custom-call | tf_op jit(solution)/shard_map/intra_other/pallas_call | solution.py:42
  23.7 1.1 %intra_mine.1.refs_4_.refs_7_.refs_10_ = f32[16,128,128]{2,1,0:T(8,128)S(1)} custom-call(bf16[128,4096]{1,0:T(8,128)(2,1)S(1)} %copy-done, bf16[128,4096]{1,0:T(8,128)(2,1)S(1)} %copy-done.1, bf16[8,4096]{1,0:T(8,128)(2,1)S(1)} %collective-permute-done.4.chip_halo_ref, bf16[8,4096]{1,0:T(8,128)(2,1)S(1)} %collective-permute-done.5.core_halo_ref, ...), custom_call_target="tpu_custom_call" | custom-call | tf_op jit(solution)/shard_map/intra_mine/pallas_call | solution.py:42
  24.8 4.8 %collective-permute-done.6.refs_4_ = bf16[560,128]{1,0:T(8,128)(2,1)S(1)} collective-permute-done((bf16[560,128]{1,0:T(8,128)(2,1)S(1)}, bf16[560,128]{1,0:T(8,128)(2,1)S(1)}, u32[]{:S(2)}, u32[]{:S(2)}) %collective-permute-start.6) | collective-permute-done | bytes 143392 | tf_op jit(solution)/shard_map/ppermute | solution.py:381
  29.6 0.4 chip_prefix.1
  30.0 0.6 %collective-permute-start.10 = (bf16[528,128]{1,0:T(8,128)(2,1)S(1)}, bf16[528,128]{1,0:T(8,128)(2,1)S(1)}, u32[]{:S(2)}, u32[]{:S(2)}) collective-permute-start(bf16[528,128]{1,0:T(8,128)(2,1)S(1)} %get-tuple-element.39.refs_3_), channel_id=1, source_target_pairs={{0,1},{1,0},{2,3},{3,2},{4,5},{5,4},{6,7},{7,6},{8,9},{9,8},{10,11... | collective-permute-start | bytes 405512 | tf_op jit(solution)/shard_map/ppermute | solution.py:381
  30.6 0.5 %collective-permute-start.9 = (bf16[528,128]{1,0:T(8,128)(2,1)S(1)}, bf16[528,128]{1,0:T(8,128)(2,1)S(1)}, u32[]{:S(2)}, u32[]{:S(2)}) collective-permute-start(bf16[528,128]{1,0:T(8,128)(2,1)S(1)} %get-tuple-element.40), channel_id=1, source_target_pairs={{0,4},{1,5},{2,6},{3,7},{4,0},{5,1},{6,2},{7,3},{8,12},{9,13},{10,... | collective-permute-start | bytes 405512 | tf_op jit(solution)/shard_map/ppermute | solution.py:381
  31.1 2.2 %collective-permute-start.7 = (bf16[528,128]{1,0:T(8,128)(2,1)S(1)}, bf16[528,128]{1,0:T(8,128)(2,1)S(1)}, u32[]{:S(2)}, u32[]{:S(2)}) collective-permute-start(bf16[528,128]{1,0:T(8,128)(2,1)S(1)} %get-tuple-element.42), channel_id=1, source_target_pairs={{0,2},{1,3},{2,0},{3,1},{4,6},{5,7},{6,4},{7,5},{8,10},{9,11},{10,... | collective-permute-start | bytes 405512 | tf_op jit(solution)/shard_map/ppermute | solution.py:381
  33.3 1.5 %out_m0_o0.1.refs_12_ = bf16[128,4096]{1,0:T(8,128)(2,1)} custom-call(bf16[128,4096]{1,0:T(8,128)(2,1)S(1)} %copy-done, f32[8,8,128]{2,1,0:T(8,128)S(1)} %cum.1.cum_ref.refs_1_, f32[1,4096]{1,0:T(1,128)S(1)} %bitcast.19, bf16[528,128]{1,0:T(8,128)(2,1)S(1)} %get-tuple-element.39.refs_3_, f32[16,128,128]{2,1,0:T(8,128)S(1)} %intra_mine.1.refs_4_.refs_7_.refs_10_, ...), custom_call_target="tpu_custom_call" | custom-call | flops 1 | bytes 1 | tf_op jit(solution)/shard_map/out_m0_o0/pallas_call | solution.py:42
  34.7 1.0 %collective-permute-done.9.refs_9_ = bf16[528,128]{1,0:T(8,128)(2,1)S(1)} collective-permute-done((bf16[528,128]{1,0:T(8,128)(2,1)S(1)}, bf16[528,128]{1,0:T(8,128)(2,1)S(1)}, u32[]{:S(2)}, u32[]{:S(2)}) %collective-permute-start.9) | collective-permute-done | bytes 135200 | tf_op jit(solution)/shard_map/ppermute | solution.py:381
  35.8 1.7 %collective-permute-done.8.refs_6_ = bf16[528,128]{1,0:T(8,128)(2,1)S(1)} collective-permute-done((bf16[528,128]{1,0:T(8,128)(2,1)S(1)}, bf16[528,128]{1,0:T(8,128)(2,1)S(1)}, u32[]{:S(2)}, u32[]{:S(2)}) %collective-permute-start.8) | collective-permute-done | bytes 135200 | tf_op jit(solution)/shard_map/ppermute | solution.py:381
  37.5 2.3 %collective-permute-done.7.refs_3_ = bf16[528,128]{1,0:T(8,128)(2,1)S(1)} collective-permute-done((bf16[528,128]{1,0:T(8,128)(2,1)S(1)}, bf16[528,128]{1,0:T(8,128)(2,1)S(1)}, u32[]{:S(2)}, u32[]{:S(2)}) %collective-permute-start.7) | collective-permute-done | bytes 135200 | tf_op jit(solution)/shard_map/ppermute | solution.py:381
  39.8 0.9 %collective-permute-start.12 = (bf16[528,128]{1,0:T(8,128)(2,1)S(1)}, bf16[528,128]{1,0:T(8,128)(2,1)S(1)}, u32[]{:S(2)}, u32[]{:S(2)}) collective-permute-start(bf16[528,128]{1,0:T(8,128)(2,1)S(1)} %collective-permute-done.7.refs_3_), channel_id=1, source_target_pairs={{0,1},{1,0},{2,3},{3,2},{4,5},{5,4},{6,7},{7,6},{8,9},{9,8},{10,11... | collective-permute-start | bytes 405512 | tf_op jit(solution)/shard_map/ppermute | solution.py:381
  40.7 0.5 %collective-permute-start.14 = (bf16[528,128]{1,0:T(8,128)(2,1)S(1)}, bf16[528,128]{1,0:T(8,128)(2,1)S(1)}, u32[]{:S(2)}, u32[]{:S(2)}) collective-permute-start(bf16[528,128]{1,0:T(8,128)(2,1)S(1)} %collective-permute-done.9.refs_9_), channel_id=1, source_target_pairs={{0,1},{1,0},{2,3},{3,2},{4,5},{5,4},{6,7},{7,6},{8,9},{9,8},{10,11... | collective-permute-start | bytes 405512 | tf_op jit(solution)/shard_map/ppermute | solution.py:381
  41.2 1.7 %out_m1_m3_m2.1.refs_12_ = bf16[128,4096]{1,0:T(8,128)(2,1)} custom-call(bf16[128,4096]{1,0:T(8,128)(2,1)S(1)} %copy-done, f32[8,8,128]{2,1,0:T(8,128)S(1)} %cum.1.cum_ref.refs_1_, f32[1,4096]{1,0:T(1,128)S(1)} %bitcast.20, bf16[528,128]{1,0:T(8,128)(2,1)S(1)} %collective-permute-done.7.refs_3_, ...), custom_call_target="tpu_custom_call", output_to_operand_aliasing={{}: (12, {})} | custom-call | flops 1 | bytes 1 | tf_op jit(solution)/shard_map/out_m1_m3_m2/pallas_call | solution.py:42
  43.0 1.7 %out_o1_o3_o2.1 = bf16[128,4096]{1,0:T(8,128)(2,1)} custom-call(bf16[128,4096]{1,0:T(8,128)(2,1)S(1)} %copy-done, f32[8,8,128]{2,1,0:T(8,128)S(1)} %cum.1.cum_ref.refs_1_, f32[1,4096]{1,0:T(1,128)S(1)} %bitcast.21, bf16[528,128]{1,0:T(8,128)(2,1)S(1)} %collective-permute-done.12.refs_3_, ...), custom_call_target="tpu_custom_call", output_to_operand_aliasing={{}: (12, {})} | custom-call | flops 1 | bytes 1 | tf_op jit(solution)/shard_map/out_o1_o3_o2/pallas_call | solution.py:42
  (32 shorter events, 1.0 us)
Async XLA Ops:
  2.5 2.7 %collective-permute-start = (bf16[4,560,128]{2,1,0:T(8,128)(2,1)S(1)}, bf16[4,560,128]{2,1,0:T(8,128)(2,1)S(1)}, u32[]{:S(2)}, u32[]{:S(2)}) collective-permute-start(bf16[4,560,128]{2,1,0:T(8,128)(2,1)S(1)} %states_other.1), channel_id=1, source_target_pairs={{0,1},{1,0},{2,3},{3,2},{4,5},{5,4},{6,7},{7,6},{8,9},{9,8},{10,11... | collective-permute-start | bytes 1720328 | tf_op jit(solution)/shard_map/ppermute | solution.py:381
  5.2 4.5 %copy-start.1 = (bf16[128,4096]{1,0:T(8,128)(2,1)S(1)}, bf16[128,4096]{1,0:T(8,128)(2,1)}, u32[]{:S(2)}) copy-start(bf16[128,4096]{1,0:T(8,128)(2,1)} %k_ref.4) | copy-start | bytes 3145732
  5.6 16.9 %copy-start.2 = (bf16[128,4096]{1,0:T(8,128)(2,1)S(1)}, bf16[128,4096]{1,0:T(8,128)(2,1)}, u32[]{:S(2)}) copy-start(bf16[128,4096]{1,0:T(8,128)(2,1)} %v_ref.3) | copy-start | bytes 3145732
  5.6 16.9 %copy-start = (bf16[128,4096]{1,0:T(8,128)(2,1)S(1)}, bf16[128,4096]{1,0:T(8,128)(2,1)}, u32[]{:S(2)}) copy-start(bf16[128,4096]{1,0:T(8,128)(2,1)} %refs_0_.5) | copy-start | bytes 3145732
  5.6 13.2 %collective-permute-start.3 = (bf16[560,128]{1,0:T(8,128)(2,1)S(1)}, bf16[560,128]{1,0:T(8,128)(2,1)S(1)}, u32[]{:S(2)}, u32[]{:S(2)}) collective-permute-start(bf16[560,128]{1,0:T(8,128)(2,1)S(1)} %get-tuple-element.35), channel_id=1, source_target_pairs={{0,4},{1,5},{2,6},{3,7},{4,0},{5,1},{6,2},{7,3},{8,12},{9,13},{10,... | collective-permute-start | bytes 430088 | tf_op jit(solution)/shard_map/ppermute | solution.py:381
  8.4 10.4 %collective-permute-start.2 = (bf16[560,128]{1,0:T(8,128)(2,1)S(1)}, bf16[560,128]{1,0:T(8,128)(2,1)S(1)}, u32[]{:S(2)}, u32[]{:S(2)}) collective-permute-start(bf16[560,128]{1,0:T(8,128)(2,1)S(1)} %get-tuple-element.36), channel_id=1, source_target_pairs={{0,6},{1,7},{2,4},{3,5},{4,2},{5,3},{6,0},{7,1},{8,14},{9,15},{10,... | collective-permute-start | bytes 430088 | tf_op jit(solution)/shard_map/ppermute | solution.py:381
  9.6 9.3 %collective-permute-start.1 = (bf16[560,128]{1,0:T(8,128)(2,1)S(1)}, bf16[560,128]{1,0:T(8,128)(2,1)S(1)}, u32[]{:S(2)}, u32[]{:S(2)}) collective-permute-start(bf16[560,128]{1,0:T(8,128)(2,1)S(1)} %get-tuple-element.37), channel_id=1, source_target_pairs={{0,2},{1,3},{2,0},{3,1},{4,6},{5,7},{6,4},{7,5},{8,10},{9,11},{10,... | collective-permute-start | bytes 430088 | tf_op jit(solution)/shard_map/ppermute | solution.py:381
  9.7 4.1 %collective-permute-start.5 = (bf16[8,4096]{1,0:T(8,128)(2,1)S(1)}, bf16[8,4096]{1,0:T(8,128)(2,1)S(1)}, u32[]{:S(2)}, u32[]{:S(2)}) collective-permute-start(bf16[8,4096]{1,0:T(8,128)(2,1)S(1)} %tail.1), channel_id=1, source_target_pairs={{0,1},{1,0},{2,3},{3,2},{4,5},{5,4},{6,7},{7,6},{8,9},{9,8},{10,11... | collective-permute-start | bytes 196616 | tf_op jit(solution)/shard_map/ppermute | solution.py:381
  10.3 8.5 %collective-permute-start.4 = (bf16[8,4096]{1,0:T(8,128)(2,1)S(1)}, bf16[8,4096]{1,0:T(8,128)(2,1)S(1)}, u32[]{:S(2)}, u32[]{:S(2)}) collective-permute-start(bf16[8,4096]{1,0:T(8,128)(2,1)S(1)} %tail.1), channel_id=1, source_target_pairs={{1,2},{3,4},{5,6},{7,8},{9,10},{11,12},{13,14},{2,1},{4,3},{6,5},{... | collective-permute-start | bytes 196616 | tf_op jit(solution)/shard_map/ppermute | solution.py:443
  13.8 19.5 %collective-permute-start.11 = (bf16[4,560,128]{2,1,0:T(8,128)(2,1)S(1)}, bf16[4,560,128]{2,1,0:T(8,128)(2,1)S(1)}, u32[]{:S(2)}, u32[]{:S(2)}) collective-permute-start(bf16[4,560,128]{2,1,0:T(8,128)(2,1)S(1)} %states_mine.1.own_ref), channel_id=1, source_target_pairs={{0,1},{1,0},{2,3},{3,2},{4,5},{5,4},{6,7},{7,6},{8,9},{9,8},{10,11... | collective-permute-start | bytes 1720328 | tf_op jit(solution)/shard_map/ppermute | solution.py:381
  18.8 3.5 %copy-start.5 = (f32[128,32]{0,1:T(8,128)S(1)}, f32[128,32]{0,1:T(8,128)}, u32[]{:S(2)}) copy-start(f32[128,32]{0,1:T(8,128)} %param.9) | copy-start | bytes 49156
  18.9 3.7 %copy-start.3 = (f32[4,4096]{1,0:T(4,128)S(1)}, f32[4,4096]{1,0:T(4,128)}, u32[]{:S(2)}) copy-start(f32[4,4096]{1,0:T(4,128)} %w_ref.3) | copy-start | bytes 196612
  19.2 10.3 %collective-permute-start.6 = (bf16[560,128]{1,0:T(8,128)(2,1)S(1)}, bf16[560,128]{1,0:T(8,128)(2,1)S(1)}, u32[]{:S(2)}, u32[]{:S(2)}) collective-permute-start(bf16[560,128]{1,0:T(8,128)(2,1)S(1)} %span_state.1), channel_id=1, source_target_pairs={{0,8},{1,9},{2,10},{3,11},{4,12},{5,13},{6,14},{7,15},{8,0},{9,1},... | collective-permute-start | bytes 430088 | tf_op jit(solution)/shard_map/ppermute | solution.py:381
  29.9 3.3 %copy-start.4 = (f32[4096]{0:T(1024)S(1)}, f32[4096]{0:T(1024)}, u32[]{:S(2)}) copy-start(f32[4096]{0:T(1024)} %param.11) | copy-start | bytes 49156
  30.0 3.3 %collective-permute-start.10 = (bf16[528,128]{1,0:T(8,128)(2,1)S(1)}, bf16[528,128]{1,0:T(8,128)(2,1)S(1)}, u32[]{:S(2)}, u32[]{:S(2)}) collective-permute-start(bf16[528,128]{1,0:T(8,128)(2,1)S(1)} %get-tuple-element.39.refs_3_), channel_id=1, source_target_pairs={{0,1},{1,0},{2,3},{3,2},{4,5},{5,4},{6,7},{7,6},{8,9},{9,8},{10,11... | collective-permute-start | bytes 405512 | tf_op jit(solution)/shard_map/ppermute | solution.py:381
  30.6 5.2 %collective-permute-start.9 = (bf16[528,128]{1,0:T(8,128)(2,1)S(1)}, bf16[528,128]{1,0:T(8,128)(2,1)S(1)}, u32[]{:S(2)}, u32[]{:S(2)}) collective-permute-start(bf16[528,128]{1,0:T(8,128)(2,1)S(1)} %get-tuple-element.40), channel_id=1, source_target_pairs={{0,4},{1,5},{2,6},{3,7},{4,0},{5,1},{6,2},{7,3},{8,12},{9,13},{10,... | collective-permute-start | bytes 405512 | tf_op jit(solution)/shard_map/ppermute | solution.py:381
  31.1 6.4 %collective-permute-start.8 = (bf16[528,128]{1,0:T(8,128)(2,1)S(1)}, bf16[528,128]{1,0:T(8,128)(2,1)S(1)}, u32[]{:S(2)}, u32[]{:S(2)}) collective-permute-start(bf16[528,128]{1,0:T(8,128)(2,1)S(1)} %get-tuple-element.41), channel_id=1, source_target_pairs={{0,6},{1,7},{2,4},{3,5},{4,2},{5,3},{6,0},{7,1},{8,14},{9,15},{10,... | collective-permute-start | bytes 405512 | tf_op jit(solution)/shard_map/ppermute | solution.py:381
  31.1 8.7 %collective-permute-start.7 = (bf16[528,128]{1,0:T(8,128)(2,1)S(1)}, bf16[528,128]{1,0:T(8,128)(2,1)S(1)}, u32[]{:S(2)}, u32[]{:S(2)}) collective-permute-start(bf16[528,128]{1,0:T(8,128)(2,1)S(1)} %get-tuple-element.42), channel_id=1, source_target_pairs={{0,2},{1,3},{2,0},{3,1},{4,6},{5,7},{6,4},{7,5},{8,10},{9,11},{10,... | collective-permute-start | bytes 405512 | tf_op jit(solution)/shard_map/ppermute | solution.py:381
  39.8 3.2 %collective-permute-start.12 = (bf16[528,128]{1,0:T(8,128)(2,1)S(1)}, bf16[528,128]{1,0:T(8,128)(2,1)S(1)}, u32[]{:S(2)}, u32[]{:S(2)}) collective-permute-start(bf16[528,128]{1,0:T(8,128)(2,1)S(1)} %collective-permute-done.7.refs_3_), channel_id=1, source_target_pairs={{0,1},{1,0},{2,3},{3,2},{4,5},{5,4},{6,7},{7,6},{8,9},{9,8},{10,11... | collective-permute-start | bytes 405512 | tf_op jit(solution)/shard_map/ppermute | solution.py:381
  40.7 2.3 %collective-permute-start.13 = (bf16[528,128]{1,0:T(8,128)(2,1)S(1)}, bf16[528,128]{1,0:T(8,128)(2,1)S(1)}, u32[]{:S(2)}, u32[]{:S(2)}) collective-permute-start(bf16[528,128]{1,0:T(8,128)(2,1)S(1)} %collective-permute-done.8.refs_6_), channel_id=1, source_target_pairs={{0,1},{1,0},{2,3},{3,2},{4,5},{5,4},{6,7},{7,6},{8,9},{9,8},{10,11... | collective-permute-start | bytes 405512 | tf_op jit(solution)/shard_map/ppermute | solution.py:381
  40.7 2.3 %collective-permute-start.14 = (bf16[528,128]{1,0:T(8,128)(2,1)S(1)}, bf16[528,128]{1,0:T(8,128)(2,1)S(1)}, u32[]{:S(2)}, u32[]{:S(2)}) collective-permute-start(bf16[528,128]{1,0:T(8,128)(2,1)S(1)} %collective-permute-done.9.refs_9_), channel_id=1, source_target_pairs={{0,1},{1,0},{2,3},{3,2},{4,5},{5,4},{6,7},{7,6},{8,9},{9,8},{10,11... | collective-permute-start | bytes 405512 | tf_op jit(solution)/shard_map/ppermute | solution.py:381

commit v6 on v5

--- a/solution.py
+++ b/solution.py
@@ -51,11 +51,6 @@
     )(*args)
 
 
-def tail_kernel(k_ref, out_ref):
-    rows = k_ref.shape[0]
-    out_ref[...] = k_ref[rows - HALO : rows, :]
-
-
 def cum_kernel(heads, decay_ref, out_ref):
     x = decay_ref[...]
     count, rows = x.shape
@@ -177,31 +172,31 @@
             out_ref[g, cols, :] = state.astype(BF16)
 
 
-def intra_kernel(
-    mine, heads, size, q_ref, k_ref, chip_halo_ref, core_halo_ref, v_ref, w_ref, cum_ref, out_ref,
-    ext, held,
-):
+def intra_kernel(mine, heads, size, q_ref, k_ref, v_ref, w_ref, cum_ref, out_ref, ext, held):
     rows = q_ref.shape[0]
-    core, _ = position()
     causal = lax.broadcasted_iota(jnp.int32, (rows, rows), 0) >= lax.broadcasted_iota(
         jnp.int32, (rows, rows), 1
     )
+    none = jnp.zeros((HALO, size), F32)
     for g in range(CHIPS):
         b = head_group(mine, g)
         cum = cum_ref[b][0:heads]
         cum_col = cum.T
+        growth = jnp.exp(-cum_col[0:HALO])
+        values = []
         for j in range(heads):
             cols = columns(b * heads * size, j * size, size)
-            halo = jnp.where(
-                core == 0, chip_halo_ref[:, cols].astype(F32), core_halo_ref[:, cols].astype(F32)
-            )
-            key_conv = conv_keys(k_ref, halo, w_ref, ext.at[j], cols)
+            key_conv = conv_keys(k_ref, none, w_ref, ext.at[j], cols)
             scores = lax.dot_general(
                 q_ref[:, cols], key_conv, (((1,), (1,)), ((), ())), preferred_element_type=F32
             )
             spread = cum_col[:, j : j + 1] - cum[j : j + 1]
             weights = jnp.where(causal, scores * jnp.exp(jnp.where(causal, spread, 0.0)), 0.0)
             held[g * heads + j] = weights.astype(BF16)
+            values.append(v_ref[0:HALO, cols].astype(F32) * growth[:, j : j + 1])
+        out_ref[CHIPS * heads, g * PARTS : (g + 1) * PARTS, :] = padded(
+            [values[j][t : t + 1] for t in range(3) for j in range(heads)]
+        ).astype(F32)
     for g in range(CHIPS):
         b = head_group(mine, g)
         for j in range(heads):
@@ -310,35 +305,56 @@
 def out_kernel(items, heads, size, *refs):
     q_ref, cum_ref, gain_ref = refs[:3]
     per_item = [refs[3 + 3 * i : 6 + 3 * i] for i in range(len(items))]
-    out_ref, mixed_ref, done_ref, sems = refs[-4:]
+    out_ref, inter_ref, score_ref, done_ref, sems = refs[-5:]
+    rows = q_ref.shape[0]
     core, _ = position()
     second = core == 1
+    row = lax.broadcasted_iota(jnp.int32, (rows, PARTS), 0)
+    edge = lax.broadcasted_iota(jnp.int32, (rows, PARTS), 1)
+    seen = [
+        (lax.rem(edge, heads) == j) & (lax.div(edge, heads) <= row) & (edge < 3 * heads)
+        for j in range(heads)
+    ]
     for i, (mine, g) in enumerate(items):
         prefix_ref, intra_ref, sib_ref = per_item[i]
         b = head_group(mine, g)
-        started = jnp.exp(cum_ref[b][0:heads]).T
         by = jnp.where(second, get_decay(sib_ref.at[g], heads, size), 1.0)
-        fixes = edge_states(
-            sib_ref[g, side(2, heads, size), :],
-            prefix_ref[heads * size : heads * size + PARTS, :],
-            heads,
+        before_chip = prefix_ref[heads * size : heads * size + PARTS, :]
+        fixes = edge_states(sib_ref[g, side(2, heads, size), :], before_chip, heads)
+        edges = jnp.where(
+            second,
+            sib_ref[g, side(1, heads, size), :].astype(F32),
+            before_chip.astype(F32),
         )
         for j in range(heads):
             cols = columns(b * heads * size, j * size, size)
-            rows = slice(j * size, (j + 1) * size)
-            sib = jnp.where(second, sib_ref[g, rows, :].astype(F32) + fixes[j], 0.0)
-            prefix = prefix_ref[rows, :].astype(F32) * by[j : j + 1] + sib
-            inter = lax.dot_general(
-                q_ref[:, cols], prefix.astype(BF16), (((1,), (1,)), ((), ())),
+            these = slice(j * size, (j + 1) * size)
+            sib = jnp.where(second, sib_ref[g, these, :].astype(F32) + fixes[j], 0.0)
+            prefix = prefix_ref[these, :].astype(F32) * by[j : j + 1] + sib
+            both = lax.dot_general(
+                q_ref[:, cols],
+                jnp.concatenate([prefix, edges], 0).astype(BF16),
+                (((1,), (1,)), ((), ())),
                 preferred_element_type=F32,
             )
-            mixed_ref[i * heads + j] = intra_ref[g * heads + j] + inter * started[:, j : j + 1]
+            inter_ref[i * heads + j] = both[:, 0:size]
+            score_ref[i * heads + j] = jnp.where(seen[j], both[:, size : size + PARTS], 0.0).astype(
+                BF16
+            )
     copies = []
     for i, (mine, g) in enumerate(items):
+        _, intra_ref, _ = per_item[i]
         b = head_group(mine, g)
+        started = jnp.exp(cum_ref[b][0:heads]).T
+        values = intra_ref[CHIPS * heads, g * PARTS : (g + 1) * PARTS, :].astype(BF16)
         for j in range(heads):
             cols = columns(b * heads * size, j * size, size)
-            mixed = mixed_ref[i * heads + j]
+            edge_part = jnp.dot(
+                score_ref[i * heads + j], values, preferred_element_type=F32
+            )
+            mixed = intra_ref[g * heads + j] + (
+                inter_ref[i * heads + j] + edge_part
+            ) * started[:, j : j + 1]
             scale = lax.rsqrt(jnp.mean(mixed * mixed, axis=1, keepdims=True) + 1e-05)
             done_ref[i, :, j * size : (j + 1) * size] = (
                 mixed * scale * gain_ref[:, cols]
@@ -410,8 +426,8 @@
         return call(
             functools.partial(intra_kernel, mine, heads, size),
             "intra_mine" if mine else "intra_other",
-            pltpu.VMEM((half, rows, size), F32),
-            q, key_input, chip_halo, core_halo, value_input, conv_weight, cum,
+            pltpu.VMEM((half + 1, rows, size), F32),
+            q, key_input, value_input, conv_weight, cum,
             scratch=[ext, held],
         )
 
@@ -429,8 +445,8 @@
     packets = {0: chip_states[0]}
     for g in EXCHANGE:
         packets[g] = swap(chip_states[g], 2 * g)
-    keys_after, decay_after, chip_states = lax.optimization_barrier(
-        (key_input, log_decay, chip_states)
+    q_after, decay_after, chip_states = lax.optimization_barrier(
+        (queries, log_decay, chip_states)
     )
     cum = call(
         functools.partial(cum_kernel, heads),
@@ -438,13 +454,8 @@
         pltpu.VMEM((SPAN, 2 * heads, rows), F32),
         decay_after.T,
     )
-    tail = call(tail_kernel, "tail", pltpu.VMEM((HALO, width), BF16), keys_after)
-    next_pairs = [(i, i + 1) for i in range(1, n - 1, 2)]
-    chip_halo = lax.ppermute(tail, "ctx", next_pairs + [(j, i) for i, j in next_pairs])
-    core_halo = swap(tail, 1)
-    *late, chip_halo, core_halo = lax.optimization_barrier(
-        (*[packets[g] for g in EXCHANGE], chip_halo, core_halo)
-    )
+    intra_mine = intra_part(True, q_after)
+    *late, intra_mine = lax.optimization_barrier((*[packets[g] for g in EXCHANGE], intra_mine))
     packets.update(zip(EXCHANGE, late))
     packets = [packets[g] for g in range(CHIPS)]
 
@@ -472,9 +483,8 @@
         before = join_spans(shift(before, SPAN * reach), before, heads, size)
         reach *= 2
     q_after, span = lax.optimization_barrier((queries, span))
-    intra_mine = intra_part(True, q_after)
     intra_other = intra_part(False, q_after)
-    before, intra_mine, intra_other = lax.optimization_barrier((before, intra_mine, intra_other))
+    before, intra_other = lax.optimization_barrier((before, intra_other))
 
     chip_prefix = call(
         functools.partial(spread_kernel, heads, size),
@@ -505,6 +515,7 @@
             cost_estimate=pl.CostEstimate(flops=1, transcendentals=0, bytes_accessed=1),
             scratch=[
                 pltpu.VMEM((len(items) * heads, rows, size), F32),
+                pltpu.VMEM((len(items) * heads, rows, PARTS), BF16),
                 pltpu.VMEM((len(items), rows, heads * size), BF16),
                 pltpu.SemaphoreType.DMA((len(items),)),
             ],

time: 45.1 us -> 43.9 us (0.973)
  starting transfers between devices: 16.1 us -> 13.4 us
  Pallas kernels: 13.5 us -> 14.4 us
  waiting for transfers between devices: 14.8 us -> 15.6 us
    ppermute x14 -> x13, waiting for transfers between devices: 9.82 us -> 15.6 us  [swap(): return lax.ppermute(x, 'ctx', [(i, i ^ mask) for i in range(n)])]
    ppermute x1 -> x0, waiting for transfers between devices: 4.96 us -> none  [on_device(): lax.ppermute(tail, 'ctx', next_pairs + [(j, i) for i, j in next_pairs])]
    ppermute x1 -> x0, starting transfers between devices: 3.42 us -> none  [on_device(): lax.ppermute(tail, 'ctx', next_pairs + [(j, i) for i, j in next_pairs])]
    pallas_call x12 -> x11, Pallas kernels: 13.5 us -> 14.4 us  [call(): pl.pallas_call(kernel, out_shape=out_shape, in_specs=in_specs, out_specs=...]
    ppermute x14 -> x13, starting transfers between devices: 12.6 us -> 13.4 us  [swap(): return lax.ppermute(x, 'ctx', [(i, i ^ mask) for i in range(n)])]
  transfers between devices with their start and end apart: 15 -> 13, of which waited for: 5 -> 7; matrix products, arithmetic and copies ran while one was open for 0% -> 0% of each run, Pallas kernels for 20% -> 22%
where the time goes in v6:
time: 43.9 us; the launch traced here: 43.7 us
  waiting for transfers between devices  15.6 us (36%)
  Pallas kernels  14.4 us (33%)
  starting transfers between devices  13.4 us (31%)
    ppermute x13, waiting for transfers between devices, swap(): return lax.ppermute(x, 'ctx', [(i, i ^ mask) for i in range(n)])  15.6 us
    pallas_call x11, Pallas kernels, call(): pl.pallas_call(kernel, out_shape=out_shape, in_specs=in_specs, out_specs=...  14.4 us
    ppermute x13, starting transfers between devices, swap(): return lax.ppermute(x, 'ctx', [(i, i ^ mask) for i in range(n)])  13.4 us
  transfers between devices with their start and end apart: 13, of which 7 were waited for; matrix products, arithmetic and copies ran while one was open for 0% of the time, Pallas kernels for 22%

profile of v6, /device:TPU:1, one launch (start us, length us, event | category | flops | bytes accessed | tf_op | source)
XLA Modules:
  0.0 43.7 jit_solution(9241279311660478070)
XLA Ops:
  0.0 2.5 %states_other.1 = bf16[4,560,128]{2,1,0:T(8,128)(2,1)S(1)} custom-call(bf16[128,4096]{1,0:T(8,128)(2,1)} %k_ref.3, bf16[128,4096]{1,0:T(8,128)(2,1)} %v_ref.3, f32[4,4096]{1,0:T(4,128)} %w_ref.3, f32[32,128]{1,0:T(8,128)} %bitcast.22), custom_call_target="tpu_custom_call" | custom-call | tf_op jit(solution)/shard_map/states_other/pallas_call | solution.py:42
  2.6 2.6 %states_mine.1.own_ref = bf16[4,560,128]{2,1,0:T(8,128)(2,1)S(1)} custom-call(bf16[128,4096]{1,0:T(8,128)(2,1)} %k_ref.3, bf16[128,4096]{1,0:T(8,128)(2,1)} %v_ref.3, f32[4,4096]{1,0:T(4,128)} %w_ref.3, f32[32,128]{1,0:T(8,128)} %bitcast.23), custom_call_target="tpu_custom_call" | custom-call | tf_op jit(solution)/shard_map/states_mine/pallas_call | solution.py:42
  5.7 2.8 %collective-permute-start.3 = (bf16[560,128]{1,0:T(8,128)(2,1)S(1)}, bf16[560,128]{1,0:T(8,128)(2,1)S(1)}, u32[]{:S(2)}, u32[]{:S(2)}) collective-permute-start(bf16[560,128]{1,0:T(8,128)(2,1)S(1)} %get-tuple-element.31), channel_id=1, source_target_pairs={{0,4},{1,5},{2,6},{3,7},{4,0},{5,1},{6,2},{7,3},{8,12},{9,13},{10,... | collective-permute-start | bytes 430088 | tf_op jit(solution)/shard_map/ppermute | solution.py:397
  8.5 1.1 %collective-permute-start.2 = (bf16[560,128]{1,0:T(8,128)(2,1)S(1)}, bf16[560,128]{1,0:T(8,128)(2,1)S(1)}, u32[]{:S(2)}, u32[]{:S(2)}) collective-permute-start(bf16[560,128]{1,0:T(8,128)(2,1)S(1)} %get-tuple-element.32), channel_id=1, source_target_pairs={{0,6},{1,7},{2,4},{3,5},{4,2},{5,3},{6,0},{7,1},{8,14},{9,15},{10,... | collective-permute-start | bytes 430088 | tf_op jit(solution)/shard_map/ppermute | solution.py:397
  9.8 0.6 %collective-permute-start.9 = (bf16[4,560,128]{2,1,0:T(8,128)(2,1)S(1)}, bf16[4,560,128]{2,1,0:T(8,128)(2,1)S(1)}, u32[]{:S(2)}, u32[]{:S(2)}) collective-permute-start(bf16[4,560,128]{2,1,0:T(8,128)(2,1)S(1)} %states_mine.1.own_ref), channel_id=1, source_target_pairs={{0,1},{1,0},{2,3},{3,2},{4,5},{5,4},{6,7},{7,6},{8,9},{9,8},{10,11... | collective-permute-start | bytes 1720328 | tf_op jit(solution)/shard_map/ppermute | solution.py:397
  10.6 1.2 %intra_mine.1.refs_4_.refs_7_.refs_10_ = f32[17,128,128]{2,1,0:T(8,128)S(1)} custom-call(bf16[128,4096]{1,0:T(8,128)(2,1)S(1)} %copy-done, bf16[128,4096]{1,0:T(8,128)(2,1)S(1)} %copy-done.1, bf16[128,4096]{1,0:T(8,128)(2,1)S(1)} %copy-done.2, f32[4,4096]{1,0:T(4,128)S(1)} %copy-done.3, f32[8,8,128]{2,1,0:T(8,128)S(1)} %cum.1.cum_ref.refs_1_), custom_call_target="tpu_custom_call" | custom-call | tf_op jit(solution)/shard_map/intra_mine/pallas_call | solution.py:42
  11.8 0.9 %collective-permute-done.3.refs_2_ = bf16[560,128]{1,0:T(8,128)(2,1)S(1)} collective-permute-done((bf16[560,128]{1,0:T(8,128)(2,1)S(1)}, bf16[560,128]{1,0:T(8,128)(2,1)S(1)}, u32[]{:S(2)}, u32[]{:S(2)}) %collective-permute-start.3) | collective-permute-done | bytes 143392 | tf_op jit(solution)/shard_map/ppermute | solution.py:397
  12.6 4.0 %collective-permute-done.2.refs_3_ = bf16[560,128]{1,0:T(8,128)(2,1)S(1)} collective-permute-done((bf16[560,128]{1,0:T(8,128)(2,1)S(1)}, bf16[560,128]{1,0:T(8,128)(2,1)S(1)}, u32[]{:S(2)}, u32[]{:S(2)}) %collective-permute-start.2) | collective-permute-done | bytes 143392 | tf_op jit(solution)/shard_map/ppermute | solution.py:397
  16.7 0.8 %collective-permute-done.1.refs_1_ = bf16[560,128]{1,0:T(8,128)(2,1)S(1)} collective-permute-done((bf16[560,128]{1,0:T(8,128)(2,1)S(1)}, bf16[560,128]{1,0:T(8,128)(2,1)S(1)}, u32[]{:S(2)}, u32[]{:S(2)}) %collective-permute-start.1) | collective-permute-done | bytes 143392 | tf_op jit(solution)/shard_map/ppermute | solution.py:397
  17.8 2.4 %collective-permute-start.4 = (bf16[560,128]{1,0:T(8,128)(2,1)S(1)}, bf16[560,128]{1,0:T(8,128)(2,1)S(1)}, u32[]{:S(2)}, u32[]{:S(2)}) collective-permute-start(bf16[560,128]{1,0:T(8,128)(2,1)S(1)} %span_state.1), channel_id=1, source_target_pairs={{0,8},{1,9},{2,10},{3,11},{4,12},{5,13},{6,14},{7,15},{8,0},{9,1},... | collective-permute-start | bytes 430088 | tf_op jit(solution)/shard_map/ppermute | solution.py:397
  20.2 1.1 %intra_other.1.refs_7_.refs_4_.refs_10_ = f32[17,128,128]{2,1,0:T(8,128)S(1)} custom-call(bf16[128,4096]{1,0:T(8,128)(2,1)S(1)} %copy-done, bf16[128,4096]{1,0:T(8,128)(2,1)S(1)} %copy-done.1, bf16[128,4096]{1,0:T(8,128)(2,1)S(1)} %copy-done.2, f32[4,4096]{1,0:T(4,128)S(1)} %copy-done.3, f32[8,8,128]{2,1,0:T(8,128)S(1)} %cum.1.cum_ref.refs_1_), custom_call_target="tpu_custom_call" | custom-call | tf_op jit(solution)/shard_map/intra_other/pallas_call | solution.py:42
  21.3 5.1 %collective-permute-done.4.refs_4_ = bf16[560,128]{1,0:T(8,128)(2,1)S(1)} collective-permute-done((bf16[560,128]{1,0:T(8,128)(2,1)S(1)}, bf16[560,128]{1,0:T(8,128)(2,1)S(1)}, u32[]{:S(2)}, u32[]{:S(2)}) %collective-permute-start.4) | collective-permute-done | bytes 143392 | tf_op jit(solution)/shard_map/ppermute | solution.py:397
  26.9 1.6 %collective-permute-start.8 = (bf16[528,128]{1,0:T(8,128)(2,1)S(1)}, bf16[528,128]{1,0:T(8,128)(2,1)S(1)}, u32[]{:S(2)}, u32[]{:S(2)}) collective-permute-start(bf16[528,128]{1,0:T(8,128)(2,1)S(1)} %get-tuple-element.35.refs_3_), channel_id=1, source_target_pairs={{0,1},{1,0},{2,3},{3,2},{4,5},{5,4},{6,7},{7,6},{8,9},{9,8},{10,11... | collective-permute-start | bytes 405512 | tf_op jit(solution)/shard_map/ppermute | solution.py:397
  28.5 0.4 collective-permute-start.7
  28.9 1.2 %collective-permute-start.6 = (bf16[528,128]{1,0:T(8,128)(2,1)S(1)}, bf16[528,128]{1,0:T(8,128)(2,1)S(1)}, u32[]{:S(2)}, u32[]{:S(2)}) collective-permute-start(bf16[528,128]{1,0:T(8,128)(2,1)S(1)} %get-tuple-element.37), channel_id=1, source_target_pairs={{0,6},{1,7},{2,4},{3,5},{4,2},{5,3},{6,0},{7,1},{8,14},{9,15},{10,... | collective-permute-start | bytes 405512 | tf_op jit(solution)/shard_map/ppermute | solution.py:397
  30.2 1.0 %collective-permute-start.5 = (bf16[528,128]{1,0:T(8,128)(2,1)S(1)}, bf16[528,128]{1,0:T(8,128)(2,1)S(1)}, u32[]{:S(2)}, u32[]{:S(2)}) collective-permute-start(bf16[528,128]{1,0:T(8,128)(2,1)S(1)} %get-tuple-element.38), channel_id=1, source_target_pairs={{0,2},{1,3},{2,0},{3,1},{4,6},{5,7},{6,4},{7,5},{8,10},{9,11},{10,... | collective-permute-start | bytes 405512 | tf_op jit(solution)/shard_map/ppermute | solution.py:397
  31.2 1.7 %out_m0_o0.1.refs_12_ = bf16[128,4096]{1,0:T(8,128)(2,1)} custom-call(bf16[128,4096]{1,0:T(8,128)(2,1)S(1)} %copy-done, f32[8,8,128]{2,1,0:T(8,128)S(1)} %cum.1.cum_ref.refs_1_, f32[1,4096]{1,0:T(1,128)S(1)} %bitcast.19, bf16[528,128]{1,0:T(8,128)(2,1)S(1)} %get-tuple-element.35.refs_3_, f32[17,128,128]{2,1,0:T(8,128)S(1)} %intra_mine.1.refs_4_.refs_7_.refs_10_, ...), custom_call_target="tpu_custom_call" | custom-call | flops 1 | bytes 1 | tf_op jit(solution)/shard_map/out_m0_o0/pallas_call | solution.py:42
  32.9 0.8 %collective-permute-done.7.refs_9_ = bf16[528,128]{1,0:T(8,128)(2,1)S(1)} collective-permute-done((bf16[528,128]{1,0:T(8,128)(2,1)S(1)}, bf16[528,128]{1,0:T(8,128)(2,1)S(1)}, u32[]{:S(2)}, u32[]{:S(2)}) %collective-permute-start.7) | collective-permute-done | bytes 135200 | tf_op jit(solution)/shard_map/ppermute | solution.py:397
  33.7 3.1 %collective-permute-done.6.refs_6_ = bf16[528,128]{1,0:T(8,128)(2,1)S(1)} collective-permute-done((bf16[528,128]{1,0:T(8,128)(2,1)S(1)}, bf16[528,128]{1,0:T(8,128)(2,1)S(1)}, u32[]{:S(2)}, u32[]{:S(2)}) %collective-permute-start.6) | collective-permute-done | bytes 135200 | tf_op jit(solution)/shard_map/ppermute | solution.py:397
  36.8 0.8 %collective-permute-done.5.refs_3_ = bf16[528,128]{1,0:T(8,128)(2,1)S(1)} collective-permute-done((bf16[528,128]{1,0:T(8,128)(2,1)S(1)}, bf16[528,128]{1,0:T(8,128)(2,1)S(1)}, u32[]{:S(2)}, u32[]{:S(2)}) %collective-permute-start.5) | collective-permute-done | bytes 135200 | tf_op jit(solution)/shard_map/ppermute | solution.py:397
  37.6 1.4 %collective-permute-start.10 = (bf16[528,128]{1,0:T(8,128)(2,1)S(1)}, bf16[528,128]{1,0:T(8,128)(2,1)S(1)}, u32[]{:S(2)}, u32[]{:S(2)}) collective-permute-start(bf16[528,128]{1,0:T(8,128)(2,1)S(1)} %collective-permute-done.5.refs_3_), channel_id=1, source_target_pairs={{0,1},{1,0},{2,3},{3,2},{4,5},{5,4},{6,7},{7,6},{8,9},{9,8},{10,11... | collective-permute-start | bytes 405512 | tf_op jit(solution)/shard_map/ppermute | solution.py:397
  39.1 0.5 %collective-permute-start.12 = (bf16[528,128]{1,0:T(8,128)(2,1)S(1)}, bf16[528,128]{1,0:T(8,128)(2,1)S(1)}, u32[]{:S(2)}, u32[]{:S(2)}) collective-permute-start(bf16[528,128]{1,0:T(8,128)(2,1)S(1)} %collective-permute-done.7.refs_9_), channel_id=1, source_target_pairs={{0,1},{1,0},{2,3},{3,2},{4,5},{5,4},{6,7},{7,6},{8,9},{9,8},{10,11... | collective-permute-start | bytes 405512 | tf_op jit(solution)/shard_map/ppermute | solution.py:397
  39.6 2.0 %out_m1_m3_m2.1.refs_12_ = bf16[128,4096]{1,0:T(8,128)(2,1)} custom-call(bf16[128,4096]{1,0:T(8,128)(2,1)S(1)} %copy-done, f32[8,8,128]{2,1,0:T(8,128)S(1)} %cum.1.cum_ref.refs_1_, f32[1,4096]{1,0:T(1,128)S(1)} %bitcast.20, bf16[528,128]{1,0:T(8,128)(2,1)S(1)} %collective-permute-done.5.refs_3_, ...), custom_call_target="tpu_custom_call", output_to_operand_aliasing={{}: (12, {})} | custom-call | flops 1 | bytes 1 | tf_op jit(solution)/shard_map/out_m1_m3_m2/pallas_call | solution.py:42
  41.7 2.0 %out_o1_o3_o2.1 = bf16[128,4096]{1,0:T(8,128)(2,1)} custom-call(bf16[128,4096]{1,0:T(8,128)(2,1)S(1)} %copy-done, f32[8,8,128]{2,1,0:T(8,128)S(1)} %cum.1.cum_ref.refs_1_, f32[1,4096]{1,0:T(1,128)S(1)} %bitcast.21, bf16[528,128]{1,0:T(8,128)(2,1)S(1)} %collective-permute-done.10.refs_3_, ...), custom_call_target="tpu_custom_call", output_to_operand_aliasing={{}: (12, {})} | custom-call | flops 1 | bytes 1 | tf_op jit(solution)/shard_map/out_o1_o3_o2/pallas_call | solution.py:42
  (27 shorter events, 1.7 us)
Async XLA Ops:
  2.5 2.8 %collective-permute-start = (bf16[4,560,128]{2,1,0:T(8,128)(2,1)S(1)}, bf16[4,560,128]{2,1,0:T(8,128)(2,1)S(1)}, u32[]{:S(2)}, u32[]{:S(2)}) collective-permute-start(bf16[4,560,128]{2,1,0:T(8,128)(2,1)S(1)} %states_other.1), channel_id=1, source_target_pairs={{0,1},{1,0},{2,3},{3,2},{4,5},{5,4},{6,7},{7,6},{8,9},{9,8},{10,11... | collective-permute-start | bytes 1720328 | tf_op jit(solution)/shard_map/ppermute | solution.py:397
  2.6 7.9 %copy-start.2 = (bf16[128,4096]{1,0:T(8,128)(2,1)S(1)}, bf16[128,4096]{1,0:T(8,128)(2,1)}, u32[]{:S(2)}) copy-start(bf16[128,4096]{1,0:T(8,128)(2,1)} %v_ref.3) | copy-start | bytes 3145732
  5.3 5.1 %copy-start.5 = (f32[128,32]{0,1:T(8,128)S(1)}, f32[128,32]{0,1:T(8,128)}, u32[]{:S(2)}) copy-start(f32[128,32]{0,1:T(8,128)} %param.9) | copy-start | bytes 49156
  5.3 5.3 %copy-start = (bf16[128,4096]{1,0:T(8,128)(2,1)S(1)}, bf16[128,4096]{1,0:T(8,128)(2,1)}, u32[]{:S(2)}) copy-start(bf16[128,4096]{1,0:T(8,128)(2,1)} %refs_0_.5) | copy-start | bytes 3145732
  5.3 5.3 %copy-start.1 = (bf16[128,4096]{1,0:T(8,128)(2,1)S(1)}, bf16[128,4096]{1,0:T(8,128)(2,1)}, u32[]{:S(2)}) copy-start(bf16[128,4096]{1,0:T(8,128)(2,1)} %k_ref.3) | copy-start | bytes 3145732
  5.3 5.3 %copy-start.3 = (f32[4,4096]{1,0:T(4,128)S(1)}, f32[4,4096]{1,0:T(4,128)}, u32[]{:S(2)}) copy-start(f32[4,4096]{1,0:T(4,128)} %w_ref.3) | copy-start | bytes 196612
  5.7 6.9 %collective-permute-start.3 = (bf16[560,128]{1,0:T(8,128)(2,1)S(1)}, bf16[560,128]{1,0:T(8,128)(2,1)S(1)}, u32[]{:S(2)}, u32[]{:S(2)}) collective-permute-start(bf16[560,128]{1,0:T(8,128)(2,1)S(1)} %get-tuple-element.31), channel_id=1, source_target_pairs={{0,4},{1,5},{2,6},{3,7},{4,0},{5,1},{6,2},{7,3},{8,12},{9,13},{10,... | collective-permute-start | bytes 430088 | tf_op jit(solution)/shard_map/ppermute | solution.py:397
  8.5 8.1 %collective-permute-start.2 = (bf16[560,128]{1,0:T(8,128)(2,1)S(1)}, bf16[560,128]{1,0:T(8,128)(2,1)S(1)}, u32[]{:S(2)}, u32[]{:S(2)}) collective-permute-start(bf16[560,128]{1,0:T(8,128)(2,1)S(1)} %get-tuple-element.32), channel_id=1, source_target_pairs={{0,6},{1,7},{2,4},{3,5},{4,2},{5,3},{6,0},{7,1},{8,14},{9,15},{10,... | collective-permute-start | bytes 430088 | tf_op jit(solution)/shard_map/ppermute | solution.py:397
  9.7 7.8 %collective-permute-start.1 = (bf16[560,128]{1,0:T(8,128)(2,1)S(1)}, bf16[560,128]{1,0:T(8,128)(2,1)S(1)}, u32[]{:S(2)}, u32[]{:S(2)}) collective-permute-start(bf16[560,128]{1,0:T(8,128)(2,1)S(1)} %get-tuple-element.33), channel_id=1, source_target_pairs={{0,2},{1,3},{2,0},{3,1},{4,6},{5,7},{6,4},{7,5},{8,10},{9,11},{10,... | collective-permute-start | bytes 430088 | tf_op jit(solution)/shard_map/ppermute | solution.py:397
  9.8 21.4 %collective-permute-start.9 = (bf16[4,560,128]{2,1,0:T(8,128)(2,1)S(1)}, bf16[4,560,128]{2,1,0:T(8,128)(2,1)S(1)}, u32[]{:S(2)}, u32[]{:S(2)}) collective-permute-start(bf16[4,560,128]{2,1,0:T(8,128)(2,1)S(1)} %states_mine.1.own_ref), channel_id=1, source_target_pairs={{0,1},{1,0},{2,3},{3,2},{4,5},{5,4},{6,7},{7,6},{8,9},{9,8},{10,11... | collective-permute-start | bytes 1720328 | tf_op jit(solution)/shard_map/ppermute | solution.py:397
  17.8 8.6 %collective-permute-start.4 = (bf16[560,128]{1,0:T(8,128)(2,1)S(1)}, bf16[560,128]{1,0:T(8,128)(2,1)S(1)}, u32[]{:S(2)}, u32[]{:S(2)}) collective-permute-start(bf16[560,128]{1,0:T(8,128)(2,1)S(1)} %span_state.1), channel_id=1, source_target_pairs={{0,8},{1,9},{2,10},{3,11},{4,12},{5,13},{6,14},{7,15},{8,0},{9,1},... | collective-permute-start | bytes 430088 | tf_op jit(solution)/shard_map/ppermute | solution.py:397
  21.3 9.9 %copy-start.4 = (f32[4096]{0:T(1024)S(1)}, f32[4096]{0:T(1024)}, u32[]{:S(2)}) copy-start(f32[4096]{0:T(1024)} %param.11) | copy-start | bytes 49156
  26.9 4.3 %collective-permute-start.8 = (bf16[528,128]{1,0:T(8,128)(2,1)S(1)}, bf16[528,128]{1,0:T(8,128)(2,1)S(1)}, u32[]{:S(2)}, u32[]{:S(2)}) collective-permute-start(bf16[528,128]{1,0:T(8,128)(2,1)S(1)} %get-tuple-element.35.refs_3_), channel_id=1, source_target_pairs={{0,1},{1,0},{2,3},{3,2},{4,5},{5,4},{6,7},{7,6},{8,9},{9,8},{10,11... | collective-permute-start | bytes 405512 | tf_op jit(solution)/shard_map/ppermute | solution.py:397
  28.5 5.2 %collective-permute-start.7 = (bf16[528,128]{1,0:T(8,128)(2,1)S(1)}, bf16[528,128]{1,0:T(8,128)(2,1)S(1)}, u32[]{:S(2)}, u32[]{:S(2)}) collective-permute-start(bf16[528,128]{1,0:T(8,128)(2,1)S(1)} %get-tuple-element.36), channel_id=1, source_target_pairs={{0,4},{1,5},{2,6},{3,7},{4,0},{5,1},{6,2},{7,3},{8,12},{9,13},{10,... | collective-permute-start | bytes 405512 | tf_op jit(solution)/shard_map/ppermute | solution.py:397
  28.9 7.9 %collective-permute-start.6 = (bf16[528,128]{1,0:T(8,128)(2,1)S(1)}, bf16[528,128]{1,0:T(8,128)(2,1)S(1)}, u32[]{:S(2)}, u32[]{:S(2)}) collective-permute-start(bf16[528,128]{1,0:T(8,128)(2,1)S(1)} %get-tuple-element.37), channel_id=1, source_target_pairs={{0,6},{1,7},{2,4},{3,5},{4,2},{5,3},{6,0},{7,1},{8,14},{9,15},{10,... | collective-permute-start | bytes 405512 | tf_op jit(solution)/shard_map/ppermute | solution.py:397
  30.2 7.5 %collective-permute-start.5 = (bf16[528,128]{1,0:T(8,128)(2,1)S(1)}, bf16[528,128]{1,0:T(8,128)(2,1)S(1)}, u32[]{:S(2)}, u32[]{:S(2)}) collective-permute-start(bf16[528,128]{1,0:T(8,128)(2,1)S(1)} %get-tuple-element.38), channel_id=1, source_target_pairs={{0,2},{1,3},{2,0},{3,1},{4,6},{5,7},{6,4},{7,5},{8,10},{9,11},{10,... | collective-permute-start | bytes 405512 | tf_op jit(solution)/shard_map/ppermute | solution.py:397
  37.6 4.0 %collective-permute-start.10 = (bf16[528,128]{1,0:T(8,128)(2,1)S(1)}, bf16[528,128]{1,0:T(8,128)(2,1)S(1)}, u32[]{:S(2)}, u32[]{:S(2)}) collective-permute-start(bf16[528,128]{1,0:T(8,128)(2,1)S(1)} %collective-permute-done.5.refs_3_), channel_id=1, source_target_pairs={{0,1},{1,0},{2,3},{3,2},{4,5},{5,4},{6,7},{7,6},{8,9},{9,8},{10,11... | collective-permute-start | bytes 405512 | tf_op jit(solution)/shard_map/ppermute | solution.py:397
  39.1 2.6 %collective-permute-start.11 = (bf16[528,128]{1,0:T(8,128)(2,1)S(1)}, bf16[528,128]{1,0:T(8,128)(2,1)S(1)}, u32[]{:S(2)}, u32[]{:S(2)}) collective-permute-start(bf16[528,128]{1,0:T(8,128)(2,1)S(1)} %collective-permute-done.6.refs_6_), channel_id=1, source_target_pairs={{0,1},{1,0},{2,3},{3,2},{4,5},{5,4},{6,7},{7,6},{8,9},{9,8},{10,11... | collective-permute-start | bytes 405512 | tf_op jit(solution)/shard_map/ppermute | solution.py:397
  39.1 2.6 %collective-permute-start.12 = (bf16[528,128]{1,0:T(8,128)(2,1)S(1)}, bf16[528,128]{1,0:T(8,128)(2,1)S(1)}, u32[]{:S(2)}, u32[]{:S(2)}) collective-permute-start(bf16[528,128]{1,0:T(8,128)(2,1)S(1)} %collective-permute-done.7.refs_9_), channel_id=1, source_target_pairs={{0,1},{1,0},{2,3},{3,2},{4,5},{5,4},{6,7},{7,6},{8,9},{9,8},{10,11... | collective-permute-start | bytes 405512 | tf_op jit(solution)/shard_map/ppermute | solution.py:397

commit v7 on v6

--- a/solution.py
+++ b/solution.py
@@ -12,7 +12,7 @@
 CHIPS = 4
 SPAN = 2 * CHIPS
 HALO = 8
-EXCHANGE = (1, 3, 2)
+EXCHANGE = (2, 3, 1)
 PARTS = 16
 VMEM = pl.BlockSpec(memory_space=pltpu.VMEM)
 HBM = pl.BlockSpec(memory_space=pltpu.HBM)
@@ -87,11 +87,11 @@
 
 
 def put_decay(out, decays, heads, size):
-    out[side(0, heads, size), :] = padded([p.astype(F32) for p in three_parts(decays)])
+    out[side(1, heads, size), :] = padded([p.astype(F32) for p in three_parts(decays)])
 
 
 def get_decay(packet, heads, size):
-    tail = packet[side(0, heads, size), :].astype(F32)
+    tail = packet[side(1, heads, size), :].astype(F32)
     return tail[0:heads] + tail[heads : 2 * heads] + tail[2 * heads : 3 * heads]
 
 
@@ -156,7 +156,7 @@
             edges.append(head_edges)
             values.append(v_buf[g, 0:HALO, cols].astype(F32) * ending[0:HALO, j : j + 1])
         put_decay(out_ref.at[g], jnp.exp(cum[heads : 2 * heads]), heads, size)
-        out_ref[g, side(1, heads, size), :] = padded(
+        out_ref[g, side(0, heads, size), :] = padded(
             [edges[j][t] for t in range(taps - 1) for j in range(heads)]
         )
         out_ref[g, side(2, heads, size), :] = padded(
@@ -220,7 +220,7 @@
             got = got_ref[g, side(part, heads, size), :].astype(F32)
             return jnp.where(first, own, got), jnp.where(first, got, own)
 
-        edges, out_edges = earlier_later(1)
+        edges, out_edges = earlier_later(0)
         out_values, values = earlier_later(2)
         fixes = edge_states(values.astype(BF16), edges.astype(BF16), heads)
         for j in range(heads):
@@ -232,7 +232,7 @@
             ).astype(BF16)
         put_decay(out_ref.at[g], own_decay * got_decay, heads, size)
         later_by = jnp.where(first, got_decay, own_decay)
-        out_ref[g, side(1, heads, size), :] = out_edges.astype(BF16)
+        out_ref[g, side(0, heads, size), :] = out_edges.astype(BF16)
         out_ref[g, side(2, heads, size), :] = padded(
             [out_values[t * heads : (t + 1) * heads] * later_by for t in range(3)]
         )
@@ -251,7 +251,7 @@
 def last_edge_kernel(heads, size, *refs):
     packets, out_ref, held = refs[:CHIPS], refs[CHIPS], refs[CHIPS + 1]
     in_order(packets, held)
-    out_ref[...] = held[CHIPS - 1, side(1, heads, size), :]
+    out_ref[...] = held[CHIPS - 1, side(0, heads, size), :]
 
 
 def span_kernel(heads, size, *refs):
@@ -259,7 +259,7 @@
     in_order(packets, held)
     decays = [get_decay(held.at[b], heads, size) for b in range(CHIPS)]
     fixes = [
-        chip_fixes(held, b, held[b - 1, side(1, heads, size), :], heads, size)
+        chip_fixes(held, b, held[b - 1, side(0, heads, size), :], heads, size)
         for b in range(1, CHIPS)
     ]
     fixes.insert(0, chip_fixes(held, 0, before[0][...], heads, size) if before else None)
@@ -274,9 +274,9 @@
     whole = decays[0]
     for b in range(1, CHIPS):
         whole = whole * decays[b]
-    put_decay(out_ref, whole, heads, size)
-    out_ref[side(1, heads, size), :] = held[CHIPS - 1, side(1, heads, size), :]
-    out_ref[side(2, heads, size), :] = held[0, side(2, heads, size), :]
+    out_ref[side(0, heads, size), :] = held[CHIPS - 1, side(0, heads, size), :]
+    if before:
+        put_decay(out_ref, whole, heads, size)
 
 
 def spread_kernel(heads, size, *refs):
@@ -285,9 +285,9 @@
     later = lax.axis_index("ctx") >= SPAN
     in_order(packets, held)
     decays = [get_decay(held.at[b], heads, size) for b in range(CHIPS)]
-    edges = known[0][...] if known else before[side(1, heads, size), :]
+    edges = known[0][...] if known else before[side(0, heads, size), :]
     edges = [jnp.where(later, edges.astype(F32), 0.0).astype(BF16)]
-    edges += [held[b, side(1, heads, size), :] for b in range(CHIPS - 1)]
+    edges += [held[b, side(0, heads, size), :] for b in range(CHIPS - 1)]
     fixes = [chip_fixes(held, b, edges[b], heads, size) for b in range(CHIPS - 1)]
     for j in range(heads):
         rows = slice(j * size, (j + 1) * size)
@@ -309,49 +309,48 @@
     rows = q_ref.shape[0]
     core, _ = position()
     second = core == 1
-    row = lax.broadcasted_iota(jnp.int32, (rows, PARTS), 0)
-    edge = lax.broadcasted_iota(jnp.int32, (rows, PARTS), 1)
-    seen = [
-        (lax.rem(edge, heads) == j) & (lax.div(edge, heads) <= row) & (edge < 3 * heads)
-        for j in range(heads)
-    ]
+    row = lax.broadcasted_iota(jnp.int32, (rows, 2 * PARTS), 0)
+    column = lax.broadcasted_iota(jnp.int32, (rows, 2 * PARTS), 1)
+    edge = lax.rem(column, PARTS)
+    causal = (lax.div(edge, heads) <= row) & (edge < 3 * heads)
+    ahead = column < PARTS
+    kept = ((ahead & (core == 1)) | causal) & (ahead | (core == 1))
+    kept = [kept & (lax.rem(edge, heads) == j) for j in range(heads)]
     for i, (mine, g) in enumerate(items):
-        prefix_ref, intra_ref, sib_ref = per_item[i]
+        prefix_ref, _, sib_ref = per_item[i]
         b = head_group(mine, g)
         by = jnp.where(second, get_decay(sib_ref.at[g], heads, size), 1.0)
-        before_chip = prefix_ref[heads * size : heads * size + PARTS, :]
-        fixes = edge_states(sib_ref[g, side(2, heads, size), :], before_chip, heads)
-        edges = jnp.where(
-            second,
-            sib_ref[g, side(1, heads, size), :].astype(F32),
-            before_chip.astype(F32),
-        )
+        edges = jnp.concatenate(
+            [
+                prefix_ref[heads * size : heads * size + PARTS, :].astype(F32),
+                sib_ref[g, side(0, heads, size), :].astype(F32),
+            ],
+            0,
+        ).astype(BF16)
         for j in range(heads):
             cols = columns(b * heads * size, j * size, size)
             these = slice(j * size, (j + 1) * size)
-            sib = jnp.where(second, sib_ref[g, these, :].astype(F32) + fixes[j], 0.0)
-            prefix = prefix_ref[these, :].astype(F32) * by[j : j + 1] + sib
+            sib = jnp.where(second, sib_ref[g, these, :].astype(F32), 0.0)
+            prefix = (prefix_ref[these, :].astype(F32) * by[j : j + 1] + sib).astype(BF16)
             both = lax.dot_general(
                 q_ref[:, cols],
-                jnp.concatenate([prefix, edges], 0).astype(BF16),
+                jnp.concatenate([prefix, edges], 0),
                 (((1,), (1,)), ((), ())),
                 preferred_element_type=F32,
             )
             inter_ref[i * heads + j] = both[:, 0:size]
-            score_ref[i * heads + j] = jnp.where(seen[j], both[:, size : size + PARTS], 0.0).astype(
-                BF16
-            )
+            score_ref[i * heads + j] = jnp.where(kept[j], both[:, size:], 0.0).astype(BF16)
     copies = []
     for i, (mine, g) in enumerate(items):
-        _, intra_ref, _ = per_item[i]
+        _, intra_ref, sib_ref = per_item[i]
         b = head_group(mine, g)
         started = jnp.exp(cum_ref[b][0:heads]).T
-        values = intra_ref[CHIPS * heads, g * PARTS : (g + 1) * PARTS, :].astype(BF16)
+        values = intra_ref[CHIPS * heads, g * PARTS : (g + 1) * PARTS, :]
+        ahead_values = jnp.where(second, sib_ref[g, side(2, heads, size), :].astype(F32), values)
+        values = jnp.concatenate([ahead_values, values], 0).astype(BF16)
         for j in range(heads):
             cols = columns(b * heads * size, j * size, size)
-            edge_part = jnp.dot(
-                score_ref[i * heads + j], values, preferred_element_type=F32
-            )
+            edge_part = jnp.dot(score_ref[i * heads + j], values, preferred_element_type=F32)
             mixed = intra_ref[g * heads + j] + (
                 inter_ref[i * heads + j] + edge_part
             ) * started[:, j : j + 1]
@@ -368,7 +367,7 @@
 
 def join_spans(earlier, later, heads, size):
     base = heads * size
-    own = side(0, heads, size)
+    own = side(1, heads, size)
 
     def decay(x):
         tail = x[own].astype(F32)
@@ -380,7 +379,7 @@
         + later[:base].astype(F32).reshape(heads, size, -1)
     ).reshape(base, -1)
     parts = three_parts(by * decay(earlier))
-    return jnp.concatenate([state.astype(BF16), *parts, later[base + 3 * heads :]], 0)
+    return jnp.concatenate([state.astype(BF16), later[base : own.start], *parts, later[own.start + 3 * heads :]], 0)
 
 
 def on_device(queries, key_input, value_input, log_decay, conv_weight, norm_gain):
@@ -473,7 +472,7 @@
     span = call(
         functools.partial(span_kernel, heads, size),
         "span_state",
-        pltpu.VMEM((packet, size), BF16),
+        pltpu.VMEM((heads * size + (2 if known else 1) * PARTS, size), BF16),
         *packets, *known,
         scratch=[order],
     )
@@ -515,7 +514,7 @@
             cost_estimate=pl.CostEstimate(flops=1, transcendentals=0, bytes_accessed=1),
             scratch=[
                 pltpu.VMEM((len(items) * heads, rows, size), F32),
-                pltpu.VMEM((len(items) * heads, rows, PARTS), BF16),
+                pltpu.VMEM((len(items) * heads, rows, 2 * PARTS), BF16),
                 pltpu.VMEM((len(items), rows, heads * size), BF16),
                 pltpu.SemaphoreType.DMA((len(items),)),
             ],

time: 43.9 us -> 42.4 us (0.966)
  starting transfers between devices: 13.4 us -> 12.7 us
  waiting for transfers between devices: 15.6 us -> 15 us
    ppermute x13, starting transfers between devices: 13.4 us -> 12.7 us  [swap(): return lax.ppermute(x, 'ctx', [(i, i ^ mask) for i in range(n)])]
    ppermute x13, waiting for transfers between devices: 15.6 us -> 15 us  [swap(): return lax.ppermute(x, 'ctx', [(i, i ^ mask) for i in range(n)])]
  transfers between devices with their start and end apart: 13 -> 13, of which waited for: 7 -> 5; matrix products, arithmetic and copies ran while one was open for 0% -> 0% of each run, Pallas kernels for 22% -> 22%
where the time goes in v7:
time: 42.4 us; the launch traced here: 42.1 us
  waiting for transfers between devices  15 us (35%)
  Pallas kernels  14.1 us (33%)
  starting transfers between devices  12.7 us (30%)
    ppermute x13, waiting for transfers between devices, swap(): return lax.ppermute(x, 'ctx', [(i, i ^ mask) for i in range(n)])  15 us
    pallas_call x11, Pallas kernels, call(): pl.pallas_call(kernel, out_shape=out_shape, in_specs=in_specs, out_specs=...  14.1 us
    ppermute x13, starting transfers between devices, swap(): return lax.ppermute(x, 'ctx', [(i, i ^ mask) for i in range(n)])  12.7 us
  transfers between devices with their start and end apart: 13, of which 5 were waited for; matrix products, arithmetic and copies ran while one was open for 0% of the time, Pallas kernels for 22%

profile of v7, /device:TPU:1, one launch (start us, length us, event | category | flops | bytes accessed | tf_op | source)
XLA Modules:
  0.0 42.1 jit_solution(1324586749142669860)
XLA Ops:
  0.0 2.5 %states_other.1 = bf16[4,560,128]{2,1,0:T(8,128)(2,1)S(1)} custom-call(bf16[128,4096]{1,0:T(8,128)(2,1)} %k_ref.3, bf16[128,4096]{1,0:T(8,128)(2,1)} %v_ref.3, f32[4,4096]{1,0:T(4,128)} %w_ref.3, f32[32,128]{1,0:T(8,128)} %bitcast.22), custom_call_target="tpu_custom_call" | custom-call | tf_op jit(solution)/shard_map/states_other/pallas_call | solution.py:42
  2.6 2.6 %states_mine.1.own_ref = bf16[4,560,128]{2,1,0:T(8,128)(2,1)S(1)} custom-call(bf16[128,4096]{1,0:T(8,128)(2,1)} %k_ref.3, bf16[128,4096]{1,0:T(8,128)(2,1)} %v_ref.3, f32[4,4096]{1,0:T(4,128)} %w_ref.3, f32[32,128]{1,0:T(8,128)} %bitcast.23), custom_call_target="tpu_custom_call" | custom-call | tf_op jit(solution)/shard_map/states_mine/pallas_call | solution.py:42
  5.3 0.4 chip_states.1
  5.7 2.8 %collective-permute-start.3 = (bf16[560,128]{1,0:T(8,128)(2,1)S(1)}, bf16[560,128]{1,0:T(8,128)(2,1)S(1)}, u32[]{:S(2)}, u32[]{:S(2)}) collective-permute-start(bf16[560,128]{1,0:T(8,128)(2,1)S(1)} %get-tuple-element.31), channel_id=1, source_target_pairs={{0,2},{1,3},{2,0},{3,1},{4,6},{5,7},{6,4},{7,5},{8,10},{9,11},{10,... | collective-permute-start | bytes 430088 | tf_op jit(solution)/shard_map/ppermute | solution.py:396
  8.5 1.2 %collective-permute-start.2 = (bf16[560,128]{1,0:T(8,128)(2,1)S(1)}, bf16[560,128]{1,0:T(8,128)(2,1)S(1)}, u32[]{:S(2)}, u32[]{:S(2)}) collective-permute-start(bf16[560,128]{1,0:T(8,128)(2,1)S(1)} %get-tuple-element.32), channel_id=1, source_target_pairs={{0,6},{1,7},{2,4},{3,5},{4,2},{5,3},{6,0},{7,1},{8,14},{9,15},{10,... | collective-permute-start | bytes 430088 | tf_op jit(solution)/shard_map/ppermute | solution.py:396
  9.8 0.6 %collective-permute-start.9 = (bf16[4,560,128]{2,1,0:T(8,128)(2,1)S(1)}, bf16[4,560,128]{2,1,0:T(8,128)(2,1)S(1)}, u32[]{:S(2)}, u32[]{:S(2)}) collective-permute-start(bf16[4,560,128]{2,1,0:T(8,128)(2,1)S(1)} %states_mine.1.own_ref), channel_id=1, source_target_pairs={{0,1},{1,0},{2,3},{3,2},{4,5},{5,4},{6,7},{7,6},{8,9},{9,8},{10,11... | collective-permute-start | bytes 1720328 | tf_op jit(solution)/shard_map/ppermute | solution.py:396
  10.6 1.2 %intra_mine.1.refs_4_.refs_7_.refs_10_ = f32[17,128,128]{2,1,0:T(8,128)S(1)} custom-call(bf16[128,4096]{1,0:T(8,128)(2,1)S(1)} %copy-done, bf16[128,4096]{1,0:T(8,128)(2,1)S(1)} %copy-done.1, bf16[128,4096]{1,0:T(8,128)(2,1)S(1)} %copy-done.2, f32[4,4096]{1,0:T(4,128)S(1)} %copy-done.3, f32[8,8,128]{2,1,0:T(8,128)S(1)} %cum.1.cum_ref.refs_1_), custom_call_target="tpu_custom_call" | custom-call | tf_op jit(solution)/shard_map/intra_mine/pallas_call | solution.py:42
  11.8 3.6 %collective-permute-done.3.refs_1_ = bf16[560,128]{1,0:T(8,128)(2,1)S(1)} collective-permute-done((bf16[560,128]{1,0:T(8,128)(2,1)S(1)}, bf16[560,128]{1,0:T(8,128)(2,1)S(1)}, u32[]{:S(2)}, u32[]{:S(2)}) %collective-permute-start.3) | collective-permute-done | bytes 143392 | tf_op jit(solution)/shard_map/ppermute | solution.py:396
  15.4 1.4 %collective-permute-done.1.refs_2_ = bf16[560,128]{1,0:T(8,128)(2,1)S(1)} collective-permute-done((bf16[560,128]{1,0:T(8,128)(2,1)S(1)}, bf16[560,128]{1,0:T(8,128)(2,1)S(1)}, u32[]{:S(2)}, u32[]{:S(2)}) %collective-permute-start.1) | collective-permute-done | bytes 143392 | tf_op jit(solution)/shard_map/ppermute | solution.py:396
  16.8 0.4 span_state.1
  17.2 2.2 %collective-permute-start.4 = (bf16[528,128]{1,0:T(8,128)(2,1)S(1)}, bf16[528,128]{1,0:T(8,128)(2,1)S(1)}, u32[]{:S(2)}, u32[]{:S(2)}) collective-permute-start(bf16[528,128]{1,0:T(8,128)(2,1)S(1)} %span_state.1), channel_id=1, source_target_pairs={{0,8},{1,9},{2,10},{3,11},{4,12},{5,13},{6,14},{7,15},{8,0},{9,1},... | collective-permute-start | bytes 405512 | tf_op jit(solution)/shard_map/ppermute | solution.py:396
  19.3 1.1 %intra_other.1.refs_7_.refs_4_.refs_10_ = f32[17,128,128]{2,1,0:T(8,128)S(1)} custom-call(bf16[128,4096]{1,0:T(8,128)(2,1)S(1)} %copy-done, bf16[128,4096]{1,0:T(8,128)(2,1)S(1)} %copy-done.1, bf16[128,4096]{1,0:T(8,128)(2,1)S(1)} %copy-done.2, f32[4,4096]{1,0:T(4,128)S(1)} %copy-done.3, f32[8,8,128]{2,1,0:T(8,128)S(1)} %cum.1.cum_ref.refs_1_), custom_call_target="tpu_custom_call" | custom-call | tf_op jit(solution)/shard_map/intra_other/pallas_call | solution.py:42
  20.5 5.2 %collective-permute-done.4.refs_4_ = bf16[528,128]{1,0:T(8,128)(2,1)S(1)} collective-permute-done((bf16[528,128]{1,0:T(8,128)(2,1)S(1)}, bf16[528,128]{1,0:T(8,128)(2,1)S(1)}, u32[]{:S(2)}, u32[]{:S(2)}) %collective-permute-start.4) | collective-permute-done | bytes 135200 | tf_op jit(solution)/shard_map/ppermute | solution.py:396
  25.7 0.4 chip_prefix.1
  26.1 1.4 %collective-permute-start.8 = (bf16[528,128]{1,0:T(8,128)(2,1)S(1)}, bf16[528,128]{1,0:T(8,128)(2,1)S(1)}, u32[]{:S(2)}, u32[]{:S(2)}) collective-permute-start(bf16[528,128]{1,0:T(8,128)(2,1)S(1)} %get-tuple-element.35.refs_3_), channel_id=1, source_target_pairs={{0,1},{1,0},{2,3},{3,2},{4,5},{5,4},{6,7},{7,6},{8,9},{9,8},{10,11... | collective-permute-start | bytes 405512 | tf_op jit(solution)/shard_map/ppermute | solution.py:396
  27.5 1.1 %collective-permute-start.7 = (bf16[528,128]{1,0:T(8,128)(2,1)S(1)}, bf16[528,128]{1,0:T(8,128)(2,1)S(1)}, u32[]{:S(2)}, u32[]{:S(2)}) collective-permute-start(bf16[528,128]{1,0:T(8,128)(2,1)S(1)} %get-tuple-element.36), channel_id=1, source_target_pairs={{0,2},{1,3},{2,0},{3,1},{4,6},{5,7},{6,4},{7,5},{8,10},{9,11},{10,... | collective-permute-start | bytes 405512 | tf_op jit(solution)/shard_map/ppermute | solution.py:396
  28.9 1.3 %collective-permute-start.5 = (bf16[528,128]{1,0:T(8,128)(2,1)S(1)}, bf16[528,128]{1,0:T(8,128)(2,1)S(1)}, u32[]{:S(2)}, u32[]{:S(2)}) collective-permute-start(bf16[528,128]{1,0:T(8,128)(2,1)S(1)} %get-tuple-element.38), channel_id=1, source_target_pairs={{0,4},{1,5},{2,6},{3,7},{4,0},{5,1},{6,2},{7,3},{8,12},{9,13},{10,... | collective-permute-start | bytes 405512 | tf_op jit(solution)/shard_map/ppermute | solution.py:396
  30.2 1.5 %out_m0_o0.1.refs_12_ = bf16[128,4096]{1,0:T(8,128)(2,1)} custom-call(bf16[128,4096]{1,0:T(8,128)(2,1)S(1)} %copy-done, f32[8,8,128]{2,1,0:T(8,128)S(1)} %cum.1.cum_ref.refs_1_, f32[1,4096]{1,0:T(1,128)S(1)} %bitcast.19, bf16[528,128]{1,0:T(8,128)(2,1)S(1)} %get-tuple-element.35.refs_3_, f32[17,128,128]{2,1,0:T(8,128)S(1)} %intra_mine.1.refs_4_.refs_7_.refs_10_, ...), custom_call_target="tpu_custom_call" | custom-call | flops 1 | bytes 1 | tf_op jit(solution)/shard_map/out_m0_o0/pallas_call | solution.py:42
  31.7 3.5 %collective-permute-done.7.refs_9_ = bf16[528,128]{1,0:T(8,128)(2,1)S(1)} collective-permute-done((bf16[528,128]{1,0:T(8,128)(2,1)S(1)}, bf16[528,128]{1,0:T(8,128)(2,1)S(1)}, u32[]{:S(2)}, u32[]{:S(2)}) %collective-permute-start.7) | collective-permute-done | bytes 135200 | tf_op jit(solution)/shard_map/ppermute | solution.py:396
  35.3 1.2 %collective-permute-done.5.refs_3_ = bf16[528,128]{1,0:T(8,128)(2,1)S(1)} collective-permute-done((bf16[528,128]{1,0:T(8,128)(2,1)S(1)}, bf16[528,128]{1,0:T(8,128)(2,1)S(1)}, u32[]{:S(2)}, u32[]{:S(2)}) %collective-permute-start.5) | collective-permute-done | bytes 135200 | tf_op jit(solution)/shard_map/ppermute | solution.py:396
  36.5 1.2 %collective-permute-start.10 = (bf16[528,128]{1,0:T(8,128)(2,1)S(1)}, bf16[528,128]{1,0:T(8,128)(2,1)S(1)}, u32[]{:S(2)}, u32[]{:S(2)}) collective-permute-start(bf16[528,128]{1,0:T(8,128)(2,1)S(1)} %collective-permute-done.5.refs_3_), channel_id=1, source_target_pairs={{0,1},{1,0},{2,3},{3,2},{4,5},{5,4},{6,7},{7,6},{8,9},{9,8},{10,11... | collective-permute-start | bytes 405512 | tf_op jit(solution)/shard_map/ppermute | solution.py:396
  37.7 0.5 %collective-permute-start.12 = (bf16[528,128]{1,0:T(8,128)(2,1)S(1)}, bf16[528,128]{1,0:T(8,128)(2,1)S(1)}, u32[]{:S(2)}, u32[]{:S(2)}) collective-permute-start(bf16[528,128]{1,0:T(8,128)(2,1)S(1)} %collective-permute-done.7.refs_9_), channel_id=1, source_target_pairs={{0,1},{1,0},{2,3},{3,2},{4,5},{5,4},{6,7},{7,6},{8,9},{9,8},{10,11... | collective-permute-start | bytes 405512 | tf_op jit(solution)/shard_map/ppermute | solution.py:396
  38.2 2.0 %out_m2_m3_m1.1.refs_12_ = bf16[128,4096]{1,0:T(8,128)(2,1)} custom-call(bf16[128,4096]{1,0:T(8,128)(2,1)S(1)} %copy-done, f32[8,8,128]{2,1,0:T(8,128)S(1)} %cum.1.cum_ref.refs_1_, f32[1,4096]{1,0:T(1,128)S(1)} %bitcast.20, bf16[528,128]{1,0:T(8,128)(2,1)S(1)} %collective-permute-done.5.refs_3_, ...), custom_call_target="tpu_custom_call", output_to_operand_aliasing={{}: (12, {})} | custom-call | flops 1 | bytes 1 | tf_op jit(solution)/shard_map/out_m2_m3_m1/pallas_call | solution.py:42
  40.2 2.0 %out_o2_o3_o1.1 = bf16[128,4096]{1,0:T(8,128)(2,1)} custom-call(bf16[128,4096]{1,0:T(8,128)(2,1)S(1)} %copy-done, f32[8,8,128]{2,1,0:T(8,128)S(1)} %cum.1.cum_ref.refs_1_, f32[1,4096]{1,0:T(1,128)S(1)} %bitcast.21, bf16[528,128]{1,0:T(8,128)(2,1)S(1)} %collective-permute-done.10.refs_3_, ...), custom_call_target="tpu_custom_call", output_to_operand_aliasing={{}: (12, {})} | custom-call | flops 1 | bytes 1 | tf_op jit(solution)/shard_map/out_o2_o3_o1/pallas_call | solution.py:42
  (27 shorter events, 0.9 us)
Async XLA Ops:
  2.5 2.8 %collective-permute-start = (bf16[4,560,128]{2,1,0:T(8,128)(2,1)S(1)}, bf16[4,560,128]{2,1,0:T(8,128)(2,1)S(1)}, u32[]{:S(2)}, u32[]{:S(2)}) collective-permute-start(bf16[4,560,128]{2,1,0:T(8,128)(2,1)S(1)} %states_other.1), channel_id=1, source_target_pairs={{0,1},{1,0},{2,3},{3,2},{4,5},{5,4},{6,7},{7,6},{8,9},{9,8},{10,11... | collective-permute-start | bytes 1720328 | tf_op jit(solution)/shard_map/ppermute | solution.py:396
  2.6 7.9 %copy-start.2 = (bf16[128,4096]{1,0:T(8,128)(2,1)S(1)}, bf16[128,4096]{1,0:T(8,128)(2,1)}, u32[]{:S(2)}) copy-start(bf16[128,4096]{1,0:T(8,128)(2,1)} %v_ref.3) | copy-start | bytes 3145732
  5.3 5.1 %copy-start.5 = (f32[128,32]{0,1:T(8,128)S(1)}, f32[128,32]{0,1:T(8,128)}, u32[]{:S(2)}) copy-start(f32[128,32]{0,1:T(8,128)} %param.9) | copy-start | bytes 49156
  5.3 5.3 %copy-start = (bf16[128,4096]{1,0:T(8,128)(2,1)S(1)}, bf16[128,4096]{1,0:T(8,128)(2,1)}, u32[]{:S(2)}) copy-start(bf16[128,4096]{1,0:T(8,128)(2,1)} %refs_0_.5) | copy-start | bytes 3145732
  5.3 5.3 %copy-start.1 = (bf16[128,4096]{1,0:T(8,128)(2,1)S(1)}, bf16[128,4096]{1,0:T(8,128)(2,1)}, u32[]{:S(2)}) copy-start(bf16[128,4096]{1,0:T(8,128)(2,1)} %k_ref.3) | copy-start | bytes 3145732
  5.3 5.3 %copy-start.3 = (f32[4,4096]{1,0:T(4,128)S(1)}, f32[4,4096]{1,0:T(4,128)}, u32[]{:S(2)}) copy-start(f32[4,4096]{1,0:T(4,128)} %w_ref.3) | copy-start | bytes 196612
  5.7 9.7 %collective-permute-start.3 = (bf16[560,128]{1,0:T(8,128)(2,1)S(1)}, bf16[560,128]{1,0:T(8,128)(2,1)S(1)}, u32[]{:S(2)}, u32[]{:S(2)}) collective-permute-start(bf16[560,128]{1,0:T(8,128)(2,1)S(1)} %get-tuple-element.31), channel_id=1, source_target_pairs={{0,2},{1,3},{2,0},{3,1},{4,6},{5,7},{6,4},{7,5},{8,10},{9,11},{10,... | collective-permute-start | bytes 430088 | tf_op jit(solution)/shard_map/ppermute | solution.py:396
  8.5 6.9 %collective-permute-start.2 = (bf16[560,128]{1,0:T(8,128)(2,1)S(1)}, bf16[560,128]{1,0:T(8,128)(2,1)S(1)}, u32[]{:S(2)}, u32[]{:S(2)}) collective-permute-start(bf16[560,128]{1,0:T(8,128)(2,1)S(1)} %get-tuple-element.32), channel_id=1, source_target_pairs={{0,6},{1,7},{2,4},{3,5},{4,2},{5,3},{6,0},{7,1},{8,14},{9,15},{10,... | collective-permute-start | bytes 430088 | tf_op jit(solution)/shard_map/ppermute | solution.py:396
  9.7 7.1 %collective-permute-start.1 = (bf16[560,128]{1,0:T(8,128)(2,1)S(1)}, bf16[560,128]{1,0:T(8,128)(2,1)S(1)}, u32[]{:S(2)}, u32[]{:S(2)}) collective-permute-start(bf16[560,128]{1,0:T(8,128)(2,1)S(1)} %get-tuple-element.33), channel_id=1, source_target_pairs={{0,4},{1,5},{2,6},{3,7},{4,0},{5,1},{6,2},{7,3},{8,12},{9,13},{10,... | collective-permute-start | bytes 430088 | tf_op jit(solution)/shard_map/ppermute | solution.py:396
  9.8 20.4 %collective-permute-start.9 = (bf16[4,560,128]{2,1,0:T(8,128)(2,1)S(1)}, bf16[4,560,128]{2,1,0:T(8,128)(2,1)S(1)}, u32[]{:S(2)}, u32[]{:S(2)}) collective-permute-start(bf16[4,560,128]{2,1,0:T(8,128)(2,1)S(1)} %states_mine.1.own_ref), channel_id=1, source_target_pairs={{0,1},{1,0},{2,3},{3,2},{4,5},{5,4},{6,7},{7,6},{8,9},{9,8},{10,11... | collective-permute-start | bytes 1720328 | tf_op jit(solution)/shard_map/ppermute | solution.py:396
  17.2 8.5 %collective-permute-start.4 = (bf16[528,128]{1,0:T(8,128)(2,1)S(1)}, bf16[528,128]{1,0:T(8,128)(2,1)S(1)}, u32[]{:S(2)}, u32[]{:S(2)}) collective-permute-start(bf16[528,128]{1,0:T(8,128)(2,1)S(1)} %span_state.1), channel_id=1, source_target_pairs={{0,8},{1,9},{2,10},{3,11},{4,12},{5,13},{6,14},{7,15},{8,0},{9,1},... | collective-permute-start | bytes 405512 | tf_op jit(solution)/shard_map/ppermute | solution.py:396
  20.5 9.7 %copy-start.4 = (f32[4096]{0:T(1024)S(1)}, f32[4096]{0:T(1024)}, u32[]{:S(2)}) copy-start(f32[4096]{0:T(1024)} %param.11) | copy-start | bytes 49156
  26.1 4.1 %collective-permute-start.8 = (bf16[528,128]{1,0:T(8,128)(2,1)S(1)}, bf16[528,128]{1,0:T(8,128)(2,1)S(1)}, u32[]{:S(2)}, u32[]{:S(2)}) collective-permute-start(bf16[528,128]{1,0:T(8,128)(2,1)S(1)} %get-tuple-element.35.refs_3_), channel_id=1, source_target_pairs={{0,1},{1,0},{2,3},{3,2},{4,5},{5,4},{6,7},{7,6},{8,9},{9,8},{10,11... | collective-permute-start | bytes 405512 | tf_op jit(solution)/shard_map/ppermute | solution.py:396
  27.5 7.7 %collective-permute-start.7 = (bf16[528,128]{1,0:T(8,128)(2,1)S(1)}, bf16[528,128]{1,0:T(8,128)(2,1)S(1)}, u32[]{:S(2)}, u32[]{:S(2)}) collective-permute-start(bf16[528,128]{1,0:T(8,128)(2,1)S(1)} %get-tuple-element.36), channel_id=1, source_target_pairs={{0,2},{1,3},{2,0},{3,1},{4,6},{5,7},{6,4},{7,5},{8,10},{9,11},{10,... | collective-permute-start | bytes 405512 | tf_op jit(solution)/shard_map/ppermute | solution.py:396
  28.6 6.7 %collective-permute-start.6 = (bf16[528,128]{1,0:T(8,128)(2,1)S(1)}, bf16[528,128]{1,0:T(8,128)(2,1)S(1)}, u32[]{:S(2)}, u32[]{:S(2)}) collective-permute-start(bf16[528,128]{1,0:T(8,128)(2,1)S(1)} %get-tuple-element.37), channel_id=1, source_target_pairs={{0,6},{1,7},{2,4},{3,5},{4,2},{5,3},{6,0},{7,1},{8,14},{9,15},{10,... | collective-permute-start | bytes 405512 | tf_op jit(solution)/shard_map/ppermute | solution.py:396
  28.9 7.6 %collective-permute-start.5 = (bf16[528,128]{1,0:T(8,128)(2,1)S(1)}, bf16[528,128]{1,0:T(8,128)(2,1)S(1)}, u32[]{:S(2)}, u32[]{:S(2)}) collective-permute-start(bf16[528,128]{1,0:T(8,128)(2,1)S(1)} %get-tuple-element.38), channel_id=1, source_target_pairs={{0,4},{1,5},{2,6},{3,7},{4,0},{5,1},{6,2},{7,3},{8,12},{9,13},{10,... | collective-permute-start | bytes 405512 | tf_op jit(solution)/shard_map/ppermute | solution.py:396
  36.5 3.7 %collective-permute-start.10 = (bf16[528,128]{1,0:T(8,128)(2,1)S(1)}, bf16[528,128]{1,0:T(8,128)(2,1)S(1)}, u32[]{:S(2)}, u32[]{:S(2)}) collective-permute-start(bf16[528,128]{1,0:T(8,128)(2,1)S(1)} %collective-permute-done.5.refs_3_), channel_id=1, source_target_pairs={{0,1},{1,0},{2,3},{3,2},{4,5},{5,4},{6,7},{7,6},{8,9},{9,8},{10,11... | collective-permute-start | bytes 405512 | tf_op jit(solution)/shard_map/ppermute | solution.py:396
  37.6 2.5 %collective-permute-start.11 = (bf16[528,128]{1,0:T(8,128)(2,1)S(1)}, bf16[528,128]{1,0:T(8,128)(2,1)S(1)}, u32[]{:S(2)}, u32[]{:S(2)}) collective-permute-start(bf16[528,128]{1,0:T(8,128)(2,1)S(1)} %collective-permute-done.6.refs_6_), channel_id=1, source_target_pairs={{0,1},{1,0},{2,3},{3,2},{4,5},{5,4},{6,7},{7,6},{8,9},{9,8},{10,11... | collective-permute-start | bytes 405512 | tf_op jit(solution)/shard_map/ppermute | solution.py:396
  37.7 2.5 %collective-permute-start.12 = (bf16[528,128]{1,0:T(8,128)(2,1)S(1)}, bf16[528,128]{1,0:T(8,128)(2,1)S(1)}, u32[]{:S(2)}, u32[]{:S(2)}) collective-permute-start(bf16[528,128]{1,0:T(8,128)(2,1)S(1)} %collective-permute-done.7.refs_9_), channel_id=1, source_target_pairs={{0,1},{1,0},{2,3},{3,2},{4,5},{5,4},{6,7},{7,6},{8,9},{9,8},{10,11... | collective-permute-start | bytes 405512 | tf_op jit(solution)/shard_map/ppermute | solution.py:396

commit v8 on v7

--- a/solution.py
+++ b/solution.py
@@ -317,8 +317,9 @@
     kept = ((ahead & (core == 1)) | causal) & (ahead | (core == 1))
     kept = [kept & (lax.rem(edge, heads) == j) for j in range(heads)]
     for i, (mine, g) in enumerate(items):
-        prefix_ref, _, sib_ref = per_item[i]
+        prefix_ref, intra_ref, sib_ref = per_item[i]
         b = head_group(mine, g)
+        started = jnp.exp(cum_ref[b][0:heads]).T
         by = jnp.where(second, get_decay(sib_ref.at[g], heads, size), 1.0)
         edges = jnp.concatenate(
             [
@@ -338,22 +339,25 @@
                 (((1,), (1,)), ((), ())),
                 preferred_element_type=F32,
             )
-            inter_ref[i * heads + j] = both[:, 0:size]
+            both = both * started[:, j : j + 1]
+            inter_ref[i * heads + j] = both[:, 0:size] + intra_ref[g * heads + j]
             score_ref[i * heads + j] = jnp.where(kept[j], both[:, size:], 0.0).astype(BF16)
     copies = []
     for i, (mine, g) in enumerate(items):
         _, intra_ref, sib_ref = per_item[i]
         b = head_group(mine, g)
-        started = jnp.exp(cum_ref[b][0:heads]).T
         values = intra_ref[CHIPS * heads, g * PARTS : (g + 1) * PARTS, :]
         ahead_values = jnp.where(second, sib_ref[g, side(2, heads, size), :].astype(F32), values)
         values = jnp.concatenate([ahead_values, values], 0).astype(BF16)
         for j in range(heads):
+            inter_ref[i * heads + j] += jnp.dot(
+                score_ref[i * heads + j], values, preferred_element_type=F32
+            )
+    for i, (mine, g) in enumerate(items):
+        b = head_group(mine, g)
+        for j in range(heads):
             cols = columns(b * heads * size, j * size, size)
-            edge_part = jnp.dot(score_ref[i * heads + j], values, preferred_element_type=F32)
-            mixed = intra_ref[g * heads + j] + (
-                inter_ref[i * heads + j] + edge_part
-            ) * started[:, j : j + 1]
+            mixed = inter_ref[i * heads + j]
             scale = lax.rsqrt(jnp.mean(mixed * mixed, axis=1, keepdims=True) + 1e-05)
             done_ref[i, :, j * size : (j + 1) * size] = (
                 mixed * scale * gain_ref[:, cols]

time: 42.4 us -> 41.6 us (0.981)
  Pallas kernels: 14.1 us -> 13.2 us
    pallas_call x11, Pallas kernels: 14.1 us -> 13.2 us  [call(): pl.pallas_call(kernel, out_shape=out_shape, in_specs=in_specs, out_specs=...]
  transfers between devices with their start and end apart: 13 -> 13, of which waited for: 5 -> 5; matrix products, arithmetic and copies ran while one was open for 0% -> 0% of each run, Pallas kernels for 22% -> 21%
where the time goes in v8:
time: 41.6 us; the launch traced here: 41.4 us
  waiting for transfers between devices  15.2 us (37%)
  Pallas kernels  13.2 us (32%)
  starting transfers between devices  12.7 us (31%)
    ppermute x13, waiting for transfers between devices, swap(): return lax.ppermute(x, 'ctx', [(i, i ^ mask) for i in range(n)])  15.2 us
    pallas_call x11, Pallas kernels, call(): pl.pallas_call(kernel, out_shape=out_shape, in_specs=in_specs, out_specs=...  13.2 us
    ppermute x13, starting transfers between devices, swap(): return lax.ppermute(x, 'ctx', [(i, i ^ mask) for i in range(n)])  12.7 us
  transfers between devices with their start and end apart: 13, of which 5 were waited for; matrix products, arithmetic and copies ran while one was open for 0% of the time, Pallas kernels for 21%

profile of v8, /device:TPU:1, one launch (start us, length us, event | category | flops | bytes accessed | tf_op | source)
XLA Modules:
  0.0 41.4 jit_solution(10907730487184734218)
XLA Ops:
  0.0 2.5 %states_other.1 = bf16[4,560,128]{2,1,0:T(8,128)(2,1)S(1)} custom-call(bf16[128,4096]{1,0:T(8,128)(2,1)} %k_ref.3, bf16[128,4096]{1,0:T(8,128)(2,1)} %v_ref.3, f32[4,4096]{1,0:T(4,128)} %w_ref.3, f32[32,128]{1,0:T(8,128)} %bitcast.22), custom_call_target="tpu_custom_call" | custom-call | tf_op jit(solution)/shard_map/states_other/pallas_call | solution.py:42
  2.6 2.6 %states_mine.1.own_ref = bf16[4,560,128]{2,1,0:T(8,128)(2,1)S(1)} custom-call(bf16[128,4096]{1,0:T(8,128)(2,1)} %k_ref.3, bf16[128,4096]{1,0:T(8,128)(2,1)} %v_ref.3, f32[4,4096]{1,0:T(4,128)} %w_ref.3, f32[32,128]{1,0:T(8,128)} %bitcast.23), custom_call_target="tpu_custom_call" | custom-call | tf_op jit(solution)/shard_map/states_mine/pallas_call | solution.py:42
  5.3 0.4 chip_states.1
  5.7 2.8 %collective-permute-start.3 = (bf16[560,128]{1,0:T(8,128)(2,1)S(1)}, bf16[560,128]{1,0:T(8,128)(2,1)S(1)}, u32[]{:S(2)}, u32[]{:S(2)}) collective-permute-start(bf16[560,128]{1,0:T(8,128)(2,1)S(1)} %get-tuple-element.31), channel_id=1, source_target_pairs={{0,2},{1,3},{2,0},{3,1},{4,6},{5,7},{6,4},{7,5},{8,10},{9,11},{10,... | collective-permute-start | bytes 430088 | tf_op jit(solution)/shard_map/ppermute | solution.py:400
  8.5 1.2 %collective-permute-start.2 = (bf16[560,128]{1,0:T(8,128)(2,1)S(1)}, bf16[560,128]{1,0:T(8,128)(2,1)S(1)}, u32[]{:S(2)}, u32[]{:S(2)}) collective-permute-start(bf16[560,128]{1,0:T(8,128)(2,1)S(1)} %get-tuple-element.32), channel_id=1, source_target_pairs={{0,6},{1,7},{2,4},{3,5},{4,2},{5,3},{6,0},{7,1},{8,14},{9,15},{10,... | collective-permute-start | bytes 430088 | tf_op jit(solution)/shard_map/ppermute | solution.py:400
  9.8 0.6 %collective-permute-start.9 = (bf16[4,560,128]{2,1,0:T(8,128)(2,1)S(1)}, bf16[4,560,128]{2,1,0:T(8,128)(2,1)S(1)}, u32[]{:S(2)}, u32[]{:S(2)}) collective-permute-start(bf16[4,560,128]{2,1,0:T(8,128)(2,1)S(1)} %states_mine.1.own_ref), channel_id=1, source_target_pairs={{0,1},{1,0},{2,3},{3,2},{4,5},{5,4},{6,7},{7,6},{8,9},{9,8},{10,11... | collective-permute-start | bytes 1720328 | tf_op jit(solution)/shard_map/ppermute | solution.py:400
  10.6 1.2 %intra_mine.1.refs_4_.refs_7_.refs_10_ = f32[17,128,128]{2,1,0:T(8,128)S(1)} custom-call(bf16[128,4096]{1,0:T(8,128)(2,1)S(1)} %copy-done, bf16[128,4096]{1,0:T(8,128)(2,1)S(1)} %copy-done.1, bf16[128,4096]{1,0:T(8,128)(2,1)S(1)} %copy-done.2, f32[4,4096]{1,0:T(4,128)S(1)} %copy-done.3, f32[8,8,128]{2,1,0:T(8,128)S(1)} %cum.1.cum_ref.refs_1_), custom_call_target="tpu_custom_call" | custom-call | tf_op jit(solution)/shard_map/intra_mine/pallas_call | solution.py:42
  11.8 3.6 %collective-permute-done.3.refs_1_ = bf16[560,128]{1,0:T(8,128)(2,1)S(1)} collective-permute-done((bf16[560,128]{1,0:T(8,128)(2,1)S(1)}, bf16[560,128]{1,0:T(8,128)(2,1)S(1)}, u32[]{:S(2)}, u32[]{:S(2)}) %collective-permute-start.3) | collective-permute-done | bytes 143392 | tf_op jit(solution)/shard_map/ppermute | solution.py:400
  15.4 1.4 %collective-permute-done.1.refs_2_ = bf16[560,128]{1,0:T(8,128)(2,1)S(1)} collective-permute-done((bf16[560,128]{1,0:T(8,128)(2,1)S(1)}, bf16[560,128]{1,0:T(8,128)(2,1)S(1)}, u32[]{:S(2)}, u32[]{:S(2)}) %collective-permute-start.1) | collective-permute-done | bytes 143392 | tf_op jit(solution)/shard_map/ppermute | solution.py:400
  16.8 0.4 span_state.1
  17.2 2.2 %collective-permute-start.4 = (bf16[528,128]{1,0:T(8,128)(2,1)S(1)}, bf16[528,128]{1,0:T(8,128)(2,1)S(1)}, u32[]{:S(2)}, u32[]{:S(2)}) collective-permute-start(bf16[528,128]{1,0:T(8,128)(2,1)S(1)} %span_state.1), channel_id=1, source_target_pairs={{0,8},{1,9},{2,10},{3,11},{4,12},{5,13},{6,14},{7,15},{8,0},{9,1},... | collective-permute-start | bytes 405512 | tf_op jit(solution)/shard_map/ppermute | solution.py:400
  19.3 1.1 %intra_other.1.refs_7_.refs_4_.refs_10_ = f32[17,128,128]{2,1,0:T(8,128)S(1)} custom-call(bf16[128,4096]{1,0:T(8,128)(2,1)S(1)} %copy-done, bf16[128,4096]{1,0:T(8,128)(2,1)S(1)} %copy-done.1, bf16[128,4096]{1,0:T(8,128)(2,1)S(1)} %copy-done.2, f32[4,4096]{1,0:T(4,128)S(1)} %copy-done.3, f32[8,8,128]{2,1,0:T(8,128)S(1)} %cum.1.cum_ref.refs_1_), custom_call_target="tpu_custom_call" | custom-call | tf_op jit(solution)/shard_map/intra_other/pallas_call | solution.py:42
  20.5 5.2 %collective-permute-done.4.refs_4_ = bf16[528,128]{1,0:T(8,128)(2,1)S(1)} collective-permute-done((bf16[528,128]{1,0:T(8,128)(2,1)S(1)}, bf16[528,128]{1,0:T(8,128)(2,1)S(1)}, u32[]{:S(2)}, u32[]{:S(2)}) %collective-permute-start.4) | collective-permute-done | bytes 135200 | tf_op jit(solution)/shard_map/ppermute | solution.py:400
  25.7 0.4 chip_prefix.1
  26.1 1.4 %collective-permute-start.8 = (bf16[528,128]{1,0:T(8,128)(2,1)S(1)}, bf16[528,128]{1,0:T(8,128)(2,1)S(1)}, u32[]{:S(2)}, u32[]{:S(2)}) collective-permute-start(bf16[528,128]{1,0:T(8,128)(2,1)S(1)} %get-tuple-element.35.refs_3_), channel_id=1, source_target_pairs={{0,1},{1,0},{2,3},{3,2},{4,5},{5,4},{6,7},{7,6},{8,9},{9,8},{10,11... | collective-permute-start | bytes 405512 | tf_op jit(solution)/shard_map/ppermute | solution.py:400
  27.5 1.1 %collective-permute-start.7 = (bf16[528,128]{1,0:T(8,128)(2,1)S(1)}, bf16[528,128]{1,0:T(8,128)(2,1)S(1)}, u32[]{:S(2)}, u32[]{:S(2)}) collective-permute-start(bf16[528,128]{1,0:T(8,128)(2,1)S(1)} %get-tuple-element.36), channel_id=1, source_target_pairs={{0,2},{1,3},{2,0},{3,1},{4,6},{5,7},{6,4},{7,5},{8,10},{9,11},{10,... | collective-permute-start | bytes 405512 | tf_op jit(solution)/shard_map/ppermute | solution.py:400
  28.9 1.3 %collective-permute-start.5 = (bf16[528,128]{1,0:T(8,128)(2,1)S(1)}, bf16[528,128]{1,0:T(8,128)(2,1)S(1)}, u32[]{:S(2)}, u32[]{:S(2)}) collective-permute-start(bf16[528,128]{1,0:T(8,128)(2,1)S(1)} %get-tuple-element.38), channel_id=1, source_target_pairs={{0,4},{1,5},{2,6},{3,7},{4,0},{5,1},{6,2},{7,3},{8,12},{9,13},{10,... | collective-permute-start | bytes 405512 | tf_op jit(solution)/shard_map/ppermute | solution.py:400
  30.2 1.3 %out_m0_o0.1.refs_12_ = bf16[128,4096]{1,0:T(8,128)(2,1)} custom-call(bf16[128,4096]{1,0:T(8,128)(2,1)S(1)} %copy-done, f32[8,8,128]{2,1,0:T(8,128)S(1)} %cum.1.cum_ref.refs_1_, f32[1,4096]{1,0:T(1,128)S(1)} %bitcast.19, bf16[528,128]{1,0:T(8,128)(2,1)S(1)} %get-tuple-element.35.refs_3_, f32[17,128,128]{2,1,0:T(8,128)S(1)} %intra_mine.1.refs_4_.refs_7_.refs_10_, ...), custom_call_target="tpu_custom_call" | custom-call | flops 1 | bytes 1 | tf_op jit(solution)/shard_map/out_m0_o0/pallas_call | solution.py:42
  31.5 3.7 %collective-permute-done.7.refs_9_ = bf16[528,128]{1,0:T(8,128)(2,1)S(1)} collective-permute-done((bf16[528,128]{1,0:T(8,128)(2,1)S(1)}, bf16[528,128]{1,0:T(8,128)(2,1)S(1)}, u32[]{:S(2)}, u32[]{:S(2)}) %collective-permute-start.7) | collective-permute-done | bytes 135200 | tf_op jit(solution)/shard_map/ppermute | solution.py:400
  35.3 1.2 %collective-permute-done.5.refs_3_ = bf16[528,128]{1,0:T(8,128)(2,1)S(1)} collective-permute-done((bf16[528,128]{1,0:T(8,128)(2,1)S(1)}, bf16[528,128]{1,0:T(8,128)(2,1)S(1)}, u32[]{:S(2)}, u32[]{:S(2)}) %collective-permute-start.5) | collective-permute-done | bytes 135200 | tf_op jit(solution)/shard_map/ppermute | solution.py:400
  36.5 1.2 %collective-permute-start.10 = (bf16[528,128]{1,0:T(8,128)(2,1)S(1)}, bf16[528,128]{1,0:T(8,128)(2,1)S(1)}, u32[]{:S(2)}, u32[]{:S(2)}) collective-permute-start(bf16[528,128]{1,0:T(8,128)(2,1)S(1)} %collective-permute-done.5.refs_3_), channel_id=1, source_target_pairs={{0,1},{1,0},{2,3},{3,2},{4,5},{5,4},{6,7},{7,6},{8,9},{9,8},{10,11... | collective-permute-start | bytes 405512 | tf_op jit(solution)/shard_map/ppermute | solution.py:400
  37.7 0.5 %collective-permute-start.12 = (bf16[528,128]{1,0:T(8,128)(2,1)S(1)}, bf16[528,128]{1,0:T(8,128)(2,1)S(1)}, u32[]{:S(2)}, u32[]{:S(2)}) collective-permute-start(bf16[528,128]{1,0:T(8,128)(2,1)S(1)} %collective-permute-done.7.refs_9_), channel_id=1, source_target_pairs={{0,1},{1,0},{2,3},{3,2},{4,5},{5,4},{6,7},{7,6},{8,9},{9,8},{10,11... | collective-permute-start | bytes 405512 | tf_op jit(solution)/shard_map/ppermute | solution.py:400
  38.2 1.6 %out_m2_m3_m1.1.refs_12_ = bf16[128,4096]{1,0:T(8,128)(2,1)} custom-call(bf16[128,4096]{1,0:T(8,128)(2,1)S(1)} %copy-done, f32[8,8,128]{2,1,0:T(8,128)S(1)} %cum.1.cum_ref.refs_1_, f32[1,4096]{1,0:T(1,128)S(1)} %bitcast.20, bf16[528,128]{1,0:T(8,128)(2,1)S(1)} %collective-permute-done.5.refs_3_, ...), custom_call_target="tpu_custom_call", output_to_operand_aliasing={{}: (12, {})} | custom-call | flops 1 | bytes 1 | tf_op jit(solution)/shard_map/out_m2_m3_m1/pallas_call | solution.py:42
  39.8 1.6 %out_o2_o3_o1.1 = bf16[128,4096]{1,0:T(8,128)(2,1)} custom-call(bf16[128,4096]{1,0:T(8,128)(2,1)S(1)} %copy-done, f32[8,8,128]{2,1,0:T(8,128)S(1)} %cum.1.cum_ref.refs_1_, f32[1,4096]{1,0:T(1,128)S(1)} %bitcast.21, bf16[528,128]{1,0:T(8,128)(2,1)S(1)} %collective-permute-done.10.refs_3_, ...), custom_call_target="tpu_custom_call", output_to_operand_aliasing={{}: (12, {})} | custom-call | flops 1 | bytes 1 | tf_op jit(solution)/shard_map/out_o2_o3_o1/pallas_call | solution.py:42
  (27 shorter events, 0.9 us)
Async XLA Ops:
  2.5 2.8 %collective-permute-start = (bf16[4,560,128]{2,1,0:T(8,128)(2,1)S(1)}, bf16[4,560,128]{2,1,0:T(8,128)(2,1)S(1)}, u32[]{:S(2)}, u32[]{:S(2)}) collective-permute-start(bf16[4,560,128]{2,1,0:T(8,128)(2,1)S(1)} %states_other.1), channel_id=1, source_target_pairs={{0,1},{1,0},{2,3},{3,2},{4,5},{5,4},{6,7},{7,6},{8,9},{9,8},{10,11... | collective-permute-start | bytes 1720328 | tf_op jit(solution)/shard_map/ppermute | solution.py:400
  2.6 7.9 %copy-start.2 = (bf16[128,4096]{1,0:T(8,128)(2,1)S(1)}, bf16[128,4096]{1,0:T(8,128)(2,1)}, u32[]{:S(2)}) copy-start(bf16[128,4096]{1,0:T(8,128)(2,1)} %v_ref.3) | copy-start | bytes 3145732
  5.3 5.1 %copy-start.5 = (f32[128,32]{0,1:T(8,128)S(1)}, f32[128,32]{0,1:T(8,128)}, u32[]{:S(2)}) copy-start(f32[128,32]{0,1:T(8,128)} %param.9) | copy-start | bytes 49156
  5.3 5.3 %copy-start = (bf16[128,4096]{1,0:T(8,128)(2,1)S(1)}, bf16[128,4096]{1,0:T(8,128)(2,1)}, u32[]{:S(2)}) copy-start(bf16[128,4096]{1,0:T(8,128)(2,1)} %refs_0_.5) | copy-start | bytes 3145732
  5.3 5.3 %copy-start.1 = (bf16[128,4096]{1,0:T(8,128)(2,1)S(1)}, bf16[128,4096]{1,0:T(8,128)(2,1)}, u32[]{:S(2)}) copy-start(bf16[128,4096]{1,0:T(8,128)(2,1)} %k_ref.3) | copy-start | bytes 3145732
  5.3 5.3 %copy-start.3 = (f32[4,4096]{1,0:T(4,128)S(1)}, f32[4,4096]{1,0:T(4,128)}, u32[]{:S(2)}) copy-start(f32[4,4096]{1,0:T(4,128)} %w_ref.3) | copy-start | bytes 196612
  5.7 9.7 %collective-permute-start.3 = (bf16[560,128]{1,0:T(8,128)(2,1)S(1)}, bf16[560,128]{1,0:T(8,128)(2,1)S(1)}, u32[]{:S(2)}, u32[]{:S(2)}) collective-permute-start(bf16[560,128]{1,0:T(8,128)(2,1)S(1)} %get-tuple-element.31), channel_id=1, source_target_pairs={{0,2},{1,3},{2,0},{3,1},{4,6},{5,7},{6,4},{7,5},{8,10},{9,11},{10,... | collective-permute-start | bytes 430088 | tf_op jit(solution)/shard_map/ppermute | solution.py:400
  8.5 6.9 %collective-permute-start.2 = (bf16[560,128]{1,0:T(8,128)(2,1)S(1)}, bf16[560,128]{1,0:T(8,128)(2,1)S(1)}, u32[]{:S(2)}, u32[]{:S(2)}) collective-permute-start(bf16[560,128]{1,0:T(8,128)(2,1)S(1)} %get-tuple-element.32), channel_id=1, source_target_pairs={{0,6},{1,7},{2,4},{3,5},{4,2},{5,3},{6,0},{7,1},{8,14},{9,15},{10,... | collective-permute-start | bytes 430088 | tf_op jit(solution)/shard_map/ppermute | solution.py:400
  9.7 7.1 %collective-permute-start.1 = (bf16[560,128]{1,0:T(8,128)(2,1)S(1)}, bf16[560,128]{1,0:T(8,128)(2,1)S(1)}, u32[]{:S(2)}, u32[]{:S(2)}) collective-permute-start(bf16[560,128]{1,0:T(8,128)(2,1)S(1)} %get-tuple-element.33), channel_id=1, source_target_pairs={{0,4},{1,5},{2,6},{3,7},{4,0},{5,1},{6,2},{7,3},{8,12},{9,13},{10,... | collective-permute-start | bytes 430088 | tf_op jit(solution)/shard_map/ppermute | solution.py:400
  9.8 20.4 %collective-permute-start.9 = (bf16[4,560,128]{2,1,0:T(8,128)(2,1)S(1)}, bf16[4,560,128]{2,1,0:T(8,128)(2,1)S(1)}, u32[]{:S(2)}, u32[]{:S(2)}) collective-permute-start(bf16[4,560,128]{2,1,0:T(8,128)(2,1)S(1)} %states_mine.1.own_ref), channel_id=1, source_target_pairs={{0,1},{1,0},{2,3},{3,2},{4,5},{5,4},{6,7},{7,6},{8,9},{9,8},{10,11... | collective-permute-start | bytes 1720328 | tf_op jit(solution)/shard_map/ppermute | solution.py:400
  17.2 8.5 %collective-permute-start.4 = (bf16[528,128]{1,0:T(8,128)(2,1)S(1)}, bf16[528,128]{1,0:T(8,128)(2,1)S(1)}, u32[]{:S(2)}, u32[]{:S(2)}) collective-permute-start(bf16[528,128]{1,0:T(8,128)(2,1)S(1)} %span_state.1), channel_id=1, source_target_pairs={{0,8},{1,9},{2,10},{3,11},{4,12},{5,13},{6,14},{7,15},{8,0},{9,1},... | collective-permute-start | bytes 405512 | tf_op jit(solution)/shard_map/ppermute | solution.py:400
  20.5 9.7 %copy-start.4 = (f32[4096]{0:T(1024)S(1)}, f32[4096]{0:T(1024)}, u32[]{:S(2)}) copy-start(f32[4096]{0:T(1024)} %param.11) | copy-start | bytes 49156
  26.1 4.1 %collective-permute-start.8 = (bf16[528,128]{1,0:T(8,128)(2,1)S(1)}, bf16[528,128]{1,0:T(8,128)(2,1)S(1)}, u32[]{:S(2)}, u32[]{:S(2)}) collective-permute-start(bf16[528,128]{1,0:T(8,128)(2,1)S(1)} %get-tuple-element.35.refs_3_), channel_id=1, source_target_pairs={{0,1},{1,0},{2,3},{3,2},{4,5},{5,4},{6,7},{7,6},{8,9},{9,8},{10,11... | collective-permute-start | bytes 405512 | tf_op jit(solution)/shard_map/ppermute | solution.py:400
  27.5 7.7 %collective-permute-start.7 = (bf16[528,128]{1,0:T(8,128)(2,1)S(1)}, bf16[528,128]{1,0:T(8,128)(2,1)S(1)}, u32[]{:S(2)}, u32[]{:S(2)}) collective-permute-start(bf16[528,128]{1,0:T(8,128)(2,1)S(1)} %get-tuple-element.36), channel_id=1, source_target_pairs={{0,2},{1,3},{2,0},{3,1},{4,6},{5,7},{6,4},{7,5},{8,10},{9,11},{10,... | collective-permute-start | bytes 405512 | tf_op jit(solution)/shard_map/ppermute | solution.py:400
  28.6 6.7 %collective-permute-start.6 = (bf16[528,128]{1,0:T(8,128)(2,1)S(1)}, bf16[528,128]{1,0:T(8,128)(2,1)S(1)}, u32[]{:S(2)}, u32[]{:S(2)}) collective-permute-start(bf16[528,128]{1,0:T(8,128)(2,1)S(1)} %get-tuple-element.37), channel_id=1, source_target_pairs={{0,6},{1,7},{2,4},{3,5},{4,2},{5,3},{6,0},{7,1},{8,14},{9,15},{10,... | collective-permute-start | bytes 405512 | tf_op jit(solution)/shard_map/ppermute | solution.py:400
  28.9 7.6 %collective-permute-start.5 = (bf16[528,128]{1,0:T(8,128)(2,1)S(1)}, bf16[528,128]{1,0:T(8,128)(2,1)S(1)}, u32[]{:S(2)}, u32[]{:S(2)}) collective-permute-start(bf16[528,128]{1,0:T(8,128)(2,1)S(1)} %get-tuple-element.38), channel_id=1, source_target_pairs={{0,4},{1,5},{2,6},{3,7},{4,0},{5,1},{6,2},{7,3},{8,12},{9,13},{10,... | collective-permute-start | bytes 405512 | tf_op jit(solution)/shard_map/ppermute | solution.py:400
  36.5 3.3 %collective-permute-start.10 = (bf16[528,128]{1,0:T(8,128)(2,1)S(1)}, bf16[528,128]{1,0:T(8,128)(2,1)S(1)}, u32[]{:S(2)}, u32[]{:S(2)}) collective-permute-start(bf16[528,128]{1,0:T(8,128)(2,1)S(1)} %collective-permute-done.5.refs_3_), channel_id=1, source_target_pairs={{0,1},{1,0},{2,3},{3,2},{4,5},{5,4},{6,7},{7,6},{8,9},{9,8},{10,11... | collective-permute-start | bytes 405512 | tf_op jit(solution)/shard_map/ppermute | solution.py:400
  37.6 2.1 %collective-permute-start.11 = (bf16[528,128]{1,0:T(8,128)(2,1)S(1)}, bf16[528,128]{1,0:T(8,128)(2,1)S(1)}, u32[]{:S(2)}, u32[]{:S(2)}) collective-permute-start(bf16[528,128]{1,0:T(8,128)(2,1)S(1)} %collective-permute-done.6.refs_6_), channel_id=1, source_target_pairs={{0,1},{1,0},{2,3},{3,2},{4,5},{5,4},{6,7},{7,6},{8,9},{9,8},{10,11... | collective-permute-start | bytes 405512 | tf_op jit(solution)/shard_map/ppermute | solution.py:400
  37.7 2.1 %collective-permute-start.12 = (bf16[528,128]{1,0:T(8,128)(2,1)S(1)}, bf16[528,128]{1,0:T(8,128)(2,1)S(1)}, u32[]{:S(2)}, u32[]{:S(2)}) collective-permute-start(bf16[528,128]{1,0:T(8,128)(2,1)S(1)} %collective-permute-done.7.refs_9_), channel_id=1, source_target_pairs={{0,1},{1,0},{2,3},{3,2},{4,5},{5,4},{6,7},{7,6},{8,9},{9,8},{10,11... | collective-permute-start | bytes 405512 | tf_op jit(solution)/shard_map/ppermute | solution.py:400

commit v9 on v8

--- a/solution.py
+++ b/solution.py
@@ -117,12 +117,11 @@
     return total.astype(BF16)
 
 
-def state_kernel(
+def fetched_state_kernel(
     mine, heads, size, k_hbm, v_hbm, w_hbm, decay_hbm, out_ref,
     k_buf, v_buf, w_buf, decay_buf, cum_ref, ext, held, sems,
 ):
-    rows, wide = k_buf.shape[1:]
-    taps = w_buf.shape[1]
+    wide = heads * size
     copies = [pltpu.make_async_copy(decay_hbm, decay_buf, sems.at[3 * CHIPS])]
     copies[0].start()
     for g in range(CHIPS):
@@ -133,28 +132,48 @@
             )
             copies[-1].start()
     copies[0].wait()
-    cum_kernel(heads, decay_buf, cum_ref)
+    groups = [(k_buf.at[g], v_buf.at[g], w_buf.at[g]) for g in range(CHIPS)]
+    waits = [copies[1 + 3 * g : 4 + 3 * g] for g in range(CHIPS)]
+    states_of(mine, heads, size, groups, waits, decay_buf, out_ref, cum_ref, ext, held)
+
+
+def state_kernel(
+    mine, heads, size, k_ref, v_ref, w_ref, decay_ref, out_ref, cum_ref, ext, held
+):
+    groups = []
+    for g in range(CHIPS):
+        cols = columns(head_group(mine, g) * heads * size, 0, heads * size)
+        groups.append((k_ref.at[:, cols], v_ref.at[:, cols], w_ref.at[:, cols]))
+    waits = [[]] * CHIPS
+    states_of(mine, heads, size, groups, waits, decay_ref, out_ref, cum_ref, ext, held)
+
+
+def states_of(mine, heads, size, groups, waits, decay_ref, out_ref, cum_ref, ext, held):
+    rows = groups[0][0].shape[0]
+    taps = groups[0][2].shape[0]
+    cum_kernel(heads, decay_ref, cum_ref)
     none = jnp.zeros((HALO, size), F32)
     for g in range(CHIPS):
-        for copy in copies[1 + 3 * g : 4 + 3 * g]:
+        k_ref, v_ref, w_ref = groups[g]
+        for copy in waits[g]:
             copy.wait()
         cum = cum_ref[head_group(mine, g)]
         ending = jnp.exp(cum[heads : 2 * heads] - cum[0:heads]).T
         edges, values = [], []
         for j in range(heads):
             cols = slice(j * size, (j + 1) * size)
-            key_conv = conv_keys(k_buf.at[g], none, w_buf.at[g], ext.at[j], cols)
+            key_conv = conv_keys(k_ref, none, w_ref, ext.at[j], cols)
             held[g * heads + j] = (key_conv.astype(F32) * ending[:, j : j + 1]).astype(BF16)
-            last = k_buf[g, rows - HALO : rows, cols].astype(F32)
+            last = k_ref[rows - HALO : rows, cols].astype(F32)
             head_edges = []
             for t in range(taps - 1):
                 terms = [
-                    w_buf[g, i : i + 1, cols] * last[HALO + t - i : HALO + t - i + 1]
+                    w_ref[i : i + 1, cols] * last[HALO + t - i : HALO + t - i + 1]
                     for i in range(t + 1, taps)
                 ]
                 head_edges.append(sum(terms[1:], terms[0]))
             edges.append(head_edges)
-            values.append(v_buf[g, 0:HALO, cols].astype(F32) * ending[0:HALO, j : j + 1])
+            values.append(v_ref[0:HALO, cols].astype(F32) * ending[0:HALO, j : j + 1])
         put_decay(out_ref.at[g], jnp.exp(cum[heads : 2 * heads]), heads, size)
         out_ref[g, side(0, heads, size), :] = padded(
             [edges[j][t] for t in range(taps - 1) for j in range(heads)]
@@ -166,7 +185,7 @@
         for j in range(heads):
             cols = slice(j * size, (j + 1) * size)
             state = lax.dot_general(
-                v_buf[g, :, cols], held[g * heads + j], (((0,), (0,)), ((), ())),
+                groups[g][1][:, cols], held[g * heads + j], (((0,), (0,)), ((), ())),
                 preferred_element_type=F32,
             )
             out_ref[g, cols, :] = state.astype(BF16)
@@ -406,23 +425,27 @@
     ext = pltpu.VMEM((heads, rows + HALO, size), F32)
     held = pltpu.VMEM((half, rows, size), BF16)
 
+    cum_shape = pltpu.VMEM((SPAN, 2 * heads, rows), F32)
+
     def states(mine):
+        scratch = [cum_shape, ext, held]
+        if not mine:
+            buf = pltpu.VMEM((CHIPS, rows, heads * size), BF16)
+            scratch = [
+                buf,
+                buf,
+                pltpu.VMEM((CHIPS, taps, heads * size), F32),
+                pltpu.VMEM((head_count, rows), F32),
+                *scratch,
+                pltpu.SemaphoreType.DMA((3 * CHIPS + 1,)),
+            ]
         return call(
-            functools.partial(state_kernel, mine, heads, size),
+            functools.partial(state_kernel if mine else fetched_state_kernel, mine, heads, size),
             "states_mine" if mine else "states_other",
             pltpu.VMEM((CHIPS, packet, size), BF16),
             key_input, value_input, conv_weight, log_decay.T,
-            in_specs=[HBM] * 4,
-            scratch=[
-                pltpu.VMEM((CHIPS, rows, heads * size), BF16),
-                pltpu.VMEM((CHIPS, rows, heads * size), BF16),
-                pltpu.VMEM((CHIPS, taps, heads * size), F32),
-                pltpu.VMEM((head_count, rows), F32),
-                pltpu.VMEM((SPAN, 2 * heads, rows), F32),
-                ext,
-                held,
-                pltpu.SemaphoreType.DMA((3 * CHIPS + 1,)),
-            ],
+            in_specs=[VMEM if mine else HBM] * 4,
+            scratch=scratch,
         )
 
     def intra_part(mine, q):
@@ -454,7 +477,7 @@
     cum = call(
         functools.partial(cum_kernel, heads),
         "cum",
-        pltpu.VMEM((SPAN, 2 * heads, rows), F32),
+        cum_shape,
         decay_after.T,
     )
     intra_mine = intra_part(True, q_after)
@@ -525,11 +548,15 @@
         )
 
     result = output([(True, 0), (False, 0)], None)
-    *late, result = lax.optimization_barrier((*[own[g] for g in EXCHANGE], result))
-    own.update(zip(EXCHANGE, late))
-    other.update({g: swap(own[g], 1) for g in EXCHANGE})
-    result = output([(True, g) for g in EXCHANGE], result)
-    return output([(False, g) for g in EXCHANGE], result)
+    *early, final = EXCHANGE[::-1]
+    *late, result = lax.optimization_barrier((*[own[g] for g in early], result))
+    own.update(zip(early, late))
+    other.update({g: swap(own[g], 1) for g in early})
+    result = output([(True, g) for g in early], result)
+    own[final], result = lax.optimization_barrier((own[final], result))
+    other[final] = swap(own[final], 1)
+    result = output([(True, final)] + [(False, g) for g in early], result)
+    return output([(False, final)], result)
 
 
 def solution(mesh):

time: 41.6 us -> 41 us (0.986)
    ppermute x13, waiting for transfers between devices: 15.2 us -> 14.8 us  [swap(): return lax.ppermute(x, 'ctx', [(i, i ^ mask) for i in range(n)])]
    pallas_call x11 -> x12, Pallas kernels: 13.2 us -> 13 us  [call(): pl.pallas_call(kernel, out_shape=out_shape, in_specs=in_specs, out_specs=...]
  transfers between devices with their start and end apart: 13 -> 13, of which waited for: 5 -> 6; matrix products, arithmetic and copies ran while one was open for 0% -> 0% of each run, Pallas kernels for 21% -> 21%
where the time goes in v9:
time: 41 us; the launch traced here: 40.9 us
  waiting for transfers between devices  14.8 us (36%)
  Pallas kernels  13 us (32%)
  starting transfers between devices  12.9 us (31%)
    ppermute x13, waiting for transfers between devices, swap(): return lax.ppermute(x, 'ctx', [(i, i ^ mask) for i in range(n)])  14.8 us
    pallas_call x12, Pallas kernels, call(): pl.pallas_call(kernel, out_shape=out_shape, in_specs=in_specs, out_specs=...  13 us
    ppermute x13, starting transfers between devices, swap(): return lax.ppermute(x, 'ctx', [(i, i ^ mask) for i in range(n)])  12.9 us
  transfers between devices with their start and end apart: 13, of which 6 were waited for; matrix products, arithmetic and copies ran while one was open for 0% of the time, Pallas kernels for 21%

profile of v9, /device:TPU:1, one launch (start us, length us, event | category | flops | bytes accessed | tf_op | source)
XLA Modules:
  0.0 40.9 jit_solution(1435158329039699003)
XLA Ops:
  0.0 2.7 %states_other.1 = bf16[4,560,128]{2,1,0:T(8,128)(2,1)S(1)} custom-call(bf16[128,4096]{1,0:T(8,128)(2,1)} %k_ref.5, bf16[128,4096]{1,0:T(8,128)(2,1)} %v_ref.5, f32[4,4096]{1,0:T(4,128)} %w_ref.5, f32[32,128]{1,0:T(8,128)} %bitcast.23), custom_call_target="tpu_custom_call" | custom-call | tf_op jit(solution)/shard_map/states_other/pallas_call | solution.py:42
  2.8 1.2 %states_mine.1.own_ref = bf16[4,560,128]{2,1,0:T(8,128)(2,1)S(1)} custom-call(bf16[128,4096]{1,0:T(8,128)(2,1)S(1)} %copy-done.1, bf16[128,4096]{1,0:T(8,128)(2,1)S(1)} %copy-done.2, f32[4,4096]{1,0:T(4,128)S(1)} %copy-done.3, f32[32,128]{1,0:T(8,128)S(1)} %bitcast.24), custom_call_target="tpu_custom_call" | custom-call | tf_op jit(solution)/shard_map/states_mine/pallas_call | solution.py:42
  4.0 0.7 %collective-permute-done.got_ref.refs_5_.refs_8_ = bf16[4,560,128]{2,1,0:T(8,128)(2,1)S(1)} collective-permute-done((bf16[4,560,128]{2,1,0:T(8,128)(2,1)S(1)}, bf16[4,560,128]{2,1,0:T(8,128)(2,1)S(1)}, u32[]{:S(2)}, u32[]{:S(2)}) %collective-permute-start) | collective-permute-done | bytes 573472 | tf_op jit(solution)/shard_map/ppermute | solution.py:419
  4.7 0.4 chip_states.1
  5.2 2.5 %collective-permute-start.1 = (bf16[560,128]{1,0:T(8,128)(2,1)S(1)}, bf16[560,128]{1,0:T(8,128)(2,1)S(1)}, u32[]{:S(2)}, u32[]{:S(2)}) collective-permute-start(bf16[560,128]{1,0:T(8,128)(2,1)S(1)} %get-tuple-element.35), channel_id=1, source_target_pairs={{0,4},{1,5},{2,6},{3,7},{4,0},{5,1},{6,2},{7,3},{8,12},{9,13},{10,... | collective-permute-start | bytes 430088 | tf_op jit(solution)/shard_map/ppermute | solution.py:419
  7.6 1.1 %collective-permute-start.2 = (bf16[560,128]{1,0:T(8,128)(2,1)S(1)}, bf16[560,128]{1,0:T(8,128)(2,1)S(1)}, u32[]{:S(2)}, u32[]{:S(2)}) collective-permute-start(bf16[560,128]{1,0:T(8,128)(2,1)S(1)} %get-tuple-element.34), channel_id=1, source_target_pairs={{0,6},{1,7},{2,4},{3,5},{4,2},{5,3},{6,0},{7,1},{8,14},{9,15},{10,... | collective-permute-start | bytes 430088 | tf_op jit(solution)/shard_map/ppermute | solution.py:419
  8.9 0.9 %collective-permute-start.9 = (bf16[4,560,128]{2,1,0:T(8,128)(2,1)S(1)}, bf16[4,560,128]{2,1,0:T(8,128)(2,1)S(1)}, u32[]{:S(2)}, u32[]{:S(2)}) collective-permute-start(bf16[4,560,128]{2,1,0:T(8,128)(2,1)S(1)} %states_mine.1.own_ref), channel_id=1, source_target_pairs={{0,1},{1,0},{2,3},{3,2},{4,5},{5,4},{6,7},{7,6},{8,9},{9,8},{10,11... | collective-permute-start | bytes 1720328 | tf_op jit(solution)/shard_map/ppermute | solution.py:419
  10.0 1.2 %intra_mine.1.refs_4_.refs_7_ = f32[17,128,128]{2,1,0:T(8,128)S(1)} custom-call(bf16[128,4096]{1,0:T(8,128)(2,1)S(1)} %copy-done, bf16[128,4096]{1,0:T(8,128)(2,1)S(1)} %copy-done.1, bf16[128,4096]{1,0:T(8,128)(2,1)S(1)} %copy-done.2, f32[4,4096]{1,0:T(4,128)S(1)} %copy-done.3, f32[8,8,128]{2,1,0:T(8,128)S(1)} %cum.1.cum_ref.refs_1_), custom_call_target="tpu_custom_call" | custom-call | tf_op jit(solution)/shard_map/intra_mine/pallas_call | solution.py:42
  11.5 3.9 %collective-permute-done.2.refs_3_ = bf16[560,128]{1,0:T(8,128)(2,1)S(1)} collective-permute-done((bf16[560,128]{1,0:T(8,128)(2,1)S(1)}, bf16[560,128]{1,0:T(8,128)(2,1)S(1)}, u32[]{:S(2)}, u32[]{:S(2)}) %collective-permute-start.2) | collective-permute-done | bytes 143392 | tf_op jit(solution)/shard_map/ppermute | solution.py:419
  15.4 1.1 %collective-permute-done.3.refs_1_ = bf16[560,128]{1,0:T(8,128)(2,1)S(1)} collective-permute-done((bf16[560,128]{1,0:T(8,128)(2,1)S(1)}, bf16[560,128]{1,0:T(8,128)(2,1)S(1)}, u32[]{:S(2)}, u32[]{:S(2)}) %collective-permute-start.3) | collective-permute-done | bytes 143392 | tf_op jit(solution)/shard_map/ppermute | solution.py:419
  16.8 2.4 %collective-permute-start.4 = (bf16[528,128]{1,0:T(8,128)(2,1)S(1)}, bf16[528,128]{1,0:T(8,128)(2,1)S(1)}, u32[]{:S(2)}, u32[]{:S(2)}) collective-permute-start(bf16[528,128]{1,0:T(8,128)(2,1)S(1)} %span_state.1), channel_id=1, source_target_pairs={{0,8},{1,9},{2,10},{3,11},{4,12},{5,13},{6,14},{7,15},{8,0},{9,1},... | collective-permute-start | bytes 405512 | tf_op jit(solution)/shard_map/ppermute | solution.py:419
  19.2 1.1 %intra_other.1.refs_7_.refs_10_.refs_4_ = f32[17,128,128]{2,1,0:T(8,128)S(1)} custom-call(bf16[128,4096]{1,0:T(8,128)(2,1)S(1)} %copy-done, bf16[128,4096]{1,0:T(8,128)(2,1)S(1)} %copy-done.1, bf16[128,4096]{1,0:T(8,128)(2,1)S(1)} %copy-done.2, f32[4,4096]{1,0:T(4,128)S(1)} %copy-done.3, f32[8,8,128]{2,1,0:T(8,128)S(1)} %cum.1.cum_ref.refs_1_), custom_call_target="tpu_custom_call" | custom-call | tf_op jit(solution)/shard_map/intra_other/pallas_call | solution.py:42
  20.3 4.8 %collective-permute-done.4.refs_4_ = bf16[528,128]{1,0:T(8,128)(2,1)S(1)} collective-permute-done((bf16[528,128]{1,0:T(8,128)(2,1)S(1)}, bf16[528,128]{1,0:T(8,128)(2,1)S(1)}, u32[]{:S(2)}, u32[]{:S(2)}) %collective-permute-start.4) | collective-permute-done | bytes 135200 | tf_op jit(solution)/shard_map/ppermute | solution.py:419
  25.1 0.4 chip_prefix.1
  25.5 1.6 %collective-permute-start.8 = (bf16[528,128]{1,0:T(8,128)(2,1)S(1)}, bf16[528,128]{1,0:T(8,128)(2,1)S(1)}, u32[]{:S(2)}, u32[]{:S(2)}) collective-permute-start(bf16[528,128]{1,0:T(8,128)(2,1)S(1)} %get-tuple-element.37.refs_3_), channel_id=1, source_target_pairs={{0,1},{1,0},{2,3},{3,2},{4,5},{5,4},{6,7},{7,6},{8,9},{9,8},{10,11... | collective-permute-start | bytes 405512 | tf_op jit(solution)/shard_map/ppermute | solution.py:419
  27.4 1.4 %collective-permute-start.7 = (bf16[528,128]{1,0:T(8,128)(2,1)S(1)}, bf16[528,128]{1,0:T(8,128)(2,1)S(1)}, u32[]{:S(2)}, u32[]{:S(2)}) collective-permute-start(bf16[528,128]{1,0:T(8,128)(2,1)S(1)} %get-tuple-element.38), channel_id=1, source_target_pairs={{0,6},{1,7},{2,4},{3,5},{4,2},{5,3},{6,0},{7,1},{8,14},{9,15},{10,... | collective-permute-start | bytes 405512 | tf_op jit(solution)/shard_map/ppermute | solution.py:419
  28.8 1.1 %collective-permute-start.5 = (bf16[528,128]{1,0:T(8,128)(2,1)S(1)}, bf16[528,128]{1,0:T(8,128)(2,1)S(1)}, u32[]{:S(2)}, u32[]{:S(2)}) collective-permute-start(bf16[528,128]{1,0:T(8,128)(2,1)S(1)} %get-tuple-element.40), channel_id=1, source_target_pairs={{0,4},{1,5},{2,6},{3,7},{4,0},{5,1},{6,2},{7,3},{8,12},{9,13},{10,... | collective-permute-start | bytes 405512 | tf_op jit(solution)/shard_map/ppermute | solution.py:419
  29.9 1.4 %out_m0_o0.1.refs_9_ = bf16[128,4096]{1,0:T(8,128)(2,1)} custom-call(bf16[128,4096]{1,0:T(8,128)(2,1)S(1)} %copy-done, f32[8,8,128]{2,1,0:T(8,128)S(1)} %cum.1.cum_ref.refs_1_, f32[1,4096]{1,0:T(1,128)S(1)} %bitcast.19, bf16[528,128]{1,0:T(8,128)(2,1)S(1)} %get-tuple-element.37.refs_3_, f32[17,128,128]{2,1,0:T(8,128)S(1)} %intra_mine.1.refs_4_.refs_7_, ...), custom_call_target="tpu_custom_call" | custom-call | flops 1 | bytes 1 | tf_op jit(solution)/shard_map/out_m0_o0/pallas_call | solution.py:42
  31.2 4.0 %collective-permute-done.6.refs_3_ = bf16[528,128]{1,0:T(8,128)(2,1)S(1)} collective-permute-done((bf16[528,128]{1,0:T(8,128)(2,1)S(1)}, bf16[528,128]{1,0:T(8,128)(2,1)S(1)}, u32[]{:S(2)}, u32[]{:S(2)}) %collective-permute-start.6) | collective-permute-done | bytes 135200 | tf_op jit(solution)/shard_map/ppermute | solution.py:419
  35.2 0.9 %collective-permute-start.11 = (bf16[528,128]{1,0:T(8,128)(2,1)S(1)}, bf16[528,128]{1,0:T(8,128)(2,1)S(1)}, u32[]{:S(2)}, u32[]{:S(2)}) collective-permute-start(bf16[528,128]{1,0:T(8,128)(2,1)S(1)} %collective-permute-done.6.refs_3_), channel_id=1, source_target_pairs={{0,1},{1,0},{2,3},{3,2},{4,5},{5,4},{6,7},{7,6},{8,9},{9,8},{10,11... | collective-permute-start | bytes 405512 | tf_op jit(solution)/shard_map/ppermute | solution.py:419
  36.1 1.4 %out_m1_m3.1.refs_12_ = bf16[128,4096]{1,0:T(8,128)(2,1)} custom-call(bf16[128,4096]{1,0:T(8,128)(2,1)S(1)} %copy-done, f32[8,8,128]{2,1,0:T(8,128)S(1)} %cum.1.cum_ref.refs_1_, f32[1,4096]{1,0:T(1,128)S(1)} %bitcast.20, bf16[528,128]{1,0:T(8,128)(2,1)S(1)} %collective-permute-done.6.refs_3_, ...), custom_call_target="tpu_custom_call", output_to_operand_aliasing={{}: (9, {})} | custom-call | flops 1 | bytes 1 | tf_op jit(solution)/shard_map/out_m1_m3/pallas_call | solution.py:42
  37.5 0.6 %collective-permute-start.10 = (bf16[528,128]{1,0:T(8,128)(2,1)S(1)}, bf16[528,128]{1,0:T(8,128)(2,1)S(1)}, u32[]{:S(2)}, u32[]{:S(2)}) collective-permute-start(bf16[528,128]{1,0:T(8,128)(2,1)S(1)} %collective-permute-done.5.refs_3_), channel_id=1, source_target_pairs={{0,1},{1,0},{2,3},{3,2},{4,5},{5,4},{6,7},{7,6},{8,9},{9,8},{10,11... | collective-permute-start | bytes 405512 | tf_op jit(solution)/shard_map/ppermute | solution.py:419
  38.0 1.6 %out_m2_o1_o3.1.refs_6_ = bf16[128,4096]{1,0:T(8,128)(2,1)} custom-call(bf16[128,4096]{1,0:T(8,128)(2,1)S(1)} %copy-done, f32[8,8,128]{2,1,0:T(8,128)S(1)} %cum.1.cum_ref.refs_1_, f32[1,4096]{1,0:T(1,128)S(1)} %bitcast.21, bf16[528,128]{1,0:T(8,128)(2,1)S(1)} %collective-permute-done.5.refs_3_, ...), custom_call_target="tpu_custom_call", output_to_operand_aliasing={{}: (12, {})} | custom-call | flops 1 | bytes 1 | tf_op jit(solution)/shard_map/out_m2_o1_o3/pallas_call | solution.py:42
  39.6 1.3 %out_o2.1 = bf16[128,4096]{1,0:T(8,128)(2,1)} custom-call(bf16[128,4096]{1,0:T(8,128)(2,1)S(1)} %copy-done, f32[8,8,128]{2,1,0:T(8,128)S(1)} %cum.1.cum_ref.refs_1_, f32[1,4096]{1,0:T(1,128)S(1)} %bitcast.22, bf16[528,128]{1,0:T(8,128)(2,1)S(1)} %collective-permute-done.10.refs_3_, ...), custom_call_target="tpu_custom_call", output_to_operand_aliasing={{}: (6, {})} | custom-call | flops 1 | bytes 1 | tf_op jit(solution)/shard_map/out_o2/pallas_call | solution.py:42
  (28 shorter events, 1.4 us)
Async XLA Ops:
  0.0 2.8 %copy-start.1 = (bf16[128,4096]{1,0:T(8,128)(2,1)S(1)}, bf16[128,4096]{1,0:T(8,128)(2,1)}, u32[]{:S(2)}) copy-start(bf16[128,4096]{1,0:T(8,128)(2,1)} %k_ref.5) | copy-start | bytes 3145732
  0.0 2.8 %copy-start.2 = (bf16[128,4096]{1,0:T(8,128)(2,1)S(1)}, bf16[128,4096]{1,0:T(8,128)(2,1)}, u32[]{:S(2)}) copy-start(bf16[128,4096]{1,0:T(8,128)(2,1)} %v_ref.5) | copy-start | bytes 3145732
  0.0 2.8 %copy-start.3 = (f32[4,4096]{1,0:T(4,128)S(1)}, f32[4,4096]{1,0:T(4,128)}, u32[]{:S(2)}) copy-start(f32[4,4096]{1,0:T(4,128)} %w_ref.5) | copy-start | bytes 196612
  0.0 2.8 %copy-start.5 = (f32[128,32]{0,1:T(8,128)S(1)}, f32[128,32]{0,1:T(8,128)}, u32[]{:S(2)}) copy-start(f32[128,32]{0,1:T(8,128)} %param.9) | copy-start | bytes 49156
  2.7 2.0 %collective-permute-start = (bf16[4,560,128]{2,1,0:T(8,128)(2,1)S(1)}, bf16[4,560,128]{2,1,0:T(8,128)(2,1)S(1)}, u32[]{:S(2)}, u32[]{:S(2)}) collective-permute-start(bf16[4,560,128]{2,1,0:T(8,128)(2,1)S(1)} %states_other.1), channel_id=1, source_target_pairs={{0,1},{1,0},{2,3},{3,2},{4,5},{5,4},{6,7},{7,6},{8,9},{9,8},{10,11... | collective-permute-start | bytes 1720328 | tf_op jit(solution)/shard_map/ppermute | solution.py:419
  4.0 6.0 %copy-start = (bf16[128,4096]{1,0:T(8,128)(2,1)S(1)}, bf16[128,4096]{1,0:T(8,128)(2,1)}, u32[]{:S(2)}) copy-start(bf16[128,4096]{1,0:T(8,128)(2,1)} %refs_0_.7) | copy-start | bytes 3145732
  5.2 6.3 %collective-permute-start.1 = (bf16[560,128]{1,0:T(8,128)(2,1)S(1)}, bf16[560,128]{1,0:T(8,128)(2,1)S(1)}, u32[]{:S(2)}, u32[]{:S(2)}) collective-permute-start(bf16[560,128]{1,0:T(8,128)(2,1)S(1)} %get-tuple-element.35), channel_id=1, source_target_pairs={{0,4},{1,5},{2,6},{3,7},{4,0},{5,1},{6,2},{7,3},{8,12},{9,13},{10,... | collective-permute-start | bytes 430088 | tf_op jit(solution)/shard_map/ppermute | solution.py:419
  7.6 7.8 %collective-permute-start.2 = (bf16[560,128]{1,0:T(8,128)(2,1)S(1)}, bf16[560,128]{1,0:T(8,128)(2,1)S(1)}, u32[]{:S(2)}, u32[]{:S(2)}) collective-permute-start(bf16[560,128]{1,0:T(8,128)(2,1)S(1)} %get-tuple-element.34), channel_id=1, source_target_pairs={{0,6},{1,7},{2,4},{3,5},{4,2},{5,3},{6,0},{7,1},{8,14},{9,15},{10,... | collective-permute-start | bytes 430088 | tf_op jit(solution)/shard_map/ppermute | solution.py:419
  8.8 7.7 %collective-permute-start.3 = (bf16[560,128]{1,0:T(8,128)(2,1)S(1)}, bf16[560,128]{1,0:T(8,128)(2,1)S(1)}, u32[]{:S(2)}, u32[]{:S(2)}) collective-permute-start(bf16[560,128]{1,0:T(8,128)(2,1)S(1)} %get-tuple-element.33), channel_id=1, source_target_pairs={{0,2},{1,3},{2,0},{3,1},{4,6},{5,7},{6,4},{7,5},{8,10},{9,11},{10,... | collective-permute-start | bytes 430088 | tf_op jit(solution)/shard_map/ppermute | solution.py:419
  8.9 20.9 %collective-permute-start.9 = (bf16[4,560,128]{2,1,0:T(8,128)(2,1)S(1)}, bf16[4,560,128]{2,1,0:T(8,128)(2,1)S(1)}, u32[]{:S(2)}, u32[]{:S(2)}) collective-permute-start(bf16[4,560,128]{2,1,0:T(8,128)(2,1)S(1)} %states_mine.1.own_ref), channel_id=1, source_target_pairs={{0,1},{1,0},{2,3},{3,2},{4,5},{5,4},{6,7},{7,6},{8,9},{9,8},{10,11... | collective-permute-start | bytes 1720328 | tf_op jit(solution)/shard_map/ppermute | solution.py:419
  16.8 8.3 %collective-permute-start.4 = (bf16[528,128]{1,0:T(8,128)(2,1)S(1)}, bf16[528,128]{1,0:T(8,128)(2,1)S(1)}, u32[]{:S(2)}, u32[]{:S(2)}) collective-permute-start(bf16[528,128]{1,0:T(8,128)(2,1)S(1)} %span_state.1), channel_id=1, source_target_pairs={{0,8},{1,9},{2,10},{3,11},{4,12},{5,13},{6,14},{7,15},{8,0},{9,1},... | collective-permute-start | bytes 405512 | tf_op jit(solution)/shard_map/ppermute | solution.py:419
  20.3 9.5 %copy-start.4 = (f32[4096]{0:T(1024)S(1)}, f32[4096]{0:T(1024)}, u32[]{:S(2)}) copy-start(f32[4096]{0:T(1024)} %param.11) | copy-start | bytes 49156
  25.5 4.3 %collective-permute-start.8 = (bf16[528,128]{1,0:T(8,128)(2,1)S(1)}, bf16[528,128]{1,0:T(8,128)(2,1)S(1)}, u32[]{:S(2)}, u32[]{:S(2)}) collective-permute-start(bf16[528,128]{1,0:T(8,128)(2,1)S(1)} %get-tuple-element.37.refs_3_), channel_id=1, source_target_pairs={{0,1},{1,0},{2,3},{3,2},{4,5},{5,4},{6,7},{7,6},{8,9},{9,8},{10,11... | collective-permute-start | bytes 405512 | tf_op jit(solution)/shard_map/ppermute | solution.py:419
  27.2 8.1 %collective-permute-start.6 = (bf16[528,128]{1,0:T(8,128)(2,1)S(1)}, bf16[528,128]{1,0:T(8,128)(2,1)S(1)}, u32[]{:S(2)}, u32[]{:S(2)}) collective-permute-start(bf16[528,128]{1,0:T(8,128)(2,1)S(1)} %get-tuple-element.39), channel_id=1, source_target_pairs={{0,2},{1,3},{2,0},{3,1},{4,6},{5,7},{6,4},{7,5},{8,10},{9,11},{10,... | collective-permute-start | bytes 405512 | tf_op jit(solution)/shard_map/ppermute | solution.py:419
  27.4 7.9 %collective-permute-start.7 = (bf16[528,128]{1,0:T(8,128)(2,1)S(1)}, bf16[528,128]{1,0:T(8,128)(2,1)S(1)}, u32[]{:S(2)}, u32[]{:S(2)}) collective-permute-start(bf16[528,128]{1,0:T(8,128)(2,1)S(1)} %get-tuple-element.38), channel_id=1, source_target_pairs={{0,6},{1,7},{2,4},{3,5},{4,2},{5,3},{6,0},{7,1},{8,14},{9,15},{10,... | collective-permute-start | bytes 405512 | tf_op jit(solution)/shard_map/ppermute | solution.py:419
  28.8 8.7 %collective-permute-start.5 = (bf16[528,128]{1,0:T(8,128)(2,1)S(1)}, bf16[528,128]{1,0:T(8,128)(2,1)S(1)}, u32[]{:S(2)}, u32[]{:S(2)}) collective-permute-start(bf16[528,128]{1,0:T(8,128)(2,1)S(1)} %get-tuple-element.40), channel_id=1, source_target_pairs={{0,4},{1,5},{2,6},{3,7},{4,0},{5,1},{6,2},{7,3},{8,12},{9,13},{10,... | collective-permute-start | bytes 405512 | tf_op jit(solution)/shard_map/ppermute | solution.py:419
  35.2 2.8 %collective-permute-start.11 = (bf16[528,128]{1,0:T(8,128)(2,1)S(1)}, bf16[528,128]{1,0:T(8,128)(2,1)S(1)}, u32[]{:S(2)}, u32[]{:S(2)}) collective-permute-start(bf16[528,128]{1,0:T(8,128)(2,1)S(1)} %collective-permute-done.6.refs_3_), channel_id=1, source_target_pairs={{0,1},{1,0},{2,3},{3,2},{4,5},{5,4},{6,7},{7,6},{8,9},{9,8},{10,11... | collective-permute-start | bytes 405512 | tf_op jit(solution)/shard_map/ppermute | solution.py:419
  36.1 2.0 %collective-permute-start.12 = (bf16[528,128]{1,0:T(8,128)(2,1)S(1)}, bf16[528,128]{1,0:T(8,128)(2,1)S(1)}, u32[]{:S(2)}, u32[]{:S(2)}) collective-permute-start(bf16[528,128]{1,0:T(8,128)(2,1)S(1)} %collective-permute-done.7.refs_6_), channel_id=1, source_target_pairs={{0,1},{1,0},{2,3},{3,2},{4,5},{5,4},{6,7},{7,6},{8,9},{9,8},{10,11... | collective-permute-start | bytes 405512 | tf_op jit(solution)/shard_map/ppermute | solution.py:419
  37.5 2.2 %collective-permute-start.10 = (bf16[528,128]{1,0:T(8,128)(2,1)S(1)}, bf16[528,128]{1,0:T(8,128)(2,1)S(1)}, u32[]{:S(2)}, u32[]{:S(2)}) collective-permute-start(bf16[528,128]{1,0:T(8,128)(2,1)S(1)} %collective-permute-done.5.refs_3_), channel_id=1, source_target_pairs={{0,1},{1,0},{2,3},{3,2},{4,5},{5,4},{6,7},{7,6},{8,9},{9,8},{10,11... | collective-permute-start | bytes 405512 | tf_op jit(solution)/shard_map/ppermute | solution.py:419

commit v10 on v9

--- a/solution.py
+++ b/solution.py
@@ -13,7 +13,9 @@
 SPAN = 2 * CHIPS
 HALO = 8
 EXCHANGE = (2, 3, 1)
-PARTS = 16
+CHUNKS = 2
+UNITS = CHUNKS * CHIPS
+PARTS = 8
 VMEM = pl.BlockSpec(memory_space=pltpu.VMEM)
 HBM = pl.BlockSpec(memory_space=pltpu.HBM)
 
@@ -23,9 +25,10 @@
     return me & 1, (me >> 1) & (CHIPS - 1)
 
 
-def head_group(mine, g):
+def head_group(mine, unit):
     core, chip = position()
-    return (core if mine else 1 - core) * CHIPS + (chip ^ g)
+    group = (core if mine else 1 - core) * CHIPS + (chip ^ (unit % CHIPS))
+    return group * CHUNKS + unit // CHIPS
 
 
 def columns(block, offset, size):
@@ -121,19 +124,23 @@
     mine, heads, size, k_hbm, v_hbm, w_hbm, decay_hbm, out_ref,
     k_buf, v_buf, w_buf, decay_buf, cum_ref, ext, held, sems,
 ):
-    wide = heads * size
+    wide = CHUNKS * heads * size
     copies = [pltpu.make_async_copy(decay_hbm, decay_buf, sems.at[3 * CHIPS])]
     copies[0].start()
     for g in range(CHIPS):
-        cols = columns(head_group(mine, g) * wide, 0, wide)
+        cols = columns(head_group(mine, g) * heads * size, 0, wide)
         for i, (source, buf) in enumerate(((k_hbm, k_buf), (w_hbm, w_buf), (v_hbm, v_buf))):
             copies.append(
                 pltpu.make_async_copy(source.at[:, cols], buf.at[g], sems.at[3 * g + i])
             )
             copies[-1].start()
     copies[0].wait()
-    groups = [(k_buf.at[g], v_buf.at[g], w_buf.at[g]) for g in range(CHIPS)]
-    waits = [copies[1 + 3 * g : 4 + 3 * g] for g in range(CHIPS)]
+    groups, waits = [], []
+    for u in range(UNITS):
+        g, part = u % CHIPS, u // CHIPS
+        cols = slice(part * heads * size, (part + 1) * heads * size)
+        groups.append(tuple(buf.at[g, :, cols] for buf in (k_buf, v_buf, w_buf)))
+        waits.append(copies[1 + 3 * g : 4 + 3 * g] if part == 0 else [])
     states_of(mine, heads, size, groups, waits, decay_buf, out_ref, cum_ref, ext, held)
 
 
@@ -141,10 +148,10 @@
     mine, heads, size, k_ref, v_ref, w_ref, decay_ref, out_ref, cum_ref, ext, held
 ):
     groups = []
-    for g in range(CHIPS):
-        cols = columns(head_group(mine, g) * heads * size, 0, heads * size)
+    for u in range(UNITS):
+        cols = columns(head_group(mine, u) * heads * size, 0, heads * size)
         groups.append((k_ref.at[:, cols], v_ref.at[:, cols], w_ref.at[:, cols]))
-    waits = [[]] * CHIPS
+    waits = [[]] * UNITS
     states_of(mine, heads, size, groups, waits, decay_ref, out_ref, cum_ref, ext, held)
 
 
@@ -153,7 +160,7 @@
     taps = groups[0][2].shape[0]
     cum_kernel(heads, decay_ref, cum_ref)
     none = jnp.zeros((HALO, size), F32)
-    for g in range(CHIPS):
+    for g in range(UNITS):
         k_ref, v_ref, w_ref = groups[g]
         for copy in waits[g]:
             copy.wait()
@@ -162,7 +169,7 @@
         edges, values = [], []
         for j in range(heads):
             cols = slice(j * size, (j + 1) * size)
-            key_conv = conv_keys(k_ref, none, w_ref, ext.at[j], cols)
+            key_conv = conv_keys(k_ref, none, w_ref, ext.at[g % 2 * heads + j], cols)
             held[g * heads + j] = (key_conv.astype(F32) * ending[:, j : j + 1]).astype(BF16)
             last = k_ref[rows - HALO : rows, cols].astype(F32)
             head_edges = []
@@ -181,7 +188,7 @@
         out_ref[g, side(2, heads, size), :] = padded(
             [values[j][t : t + 1] for t in range(taps - 1) for j in range(heads)]
         )
-    for g in range(CHIPS):
+    for g in range(UNITS):
         for j in range(heads):
             cols = slice(j * size, (j + 1) * size)
             state = lax.dot_general(
@@ -197,7 +204,7 @@
         jnp.int32, (rows, rows), 1
     )
     none = jnp.zeros((HALO, size), F32)
-    for g in range(CHIPS):
+    for g in range(UNITS):
         b = head_group(mine, g)
         cum = cum_ref[b][0:heads]
         cum_col = cum.T
@@ -205,7 +212,7 @@
         values = []
         for j in range(heads):
             cols = columns(b * heads * size, j * size, size)
-            key_conv = conv_keys(k_ref, none, w_ref, ext.at[j], cols)
+            key_conv = conv_keys(k_ref, none, w_ref, ext.at[g % 2 * heads + j], cols)
             scores = lax.dot_general(
                 q_ref[:, cols], key_conv, (((1,), (1,)), ((), ())), preferred_element_type=F32
             )
@@ -213,10 +220,10 @@
             weights = jnp.where(causal, scores * jnp.exp(jnp.where(causal, spread, 0.0)), 0.0)
             held[g * heads + j] = weights.astype(BF16)
             values.append(v_ref[0:HALO, cols].astype(F32) * growth[:, j : j + 1])
-        out_ref[CHIPS * heads, g * PARTS : (g + 1) * PARTS, :] = padded(
+        out_ref[UNITS * heads, g * PARTS : (g + 1) * PARTS, :] = padded(
             [values[j][t : t + 1] for t in range(3) for j in range(heads)]
         ).astype(F32)
-    for g in range(CHIPS):
+    for g in range(UNITS):
         b = head_group(mine, g)
         for j in range(heads):
             cols = columns(b * heads * size, j * size, size)
@@ -228,7 +235,7 @@
 def chip_kernel(heads, size, own_ref, got_ref, out_ref):
     core, _ = position()
     first = core == 0
-    for g in range(CHIPS):
+    for g in range(UNITS):
         own_decay = get_decay(own_ref.at[g], heads, size)
         got_decay = get_decay(got_ref.at[g], heads, size)
         own_by = jnp.where(first, got_decay, 1.0)
@@ -365,7 +372,7 @@
     for i, (mine, g) in enumerate(items):
         _, intra_ref, sib_ref = per_item[i]
         b = head_group(mine, g)
-        values = intra_ref[CHIPS * heads, g * PARTS : (g + 1) * PARTS, :]
+        values = intra_ref[UNITS * heads, g * PARTS : (g + 1) * PARTS, :]
         ahead_values = jnp.where(second, sib_ref[g, side(2, heads, size), :].astype(F32), values)
         values = jnp.concatenate([ahead_values, values], 0).astype(BF16)
         for j in range(heads):
@@ -409,9 +416,9 @@
     rows, width = queries.shape
     head_count = log_decay.shape[1]
     size = width // head_count
-    heads = head_count // SPAN
+    heads = head_count // (SPAN * CHUNKS)
     taps = conv_weight.shape[0]
-    half = CHIPS * heads
+    half = UNITS * heads
     packet = heads * size + 3 * PARTS
     n = lax.axis_size("ctx")
 
@@ -422,19 +429,19 @@
         return lax.ppermute(x, "ctx", [(i, i + by) for i in range(n - by)])
 
     gain = norm_gain.reshape(1, width)
-    ext = pltpu.VMEM((heads, rows + HALO, size), F32)
+    ext = pltpu.VMEM((2 * heads, rows + HALO, size), F32)
     held = pltpu.VMEM((half, rows, size), BF16)
 
-    cum_shape = pltpu.VMEM((SPAN, 2 * heads, rows), F32)
+    cum_shape = pltpu.VMEM((SPAN * CHUNKS, 2 * heads, rows), F32)
 
     def states(mine):
         scratch = [cum_shape, ext, held]
         if not mine:
-            buf = pltpu.VMEM((CHIPS, rows, heads * size), BF16)
+            buf = pltpu.VMEM((CHIPS, rows, CHUNKS * heads * size), BF16)
             scratch = [
                 buf,
                 buf,
-                pltpu.VMEM((CHIPS, taps, heads * size), F32),
+                pltpu.VMEM((CHIPS, taps, CHUNKS * heads * size), F32),
                 pltpu.VMEM((head_count, rows), F32),
                 *scratch,
                 pltpu.SemaphoreType.DMA((3 * CHIPS + 1,)),
@@ -442,7 +449,7 @@
         return call(
             functools.partial(state_kernel if mine else fetched_state_kernel, mine, heads, size),
             "states_mine" if mine else "states_other",
-            pltpu.VMEM((CHIPS, packet, size), BF16),
+            pltpu.VMEM((UNITS, packet, size), BF16),
             key_input, value_input, conv_weight, log_decay.T,
             in_specs=[VMEM if mine else HBM] * 4,
             scratch=scratch,
@@ -465,12 +472,42 @@
     chip_states = call(
         functools.partial(chip_kernel, heads, size),
         "chip_states",
-        pltpu.VMEM((CHIPS, packet, size), BF16),
+        pltpu.VMEM((UNITS, packet, size), BF16),
         mine, got,
     )
-    packets = {0: chip_states[0]}
-    for g in EXCHANGE:
-        packets[g] = swap(chip_states[g], 2 * g)
+    order = pltpu.VMEM((CHIPS, packet, size), BF16)
+
+    def joined(packets):
+        known = []
+        if n > 2 * SPAN:
+            edge = call(
+                functools.partial(last_edge_kernel, heads, size),
+                "last_edge",
+                pltpu.VMEM((PARTS, size), BF16),
+                *packets,
+                scratch=[order],
+            )
+            known = [shift(edge, SPAN)]
+        span = call(
+            functools.partial(span_kernel, heads, size),
+            "span_state",
+            pltpu.VMEM((heads * size + (2 if known else 1) * PARTS, size), BF16),
+            *packets, *known,
+            scratch=[order],
+        )
+        before = swap(span, SPAN) if n == 2 * SPAN else shift(span, SPAN)
+        reach = 1
+        while reach < n // SPAN - 1:
+            before = join_spans(shift(before, SPAN * reach), before, heads, size)
+            reach *= 2
+        return span, before, known
+
+    packets = []
+    for part in range(CHUNKS):
+        these = {0: chip_states[part * CHIPS]}
+        for g in EXCHANGE:
+            these[g] = swap(chip_states[part * CHIPS + g], 2 * g)
+        packets.append([these[g] for g in range(CHIPS)])
     q_after, decay_after, chip_states = lax.optimization_barrier(
         (queries, log_decay, chip_states)
     )
@@ -481,48 +518,31 @@
         decay_after.T,
     )
     intra_mine = intra_part(True, q_after)
-    *late, intra_mine = lax.optimization_barrier((*[packets[g] for g in EXCHANGE], intra_mine))
-    packets.update(zip(EXCHANGE, late))
-    packets = [packets[g] for g in range(CHIPS)]
-
-    order = pltpu.VMEM((CHIPS, packet, size), BF16)
-    known = []
-    if n > 2 * SPAN:
-        edge = call(
-            functools.partial(last_edge_kernel, heads, size),
-            "last_edge",
-            pltpu.VMEM((PARTS, size), BF16),
-            *packets,
+    last = packets[-1]
+    *late, intra_mine = lax.optimization_barrier((*[last[g] for g in EXCHANGE], intra_mine))
+    for g, x in zip(EXCHANGE, late):
+        last[g] = x
+
+    spans, befores, knowns = zip(*[joined(p) for p in packets])
+    q_after, _ = lax.optimization_barrier((queries, spans[-1]))
+    intra_other = intra_part(False, q_after)
+    before, intra_other = lax.optimization_barrier((befores[-1], intra_other))
+    befores = [*befores[:-1], before]
+
+    own, other = {}, {}
+    for part in range(CHUNKS):
+        chip_prefix = call(
+            functools.partial(spread_kernel, heads, size),
+            "chip_prefix",
+            pltpu.VMEM((CHIPS, heads * size + PARTS, size), BF16),
+            *packets[part], befores[part], *knowns[part],
             scratch=[order],
         )
-        known = [shift(edge, SPAN)]
-    span = call(
-        functools.partial(span_kernel, heads, size),
-        "span_state",
-        pltpu.VMEM((heads * size + (2 if known else 1) * PARTS, size), BF16),
-        *packets, *known,
-        scratch=[order],
-    )
-    before = swap(span, SPAN) if n == 2 * SPAN else shift(span, SPAN)
-    reach = 1
-    while reach < n // SPAN - 1:
-        before = join_spans(shift(before, SPAN * reach), before, heads, size)
-        reach *= 2
-    q_after, span = lax.optimization_barrier((queries, span))
-    intra_other = intra_part(False, q_after)
-    before, intra_other = lax.optimization_barrier((before, intra_other))
-
-    chip_prefix = call(
-        functools.partial(spread_kernel, heads, size),
-        "chip_prefix",
-        pltpu.VMEM((CHIPS, heads * size + PARTS, size), BF16),
-        *packets, before, *known,
-        scratch=[order],
-    )
-    own = {0: chip_prefix[0]}
-    for g in EXCHANGE:
-        own[g] = swap(chip_prefix[g], 2 * g)
-    other = {0: swap(own[0], 1)}
+        first = part * CHIPS
+        own[first] = chip_prefix[0]
+        for g in EXCHANGE:
+            own[first + g] = swap(chip_prefix[g], 2 * g)
+        other[first] = swap(own[first], 1)
 
     def output(items, result):
         args = [queries, cum, gain]
@@ -547,16 +567,17 @@
             ],
         )
 
-    result = output([(True, 0), (False, 0)], None)
-    *early, final = EXCHANGE[::-1]
-    *late, result = lax.optimization_barrier((*[own[g] for g in early], result))
-    own.update(zip(early, late))
-    other.update({g: swap(own[g], 1) for g in early})
-    result = output([(True, g) for g in early], result)
-    own[final], result = lax.optimization_barrier((own[final], result))
-    other[final] = swap(own[final], 1)
-    result = output([(True, final)] + [(False, g) for g in early], result)
-    return output([(False, final)], result)
+    result = None
+    for part in range(CHUNKS):
+        first = part * CHIPS
+        units = [first + g for g in EXCHANGE]
+        result = output([(True, first), (False, first)], result)
+        *late, result = lax.optimization_barrier((*[own[u] for u in units], result))
+        own.update(zip(units, late))
+        other.update({u: swap(own[u], 1) for u in units})
+        result = output([(True, u) for u in units], result)
+        result = output([(False, u) for u in units], result)
+    return result
 
 
 def solution(mesh):

time: 41 us -> 42.3 us (1.032)
  waiting for transfers between devices: 14.8 us -> 1.14 us
  starting transfers between devices: 12.9 us -> 24.7 us
  Pallas kernels: 13 us -> 15.9 us
    ppermute x13 -> x24, waiting for transfers between devices: 14.8 us -> 1.14 us  [swap(): return lax.ppermute(x, 'ctx', [(i, i ^ mask) for i in range(n)])]
    ppermute x13 -> x24, starting transfers between devices: 12.9 us -> 24.7 us  [swap(): return lax.ppermute(x, 'ctx', [(i, i ^ mask) for i in range(n)])]
    pallas_call x12 -> x16, Pallas kernels: 13 us -> 15.9 us  [call(): pl.pallas_call(kernel, out_shape=out_shape, in_specs=in_specs, out_specs=...]
  transfers between devices with their start and end apart: 13 -> 24, of which waited for: 6 -> 2; matrix products, arithmetic and copies ran while one was open for 0% -> 0% of each run, Pallas kernels for 21% -> 28%
where the time goes in v10:
time: 42.3 us; the launch traced here: 42.1 us
  starting transfers between devices  24.7 us (58%)
  Pallas kernels  15.9 us (38%)
  waiting for transfers between devices  1.14 us (3%)
    ppermute x24, starting transfers between devices, swap(): return lax.ppermute(x, 'ctx', [(i, i ^ mask) for i in range(n)])  24.7 us
    pallas_call x16, Pallas kernels, call(): pl.pallas_call(kernel, out_shape=out_shape, in_specs=in_specs, out_specs=...  15.9 us
    ppermute x24, waiting for transfers between devices, swap(): return lax.ppermute(x, 'ctx', [(i, i ^ mask) for i in range(n)])  1.14 us
  transfers between devices with their start and end apart: 24, of which 2 were waited for; matrix products, arithmetic and copies ran while one was open for 0% of the time, Pallas kernels for 28%

profile of v10, /device:TPU:1, one launch (start us, length us, event | category | flops | bytes accessed | tf_op | source)
XLA Modules:
  0.0 42.1 jit_solution(3245230553869928828)
XLA Ops:
  0.0 2.8 %states_other.1 = bf16[8,280,128]{2,1,0:T(8,128)(2,1)S(1)} custom-call(bf16[128,4096]{1,0:T(8,128)(2,1)} %k_ref.5, bf16[128,4096]{1,0:T(8,128)(2,1)} %v_ref.5, f32[4,4096]{1,0:T(4,128)} %w_ref.5, f32[32,128]{1,0:T(8,128)} %bitcast.41), custom_call_target="tpu_custom_call" | custom-call | tf_op jit(solution)/shard_map/states_other/pallas_call | solution.py:45
  3.0 1.5 %states_mine.1.own_ref = bf16[8,280,128]{2,1,0:T(8,128)(2,1)S(1)} custom-call(bf16[128,4096]{1,0:T(8,128)(2,1)S(1)} %copy-done.1, bf16[128,4096]{1,0:T(8,128)(2,1)S(1)} %copy-done.2, f32[4,4096]{1,0:T(4,128)S(1)} %copy-done.3, f32[32,128]{1,0:T(8,128)S(1)} %bitcast.42), custom_call_target="tpu_custom_call" | custom-call | tf_op jit(solution)/shard_map/states_mine/pallas_call | solution.py:45
  4.5 0.5 %collective-permute-start.9 = (bf16[8,280,128]{2,1,0:T(8,128)(2,1)S(1)}, bf16[8,280,128]{2,1,0:T(8,128)(2,1)S(1)}, u32[]{:S(2)}, u32[]{:S(2)}) collective-permute-start(bf16[8,280,128]{2,1,0:T(8,128)(2,1)S(1)} %states_mine.1.own_ref), channel_id=1, source_target_pairs={{0,1},{1,0},{2,3},{3,2},{4,5},{5,4},{6,7},{7,6},{8,9},{9,8},{10,11... | collective-permute-start | bytes 1720328 | tf_op jit(solution)/shard_map/ppermute | solution.py:426
  5.4 3.4 %collective-permute-start.12 = (bf16[280,128]{1,0:T(8,128)(2,1)S(1)}, bf16[280,128]{1,0:T(8,128)(2,1)S(1)}, u32[]{:S(2)}, u32[]{:S(2)}) collective-permute-start(bf16[280,128]{1,0:T(8,128)(2,1)S(1)} %get-tuple-element.39), channel_id=1, source_target_pairs={{0,6},{1,7},{2,4},{3,5},{4,2},{5,3},{6,0},{7,1},{8,14},{9,15},{10,... | collective-permute-start | bytes 215048 | tf_op jit(solution)/shard_map/ppermute | solution.py:426
  9.2 1.3 %collective-permute-start.3 = (bf16[280,128]{1,0:T(8,128)(2,1)S(1)}, bf16[280,128]{1,0:T(8,128)(2,1)S(1)}, u32[]{:S(2)}, u32[]{:S(2)}) collective-permute-start(bf16[280,128]{1,0:T(8,128)(2,1)S(1)} %get-tuple-element.43), channel_id=1, source_target_pairs={{0,2},{1,3},{2,0},{3,1},{4,6},{5,7},{6,4},{7,5},{8,10},{9,11},{10,... | collective-permute-start | bytes 215048 | tf_op jit(solution)/shard_map/ppermute | solution.py:426
  10.4 0.6 %collective-permute-done.12.refs_3_ = bf16[280,128]{1,0:T(8,128)(2,1)S(1)} collective-permute-done((bf16[280,128]{1,0:T(8,128)(2,1)S(1)}, bf16[280,128]{1,0:T(8,128)(2,1)S(1)}, u32[]{:S(2)}, u32[]{:S(2)}) %collective-permute-start.12) | collective-permute-done | bytes 71712 | tf_op jit(solution)/shard_map/ppermute | solution.py:426
  11.0 1.9 %collective-permute-start.2 = (bf16[280,128]{1,0:T(8,128)(2,1)S(1)}, bf16[280,128]{1,0:T(8,128)(2,1)S(1)}, u32[]{:S(2)}, u32[]{:S(2)}) collective-permute-start(bf16[280,128]{1,0:T(8,128)(2,1)S(1)} %get-tuple-element.44), channel_id=1, source_target_pairs={{0,6},{1,7},{2,4},{3,5},{4,2},{5,3},{6,0},{7,1},{8,14},{9,15},{10,... | collective-permute-start | bytes 215048 | tf_op jit(solution)/shard_map/ppermute | solution.py:426
  12.9 0.8 %collective-permute-start.1 = (bf16[280,128]{1,0:T(8,128)(2,1)S(1)}, bf16[280,128]{1,0:T(8,128)(2,1)S(1)}, u32[]{:S(2)}, u32[]{:S(2)}) collective-permute-start(bf16[280,128]{1,0:T(8,128)(2,1)S(1)} %get-tuple-element.45), channel_id=1, source_target_pairs={{0,4},{1,5},{2,6},{3,7},{4,0},{5,1},{6,2},{7,3},{8,12},{9,13},{10,... | collective-permute-start | bytes 215048 | tf_op jit(solution)/shard_map/ppermute | solution.py:426
  14.0 2.4 %collective-permute-start.13 = (bf16[264,128]{1,0:T(8,128)(2,1)S(1)}, bf16[264,128]{1,0:T(8,128)(2,1)S(1)}, u32[]{:S(2)}, u32[]{:S(2)}) collective-permute-start(bf16[264,128]{1,0:T(8,128)(2,1)S(1)} %span_state.3), channel_id=1, source_target_pairs={{0,8},{1,9},{2,10},{3,11},{4,12},{5,13},{6,14},{7,15},{8,0},{9,1},... | collective-permute-start | bytes 202760 | tf_op jit(solution)/shard_map/ppermute | solution.py:426
  16.6 1.2 %intra_mine.1.refs_4_.refs_7_.refs_10_ = f32[17,128,128]{2,1,0:T(8,128)S(1)} custom-call(bf16[128,4096]{1,0:T(8,128)(2,1)S(1)} %copy-done, bf16[128,4096]{1,0:T(8,128)(2,1)S(1)} %copy-done.1, bf16[128,4096]{1,0:T(8,128)(2,1)S(1)} %copy-done.2, f32[4,4096]{1,0:T(4,128)S(1)} %copy-done.3, f32[16,4,128]{2,1,0:T(4,128)S(1)} %cum.1.cum_ref.refs_1_), custom_call_target="tpu_custom_call" | custom-call | tf_op jit(solution)/shard_map/intra_mine/pallas_call | solution.py:45
  18.1 0.7 %collective-permute-start.4 = (bf16[264,128]{1,0:T(8,128)(2,1)S(1)}, bf16[264,128]{1,0:T(8,128)(2,1)S(1)}, u32[]{:S(2)}, u32[]{:S(2)}) collective-permute-start(bf16[264,128]{1,0:T(8,128)(2,1)S(1)} %span_state.2), channel_id=1, source_target_pairs={{0,8},{1,9},{2,10},{3,11},{4,12},{5,13},{6,14},{7,15},{8,0},{9,1},... | collective-permute-start | bytes 202760 | tf_op jit(solution)/shard_map/ppermute | solution.py:426
  19.1 4.0 %collective-permute-start.17 = (bf16[264,128]{1,0:T(8,128)(2,1)S(1)}, bf16[264,128]{1,0:T(8,128)(2,1)S(1)}, u32[]{:S(2)}, u32[]{:S(2)}) collective-permute-start(bf16[264,128]{1,0:T(8,128)(2,1)S(1)} %get-tuple-element.47.refs_3_), channel_id=1, source_target_pairs={{0,1},{1,0},{2,3},{3,2},{4,5},{5,4},{6,7},{7,6},{8,9},{9,8},{10,11... | collective-permute-start | bytes 202760 | tf_op jit(solution)/shard_map/ppermute | solution.py:426
  23.4 2.1 %collective-permute-start.15 = (bf16[264,128]{1,0:T(8,128)(2,1)S(1)}, bf16[264,128]{1,0:T(8,128)(2,1)S(1)}, u32[]{:S(2)}, u32[]{:S(2)}) collective-permute-start(bf16[264,128]{1,0:T(8,128)(2,1)S(1)} %get-tuple-element.49), channel_id=1, source_target_pairs={{0,6},{1,7},{2,4},{3,5},{4,2},{5,3},{6,0},{7,1},{8,14},{9,15},{10,... | collective-permute-start | bytes 202760 | tf_op jit(solution)/shard_map/ppermute | solution.py:426
  25.7 1.1 %intra_other.1.refs_7_.refs_4_.refs_10_ = f32[17,128,128]{2,1,0:T(8,128)S(1)} custom-call(bf16[128,4096]{1,0:T(8,128)(2,1)S(1)} %copy-done, bf16[128,4096]{1,0:T(8,128)(2,1)S(1)} %copy-done.1, bf16[128,4096]{1,0:T(8,128)(2,1)S(1)} %copy-done.2, f32[4,4096]{1,0:T(4,128)S(1)} %copy-done.3, f32[16,4,128]{2,1,0:T(4,128)S(1)} %cum.1.cum_ref.refs_1_), custom_call_target="tpu_custom_call" | custom-call | tf_op jit(solution)/shard_map/intra_other/pallas_call | solution.py:45
  27.2 1.2 %out_m0_o0.1.refs_12_ = bf16[128,4096]{1,0:T(8,128)(2,1)} custom-call(bf16[128,4096]{1,0:T(8,128)(2,1)S(1)} %copy-done, f32[16,4,128]{2,1,0:T(4,128)S(1)} %cum.1.cum_ref.refs_1_, f32[1,4096]{1,0:T(1,128)S(1)} %bitcast.35, bf16[264,128]{1,0:T(8,128)(2,1)S(1)} %get-tuple-element.47.refs_3_, f32[17,128,128]{2,1,0:T(8,128)S(1)} %intra_mine.1.refs_4_.refs_7_.refs_10_, ...), custom_call_target="tpu_custom_call" | custom-call | flops 1 | bytes 1 | tf_op jit(solution)/shard_map/out_m0_o0/pallas_call | solution.py:45
  28.9 1.5 %collective-permute-start.18 = (bf16[264,128]{1,0:T(8,128)(2,1)S(1)}, bf16[264,128]{1,0:T(8,128)(2,1)S(1)}, u32[]{:S(2)}, u32[]{:S(2)}) collective-permute-start(bf16[264,128]{1,0:T(8,128)(2,1)S(1)} %collective-permute-done.14.refs_3_), channel_id=1, source_target_pairs={{0,1},{1,0},{2,3},{3,2},{4,5},{5,4},{6,7},{7,6},{8,9},{9,8},{10,11... | collective-permute-start | bytes 202760 | tf_op jit(solution)/shard_map/ppermute | solution.py:426
  30.9 0.8 %collective-permute-start.8 = (bf16[264,128]{1,0:T(8,128)(2,1)S(1)}, bf16[264,128]{1,0:T(8,128)(2,1)S(1)}, u32[]{:S(2)}, u32[]{:S(2)}) collective-permute-start(bf16[264,128]{1,0:T(8,128)(2,1)S(1)} %get-tuple-element.51.refs_3_), channel_id=1, source_target_pairs={{0,1},{1,0},{2,3},{3,2},{4,5},{5,4},{6,7},{7,6},{8,9},{9,8},{10,11... | collective-permute-start | bytes 202760 | tf_op jit(solution)/shard_map/ppermute | solution.py:426
  31.7 1.8 %collective-permute-start.6 = (bf16[264,128]{1,0:T(8,128)(2,1)S(1)}, bf16[264,128]{1,0:T(8,128)(2,1)S(1)}, u32[]{:S(2)}, u32[]{:S(2)}) collective-permute-start(bf16[264,128]{1,0:T(8,128)(2,1)S(1)} %get-tuple-element.53), channel_id=1, source_target_pairs={{0,6},{1,7},{2,4},{3,5},{4,2},{5,3},{6,0},{7,1},{8,14},{9,15},{10,... | collective-permute-start | bytes 202760 | tf_op jit(solution)/shard_map/ppermute | solution.py:426
  33.9 1.3 %out_m2_m3_m1.1.refs_12_ = bf16[128,4096]{1,0:T(8,128)(2,1)} custom-call(bf16[128,4096]{1,0:T(8,128)(2,1)S(1)} %copy-done, f32[16,4,128]{2,1,0:T(4,128)S(1)} %cum.1.cum_ref.refs_1_, f32[1,4096]{1,0:T(1,128)S(1)} %bitcast.36, bf16[264,128]{1,0:T(8,128)(2,1)S(1)} %collective-permute-done.14.refs_3_, ...), custom_call_target="tpu_custom_call", output_to_operand_aliasing={{}: (12, {})} | custom-call | flops 1 | bytes 1 | tf_op jit(solution)/shard_map/out_m2_m3_m1/pallas_call | solution.py:45
  35.3 1.3 %out_o2_o3_o1.1.refs_9_ = bf16[128,4096]{1,0:T(8,128)(2,1)} custom-call(bf16[128,4096]{1,0:T(8,128)(2,1)S(1)} %copy-done, f32[16,4,128]{2,1,0:T(4,128)S(1)} %cum.1.cum_ref.refs_1_, f32[1,4096]{1,0:T(1,128)S(1)} %bitcast.37, bf16[264,128]{1,0:T(8,128)(2,1)S(1)} %collective-permute-done.18.refs_3_, ...), custom_call_target="tpu_custom_call", output_to_operand_aliasing={{}: (12, {})} | custom-call | flops 1 | bytes 1 | tf_op jit(solution)/shard_map/out_o2_o3_o1/pallas_call | solution.py:45
  36.6 1.2 %out_m4_o4.1.refs_12_ = bf16[128,4096]{1,0:T(8,128)(2,1)} custom-call(bf16[128,4096]{1,0:T(8,128)(2,1)S(1)} %copy-done, f32[16,4,128]{2,1,0:T(4,128)S(1)} %cum.1.cum_ref.refs_1_, f32[1,4096]{1,0:T(1,128)S(1)} %bitcast.38, bf16[264,128]{1,0:T(8,128)(2,1)S(1)} %get-tuple-element.51.refs_3_, ...), custom_call_target="tpu_custom_call", output_to_operand_aliasing={{}: (9, {})} | custom-call | flops 1 | bytes 1 | tf_op jit(solution)/shard_map/out_m4_o4/pallas_call | solution.py:45
  37.8 1.1 %collective-permute-start.21 = (bf16[264,128]{1,0:T(8,128)(2,1)S(1)}, bf16[264,128]{1,0:T(8,128)(2,1)S(1)}, u32[]{:S(2)}, u32[]{:S(2)}) collective-permute-start(bf16[264,128]{1,0:T(8,128)(2,1)S(1)} %collective-permute-done.5.refs_3_), channel_id=1, source_target_pairs={{0,1},{1,0},{2,3},{3,2},{4,5},{5,4},{6,7},{7,6},{8,9},{9,8},{10,11... | collective-permute-start | bytes 202760 | tf_op jit(solution)/shard_map/ppermute | solution.py:426
  39.5 1.3 %out_m6_m7_m5.1.refs_12_ = bf16[128,4096]{1,0:T(8,128)(2,1)} custom-call(bf16[128,4096]{1,0:T(8,128)(2,1)S(1)} %copy-done, f32[16,4,128]{2,1,0:T(4,128)S(1)} %cum.1.cum_ref.refs_1_, f32[1,4096]{1,0:T(1,128)S(1)} %bitcast.39, bf16[264,128]{1,0:T(8,128)(2,1)S(1)} %collective-permute-done.5.refs_3_, ...), custom_call_target="tpu_custom_call", output_to_operand_aliasing={{}: (12, {})} | custom-call | flops 1 | bytes 1 | tf_op jit(solution)/shard_map/out_m6_m7_m5/pallas_call | solution.py:45
  40.8 1.3 %out_o6_o7_o5.1 = bf16[128,4096]{1,0:T(8,128)(2,1)} custom-call(bf16[128,4096]{1,0:T(8,128)(2,1)S(1)} %copy-done, f32[16,4,128]{2,1,0:T(4,128)S(1)} %cum.1.cum_ref.refs_1_, f32[1,4096]{1,0:T(1,128)S(1)} %bitcast.40, bf16[264,128]{1,0:T(8,128)(2,1)S(1)} %collective-permute-done.21.refs_3_, ...), custom_call_target="tpu_custom_call", output_to_operand_aliasing={{}: (12, {})} | custom-call | flops 1 | bytes 1 | tf_op jit(solution)/shard_map/out_o6_o7_o5/pallas_call | solution.py:45
  (55 shorter events, 4.8 us)
Async XLA Ops:
  2.9 2.1 %collective-permute-start = (bf16[8,280,128]{2,1,0:T(8,128)(2,1)S(1)}, bf16[8,280,128]{2,1,0:T(8,128)(2,1)S(1)}, u32[]{:S(2)}, u32[]{:S(2)}) collective-permute-start(bf16[8,280,128]{2,1,0:T(8,128)(2,1)S(1)} %states_other.1), channel_id=1, source_target_pairs={{0,1},{1,0},{2,3},{3,2},{4,5},{5,4},{6,7},{7,6},{8,9},{9,8},{10,11... | collective-permute-start | bytes 1720328 | tf_op jit(solution)/shard_map/ppermute | solution.py:426
  4.5 22.7 %collective-permute-start.9 = (bf16[8,280,128]{2,1,0:T(8,128)(2,1)S(1)}, bf16[8,280,128]{2,1,0:T(8,128)(2,1)S(1)}, u32[]{:S(2)}, u32[]{:S(2)}) collective-permute-start(bf16[8,280,128]{2,1,0:T(8,128)(2,1)S(1)} %states_mine.1.own_ref), channel_id=1, source_target_pairs={{0,1},{1,0},{2,3},{3,2},{4,5},{5,4},{6,7},{7,6},{8,9},{9,8},{10,11... | collective-permute-start | bytes 1720328 | tf_op jit(solution)/shard_map/ppermute | solution.py:426
  5.4 5.6 %collective-permute-start.12 = (bf16[280,128]{1,0:T(8,128)(2,1)S(1)}, bf16[280,128]{1,0:T(8,128)(2,1)S(1)}, u32[]{:S(2)}, u32[]{:S(2)}) collective-permute-start(bf16[280,128]{1,0:T(8,128)(2,1)S(1)} %get-tuple-element.39), channel_id=1, source_target_pairs={{0,6},{1,7},{2,4},{3,5},{4,2},{5,3},{6,0},{7,1},{8,14},{9,15},{10,... | collective-permute-start | bytes 215048 | tf_op jit(solution)/shard_map/ppermute | solution.py:426
  8.8 4.1 %collective-permute-start.11 = (bf16[280,128]{1,0:T(8,128)(2,1)S(1)}, bf16[280,128]{1,0:T(8,128)(2,1)S(1)}, u32[]{:S(2)}, u32[]{:S(2)}) collective-permute-start(bf16[280,128]{1,0:T(8,128)(2,1)S(1)} %get-tuple-element.40), channel_id=1, source_target_pairs={{0,4},{1,5},{2,6},{3,7},{4,0},{5,1},{6,2},{7,3},{8,12},{9,13},{10,... | collective-permute-start | bytes 215048 | tf_op jit(solution)/shard_map/ppermute | solution.py:426
  9.0 4.7 %collective-permute-start.10 = (bf16[280,128]{1,0:T(8,128)(2,1)S(1)}, bf16[280,128]{1,0:T(8,128)(2,1)S(1)}, u32[]{:S(2)}, u32[]{:S(2)}) collective-permute-start(bf16[280,128]{1,0:T(8,128)(2,1)S(1)} %get-tuple-element.41), channel_id=1, source_target_pairs={{0,2},{1,3},{2,0},{3,1},{4,6},{5,7},{6,4},{7,5},{8,10},{9,11},{10,... | collective-permute-start | bytes 215048 | tf_op jit(solution)/shard_map/ppermute | solution.py:426
  9.2 8.6 %collective-permute-start.3 = (bf16[280,128]{1,0:T(8,128)(2,1)S(1)}, bf16[280,128]{1,0:T(8,128)(2,1)S(1)}, u32[]{:S(2)}, u32[]{:S(2)}) collective-permute-start(bf16[280,128]{1,0:T(8,128)(2,1)S(1)} %get-tuple-element.43), channel_id=1, source_target_pairs={{0,2},{1,3},{2,0},{3,1},{4,6},{5,7},{6,4},{7,5},{8,10},{9,11},{10,... | collective-permute-start | bytes 215048 | tf_op jit(solution)/shard_map/ppermute | solution.py:426
  11.0 6.7 %collective-permute-start.2 = (bf16[280,128]{1,0:T(8,128)(2,1)S(1)}, bf16[280,128]{1,0:T(8,128)(2,1)S(1)}, u32[]{:S(2)}, u32[]{:S(2)}) collective-permute-start(bf16[280,128]{1,0:T(8,128)(2,1)S(1)} %get-tuple-element.44), channel_id=1, source_target_pairs={{0,6},{1,7},{2,4},{3,5},{4,2},{5,3},{6,0},{7,1},{8,14},{9,15},{10,... | collective-permute-start | bytes 215048 | tf_op jit(solution)/shard_map/ppermute | solution.py:426
  12.9 4.8 %collective-permute-start.1 = (bf16[280,128]{1,0:T(8,128)(2,1)S(1)}, bf16[280,128]{1,0:T(8,128)(2,1)S(1)}, u32[]{:S(2)}, u32[]{:S(2)}) collective-permute-start(bf16[280,128]{1,0:T(8,128)(2,1)S(1)} %get-tuple-element.45), channel_id=1, source_target_pairs={{0,4},{1,5},{2,6},{3,7},{4,0},{5,1},{6,2},{7,3},{8,12},{9,13},{10,... | collective-permute-start | bytes 215048 | tf_op jit(solution)/shard_map/ppermute | solution.py:426
  14.0 4.8 %collective-permute-start.13 = (bf16[264,128]{1,0:T(8,128)(2,1)S(1)}, bf16[264,128]{1,0:T(8,128)(2,1)S(1)}, u32[]{:S(2)}, u32[]{:S(2)}) collective-permute-start(bf16[264,128]{1,0:T(8,128)(2,1)S(1)} %span_state.3), channel_id=1, source_target_pairs={{0,8},{1,9},{2,10},{3,11},{4,12},{5,13},{6,14},{7,15},{8,0},{9,1},... | collective-permute-start | bytes 202760 | tf_op jit(solution)/shard_map/ppermute | solution.py:426
  18.1 7.4 %collective-permute-start.4 = (bf16[264,128]{1,0:T(8,128)(2,1)S(1)}, bf16[264,128]{1,0:T(8,128)(2,1)S(1)}, u32[]{:S(2)}, u32[]{:S(2)}) collective-permute-start(bf16[264,128]{1,0:T(8,128)(2,1)S(1)} %span_state.2), channel_id=1, source_target_pairs={{0,8},{1,9},{2,10},{3,11},{4,12},{5,13},{6,14},{7,15},{8,0},{9,1},... | collective-permute-start | bytes 202760 | tf_op jit(solution)/shard_map/ppermute | solution.py:426
  19.1 8.1 %collective-permute-start.17 = (bf16[264,128]{1,0:T(8,128)(2,1)S(1)}, bf16[264,128]{1,0:T(8,128)(2,1)S(1)}, u32[]{:S(2)}, u32[]{:S(2)}) collective-permute-start(bf16[264,128]{1,0:T(8,128)(2,1)S(1)} %get-tuple-element.47.refs_3_), channel_id=1, source_target_pairs={{0,1},{1,0},{2,3},{3,2},{4,5},{5,4},{6,7},{7,6},{8,9},{9,8},{10,11... | collective-permute-start | bytes 202760 | tf_op jit(solution)/shard_map/ppermute | solution.py:426
  23.1 5.3 %collective-permute-start.16 = (bf16[264,128]{1,0:T(8,128)(2,1)S(1)}, bf16[264,128]{1,0:T(8,128)(2,1)S(1)}, u32[]{:S(2)}, u32[]{:S(2)}) collective-permute-start(bf16[264,128]{1,0:T(8,128)(2,1)S(1)} %get-tuple-element.48), channel_id=1, source_target_pairs={{0,2},{1,3},{2,0},{3,1},{4,6},{5,7},{6,4},{7,5},{8,10},{9,11},{10,... | collective-permute-start | bytes 202760 | tf_op jit(solution)/shard_map/ppermute | solution.py:426
  23.4 5.0 %collective-permute-start.15 = (bf16[264,128]{1,0:T(8,128)(2,1)S(1)}, bf16[264,128]{1,0:T(8,128)(2,1)S(1)}, u32[]{:S(2)}, u32[]{:S(2)}) collective-permute-start(bf16[264,128]{1,0:T(8,128)(2,1)S(1)} %get-tuple-element.49), channel_id=1, source_target_pairs={{0,6},{1,7},{2,4},{3,5},{4,2},{5,3},{6,0},{7,1},{8,14},{9,15},{10,... | collective-permute-start | bytes 202760 | tf_op jit(solution)/shard_map/ppermute | solution.py:426
  25.5 3.4 %collective-permute-start.14 = (bf16[264,128]{1,0:T(8,128)(2,1)S(1)}, bf16[264,128]{1,0:T(8,128)(2,1)S(1)}, u32[]{:S(2)}, u32[]{:S(2)}) collective-permute-start(bf16[264,128]{1,0:T(8,128)(2,1)S(1)} %get-tuple-element.50), channel_id=1, source_target_pairs={{0,4},{1,5},{2,6},{3,7},{4,0},{5,1},{6,2},{7,3},{8,12},{9,13},{10,... | collective-permute-start | bytes 202760 | tf_op jit(solution)/shard_map/ppermute | solution.py:426
  28.9 2.8 %collective-permute-start.18 = (bf16[264,128]{1,0:T(8,128)(2,1)S(1)}, bf16[264,128]{1,0:T(8,128)(2,1)S(1)}, u32[]{:S(2)}, u32[]{:S(2)}) collective-permute-start(bf16[264,128]{1,0:T(8,128)(2,1)S(1)} %collective-permute-done.14.refs_3_), channel_id=1, source_target_pairs={{0,1},{1,0},{2,3},{3,2},{4,5},{5,4},{6,7},{7,6},{8,9},{9,8},{10,11... | collective-permute-start | bytes 202760 | tf_op jit(solution)/shard_map/ppermute | solution.py:426
  30.4 3.2 %collective-permute-start.19 = (bf16[264,128]{1,0:T(8,128)(2,1)S(1)}, bf16[264,128]{1,0:T(8,128)(2,1)S(1)}, u32[]{:S(2)}, u32[]{:S(2)}) collective-permute-start(bf16[264,128]{1,0:T(8,128)(2,1)S(1)} %collective-permute-done.15.refs_6_), channel_id=1, source_target_pairs={{0,1},{1,0},{2,3},{3,2},{4,5},{5,4},{6,7},{7,6},{8,9},{9,8},{10,11... | collective-permute-start | bytes 202760 | tf_op jit(solution)/shard_map/ppermute | solution.py:426
  30.4 7.4 %collective-permute-start.7 = (bf16[264,128]{1,0:T(8,128)(2,1)S(1)}, bf16[264,128]{1,0:T(8,128)(2,1)S(1)}, u32[]{:S(2)}, u32[]{:S(2)}) collective-permute-start(bf16[264,128]{1,0:T(8,128)(2,1)S(1)} %get-tuple-element.52), channel_id=1, source_target_pairs={{0,2},{1,3},{2,0},{3,1},{4,6},{5,7},{6,4},{7,5},{8,10},{9,11},{10,... | collective-permute-start | bytes 202760 | tf_op jit(solution)/shard_map/ppermute | solution.py:426
  30.9 5.7 %collective-permute-start.8 = (bf16[264,128]{1,0:T(8,128)(2,1)S(1)}, bf16[264,128]{1,0:T(8,128)(2,1)S(1)}, u32[]{:S(2)}, u32[]{:S(2)}) collective-permute-start(bf16[264,128]{1,0:T(8,128)(2,1)S(1)} %get-tuple-element.51.refs_3_), channel_id=1, source_target_pairs={{0,1},{1,0},{2,3},{3,2},{4,5},{5,4},{6,7},{7,6},{8,9},{9,8},{10,11... | collective-permute-start | bytes 202760 | tf_op jit(solution)/shard_map/ppermute | solution.py:426
  31.7 3.5 %collective-permute-start.20 = (bf16[264,128]{1,0:T(8,128)(2,1)S(1)}, bf16[264,128]{1,0:T(8,128)(2,1)S(1)}, u32[]{:S(2)}, u32[]{:S(2)}) collective-permute-start(bf16[264,128]{1,0:T(8,128)(2,1)S(1)} %collective-permute-done.16.refs_9_), channel_id=1, source_target_pairs={{0,1},{1,0},{2,3},{3,2},{4,5},{5,4},{6,7},{7,6},{8,9},{9,8},{10,11... | collective-permute-start | bytes 202760 | tf_op jit(solution)/shard_map/ppermute | solution.py:426
  31.7 6.1 %collective-permute-start.6 = (bf16[264,128]{1,0:T(8,128)(2,1)S(1)}, bf16[264,128]{1,0:T(8,128)(2,1)S(1)}, u32[]{:S(2)}, u32[]{:S(2)}) collective-permute-start(bf16[264,128]{1,0:T(8,128)(2,1)S(1)} %get-tuple-element.53), channel_id=1, source_target_pairs={{0,6},{1,7},{2,4},{3,5},{4,2},{5,3},{6,0},{7,1},{8,14},{9,15},{10,... | collective-permute-start | bytes 202760 | tf_op jit(solution)/shard_map/ppermute | solution.py:426
  33.6 4.3 %collective-permute-start.5 = (bf16[264,128]{1,0:T(8,128)(2,1)S(1)}, bf16[264,128]{1,0:T(8,128)(2,1)S(1)}, u32[]{:S(2)}, u32[]{:S(2)}) collective-permute-start(bf16[264,128]{1,0:T(8,128)(2,1)S(1)} %get-tuple-element.54), channel_id=1, source_target_pairs={{0,4},{1,5},{2,6},{3,7},{4,0},{5,1},{6,2},{7,3},{8,12},{9,13},{10,... | collective-permute-start | bytes 202760 | tf_op jit(solution)/shard_map/ppermute | solution.py:426
  37.8 3.0 %collective-permute-start.21 = (bf16[264,128]{1,0:T(8,128)(2,1)S(1)}, bf16[264,128]{1,0:T(8,128)(2,1)S(1)}, u32[]{:S(2)}, u32[]{:S(2)}) collective-permute-start(bf16[264,128]{1,0:T(8,128)(2,1)S(1)} %collective-permute-done.5.refs_3_), channel_id=1, source_target_pairs={{0,1},{1,0},{2,3},{3,2},{4,5},{5,4},{6,7},{7,6},{8,9},{9,8},{10,11... | collective-permute-start | bytes 202760 | tf_op jit(solution)/shard_map/ppermute | solution.py:426
  39.0 1.8 %collective-permute-start.22 = (bf16[264,128]{1,0:T(8,128)(2,1)S(1)}, bf16[264,128]{1,0:T(8,128)(2,1)S(1)}, u32[]{:S(2)}, u32[]{:S(2)}) collective-permute-start(bf16[264,128]{1,0:T(8,128)(2,1)S(1)} %collective-permute-done.6.refs_6_), channel_id=1, source_target_pairs={{0,1},{1,0},{2,3},{3,2},{4,5},{5,4},{6,7},{7,6},{8,9},{9,8},{10,11... | collective-permute-start | bytes 202760 | tf_op jit(solution)/shard_map/ppermute | solution.py:426
  39.0 1.8 %collective-permute-start.23 = (bf16[264,128]{1,0:T(8,128)(2,1)S(1)}, bf16[264,128]{1,0:T(8,128)(2,1)S(1)}, u32[]{:S(2)}, u32[]{:S(2)}) collective-permute-start(bf16[264,128]{1,0:T(8,128)(2,1)S(1)} %collective-permute-done.7.refs_9_), channel_id=1, source_target_pairs={{0,1},{1,0},{2,3},{3,2},{4,5},{5,4},{6,7},{7,6},{8,9},{9,8},{10,11... | collective-permute-start | bytes 202760 | tf_op jit(solution)/shard_map/ppermute | solution.py:426
  (6 other events, 24.9 us)

commit v11 on v10

--- a/solution.py
+++ b/solution.py
@@ -328,10 +328,31 @@
         out_ref[chip ^ b, heads * size : heads * size + PARTS, :] = edges[b]
 
 
-def out_kernel(items, heads, size, *refs):
+def last_out_kernel(items, earlier, heads, size, *refs):
+    count = 3 + 3 * len(items)
+    made = refs[count : count + len(earlier)]
+    out_ref, inter_ref, score_ref, done_ref, sems = refs[-5:]
+    copies = []
+
+    def write(item, source):
+        cols = columns(head_group(*item) * heads * size, 0, heads * size)
+        copies.append(
+            pltpu.make_async_copy(source, out_ref.at[:, cols], sems.at[len(copies)])
+        )
+        copies[-1].start()
+
+    for there, ref in zip(earlier, made):
+        for i, item in enumerate(there):
+            write(item, ref.at[i])
+    out_kernel(items, heads, size, *refs[:count], done_ref, inter_ref, score_ref, write=write)
+    for copy in copies:
+        copy.wait()
+
+
+def out_kernel(items, heads, size, *refs, write=None):
     q_ref, cum_ref, gain_ref = refs[:3]
     per_item = [refs[3 + 3 * i : 6 + 3 * i] for i in range(len(items))]
-    out_ref, inter_ref, score_ref, done_ref, sems = refs[-5:]
+    done_ref, inter_ref, score_ref = refs[-3:]
     rows = q_ref.shape[0]
     core, _ = position()
     second = core == 1
@@ -368,7 +389,6 @@
             both = both * started[:, j : j + 1]
             inter_ref[i * heads + j] = both[:, 0:size] + intra_ref[g * heads + j]
             score_ref[i * heads + j] = jnp.where(kept[j], both[:, size:], 0.0).astype(BF16)
-    copies = []
     for i, (mine, g) in enumerate(items):
         _, intra_ref, sib_ref = per_item[i]
         b = head_group(mine, g)
@@ -388,11 +408,8 @@
             done_ref[i, :, j * size : (j + 1) * size] = (
                 mixed * scale * gain_ref[:, cols]
             ).astype(BF16)
-        wide = columns(b * heads * size, 0, heads * size)
-        copies.append(pltpu.make_async_copy(done_ref.at[i], out_ref.at[:, wide], sems.at[i]))
-        copies[-1].start()
-    for copy in copies:
-        copy.wait()
+        if write is not None:
+            write((mine, g), done_ref.at[i])
 
 
 def join_spans(earlier, later, heads, size):
@@ -544,40 +561,51 @@
             own[first + g] = swap(chip_prefix[g], 2 * g)
         other[first] = swap(own[first], 1)
 
-    def output(items, result):
+    def output(items, earlier=None):
         args = [queries, cum, gain]
-        for mine, g in items:
-            args += [own[g], intra_mine, got] if mine else [other[g], intra_other, got_late]
-        count = len(args)
-        extra = [] if result is None else [result]
+        for mine, u in items:
+            args += [own[u], intra_mine, got] if mine else [other[u], intra_other, got_late]
+        done = pltpu.VMEM((len(items), rows, heads * size), BF16)
+        scratch = [
+            pltpu.VMEM((len(items) * heads, rows, size), F32),
+            pltpu.VMEM((len(items) * heads, rows, 2 * PARTS), BF16),
+        ]
+        kernel = functools.partial(out_kernel, items, heads, size)
+        hints = {
+            "cost_estimate": pl.CostEstimate(flops=1, transcendentals=0, bytes_accessed=1),
+        }
+        name = "out_" + "_".join(("m" if mine else "o") + str(u) for mine, u in items)
+        if earlier is None:
+            return call(kernel, name, done, *args, scratch=scratch, **hints)
+        there, made = zip(*earlier)
         return call(
-            functools.partial(out_kernel, items, heads, size),
-            "out_" + "_".join(("m" if mine else "o") + str(g) for mine, g in items),
+            functools.partial(last_out_kernel, items, there, heads, size),
+            name,
             jax.ShapeDtypeStruct((rows, width), BF16),
-            *args, *extra,
-            in_specs=[VMEM] * count + [HBM] * len(extra),
+            *args, *made,
             out_specs=HBM,
-            input_output_aliases={count: 0} if extra else {},
-            cost_estimate=pl.CostEstimate(flops=1, transcendentals=0, bytes_accessed=1),
-            scratch=[
-                pltpu.VMEM((len(items) * heads, rows, size), F32),
-                pltpu.VMEM((len(items) * heads, rows, 2 * PARTS), BF16),
-                pltpu.VMEM((len(items), rows, heads * size), BF16),
-                pltpu.SemaphoreType.DMA((len(items),)),
-            ],
-        )
-
-    result = None
+            scratch=[*scratch, done, pltpu.SemaphoreType.DMA((2 * UNITS,))],
+            **hints,
+        )
+
+    earlier = []
     for part in range(CHUNKS):
         first = part * CHIPS
         units = [first + g for g in EXCHANGE]
-        result = output([(True, first), (False, first)], result)
-        *late, result = lax.optimization_barrier((*[own[u] for u in units], result))
+        items = [(True, first), (False, first)]
+        made = [output(items)] + [x for _, x in earlier[-1:]]
+        late, made = lax.optimization_barrier(([own[u] for u in units], made))
+        earlier = earlier[:-1] + [(there, x) for (there, _), x in zip(earlier[-1:], made[1:])]
+        earlier.append((items, made[0]))
         own.update(zip(units, late))
         other.update({u: swap(own[u], 1) for u in units})
-        result = output([(True, u) for u in units], result)
-        result = output([(False, u) for u in units], result)
-    return result
+        items = [(True, u) for u in units]
+        if part < CHUNKS - 1:
+            others = [(False, u) for u in units]
+            earlier += [(others, output(others)), (items, output(items))]
+        else:
+            earlier.append((items, output(items)))
+    return output([(False, u) for u in units], earlier)
 
 
 def solution(mesh):

time: 42.3 us -> 40.2 us (0.950)
  Pallas kernels: 15.9 us -> 12.8 us
  starting transfers between devices: 24.7 us -> 26.3 us
  waiting for transfers between devices: 1.14 us -> 0.51 us
    pallas_call x16, Pallas kernels: 15.9 us -> 12.8 us  [call(): pl.pallas_call(kernel, out_shape=out_shape, in_specs=in_specs, out_specs=...]
    ppermute x24, starting transfers between devices: 24.7 us -> 26.3 us  [swap(): return lax.ppermute(x, 'ctx', [(i, i ^ mask) for i in range(n)])]
    ppermute x24, waiting for transfers between devices: 1.14 us -> 0.51 us  [swap(): return lax.ppermute(x, 'ctx', [(i, i ^ mask) for i in range(n)])]
  transfers between devices with their start and end apart: 24 -> 24, of which waited for: 2 -> 1; matrix products, arithmetic and copies ran while one was open for 0% -> 0% of each run, Pallas kernels for 28% -> 20%
where the time goes in v11:
time: 40.2 us; the launch traced here: 40.1 us
  starting transfers between devices  26.3 us (65%)
  Pallas kernels  12.8 us (32%)
  waiting for transfers between devices  0.51 us (1%)
    ppermute x24, starting transfers between devices, swap(): return lax.ppermute(x, 'ctx', [(i, i ^ mask) for i in range(n)])  26.3 us
    pallas_call x16, Pallas kernels, call(): pl.pallas_call(kernel, out_shape=out_shape, in_specs=in_specs, out_specs=...  12.8 us
  transfers between devices with their start and end apart: 24, of which 1 were waited for; matrix products, arithmetic and copies ran while one was open for 0% of the time, Pallas kernels for 20%

profile of v11, /device:TPU:1, one launch (start us, length us, event | category | flops | bytes accessed | tf_op | source)
XLA Modules:
  0.0 40.1 jit_solution(16618965470063643044)
XLA Ops:
  0.0 2.8 %states_other.1 = bf16[8,280,128]{2,1,0:T(8,128)(2,1)S(1)} custom-call(bf16[128,4096]{1,0:T(8,128)(2,1)} %k_ref.5, bf16[128,4096]{1,0:T(8,128)(2,1)} %v_ref.5, f32[4,4096]{1,0:T(4,128)} %w_ref.5, f32[32,128]{1,0:T(8,128)} %bitcast.41), custom_call_target="tpu_custom_call" | custom-call | tf_op jit(solution)/shard_map/states_other/pallas_call | solution.py:45
  3.0 1.5 %states_mine.1.own_ref = bf16[8,280,128]{2,1,0:T(8,128)(2,1)S(1)} custom-call(bf16[128,4096]{1,0:T(8,128)(2,1)S(1)} %copy-done.1, bf16[128,4096]{1,0:T(8,128)(2,1)S(1)} %copy-done.2, f32[4,4096]{1,0:T(4,128)S(1)} %copy-done.3, f32[32,128]{1,0:T(8,128)S(1)} %bitcast.42), custom_call_target="tpu_custom_call" | custom-call | tf_op jit(solution)/shard_map/states_mine/pallas_call | solution.py:45
  5.4 3.4 %collective-permute-start.12 = (bf16[280,128]{1,0:T(8,128)(2,1)S(1)}, bf16[280,128]{1,0:T(8,128)(2,1)S(1)}, u32[]{:S(2)}, u32[]{:S(2)}) collective-permute-start(bf16[280,128]{1,0:T(8,128)(2,1)S(1)} %get-tuple-element.41), channel_id=1, source_target_pairs={{0,6},{1,7},{2,4},{3,5},{4,2},{5,3},{6,0},{7,1},{8,14},{9,15},{10,... | collective-permute-start | bytes 215048 | tf_op jit(solution)/shard_map/ppermute | solution.py:443
  9.2 0.9 %collective-permute-start.9 = (bf16[8,280,128]{2,1,0:T(8,128)(2,1)S(1)}, bf16[8,280,128]{2,1,0:T(8,128)(2,1)S(1)}, u32[]{:S(2)}, u32[]{:S(2)}) collective-permute-start(bf16[8,280,128]{2,1,0:T(8,128)(2,1)S(1)} %states_mine.1.own_ref), channel_id=1, source_target_pairs={{0,1},{1,0},{2,3},{3,2},{4,5},{5,4},{6,7},{7,6},{8,9},{9,8},{10,11... | collective-permute-start | bytes 1720328 | tf_op jit(solution)/shard_map/ppermute | solution.py:443
  10.1 1.6 %collective-permute-start.3 = (bf16[280,128]{1,0:T(8,128)(2,1)S(1)}, bf16[280,128]{1,0:T(8,128)(2,1)S(1)}, u32[]{:S(2)}, u32[]{:S(2)}) collective-permute-start(bf16[280,128]{1,0:T(8,128)(2,1)S(1)} %get-tuple-element.45), channel_id=1, source_target_pairs={{0,2},{1,3},{2,0},{3,1},{4,6},{5,7},{6,4},{7,5},{8,10},{9,11},{10,... | collective-permute-start | bytes 215048 | tf_op jit(solution)/shard_map/ppermute | solution.py:443
  11.7 1.3 %collective-permute-start.2 = (bf16[280,128]{1,0:T(8,128)(2,1)S(1)}, bf16[280,128]{1,0:T(8,128)(2,1)S(1)}, u32[]{:S(2)}, u32[]{:S(2)}) collective-permute-start(bf16[280,128]{1,0:T(8,128)(2,1)S(1)} %get-tuple-element.46), channel_id=1, source_target_pairs={{0,6},{1,7},{2,4},{3,5},{4,2},{5,3},{6,0},{7,1},{8,14},{9,15},{10,... | collective-permute-start | bytes 215048 | tf_op jit(solution)/shard_map/ppermute | solution.py:443
  12.9 0.8 %collective-permute-start.1 = (bf16[280,128]{1,0:T(8,128)(2,1)S(1)}, bf16[280,128]{1,0:T(8,128)(2,1)S(1)}, u32[]{:S(2)}, u32[]{:S(2)}) collective-permute-start(bf16[280,128]{1,0:T(8,128)(2,1)S(1)} %get-tuple-element.47), channel_id=1, source_target_pairs={{0,4},{1,5},{2,6},{3,7},{4,0},{5,1},{6,2},{7,3},{8,12},{9,13},{10,... | collective-permute-start | bytes 215048 | tf_op jit(solution)/shard_map/ppermute | solution.py:443
  14.1 2.4 %collective-permute-start.13 = (bf16[264,128]{1,0:T(8,128)(2,1)S(1)}, bf16[264,128]{1,0:T(8,128)(2,1)S(1)}, u32[]{:S(2)}, u32[]{:S(2)}) collective-permute-start(bf16[264,128]{1,0:T(8,128)(2,1)S(1)} %span_state.3), channel_id=1, source_target_pairs={{0,8},{1,9},{2,10},{3,11},{4,12},{5,13},{6,14},{7,15},{8,0},{9,1},... | collective-permute-start | bytes 202760 | tf_op jit(solution)/shard_map/ppermute | solution.py:443
  16.6 1.2 %intra_mine.1.refs_4_.refs_7_.refs_10_ = f32[17,128,128]{2,1,0:T(8,128)S(1)} custom-call(bf16[128,4096]{1,0:T(8,128)(2,1)S(1)} %copy-done, bf16[128,4096]{1,0:T(8,128)(2,1)S(1)} %copy-done.1, bf16[128,4096]{1,0:T(8,128)(2,1)S(1)} %copy-done.2, f32[4,4096]{1,0:T(4,128)S(1)} %copy-done.3, f32[16,4,128]{2,1,0:T(4,128)S(1)} %cum.1.cum_ref.refs_1_), custom_call_target="tpu_custom_call" | custom-call | tf_op jit(solution)/shard_map/intra_mine/pallas_call | solution.py:45
  18.1 0.7 %collective-permute-start.4 = (bf16[264,128]{1,0:T(8,128)(2,1)S(1)}, bf16[264,128]{1,0:T(8,128)(2,1)S(1)}, u32[]{:S(2)}, u32[]{:S(2)}) collective-permute-start(bf16[264,128]{1,0:T(8,128)(2,1)S(1)} %span_state.2), channel_id=1, source_target_pairs={{0,8},{1,9},{2,10},{3,11},{4,12},{5,13},{6,14},{7,15},{8,0},{9,1},... | collective-permute-start | bytes 202760 | tf_op jit(solution)/shard_map/ppermute | solution.py:443
  18.8 1.1 %intra_other.1.refs_7_.refs_4_.refs_10_ = f32[17,128,128]{2,1,0:T(8,128)S(1)} custom-call(bf16[128,4096]{1,0:T(8,128)(2,1)S(1)} %copy-done, bf16[128,4096]{1,0:T(8,128)(2,1)S(1)} %copy-done.1, bf16[128,4096]{1,0:T(8,128)(2,1)S(1)} %copy-done.2, f32[4,4096]{1,0:T(4,128)S(1)} %copy-done.3, f32[16,4,128]{2,1,0:T(4,128)S(1)} %cum.1.cum_ref.refs_1_), custom_call_target="tpu_custom_call" | custom-call | tf_op jit(solution)/shard_map/intra_other/pallas_call | solution.py:45
  20.3 2.3 %collective-permute-start.16 = (bf16[264,128]{1,0:T(8,128)(2,1)S(1)}, bf16[264,128]{1,0:T(8,128)(2,1)S(1)}, u32[]{:S(2)}, u32[]{:S(2)}) collective-permute-start(bf16[264,128]{1,0:T(8,128)(2,1)S(1)} %get-tuple-element.50), channel_id=1, source_target_pairs={{0,2},{1,3},{2,0},{3,1},{4,6},{5,7},{6,4},{7,5},{8,10},{9,11},{10,... | collective-permute-start | bytes 202760 | tf_op jit(solution)/shard_map/ppermute | solution.py:443
  22.6 1.2 %collective-permute-start.14 = (bf16[264,128]{1,0:T(8,128)(2,1)S(1)}, bf16[264,128]{1,0:T(8,128)(2,1)S(1)}, u32[]{:S(2)}, u32[]{:S(2)}) collective-permute-start(bf16[264,128]{1,0:T(8,128)(2,1)S(1)} %get-tuple-element.52), channel_id=1, source_target_pairs={{0,4},{1,5},{2,6},{3,7},{4,0},{5,1},{6,2},{7,3},{8,12},{9,13},{10,... | collective-permute-start | bytes 202760 | tf_op jit(solution)/shard_map/ppermute | solution.py:443
  23.8 3.9 %collective-permute-start.17 = (bf16[264,128]{1,0:T(8,128)(2,1)S(1)}, bf16[264,128]{1,0:T(8,128)(2,1)S(1)}, u32[]{:S(2)}, u32[]{:S(2)}) collective-permute-start(bf16[264,128]{1,0:T(8,128)(2,1)S(1)} %get-tuple-element.49.refs_3_), channel_id=1, source_target_pairs={{0,1},{1,0},{2,3},{3,2},{4,5},{5,4},{6,7},{7,6},{8,9},{9,8},{10,11... | collective-permute-start | bytes 202760 | tf_op jit(solution)/shard_map/ppermute | solution.py:443
  28.0 0.6 %collective-permute-start.7 = (bf16[264,128]{1,0:T(8,128)(2,1)S(1)}, bf16[264,128]{1,0:T(8,128)(2,1)S(1)}, u32[]{:S(2)}, u32[]{:S(2)}) collective-permute-start(bf16[264,128]{1,0:T(8,128)(2,1)S(1)} %get-tuple-element.54), channel_id=1, source_target_pairs={{0,2},{1,3},{2,0},{3,1},{4,6},{5,7},{6,4},{7,5},{8,10},{9,11},{10,... | collective-permute-start | bytes 202760 | tf_op jit(solution)/shard_map/ppermute | solution.py:443
  29.0 1.8 %collective-permute-start.6 = (bf16[264,128]{1,0:T(8,128)(2,1)S(1)}, bf16[264,128]{1,0:T(8,128)(2,1)S(1)}, u32[]{:S(2)}, u32[]{:S(2)}) collective-permute-start(bf16[264,128]{1,0:T(8,128)(2,1)S(1)} %get-tuple-element.55), channel_id=1, source_target_pairs={{0,6},{1,7},{2,4},{3,5},{4,2},{5,3},{6,0},{7,1},{8,14},{9,15},{10,... | collective-permute-start | bytes 202760 | tf_op jit(solution)/shard_map/ppermute | solution.py:443
  31.1 0.5 %out_m0_o0.1.refs_12_ = bf16[2,128,256]{2,1,0:T(8,128)(2,1)S(1)} custom-call(bf16[128,4096]{1,0:T(8,128)(2,1)S(1)} %copy-done, f32[16,4,128]{2,1,0:T(4,128)S(1)} %cum.1.cum_ref.refs_1_, f32[1,4096]{1,0:T(1,128)S(1)} %bitcast.35, bf16[264,128]{1,0:T(8,128)(2,1)S(1)} %get-tuple-element.49.refs_3_, f32[17,128,128]{2,1,0:T(8,128)S(1)} %intra_mine.1.refs_4_.refs_7_.refs_10_, ...), custom_call_target="tpu_custom_call" | custom-call | flops 1 | bytes 1 | tf_op jit(solution)/shard_map/out_m0_o0/pallas_call | solution.py:45
  31.6 1.9 %collective-permute-start.21 = (bf16[264,128]{1,0:T(8,128)(2,1)S(1)}, bf16[264,128]{1,0:T(8,128)(2,1)S(1)}, u32[]{:S(2)}, u32[]{:S(2)}) collective-permute-start(bf16[264,128]{1,0:T(8,128)(2,1)S(1)} %collective-permute-done.14.refs_3_), channel_id=1, source_target_pairs={{0,1},{1,0},{2,3},{3,2},{4,5},{5,4},{6,7},{7,6},{8,9},{9,8},{10,11... | collective-permute-start | bytes 202760 | tf_op jit(solution)/shard_map/ppermute | solution.py:443
  33.6 0.5 %out_m4_o4.1.refs_15_ = bf16[2,128,256]{2,1,0:T(8,128)(2,1)S(1)} custom-call(bf16[128,4096]{1,0:T(8,128)(2,1)S(1)} %copy-done, f32[16,4,128]{2,1,0:T(4,128)S(1)} %cum.1.cum_ref.refs_1_, f32[1,4096]{1,0:T(1,128)S(1)} %bitcast.36, bf16[264,128]{1,0:T(8,128)(2,1)S(1)} %get-tuple-element.53.refs_3_, f32[17,128,128]{2,1,0:T(8,128)S(1)} %intra_mine.1.refs_4_.refs_7_.refs_10_, ...), custom_call_target="tpu_custom_call" | custom-call | flops 1 | bytes 1 | tf_op jit(solution)/shard_map/out_m4_o4/pallas_call | solution.py:45
  34.2 0.6 %out_m2_m3_m1.1.refs_14_ = bf16[3,128,256]{2,1,0:T(8,128)(2,1)S(1)} custom-call(bf16[128,4096]{1,0:T(8,128)(2,1)S(1)} %copy-done, f32[16,4,128]{2,1,0:T(4,128)S(1)} %cum.1.cum_ref.refs_1_, f32[1,4096]{1,0:T(1,128)S(1)} %bitcast.37, bf16[264,128]{1,0:T(8,128)(2,1)S(1)} %collective-permute-done.14.refs_3_, ...), custom_call_target="tpu_custom_call" | custom-call | flops 1 | bytes 1 | tf_op jit(solution)/shard_map/out_m2_m3_m1/pallas_call | solution.py:45
  35.3 1.3 %collective-permute-start.18 = (bf16[264,128]{1,0:T(8,128)(2,1)S(1)}, bf16[264,128]{1,0:T(8,128)(2,1)S(1)}, u32[]{:S(2)}, u32[]{:S(2)}) collective-permute-start(bf16[264,128]{1,0:T(8,128)(2,1)S(1)} %collective-permute-done.5.refs_3_), channel_id=1, source_target_pairs={{0,1},{1,0},{2,3},{3,2},{4,5},{5,4},{6,7},{7,6},{8,9},{9,8},{10,11... | collective-permute-start | bytes 202760 | tf_op jit(solution)/shard_map/ppermute | solution.py:443
  37.2 0.6 %out_m6_m7_m5.1.refs_16_ = bf16[3,128,256]{2,1,0:T(8,128)(2,1)S(1)} custom-call(bf16[128,4096]{1,0:T(8,128)(2,1)S(1)} %copy-done, f32[16,4,128]{2,1,0:T(4,128)S(1)} %cum.1.cum_ref.refs_1_, f32[1,4096]{1,0:T(1,128)S(1)} %bitcast.38, bf16[264,128]{1,0:T(8,128)(2,1)S(1)} %collective-permute-done.5.refs_3_, ...), custom_call_target="tpu_custom_call" | custom-call | flops 1 | bytes 1 | tf_op jit(solution)/shard_map/out_m6_m7_m5/pallas_call | solution.py:45
  37.8 0.6 %out_o2_o3_o1.1.refs_13_ = bf16[3,128,256]{2,1,0:T(8,128)(2,1)S(1)} custom-call(bf16[128,4096]{1,0:T(8,128)(2,1)S(1)} %copy-done, f32[16,4,128]{2,1,0:T(4,128)S(1)} %cum.1.cum_ref.refs_1_, f32[1,4096]{1,0:T(1,128)S(1)} %bitcast.39, bf16[264,128]{1,0:T(8,128)(2,1)S(1)} %collective-permute-done.21.refs_3_, ...), custom_call_target="tpu_custom_call" | custom-call | flops 1 | bytes 1 | tf_op jit(solution)/shard_map/out_o2_o3_o1/pallas_call | solution.py:45
  38.5 1.5 %out_o6_o7_o5.1 = bf16[128,4096]{1,0:T(8,128)(2,1)} custom-call(bf16[128,4096]{1,0:T(8,128)(2,1)S(1)} %copy-done, f32[16,4,128]{2,1,0:T(4,128)S(1)} %cum.1.cum_ref.refs_1_, f32[1,4096]{1,0:T(1,128)S(1)} %bitcast.40, bf16[264,128]{1,0:T(8,128)(2,1)S(1)} %collective-permute-done.18.refs_3_, f32[17,128,128]{2,1,0:T(8,128)S(1)} %intra_other.1.refs_7_.refs_4_.refs_10_, ...), custom_call_target="tpu_custom_call" | custom-call | flops 1 | bytes 1 | tf_op jit(solution)/shard_map/out_o6_o7_o5/pallas_call | solution.py:45
  (55 shorter events, 4.5 us)
Async XLA Ops:
  2.9 2.0 %collective-permute-start = (bf16[8,280,128]{2,1,0:T(8,128)(2,1)S(1)}, bf16[8,280,128]{2,1,0:T(8,128)(2,1)S(1)}, u32[]{:S(2)}, u32[]{:S(2)}) collective-permute-start(bf16[8,280,128]{2,1,0:T(8,128)(2,1)S(1)} %states_other.1), channel_id=1, source_target_pairs={{0,1},{1,0},{2,3},{3,2},{4,5},{5,4},{6,7},{7,6},{8,9},{9,8},{10,11... | collective-permute-start | bytes 1720328 | tf_op jit(solution)/shard_map/ppermute | solution.py:443
  5.4 6.3 %collective-permute-start.12 = (bf16[280,128]{1,0:T(8,128)(2,1)S(1)}, bf16[280,128]{1,0:T(8,128)(2,1)S(1)}, u32[]{:S(2)}, u32[]{:S(2)}) collective-permute-start(bf16[280,128]{1,0:T(8,128)(2,1)S(1)} %get-tuple-element.41), channel_id=1, source_target_pairs={{0,6},{1,7},{2,4},{3,5},{4,2},{5,3},{6,0},{7,1},{8,14},{9,15},{10,... | collective-permute-start | bytes 215048 | tf_op jit(solution)/shard_map/ppermute | solution.py:443
  8.8 4.1 %collective-permute-start.11 = (bf16[280,128]{1,0:T(8,128)(2,1)S(1)}, bf16[280,128]{1,0:T(8,128)(2,1)S(1)}, u32[]{:S(2)}, u32[]{:S(2)}) collective-permute-start(bf16[280,128]{1,0:T(8,128)(2,1)S(1)} %get-tuple-element.42), channel_id=1, source_target_pairs={{0,4},{1,5},{2,6},{3,7},{4,0},{5,1},{6,2},{7,3},{8,12},{9,13},{10,... | collective-permute-start | bytes 215048 | tf_op jit(solution)/shard_map/ppermute | solution.py:443
  9.0 4.8 %collective-permute-start.10 = (bf16[280,128]{1,0:T(8,128)(2,1)S(1)}, bf16[280,128]{1,0:T(8,128)(2,1)S(1)}, u32[]{:S(2)}, u32[]{:S(2)}) collective-permute-start(bf16[280,128]{1,0:T(8,128)(2,1)S(1)} %get-tuple-element.43), channel_id=1, source_target_pairs={{0,2},{1,3},{2,0},{3,1},{4,6},{5,7},{6,4},{7,5},{8,10},{9,11},{10,... | collective-permute-start | bytes 215048 | tf_op jit(solution)/shard_map/ppermute | solution.py:443
  9.2 18.9 %collective-permute-start.9 = (bf16[8,280,128]{2,1,0:T(8,128)(2,1)S(1)}, bf16[8,280,128]{2,1,0:T(8,128)(2,1)S(1)}, u32[]{:S(2)}, u32[]{:S(2)}) collective-permute-start(bf16[8,280,128]{2,1,0:T(8,128)(2,1)S(1)} %states_mine.1.own_ref), channel_id=1, source_target_pairs={{0,1},{1,0},{2,3},{3,2},{4,5},{5,4},{6,7},{7,6},{8,9},{9,8},{10,11... | collective-permute-start | bytes 1720328 | tf_op jit(solution)/shard_map/ppermute | solution.py:443
  10.1 7.7 %collective-permute-start.3 = (bf16[280,128]{1,0:T(8,128)(2,1)S(1)}, bf16[280,128]{1,0:T(8,128)(2,1)S(1)}, u32[]{:S(2)}, u32[]{:S(2)}) collective-permute-start(bf16[280,128]{1,0:T(8,128)(2,1)S(1)} %get-tuple-element.45), channel_id=1, source_target_pairs={{0,2},{1,3},{2,0},{3,1},{4,6},{5,7},{6,4},{7,5},{8,10},{9,11},{10,... | collective-permute-start | bytes 215048 | tf_op jit(solution)/shard_map/ppermute | solution.py:443
  11.7 6.1 %collective-permute-start.2 = (bf16[280,128]{1,0:T(8,128)(2,1)S(1)}, bf16[280,128]{1,0:T(8,128)(2,1)S(1)}, u32[]{:S(2)}, u32[]{:S(2)}) collective-permute-start(bf16[280,128]{1,0:T(8,128)(2,1)S(1)} %get-tuple-element.46), channel_id=1, source_target_pairs={{0,6},{1,7},{2,4},{3,5},{4,2},{5,3},{6,0},{7,1},{8,14},{9,15},{10,... | collective-permute-start | bytes 215048 | tf_op jit(solution)/shard_map/ppermute | solution.py:443
  12.9 4.9 %collective-permute-start.1 = (bf16[280,128]{1,0:T(8,128)(2,1)S(1)}, bf16[280,128]{1,0:T(8,128)(2,1)S(1)}, u32[]{:S(2)}, u32[]{:S(2)}) collective-permute-start(bf16[280,128]{1,0:T(8,128)(2,1)S(1)} %get-tuple-element.47), channel_id=1, source_target_pairs={{0,4},{1,5},{2,6},{3,7},{4,0},{5,1},{6,2},{7,3},{8,12},{9,13},{10,... | collective-permute-start | bytes 215048 | tf_op jit(solution)/shard_map/ppermute | solution.py:443
  14.1 5.9 %collective-permute-start.13 = (bf16[264,128]{1,0:T(8,128)(2,1)S(1)}, bf16[264,128]{1,0:T(8,128)(2,1)S(1)}, u32[]{:S(2)}, u32[]{:S(2)}) collective-permute-start(bf16[264,128]{1,0:T(8,128)(2,1)S(1)} %span_state.3), channel_id=1, source_target_pairs={{0,8},{1,9},{2,10},{3,11},{4,12},{5,13},{6,14},{7,15},{8,0},{9,1},... | collective-permute-start | bytes 202760 | tf_op jit(solution)/shard_map/ppermute | solution.py:443
  18.1 5.7 %collective-permute-start.4 = (bf16[264,128]{1,0:T(8,128)(2,1)S(1)}, bf16[264,128]{1,0:T(8,128)(2,1)S(1)}, u32[]{:S(2)}, u32[]{:S(2)}) collective-permute-start(bf16[264,128]{1,0:T(8,128)(2,1)S(1)} %span_state.2), channel_id=1, source_target_pairs={{0,8},{1,9},{2,10},{3,11},{4,12},{5,13},{6,14},{7,15},{8,0},{9,1},... | collective-permute-start | bytes 202760 | tf_op jit(solution)/shard_map/ppermute | solution.py:443
  20.3 8.4 %collective-permute-start.16 = (bf16[264,128]{1,0:T(8,128)(2,1)S(1)}, bf16[264,128]{1,0:T(8,128)(2,1)S(1)}, u32[]{:S(2)}, u32[]{:S(2)}) collective-permute-start(bf16[264,128]{1,0:T(8,128)(2,1)S(1)} %get-tuple-element.50), channel_id=1, source_target_pairs={{0,2},{1,3},{2,0},{3,1},{4,6},{5,7},{6,4},{7,5},{8,10},{9,11},{10,... | collective-permute-start | bytes 202760 | tf_op jit(solution)/shard_map/ppermute | solution.py:443
  22.6 6.4 %collective-permute-start.15 = (bf16[264,128]{1,0:T(8,128)(2,1)S(1)}, bf16[264,128]{1,0:T(8,128)(2,1)S(1)}, u32[]{:S(2)}, u32[]{:S(2)}) collective-permute-start(bf16[264,128]{1,0:T(8,128)(2,1)S(1)} %get-tuple-element.51), channel_id=1, source_target_pairs={{0,6},{1,7},{2,4},{3,5},{4,2},{5,3},{6,0},{7,1},{8,14},{9,15},{10,... | collective-permute-start | bytes 202760 | tf_op jit(solution)/shard_map/ppermute | solution.py:443
  22.6 9.0 %collective-permute-start.14 = (bf16[264,128]{1,0:T(8,128)(2,1)S(1)}, bf16[264,128]{1,0:T(8,128)(2,1)S(1)}, u32[]{:S(2)}, u32[]{:S(2)}) collective-permute-start(bf16[264,128]{1,0:T(8,128)(2,1)S(1)} %get-tuple-element.52), channel_id=1, source_target_pairs={{0,4},{1,5},{2,6},{3,7},{4,0},{5,1},{6,2},{7,3},{8,12},{9,13},{10,... | collective-permute-start | bytes 202760 | tf_op jit(solution)/shard_map/ppermute | solution.py:443
  23.8 7.0 %collective-permute-start.17 = (bf16[264,128]{1,0:T(8,128)(2,1)S(1)}, bf16[264,128]{1,0:T(8,128)(2,1)S(1)}, u32[]{:S(2)}, u32[]{:S(2)}) collective-permute-start(bf16[264,128]{1,0:T(8,128)(2,1)S(1)} %get-tuple-element.49.refs_3_), channel_id=1, source_target_pairs={{0,1},{1,0},{2,3},{3,2},{4,5},{5,4},{6,7},{7,6},{8,9},{9,8},{10,11... | collective-permute-start | bytes 202760 | tf_op jit(solution)/shard_map/ppermute | solution.py:443
  28.0 6.8 %collective-permute-start.7 = (bf16[264,128]{1,0:T(8,128)(2,1)S(1)}, bf16[264,128]{1,0:T(8,128)(2,1)S(1)}, u32[]{:S(2)}, u32[]{:S(2)}) collective-permute-start(bf16[264,128]{1,0:T(8,128)(2,1)S(1)} %get-tuple-element.54), channel_id=1, source_target_pairs={{0,2},{1,3},{2,0},{3,1},{4,6},{5,7},{6,4},{7,5},{8,10},{9,11},{10,... | collective-permute-start | bytes 202760 | tf_op jit(solution)/shard_map/ppermute | solution.py:443
  28.7 4.9 %collective-permute-start.8 = (bf16[264,128]{1,0:T(8,128)(2,1)S(1)}, bf16[264,128]{1,0:T(8,128)(2,1)S(1)}, u32[]{:S(2)}, u32[]{:S(2)}) collective-permute-start(bf16[264,128]{1,0:T(8,128)(2,1)S(1)} %get-tuple-element.53.refs_3_), channel_id=1, source_target_pairs={{0,1},{1,0},{2,3},{3,2},{4,5},{5,4},{6,7},{7,6},{8,9},{9,8},{10,11... | collective-permute-start | bytes 202760 | tf_op jit(solution)/shard_map/ppermute | solution.py:443
  29.0 6.4 %collective-permute-start.6 = (bf16[264,128]{1,0:T(8,128)(2,1)S(1)}, bf16[264,128]{1,0:T(8,128)(2,1)S(1)}, u32[]{:S(2)}, u32[]{:S(2)}) collective-permute-start(bf16[264,128]{1,0:T(8,128)(2,1)S(1)} %get-tuple-element.55), channel_id=1, source_target_pairs={{0,6},{1,7},{2,4},{3,5},{4,2},{5,3},{6,0},{7,1},{8,14},{9,15},{10,... | collective-permute-start | bytes 202760 | tf_op jit(solution)/shard_map/ppermute | solution.py:443
  30.8 4.5 %collective-permute-start.5 = (bf16[264,128]{1,0:T(8,128)(2,1)S(1)}, bf16[264,128]{1,0:T(8,128)(2,1)S(1)}, u32[]{:S(2)}, u32[]{:S(2)}) collective-permute-start(bf16[264,128]{1,0:T(8,128)(2,1)S(1)} %get-tuple-element.56), channel_id=1, source_target_pairs={{0,4},{1,5},{2,6},{3,7},{4,0},{5,1},{6,2},{7,3},{8,12},{9,13},{10,... | collective-permute-start | bytes 202760 | tf_op jit(solution)/shard_map/ppermute | solution.py:443
  31.6 5.0 %collective-permute-start.21 = (bf16[264,128]{1,0:T(8,128)(2,1)S(1)}, bf16[264,128]{1,0:T(8,128)(2,1)S(1)}, u32[]{:S(2)}, u32[]{:S(2)}) collective-permute-start(bf16[264,128]{1,0:T(8,128)(2,1)S(1)} %collective-permute-done.14.refs_3_), channel_id=1, source_target_pairs={{0,1},{1,0},{2,3},{3,2},{4,5},{5,4},{6,7},{7,6},{8,9},{9,8},{10,11... | collective-permute-start | bytes 202760 | tf_op jit(solution)/shard_map/ppermute | solution.py:443
  33.5 4.3 %collective-permute-start.22 = (bf16[264,128]{1,0:T(8,128)(2,1)S(1)}, bf16[264,128]{1,0:T(8,128)(2,1)S(1)}, u32[]{:S(2)}, u32[]{:S(2)}) collective-permute-start(bf16[264,128]{1,0:T(8,128)(2,1)S(1)} %collective-permute-done.15.refs_6_), channel_id=1, source_target_pairs={{0,1},{1,0},{2,3},{3,2},{4,5},{5,4},{6,7},{7,6},{8,9},{9,8},{10,11... | collective-permute-start | bytes 202760 | tf_op jit(solution)/shard_map/ppermute | solution.py:443
  34.8 3.0 %collective-permute-start.23 = (bf16[264,128]{1,0:T(8,128)(2,1)S(1)}, bf16[264,128]{1,0:T(8,128)(2,1)S(1)}, u32[]{:S(2)}, u32[]{:S(2)}) collective-permute-start(bf16[264,128]{1,0:T(8,128)(2,1)S(1)} %collective-permute-done.16.refs_9_), channel_id=1, source_target_pairs={{0,1},{1,0},{2,3},{3,2},{4,5},{5,4},{6,7},{7,6},{8,9},{9,8},{10,11... | collective-permute-start | bytes 202760 | tf_op jit(solution)/shard_map/ppermute | solution.py:443
  35.3 3.2 %collective-permute-start.18 = (bf16[264,128]{1,0:T(8,128)(2,1)S(1)}, bf16[264,128]{1,0:T(8,128)(2,1)S(1)}, u32[]{:S(2)}, u32[]{:S(2)}) collective-permute-start(bf16[264,128]{1,0:T(8,128)(2,1)S(1)} %collective-permute-done.5.refs_3_), channel_id=1, source_target_pairs={{0,1},{1,0},{2,3},{3,2},{4,5},{5,4},{6,7},{7,6},{8,9},{9,8},{10,11... | collective-permute-start | bytes 202760 | tf_op jit(solution)/shard_map/ppermute | solution.py:443
  36.7 1.8 %collective-permute-start.19 = (bf16[264,128]{1,0:T(8,128)(2,1)S(1)}, bf16[264,128]{1,0:T(8,128)(2,1)S(1)}, u32[]{:S(2)}, u32[]{:S(2)}) collective-permute-start(bf16[264,128]{1,0:T(8,128)(2,1)S(1)} %collective-permute-done.6.refs_6_), channel_id=1, source_target_pairs={{0,1},{1,0},{2,3},{3,2},{4,5},{5,4},{6,7},{7,6},{8,9},{9,8},{10,11... | collective-permute-start | bytes 202760 | tf_op jit(solution)/shard_map/ppermute | solution.py:443
  36.7 1.8 %collective-permute-start.20 = (bf16[264,128]{1,0:T(8,128)(2,1)S(1)}, bf16[264,128]{1,0:T(8,128)(2,1)S(1)}, u32[]{:S(2)}, u32[]{:S(2)}) collective-permute-start(bf16[264,128]{1,0:T(8,128)(2,1)S(1)} %collective-permute-done.7.refs_9_), channel_id=1, source_target_pairs={{0,1},{1,0},{2,3},{3,2},{4,5},{5,4},{6,7},{7,6},{8,9},{9,8},{10,11... | collective-permute-start | bytes 202760 | tf_op jit(solution)/shard_map/ppermute | solution.py:443
  (6 other events, 34.4 us)

commit v12 on v11

--- a/solution.py
+++ b/solution.py
@@ -15,6 +15,7 @@
 EXCHANGE = (2, 3, 1)
 CHUNKS = 2
 UNITS = CHUNKS * CHIPS
+SHIFTS = ((0,), (1,))
 PARTS = 8
 VMEM = pl.BlockSpec(memory_space=pltpu.VMEM)
 HBM = pl.BlockSpec(memory_space=pltpu.HBM)
@@ -236,6 +237,7 @@
     core, _ = position()
     first = core == 0
     for g in range(UNITS):
+        to = out_ref.at[g % CHIPS, g // CHIPS]
         own_decay = get_decay(own_ref.at[g], heads, size)
         got_decay = get_decay(got_ref.at[g], heads, size)
         own_by = jnp.where(first, got_decay, 1.0)
@@ -251,23 +253,23 @@
         fixes = edge_states(values.astype(BF16), edges.astype(BF16), heads)
         for j in range(heads):
             rows = slice(j * size, (j + 1) * size)
-            out_ref[g, rows, :] = (
+            to[rows, :] = (
                 own_ref[g, rows, :].astype(F32) * own_by[j : j + 1]
                 + got_ref[g, rows, :].astype(F32) * got_by[j : j + 1]
                 + fixes[j]
             ).astype(BF16)
-        put_decay(out_ref.at[g], own_decay * got_decay, heads, size)
+        put_decay(to, own_decay * got_decay, heads, size)
         later_by = jnp.where(first, got_decay, own_decay)
-        out_ref[g, side(0, heads, size), :] = out_edges.astype(BF16)
-        out_ref[g, side(2, heads, size), :] = padded(
+        to[side(0, heads, size), :] = out_edges.astype(BF16)
+        to[side(2, heads, size), :] = padded(
             [out_values[t * heads : (t + 1) * heads] * later_by for t in range(3)]
         )
 
 
-def in_order(packets, held):
+def in_order(packets, part, held):
     _, chip = position()
     for g in range(CHIPS):
-        held[chip ^ g] = packets[g][...]
+        held[chip ^ g] = packets[g][part]
 
 
 def chip_fixes(held, b, edges, heads, size):
@@ -276,19 +278,26 @@
 
 def last_edge_kernel(heads, size, *refs):
     packets, out_ref, held = refs[:CHIPS], refs[CHIPS], refs[CHIPS + 1]
-    in_order(packets, held)
-    out_ref[...] = held[CHIPS - 1, side(0, heads, size), :]
-
-
-def span_kernel(heads, size, *refs):
-    packets, before, (out_ref, held) = refs[:CHIPS], refs[CHIPS:-2], refs[-2:]
-    in_order(packets, held)
+    for part in range(CHUNKS):
+        in_order(packets, part, held)
+        out_ref[part] = held[CHIPS - 1, side(0, heads, size), :]
+
+
+def span_kernel(parts, heads, size, *refs):
+    packets, before, (whole_ref, held) = refs[:CHIPS], refs[CHIPS:-2], refs[-2:]
+    for i, part in enumerate(parts):
+        known = [before[0][part]] if before else []
+        span_of(part, known, heads, size, packets, whole_ref.at[i], held)
+
+
+def span_of(part, before, heads, size, packets, out_ref, held):
+    in_order(packets, part, held)
     decays = [get_decay(held.at[b], heads, size) for b in range(CHIPS)]
     fixes = [
         chip_fixes(held, b, held[b - 1, side(0, heads, size), :], heads, size)
         for b in range(1, CHIPS)
     ]
-    fixes.insert(0, chip_fixes(held, 0, before[0][...], heads, size) if before else None)
+    fixes.insert(0, chip_fixes(held, 0, before[0], heads, size) if before else None)
     for j in range(heads):
         rows = slice(j * size, (j + 1) * size)
         acc = held[0, rows, :].astype(F32)
@@ -305,19 +314,19 @@
         put_decay(out_ref, whole, heads, size)
 
 
-def spread_kernel(heads, size, *refs):
+def spread_kernel(part, place, heads, size, *refs):
     packets, before, known, (out_ref, held) = refs[:CHIPS], refs[CHIPS], refs[CHIPS + 1 : -2], refs[-2:]
     _, chip = position()
     later = lax.axis_index("ctx") >= SPAN
-    in_order(packets, held)
+    in_order(packets, part, held)
     decays = [get_decay(held.at[b], heads, size) for b in range(CHIPS)]
-    edges = known[0][...] if known else before[side(0, heads, size), :]
+    edges = known[0][part] if known else before[place, side(0, heads, size), :]
     edges = [jnp.where(later, edges.astype(F32), 0.0).astype(BF16)]
     edges += [held[b, side(0, heads, size), :] for b in range(CHIPS - 1)]
     fixes = [chip_fixes(held, b, edges[b], heads, size) for b in range(CHIPS - 1)]
     for j in range(heads):
         rows = slice(j * size, (j + 1) * size)
-        acc = jnp.where(later, before[rows, :].astype(F32), 0.0)
+        acc = jnp.where(later, before[place, rows, :].astype(F32), 0.0)
         out_ref[chip, rows, :] = acc.astype(BF16)
         for b in range(1, CHIPS):
             acc = acc * decays[b - 1][j : j + 1] + (
@@ -489,42 +498,14 @@
     chip_states = call(
         functools.partial(chip_kernel, heads, size),
         "chip_states",
-        pltpu.VMEM((UNITS, packet, size), BF16),
+        pltpu.VMEM((CHIPS, CHUNKS, packet, size), BF16),
         mine, got,
     )
     order = pltpu.VMEM((CHIPS, packet, size), BF16)
 
-    def joined(packets):
-        known = []
-        if n > 2 * SPAN:
-            edge = call(
-                functools.partial(last_edge_kernel, heads, size),
-                "last_edge",
-                pltpu.VMEM((PARTS, size), BF16),
-                *packets,
-                scratch=[order],
-            )
-            known = [shift(edge, SPAN)]
-        span = call(
-            functools.partial(span_kernel, heads, size),
-            "span_state",
-            pltpu.VMEM((heads * size + (2 if known else 1) * PARTS, size), BF16),
-            *packets, *known,
-            scratch=[order],
-        )
-        before = swap(span, SPAN) if n == 2 * SPAN else shift(span, SPAN)
-        reach = 1
-        while reach < n // SPAN - 1:
-            before = join_spans(shift(before, SPAN * reach), before, heads, size)
-            reach *= 2
-        return span, before, known
-
-    packets = []
-    for part in range(CHUNKS):
-        these = {0: chip_states[part * CHIPS]}
-        for g in EXCHANGE:
-            these[g] = swap(chip_states[part * CHIPS + g], 2 * g)
-        packets.append([these[g] for g in range(CHIPS)])
+    packets = {0: chip_states[0]}
+    for g in EXCHANGE:
+        packets[g] = swap(chip_states[g], 2 * g)
     q_after, decay_after, chip_states = lax.optimization_barrier(
         (queries, log_decay, chip_states)
     )
@@ -535,24 +516,56 @@
         decay_after.T,
     )
     intra_mine = intra_part(True, q_after)
-    last = packets[-1]
-    *late, intra_mine = lax.optimization_barrier((*[last[g] for g in EXCHANGE], intra_mine))
-    for g, x in zip(EXCHANGE, late):
-        last[g] = x
-
-    spans, befores, knowns = zip(*[joined(p) for p in packets])
+    *late, intra_mine = lax.optimization_barrier((*[packets[g] for g in EXCHANGE], intra_mine))
+    packets.update(zip(EXCHANGE, late))
+    packets = [packets[g] for g in range(CHIPS)]
+
+    known = []
+    if n > 2 * SPAN:
+        edge = call(
+            functools.partial(last_edge_kernel, heads, size),
+            "last_edge",
+            pltpu.VMEM((CHUNKS, PARTS, size), BF16),
+            *packets,
+            scratch=[order],
+        )
+        known = [shift(edge, SPAN)]
+
+    def joined(parts):
+        span = call(
+            functools.partial(span_kernel, parts, heads, size),
+            "span_state",
+            pltpu.VMEM((len(parts), heads * size + (2 if known else 1) * PARTS, size), BF16),
+            *packets, *known,
+            scratch=[order],
+        )
+        before = swap(span, SPAN) if n == 2 * SPAN else shift(span, SPAN)
+        reach = 1
+        while reach < n // SPAN - 1:
+            before = jax.vmap(functools.partial(join_spans, heads=heads, size=size))(
+                shift(before, SPAN * reach), before
+            )
+            reach *= 2
+        return span, before
+
+    spans, befores = zip(*[joined(parts) for parts in SHIFTS])
     q_after, _ = lax.optimization_barrier((queries, spans[-1]))
     intra_other = intra_part(False, q_after)
     before, intra_other = lax.optimization_barrier((befores[-1], intra_other))
     befores = [*befores[:-1], before]
+    ahead = {
+        part: (place, before)
+        for parts, before in zip(SHIFTS, befores)
+        for place, part in enumerate(parts)
+    }
 
     own, other = {}, {}
     for part in range(CHUNKS):
         chip_prefix = call(
-            functools.partial(spread_kernel, heads, size),
+            functools.partial(spread_kernel, part, ahead[part][0], heads, size),
             "chip_prefix",
             pltpu.VMEM((CHIPS, heads * size + PARTS, size), BF16),
-            *packets[part], befores[part], *knowns[part],
+            *packets, ahead[part][1], *known,
             scratch=[order],
         )
         first = part * CHIPS

time: 40.2 us -> 40.4 us (level)
  waiting for transfers between devices: 0.51 us -> 5.07 us
  starting transfers between devices: 26.3 us -> 22 us
    ppermute x24 -> x21, waiting for transfers between devices: 0.51 us -> 5.07 us  [swap(): return lax.ppermute(x, 'ctx', [(i, i ^ mask) for i in range(n)])]
    ppermute x24 -> x21, starting transfers between devices: 26.3 us -> 22 us  [swap(): return lax.ppermute(x, 'ctx', [(i, i ^ mask) for i in range(n)])]
  transfers between devices with their start and end apart: 24 -> 21, of which waited for: 1 -> 5; matrix products, arithmetic and copies ran while one was open for 0% -> 0% of each run, Pallas kernels for 20% -> 20%
where the time goes in v12:
time: 40.4 us; the launch traced here: 40.2 us
  starting transfers between devices  22 us (54%)
  Pallas kernels  12.8 us (32%)
  waiting for transfers between devices  5.07 us (13%)
    ppermute x21, starting transfers between devices, swap(): return lax.ppermute(x, 'ctx', [(i, i ^ mask) for i in range(n)])  22 us
    pallas_call x16, Pallas kernels, call(): pl.pallas_call(kernel, out_shape=out_shape, in_specs=in_specs, out_specs=...  12.8 us
    ppermute x21, waiting for transfers between devices, swap(): return lax.ppermute(x, 'ctx', [(i, i ^ mask) for i in range(n)])  5.07 us
  transfers between devices with their start and end apart: 21, of which 5 were waited for; matrix products, arithmetic and copies ran while one was open for 0% of the time, Pallas kernels for 20%

profile of v12, /device:TPU:1, one launch (start us, length us, event | category | flops | bytes accessed | tf_op | source)
XLA Modules:
  0.0 40.2 jit_solution(181673537862131546)
XLA Ops:
  0.0 2.8 %states_other.1 = bf16[8,280,128]{2,1,0:T(8,128)(2,1)S(1)} custom-call(bf16[128,4096]{1,0:T(8,128)(2,1)} %k_ref.5, bf16[128,4096]{1,0:T(8,128)(2,1)} %v_ref.5, f32[4,4096]{1,0:T(4,128)} %w_ref.5, f32[32,128]{1,0:T(8,128)} %bitcast.33), custom_call_target="tpu_custom_call" | custom-call | tf_op jit(solution)/shard_map/states_other/pallas_call | solution.py:46
  3.0 1.5 %states_mine.1.own_ref = bf16[8,280,128]{2,1,0:T(8,128)(2,1)S(1)} custom-call(bf16[128,4096]{1,0:T(8,128)(2,1)S(1)} %copy-done.1, bf16[128,4096]{1,0:T(8,128)(2,1)S(1)} %copy-done.2, f32[4,4096]{1,0:T(4,128)S(1)} %copy-done.3, f32[32,128]{1,0:T(8,128)S(1)} %bitcast.34), custom_call_target="tpu_custom_call" | custom-call | tf_op jit(solution)/shard_map/states_mine/pallas_call | solution.py:46
  5.3 2.4 %collective-permute-start.3 = (bf16[2,280,128]{2,1,0:T(8,128)(2,1)S(1)}, bf16[2,280,128]{2,1,0:T(8,128)(2,1)S(1)}, u32[]{:S(2)}, u32[]{:S(2)}) collective-permute-start(bf16[2,280,128]{2,1,0:T(8,128)(2,1)S(1)} %get-tuple-element.41), channel_id=1, source_target_pairs={{0,2},{1,3},{2,0},{3,1},{4,6},{5,7},{6,4},{7,5},{8,10},{9,11},{10,... | collective-permute-start | bytes 430088 | tf_op jit(solution)/shard_map/ppermute | solution.py:452
  7.8 1.2 %collective-permute-start.2 = (bf16[2,280,128]{2,1,0:T(8,128)(2,1)S(1)}, bf16[2,280,128]{2,1,0:T(8,128)(2,1)S(1)}, u32[]{:S(2)}, u32[]{:S(2)}) collective-permute-start(bf16[2,280,128]{2,1,0:T(8,128)(2,1)S(1)} %get-tuple-element.42), channel_id=1, source_target_pairs={{0,6},{1,7},{2,4},{3,5},{4,2},{5,3},{6,0},{7,1},{8,14},{9,15},{10,... | collective-permute-start | bytes 430088 | tf_op jit(solution)/shard_map/ppermute | solution.py:452
  9.1 0.9 %collective-permute-start.9 = (bf16[8,280,128]{2,1,0:T(8,128)(2,1)S(1)}, bf16[8,280,128]{2,1,0:T(8,128)(2,1)S(1)}, u32[]{:S(2)}, u32[]{:S(2)}) collective-permute-start(bf16[8,280,128]{2,1,0:T(8,128)(2,1)S(1)} %states_mine.1.own_ref), channel_id=1, source_target_pairs={{0,1},{1,0},{2,3},{3,2},{4,5},{5,4},{6,7},{7,6},{8,9},{9,8},{10,11... | collective-permute-start | bytes 1720328 | tf_op jit(solution)/shard_map/ppermute | solution.py:452
  10.2 1.1 %intra_mine.1.refs_4_.refs_7_.refs_10_ = f32[17,128,128]{2,1,0:T(8,128)S(1)} custom-call(bf16[128,4096]{1,0:T(8,128)(2,1)S(1)} %copy-done, bf16[128,4096]{1,0:T(8,128)(2,1)S(1)} %copy-done.1, bf16[128,4096]{1,0:T(8,128)(2,1)S(1)} %copy-done.2, f32[4,4096]{1,0:T(4,128)S(1)} %copy-done.3, f32[16,4,128]{2,1,0:T(4,128)S(1)} %cum.1.cum_ref.refs_1_), custom_call_target="tpu_custom_call" | custom-call | tf_op jit(solution)/shard_map/intra_mine/pallas_call | solution.py:46
  11.4 2.4 %collective-permute-done.3.refs_1_ = bf16[2,280,128]{2,1,0:T(8,128)(2,1)S(1)} collective-permute-done((bf16[2,280,128]{2,1,0:T(8,128)(2,1)S(1)}, bf16[2,280,128]{2,1,0:T(8,128)(2,1)S(1)}, u32[]{:S(2)}, u32[]{:S(2)}) %collective-permute-start.3) | collective-permute-done | bytes 143392 | tf_op jit(solution)/shard_map/ppermute | solution.py:452
  13.8 1.9 %collective-permute-done.1.refs_2_ = bf16[2,280,128]{2,1,0:T(8,128)(2,1)S(1)} collective-permute-done((bf16[2,280,128]{2,1,0:T(8,128)(2,1)S(1)}, bf16[2,280,128]{2,1,0:T(8,128)(2,1)S(1)}, u32[]{:S(2)}, u32[]{:S(2)}) %collective-permute-start.1) | collective-permute-done | bytes 143392 | tf_op jit(solution)/shard_map/ppermute | solution.py:452
  16.0 2.2 %collective-permute-start.10 = (bf16[1,264,128]{2,1,0:T(8,128)(2,1)S(1)}, bf16[1,264,128]{2,1,0:T(8,128)(2,1)S(1)}, u32[]{:S(2)}, u32[]{:S(2)}) collective-permute-start(bf16[1,264,128]{2,1,0:T(8,128)(2,1)S(1)} %span_state.3), channel_id=1, source_target_pairs={{0,8},{1,9},{2,10},{3,11},{4,12},{5,13},{6,14},{7,15},{8,0},{9,1},... | collective-permute-start | bytes 202760 | tf_op jit(solution)/shard_map/ppermute | solution.py:452
  18.8 1.1 %intra_other.1.refs_7_.refs_4_.refs_10_ = f32[17,128,128]{2,1,0:T(8,128)S(1)} custom-call(bf16[128,4096]{1,0:T(8,128)(2,1)S(1)} %copy-done, bf16[128,4096]{1,0:T(8,128)(2,1)S(1)} %copy-done.1, bf16[128,4096]{1,0:T(8,128)(2,1)S(1)} %copy-done.2, f32[4,4096]{1,0:T(4,128)S(1)} %copy-done.3, f32[16,4,128]{2,1,0:T(4,128)S(1)} %cum.1.cum_ref.refs_1_), custom_call_target="tpu_custom_call" | custom-call | tf_op jit(solution)/shard_map/intra_other/pallas_call | solution.py:46
  20.4 1.1 %collective-permute-start.13 = (bf16[264,128]{1,0:T(8,128)(2,1)S(1)}, bf16[264,128]{1,0:T(8,128)(2,1)S(1)}, u32[]{:S(2)}, u32[]{:S(2)}) collective-permute-start(bf16[264,128]{1,0:T(8,128)(2,1)S(1)} %get-tuple-element.46), channel_id=1, source_target_pairs={{0,2},{1,3},{2,0},{3,1},{4,6},{5,7},{6,4},{7,5},{8,10},{9,11},{10,... | collective-permute-start | bytes 202760 | tf_op jit(solution)/shard_map/ppermute | solution.py:452
  21.6 3.5 %collective-permute-start.12 = (bf16[264,128]{1,0:T(8,128)(2,1)S(1)}, bf16[264,128]{1,0:T(8,128)(2,1)S(1)}, u32[]{:S(2)}, u32[]{:S(2)}) collective-permute-start(bf16[264,128]{1,0:T(8,128)(2,1)S(1)} %get-tuple-element.47), channel_id=1, source_target_pairs={{0,6},{1,7},{2,4},{3,5},{4,2},{5,3},{6,0},{7,1},{8,14},{9,15},{10,... | collective-permute-start | bytes 202760 | tf_op jit(solution)/shard_map/ppermute | solution.py:452
  25.2 2.2 %collective-permute-start.14 = (bf16[264,128]{1,0:T(8,128)(2,1)S(1)}, bf16[264,128]{1,0:T(8,128)(2,1)S(1)}, u32[]{:S(2)}, u32[]{:S(2)}) collective-permute-start(bf16[264,128]{1,0:T(8,128)(2,1)S(1)} %get-tuple-element.45.refs_3_), channel_id=1, source_target_pairs={{0,1},{1,0},{2,3},{3,2},{4,5},{5,4},{6,7},{7,6},{8,9},{9,8},{10,11... | collective-permute-start | bytes 202760 | tf_op jit(solution)/shard_map/ppermute | solution.py:452
  27.7 1.3 %collective-permute-start.7 = (bf16[264,128]{1,0:T(8,128)(2,1)S(1)}, bf16[264,128]{1,0:T(8,128)(2,1)S(1)}, u32[]{:S(2)}, u32[]{:S(2)}) collective-permute-start(bf16[264,128]{1,0:T(8,128)(2,1)S(1)} %get-tuple-element.50), channel_id=1, source_target_pairs={{0,2},{1,3},{2,0},{3,1},{4,6},{5,7},{6,4},{7,5},{8,10},{9,11},{10,... | collective-permute-start | bytes 202760 | tf_op jit(solution)/shard_map/ppermute | solution.py:452
  29.3 1.7 %collective-permute-start.6 = (bf16[264,128]{1,0:T(8,128)(2,1)S(1)}, bf16[264,128]{1,0:T(8,128)(2,1)S(1)}, u32[]{:S(2)}, u32[]{:S(2)}) collective-permute-start(bf16[264,128]{1,0:T(8,128)(2,1)S(1)} %get-tuple-element.51), channel_id=1, source_target_pairs={{0,6},{1,7},{2,4},{3,5},{4,2},{5,3},{6,0},{7,1},{8,14},{9,15},{10,... | collective-permute-start | bytes 202760 | tf_op jit(solution)/shard_map/ppermute | solution.py:452
  31.1 0.5 %out_m0_o0.1.refs_12_ = bf16[2,128,256]{2,1,0:T(8,128)(2,1)S(1)} custom-call(bf16[128,4096]{1,0:T(8,128)(2,1)S(1)} %copy-done, f32[16,4,128]{2,1,0:T(4,128)S(1)} %cum.1.cum_ref.refs_1_, f32[1,4096]{1,0:T(1,128)S(1)} %bitcast.27, bf16[264,128]{1,0:T(8,128)(2,1)S(1)} %get-tuple-element.45.refs_3_, f32[17,128,128]{2,1,0:T(8,128)S(1)} %intra_mine.1.refs_4_.refs_7_.refs_10_, ...), custom_call_target="tpu_custom_call" | custom-call | flops 1 | bytes 1 | tf_op jit(solution)/shard_map/out_m0_o0/pallas_call | solution.py:46
  31.6 1.6 %collective-permute-start.18 = (bf16[264,128]{1,0:T(8,128)(2,1)S(1)}, bf16[264,128]{1,0:T(8,128)(2,1)S(1)}, u32[]{:S(2)}, u32[]{:S(2)}) collective-permute-start(bf16[264,128]{1,0:T(8,128)(2,1)S(1)} %collective-permute-done.11.refs_3_), channel_id=1, source_target_pairs={{0,1},{1,0},{2,3},{3,2},{4,5},{5,4},{6,7},{7,6},{8,9},{9,8},{10,11... | collective-permute-start | bytes 202760 | tf_op jit(solution)/shard_map/ppermute | solution.py:452
  33.3 0.5 %out_m4_o4.1.refs_15_ = bf16[2,128,256]{2,1,0:T(8,128)(2,1)S(1)} custom-call(bf16[128,4096]{1,0:T(8,128)(2,1)S(1)} %copy-done, f32[16,4,128]{2,1,0:T(4,128)S(1)} %cum.1.cum_ref.refs_1_, f32[1,4096]{1,0:T(1,128)S(1)} %bitcast.28, bf16[264,128]{1,0:T(8,128)(2,1)S(1)} %get-tuple-element.49.refs_3_, f32[17,128,128]{2,1,0:T(8,128)S(1)} %intra_mine.1.refs_4_.refs_7_.refs_10_, ...), custom_call_target="tpu_custom_call" | custom-call | flops 1 | bytes 1 | tf_op jit(solution)/shard_map/out_m4_o4/pallas_call | solution.py:46
  33.8 0.6 %out_m2_m3_m1.1.refs_14_ = bf16[3,128,256]{2,1,0:T(8,128)(2,1)S(1)} custom-call(bf16[128,4096]{1,0:T(8,128)(2,1)S(1)} %copy-done, f32[16,4,128]{2,1,0:T(4,128)S(1)} %cum.1.cum_ref.refs_1_, f32[1,4096]{1,0:T(1,128)S(1)} %bitcast.29, bf16[264,128]{1,0:T(8,128)(2,1)S(1)} %collective-permute-done.11.refs_3_, ...), custom_call_target="tpu_custom_call" | custom-call | flops 1 | bytes 1 | tf_op jit(solution)/shard_map/out_m2_m3_m1/pallas_call | solution.py:46
  35.1 1.7 %collective-permute-start.15 = (bf16[264,128]{1,0:T(8,128)(2,1)S(1)}, bf16[264,128]{1,0:T(8,128)(2,1)S(1)}, u32[]{:S(2)}, u32[]{:S(2)}) collective-permute-start(bf16[264,128]{1,0:T(8,128)(2,1)S(1)} %collective-permute-done.5.refs_3_), channel_id=1, source_target_pairs={{0,1},{1,0},{2,3},{3,2},{4,5},{5,4},{6,7},{7,6},{8,9},{9,8},{10,11... | collective-permute-start | bytes 202760 | tf_op jit(solution)/shard_map/ppermute | solution.py:452
  36.8 0.5 %collective-permute-start.17 = (bf16[264,128]{1,0:T(8,128)(2,1)S(1)}, bf16[264,128]{1,0:T(8,128)(2,1)S(1)}, u32[]{:S(2)}, u32[]{:S(2)}) collective-permute-start(bf16[264,128]{1,0:T(8,128)(2,1)S(1)} %collective-permute-done.7.refs_9_), channel_id=1, source_target_pairs={{0,1},{1,0},{2,3},{3,2},{4,5},{5,4},{6,7},{7,6},{8,9},{9,8},{10,11... | collective-permute-start | bytes 202760 | tf_op jit(solution)/shard_map/ppermute | solution.py:452
  37.3 0.6 %out_m6_m7_m5.1.refs_16_ = bf16[3,128,256]{2,1,0:T(8,128)(2,1)S(1)} custom-call(bf16[128,4096]{1,0:T(8,128)(2,1)S(1)} %copy-done, f32[16,4,128]{2,1,0:T(4,128)S(1)} %cum.1.cum_ref.refs_1_, f32[1,4096]{1,0:T(1,128)S(1)} %bitcast.30, bf16[264,128]{1,0:T(8,128)(2,1)S(1)} %collective-permute-done.5.refs_3_, ...), custom_call_target="tpu_custom_call" | custom-call | flops 1 | bytes 1 | tf_op jit(solution)/shard_map/out_m6_m7_m5/pallas_call | solution.py:46
  38.0 0.6 %out_o2_o3_o1.1.refs_13_ = bf16[3,128,256]{2,1,0:T(8,128)(2,1)S(1)} custom-call(bf16[128,4096]{1,0:T(8,128)(2,1)S(1)} %copy-done, f32[16,4,128]{2,1,0:T(4,128)S(1)} %cum.1.cum_ref.refs_1_, f32[1,4096]{1,0:T(1,128)S(1)} %bitcast.31, bf16[264,128]{1,0:T(8,128)(2,1)S(1)} %collective-permute-done.18.refs_3_, ...), custom_call_target="tpu_custom_call" | custom-call | flops 1 | bytes 1 | tf_op jit(solution)/shard_map/out_o2_o3_o1/pallas_call | solution.py:46
  38.7 1.5 %out_o6_o7_o5.1 = bf16[128,4096]{1,0:T(8,128)(2,1)} custom-call(bf16[128,4096]{1,0:T(8,128)(2,1)S(1)} %copy-done, f32[16,4,128]{2,1,0:T(4,128)S(1)} %cum.1.cum_ref.refs_1_, f32[1,4096]{1,0:T(1,128)S(1)} %bitcast.32, bf16[264,128]{1,0:T(8,128)(2,1)S(1)} %collective-permute-done.15.refs_3_, f32[17,128,128]{2,1,0:T(8,128)S(1)} %intra_other.1.refs_7_.refs_4_.refs_10_, ...), custom_call_target="tpu_custom_call" | custom-call | flops 1 | bytes 1 | tf_op jit(solution)/shard_map/out_o6_o7_o5/pallas_call | solution.py:46
  (49 shorter events, 4.1 us)
Async XLA Ops:
  0.0 3.0 %copy-start.3 = (f32[4,4096]{1,0:T(4,128)S(1)}, f32[4,4096]{1,0:T(4,128)}, u32[]{:S(2)}) copy-start(f32[4,4096]{1,0:T(4,128)} %w_ref.5) | copy-start | bytes 196612
  2.9 2.0 %collective-permute-start = (bf16[8,280,128]{2,1,0:T(8,128)(2,1)S(1)}, bf16[8,280,128]{2,1,0:T(8,128)(2,1)S(1)}, u32[]{:S(2)}, u32[]{:S(2)}) collective-permute-start(bf16[8,280,128]{2,1,0:T(8,128)(2,1)S(1)} %states_other.1), channel_id=1, source_target_pairs={{0,1},{1,0},{2,3},{3,2},{4,5},{5,4},{6,7},{7,6},{8,9},{9,8},{10,11... | collective-permute-start | bytes 1720328 | tf_op jit(solution)/shard_map/ppermute | solution.py:452
  4.5 5.7 %copy-start = (bf16[128,4096]{1,0:T(8,128)(2,1)S(1)}, bf16[128,4096]{1,0:T(8,128)(2,1)}, u32[]{:S(2)}) copy-start(bf16[128,4096]{1,0:T(8,128)(2,1)} %refs_0_.11) | copy-start | bytes 3145732
  5.3 8.4 %collective-permute-start.3 = (bf16[2,280,128]{2,1,0:T(8,128)(2,1)S(1)}, bf16[2,280,128]{2,1,0:T(8,128)(2,1)S(1)}, u32[]{:S(2)}, u32[]{:S(2)}) collective-permute-start(bf16[2,280,128]{2,1,0:T(8,128)(2,1)S(1)} %get-tuple-element.41), channel_id=1, source_target_pairs={{0,2},{1,3},{2,0},{3,1},{4,6},{5,7},{6,4},{7,5},{8,10},{9,11},{10,... | collective-permute-start | bytes 430088 | tf_op jit(solution)/shard_map/ppermute | solution.py:452
  7.8 6.0 %collective-permute-start.2 = (bf16[2,280,128]{2,1,0:T(8,128)(2,1)S(1)}, bf16[2,280,128]{2,1,0:T(8,128)(2,1)S(1)}, u32[]{:S(2)}, u32[]{:S(2)}) collective-permute-start(bf16[2,280,128]{2,1,0:T(8,128)(2,1)S(1)} %get-tuple-element.42), channel_id=1, source_target_pairs={{0,6},{1,7},{2,4},{3,5},{4,2},{5,3},{6,0},{7,1},{8,14},{9,15},{10,... | collective-permute-start | bytes 430088 | tf_op jit(solution)/shard_map/ppermute | solution.py:452
  9.0 6.7 %collective-permute-start.1 = (bf16[2,280,128]{2,1,0:T(8,128)(2,1)S(1)}, bf16[2,280,128]{2,1,0:T(8,128)(2,1)S(1)}, u32[]{:S(2)}, u32[]{:S(2)}) collective-permute-start(bf16[2,280,128]{2,1,0:T(8,128)(2,1)S(1)} %get-tuple-element.43), channel_id=1, source_target_pairs={{0,4},{1,5},{2,6},{3,7},{4,0},{5,1},{6,2},{7,3},{8,12},{9,13},{10,... | collective-permute-start | bytes 430088 | tf_op jit(solution)/shard_map/ppermute | solution.py:452
  9.1 18.6 %collective-permute-start.9 = (bf16[8,280,128]{2,1,0:T(8,128)(2,1)S(1)}, bf16[8,280,128]{2,1,0:T(8,128)(2,1)S(1)}, u32[]{:S(2)}, u32[]{:S(2)}) collective-permute-start(bf16[8,280,128]{2,1,0:T(8,128)(2,1)S(1)} %states_mine.1.own_ref), channel_id=1, source_target_pairs={{0,1},{1,0},{2,3},{3,2},{4,5},{5,4},{6,7},{7,6},{8,9},{9,8},{10,11... | collective-permute-start | bytes 1720328 | tf_op jit(solution)/shard_map/ppermute | solution.py:452
  16.0 4.1 %collective-permute-start.10 = (bf16[1,264,128]{2,1,0:T(8,128)(2,1)S(1)}, bf16[1,264,128]{2,1,0:T(8,128)(2,1)S(1)}, u32[]{:S(2)}, u32[]{:S(2)}) collective-permute-start(bf16[1,264,128]{2,1,0:T(8,128)(2,1)S(1)} %span_state.3), channel_id=1, source_target_pairs={{0,8},{1,9},{2,10},{3,11},{4,12},{5,13},{6,14},{7,15},{8,0},{9,1},... | collective-permute-start | bytes 202760 | tf_op jit(solution)/shard_map/ppermute | solution.py:452
  18.5 6.7 %collective-permute-start.4 = (bf16[1,264,128]{2,1,0:T(8,128)(2,1)S(1)}, bf16[1,264,128]{2,1,0:T(8,128)(2,1)S(1)}, u32[]{:S(2)}, u32[]{:S(2)}) collective-permute-start(bf16[1,264,128]{2,1,0:T(8,128)(2,1)S(1)} %span_state.2), channel_id=1, source_target_pairs={{0,8},{1,9},{2,10},{3,11},{4,12},{5,13},{6,14},{7,15},{8,0},{9,1},... | collective-permute-start | bytes 202760 | tf_op jit(solution)/shard_map/ppermute | solution.py:452
  20.4 10.7 %copy-start.4 = (f32[4096]{0:T(1024)S(1)}, f32[4096]{0:T(1024)}, u32[]{:S(2)}) copy-start(f32[4096]{0:T(1024)} %param.11) | copy-start | bytes 49156
  20.4 8.5 %collective-permute-start.13 = (bf16[264,128]{1,0:T(8,128)(2,1)S(1)}, bf16[264,128]{1,0:T(8,128)(2,1)S(1)}, u32[]{:S(2)}, u32[]{:S(2)}) collective-permute-start(bf16[264,128]{1,0:T(8,128)(2,1)S(1)} %get-tuple-element.46), channel_id=1, source_target_pairs={{0,2},{1,3},{2,0},{3,1},{4,6},{5,7},{6,4},{7,5},{8,10},{9,11},{10,... | collective-permute-start | bytes 202760 | tf_op jit(solution)/shard_map/ppermute | solution.py:452
  21.6 7.7 %collective-permute-start.12 = (bf16[264,128]{1,0:T(8,128)(2,1)S(1)}, bf16[264,128]{1,0:T(8,128)(2,1)S(1)}, u32[]{:S(2)}, u32[]{:S(2)}) collective-permute-start(bf16[264,128]{1,0:T(8,128)(2,1)S(1)} %get-tuple-element.47), channel_id=1, source_target_pairs={{0,6},{1,7},{2,4},{3,5},{4,2},{5,3},{6,0},{7,1},{8,14},{9,15},{10,... | collective-permute-start | bytes 202760 | tf_op jit(solution)/shard_map/ppermute | solution.py:452
  25.1 6.5 %collective-permute-start.11 = (bf16[264,128]{1,0:T(8,128)(2,1)S(1)}, bf16[264,128]{1,0:T(8,128)(2,1)S(1)}, u32[]{:S(2)}, u32[]{:S(2)}) collective-permute-start(bf16[264,128]{1,0:T(8,128)(2,1)S(1)} %get-tuple-element.48), channel_id=1, source_target_pairs={{0,4},{1,5},{2,6},{3,7},{4,0},{5,1},{6,2},{7,3},{8,12},{9,13},{10,... | collective-permute-start | bytes 202760 | tf_op jit(solution)/shard_map/ppermute | solution.py:452
  25.2 5.8 %collective-permute-start.14 = (bf16[264,128]{1,0:T(8,128)(2,1)S(1)}, bf16[264,128]{1,0:T(8,128)(2,1)S(1)}, u32[]{:S(2)}, u32[]{:S(2)}) collective-permute-start(bf16[264,128]{1,0:T(8,128)(2,1)S(1)} %get-tuple-element.45.refs_3_), channel_id=1, source_target_pairs={{0,1},{1,0},{2,3},{3,2},{4,5},{5,4},{6,7},{7,6},{8,9},{9,8},{10,11... | collective-permute-start | bytes 202760 | tf_op jit(solution)/shard_map/ppermute | solution.py:452
  27.7 6.8 %collective-permute-start.7 = (bf16[264,128]{1,0:T(8,128)(2,1)S(1)}, bf16[264,128]{1,0:T(8,128)(2,1)S(1)}, u32[]{:S(2)}, u32[]{:S(2)}) collective-permute-start(bf16[264,128]{1,0:T(8,128)(2,1)S(1)} %get-tuple-element.50), channel_id=1, source_target_pairs={{0,2},{1,3},{2,0},{3,1},{4,6},{5,7},{6,4},{7,5},{8,10},{9,11},{10,... | collective-permute-start | bytes 202760 | tf_op jit(solution)/shard_map/ppermute | solution.py:452
  29.0 4.2 %collective-permute-start.8 = (bf16[264,128]{1,0:T(8,128)(2,1)S(1)}, bf16[264,128]{1,0:T(8,128)(2,1)S(1)}, u32[]{:S(2)}, u32[]{:S(2)}) collective-permute-start(bf16[264,128]{1,0:T(8,128)(2,1)S(1)} %get-tuple-element.49.refs_3_), channel_id=1, source_target_pairs={{0,1},{1,0},{2,3},{3,2},{4,5},{5,4},{6,7},{7,6},{8,9},{9,8},{10,11... | collective-permute-start | bytes 202760 | tf_op jit(solution)/shard_map/ppermute | solution.py:452
  29.3 5.7 %collective-permute-start.6 = (bf16[264,128]{1,0:T(8,128)(2,1)S(1)}, bf16[264,128]{1,0:T(8,128)(2,1)S(1)}, u32[]{:S(2)}, u32[]{:S(2)}) collective-permute-start(bf16[264,128]{1,0:T(8,128)(2,1)S(1)} %get-tuple-element.51), channel_id=1, source_target_pairs={{0,6},{1,7},{2,4},{3,5},{4,2},{5,3},{6,0},{7,1},{8,14},{9,15},{10,... | collective-permute-start | bytes 202760 | tf_op jit(solution)/shard_map/ppermute | solution.py:452
  31.0 4.1 %collective-permute-start.5 = (bf16[264,128]{1,0:T(8,128)(2,1)S(1)}, bf16[264,128]{1,0:T(8,128)(2,1)S(1)}, u32[]{:S(2)}, u32[]{:S(2)}) collective-permute-start(bf16[264,128]{1,0:T(8,128)(2,1)S(1)} %get-tuple-element.52), channel_id=1, source_target_pairs={{0,4},{1,5},{2,6},{3,7},{4,0},{5,1},{6,2},{7,3},{8,12},{9,13},{10,... | collective-permute-start | bytes 202760 | tf_op jit(solution)/shard_map/ppermute | solution.py:452
  31.6 5.2 %collective-permute-start.18 = (bf16[264,128]{1,0:T(8,128)(2,1)S(1)}, bf16[264,128]{1,0:T(8,128)(2,1)S(1)}, u32[]{:S(2)}, u32[]{:S(2)}) collective-permute-start(bf16[264,128]{1,0:T(8,128)(2,1)S(1)} %collective-permute-done.11.refs_3_), channel_id=1, source_target_pairs={{0,1},{1,0},{2,3},{3,2},{4,5},{5,4},{6,7},{7,6},{8,9},{9,8},{10,11... | collective-permute-start | bytes 202760 | tf_op jit(solution)/shard_map/ppermute | solution.py:452
  33.2 4.8 %collective-permute-start.19 = (bf16[264,128]{1,0:T(8,128)(2,1)S(1)}, bf16[264,128]{1,0:T(8,128)(2,1)S(1)}, u32[]{:S(2)}, u32[]{:S(2)}) collective-permute-start(bf16[264,128]{1,0:T(8,128)(2,1)S(1)} %collective-permute-done.12.refs_6_), channel_id=1, source_target_pairs={{0,1},{1,0},{2,3},{3,2},{4,5},{5,4},{6,7},{7,6},{8,9},{9,8},{10,11... | collective-permute-start | bytes 202760 | tf_op jit(solution)/shard_map/ppermute | solution.py:452
  34.5 3.5 %collective-permute-start.20 = (bf16[264,128]{1,0:T(8,128)(2,1)S(1)}, bf16[264,128]{1,0:T(8,128)(2,1)S(1)}, u32[]{:S(2)}, u32[]{:S(2)}) collective-permute-start(bf16[264,128]{1,0:T(8,128)(2,1)S(1)} %collective-permute-done.13.refs_9_), channel_id=1, source_target_pairs={{0,1},{1,0},{2,3},{3,2},{4,5},{5,4},{6,7},{7,6},{8,9},{9,8},{10,11... | collective-permute-start | bytes 202760 | tf_op jit(solution)/shard_map/ppermute | solution.py:452
  35.1 3.6 %collective-permute-start.15 = (bf16[264,128]{1,0:T(8,128)(2,1)S(1)}, bf16[264,128]{1,0:T(8,128)(2,1)S(1)}, u32[]{:S(2)}, u32[]{:S(2)}) collective-permute-start(bf16[264,128]{1,0:T(8,128)(2,1)S(1)} %collective-permute-done.5.refs_3_), channel_id=1, source_target_pairs={{0,1},{1,0},{2,3},{3,2},{4,5},{5,4},{6,7},{7,6},{8,9},{9,8},{10,11... | collective-permute-start | bytes 202760 | tf_op jit(solution)/shard_map/ppermute | solution.py:452
  36.8 1.8 %collective-permute-start.16 = (bf16[264,128]{1,0:T(8,128)(2,1)S(1)}, bf16[264,128]{1,0:T(8,128)(2,1)S(1)}, u32[]{:S(2)}, u32[]{:S(2)}) collective-permute-start(bf16[264,128]{1,0:T(8,128)(2,1)S(1)} %collective-permute-done.6.refs_6_), channel_id=1, source_target_pairs={{0,1},{1,0},{2,3},{3,2},{4,5},{5,4},{6,7},{7,6},{8,9},{9,8},{10,11... | collective-permute-start | bytes 202760 | tf_op jit(solution)/shard_map/ppermute | solution.py:452
  36.8 1.8 %collective-permute-start.17 = (bf16[264,128]{1,0:T(8,128)(2,1)S(1)}, bf16[264,128]{1,0:T(8,128)(2,1)S(1)}, u32[]{:S(2)}, u32[]{:S(2)}) collective-permute-start(bf16[264,128]{1,0:T(8,128)(2,1)S(1)} %collective-permute-done.7.refs_9_), channel_id=1, source_target_pairs={{0,1},{1,0},{2,3},{3,2},{4,5},{5,4},{6,7},{7,6},{8,9},{9,8},{10,11... | collective-permute-start | bytes 202760 | tf_op jit(solution)/shard_map/ppermute | solution.py:452
  (3 other events, 9.0 us)

commit v13 on v12

--- a/solution.py
+++ b/solution.py
@@ -531,7 +531,7 @@
         )
         known = [shift(edge, SPAN)]
 
-    def joined(parts):
+    def joined(parts, packets):
         span = call(
             functools.partial(span_kernel, parts, heads, size),
             "span_state",
@@ -548,11 +548,11 @@
             reach *= 2
         return span, before
 
-    spans, befores = zip(*[joined(parts) for parts in SHIFTS])
-    q_after, _ = lax.optimization_barrier((queries, spans[-1]))
+    span, before = joined(SHIFTS[0], packets)
+    q_after, _ = lax.optimization_barrier((queries, span))
     intra_other = intra_part(False, q_after)
-    before, intra_other = lax.optimization_barrier((befores[-1], intra_other))
-    befores = [*befores[:-1], before]
+    packets_after, intra_other = lax.optimization_barrier((packets, intra_other))
+    befores = [before] + [joined(parts, packets_after)[1] for parts in SHIFTS[1:]]
     ahead = {
         part: (place, before)
         for parts, before in zip(SHIFTS, befores)

time: 40.4 us -> 40.7 us (level)
  waiting for transfers between devices: 5.07 us -> 5.58 us
    ppermute x21, waiting for transfers between devices: 5.07 us -> 5.58 us  [swap(): return lax.ppermute(x, 'ctx', [(i, i ^ mask) for i in range(n)])]
where the time goes in v13:
time: 40.7 us; the launch traced here: 40.6 us
  starting transfers between devices  21.8 us (54%)
  Pallas kernels  12.8 us (31%)
  waiting for transfers between devices  5.58 us (14%)
    ppermute x21, starting transfers between devices, swap(): return lax.ppermute(x, 'ctx', [(i, i ^ mask) for i in range(n)])  21.8 us
    pallas_call x16, Pallas kernels, call(): pl.pallas_call(kernel, out_shape=out_shape, in_specs=in_specs, out_specs=...  12.8 us
    ppermute x21, waiting for transfers between devices, swap(): return lax.ppermute(x, 'ctx', [(i, i ^ mask) for i in range(n)])  5.58 us
  transfers between devices with their start and end apart: 21, of which 5 were waited for; matrix products, arithmetic and copies ran while one was open for 0% of the time, Pallas kernels for 20%

profile of v13, /device:TPU:1, one launch (start us, length us, event | category | flops | bytes accessed | tf_op | source)
XLA Modules:
  0.0 40.6 jit_solution(11708762992073652866)
XLA Ops:
  0.0 2.8 %states_other.1 = bf16[8,280,128]{2,1,0:T(8,128)(2,1)S(1)} custom-call(bf16[128,4096]{1,0:T(8,128)(2,1)} %k_ref.5, bf16[128,4096]{1,0:T(8,128)(2,1)} %v_ref.5, f32[4,4096]{1,0:T(4,128)} %w_ref.5, f32[32,128]{1,0:T(8,128)} %bitcast.33), custom_call_target="tpu_custom_call" | custom-call | tf_op jit(solution)/shard_map/states_other/pallas_call | solution.py:46
  3.0 1.5 %states_mine.1.own_ref = bf16[8,280,128]{2,1,0:T(8,128)(2,1)S(1)} custom-call(bf16[128,4096]{1,0:T(8,128)(2,1)S(1)} %copy-done.1, bf16[128,4096]{1,0:T(8,128)(2,1)S(1)} %copy-done.2, f32[4,4096]{1,0:T(4,128)S(1)} %copy-done.3, f32[32,128]{1,0:T(8,128)S(1)} %bitcast.34), custom_call_target="tpu_custom_call" | custom-call | tf_op jit(solution)/shard_map/states_mine/pallas_call | solution.py:46
  5.3 2.4 %collective-permute-start.3 = (bf16[2,280,128]{2,1,0:T(8,128)(2,1)S(1)}, bf16[2,280,128]{2,1,0:T(8,128)(2,1)S(1)}, u32[]{:S(2)}, u32[]{:S(2)}) collective-permute-start(bf16[2,280,128]{2,1,0:T(8,128)(2,1)S(1)} %get-tuple-element.47), channel_id=1, source_target_pairs={{0,2},{1,3},{2,0},{3,1},{4,6},{5,7},{6,4},{7,5},{8,10},{9,11},{10,... | collective-permute-start | bytes 430088 | tf_op jit(solution)/shard_map/ppermute | solution.py:452
  7.8 1.2 %collective-permute-start.2 = (bf16[2,280,128]{2,1,0:T(8,128)(2,1)S(1)}, bf16[2,280,128]{2,1,0:T(8,128)(2,1)S(1)}, u32[]{:S(2)}, u32[]{:S(2)}) collective-permute-start(bf16[2,280,128]{2,1,0:T(8,128)(2,1)S(1)} %get-tuple-element.48), channel_id=1, source_target_pairs={{0,6},{1,7},{2,4},{3,5},{4,2},{5,3},{6,0},{7,1},{8,14},{9,15},{10,... | collective-permute-start | bytes 430088 | tf_op jit(solution)/shard_map/ppermute | solution.py:452
  9.1 0.9 %collective-permute-start.9 = (bf16[8,280,128]{2,1,0:T(8,128)(2,1)S(1)}, bf16[8,280,128]{2,1,0:T(8,128)(2,1)S(1)}, u32[]{:S(2)}, u32[]{:S(2)}) collective-permute-start(bf16[8,280,128]{2,1,0:T(8,128)(2,1)S(1)} %states_mine.1.own_ref), channel_id=1, source_target_pairs={{0,1},{1,0},{2,3},{3,2},{4,5},{5,4},{6,7},{7,6},{8,9},{9,8},{10,11... | collective-permute-start | bytes 1720328 | tf_op jit(solution)/shard_map/ppermute | solution.py:452
  10.2 1.1 %intra_mine.1.refs_4_.refs_7_.refs_10_ = f32[17,128,128]{2,1,0:T(8,128)S(1)} custom-call(bf16[128,4096]{1,0:T(8,128)(2,1)S(1)} %copy-done, bf16[128,4096]{1,0:T(8,128)(2,1)S(1)} %copy-done.1, bf16[128,4096]{1,0:T(8,128)(2,1)S(1)} %copy-done.2, f32[4,4096]{1,0:T(4,128)S(1)} %copy-done.3, f32[16,4,128]{2,1,0:T(4,128)S(1)} %cum.1.cum_ref.refs_1_), custom_call_target="tpu_custom_call" | custom-call | tf_op jit(solution)/shard_map/intra_mine/pallas_call | solution.py:46
  11.4 2.4 %collective-permute-done.3.refs_1_ = bf16[2,280,128]{2,1,0:T(8,128)(2,1)S(1)} collective-permute-done((bf16[2,280,128]{2,1,0:T(8,128)(2,1)S(1)}, bf16[2,280,128]{2,1,0:T(8,128)(2,1)S(1)}, u32[]{:S(2)}, u32[]{:S(2)}) %collective-permute-start.3) | collective-permute-done | bytes 143392 | tf_op jit(solution)/shard_map/ppermute | solution.py:452
  13.8 1.9 %collective-permute-done.1.refs_2_ = bf16[2,280,128]{2,1,0:T(8,128)(2,1)S(1)} collective-permute-done((bf16[2,280,128]{2,1,0:T(8,128)(2,1)S(1)}, bf16[2,280,128]{2,1,0:T(8,128)(2,1)S(1)}, u32[]{:S(2)}, u32[]{:S(2)}) %collective-permute-start.1) | collective-permute-done | bytes 143392 | tf_op jit(solution)/shard_map/ppermute | solution.py:452
  16.0 2.2 %collective-permute-start.10 = (bf16[1,264,128]{2,1,0:T(8,128)(2,1)S(1)}, bf16[1,264,128]{2,1,0:T(8,128)(2,1)S(1)}, u32[]{:S(2)}, u32[]{:S(2)}) collective-permute-start(bf16[1,264,128]{2,1,0:T(8,128)(2,1)S(1)} %span_state.2), channel_id=1, source_target_pairs={{0,8},{1,9},{2,10},{3,11},{4,12},{5,13},{6,14},{7,15},{8,0},{9,1},... | collective-permute-start | bytes 202760 | tf_op jit(solution)/shard_map/ppermute | solution.py:452
  18.2 1.1 %intra_other.1.refs_7_.refs_4_.refs_10_ = f32[17,128,128]{2,1,0:T(8,128)S(1)} custom-call(bf16[128,4096]{1,0:T(8,128)(2,1)S(1)} %copy-done, bf16[128,4096]{1,0:T(8,128)(2,1)S(1)} %copy-done.1, bf16[128,4096]{1,0:T(8,128)(2,1)S(1)} %copy-done.2, f32[4,4096]{1,0:T(4,128)S(1)} %copy-done.3, f32[16,4,128]{2,1,0:T(4,128)S(1)} %cum.1.cum_ref.refs_1_), custom_call_target="tpu_custom_call" | custom-call | tf_op jit(solution)/shard_map/intra_other/pallas_call | solution.py:46
  20.4 1.1 %collective-permute-start.13 = (bf16[264,128]{1,0:T(8,128)(2,1)S(1)}, bf16[264,128]{1,0:T(8,128)(2,1)S(1)}, u32[]{:S(2)}, u32[]{:S(2)}) collective-permute-start(bf16[264,128]{1,0:T(8,128)(2,1)S(1)} %get-tuple-element.52), channel_id=1, source_target_pairs={{0,2},{1,3},{2,0},{3,1},{4,6},{5,7},{6,4},{7,5},{8,10},{9,11},{10,... | collective-permute-start | bytes 202760 | tf_op jit(solution)/shard_map/ppermute | solution.py:452
  21.6 1.3 %collective-permute-start.12 = (bf16[264,128]{1,0:T(8,128)(2,1)S(1)}, bf16[264,128]{1,0:T(8,128)(2,1)S(1)}, u32[]{:S(2)}, u32[]{:S(2)}) collective-permute-start(bf16[264,128]{1,0:T(8,128)(2,1)S(1)} %get-tuple-element.53), channel_id=1, source_target_pairs={{0,6},{1,7},{2,4},{3,5},{4,2},{5,3},{6,0},{7,1},{8,14},{9,15},{10,... | collective-permute-start | bytes 202760 | tf_op jit(solution)/shard_map/ppermute | solution.py:452
  23.1 0.6 %collective-permute-done.4.refs_4_ = bf16[1,264,128]{2,1,0:T(8,128)(2,1)S(1)} collective-permute-done((bf16[1,264,128]{2,1,0:T(8,128)(2,1)S(1)}, bf16[1,264,128]{2,1,0:T(8,128)(2,1)S(1)}, u32[]{:S(2)}, u32[]{:S(2)}) %collective-permute-start.4) | collective-permute-done | bytes 67616 | tf_op jit(solution)/shard_map/ppermute | solution.py:452
  23.7 4.0 %collective-permute-start.14 = (bf16[264,128]{1,0:T(8,128)(2,1)S(1)}, bf16[264,128]{1,0:T(8,128)(2,1)S(1)}, u32[]{:S(2)}, u32[]{:S(2)}) collective-permute-start(bf16[264,128]{1,0:T(8,128)(2,1)S(1)} %get-tuple-element.51.refs_3_), channel_id=1, source_target_pairs={{0,1},{1,0},{2,3},{3,2},{4,5},{5,4},{6,7},{7,6},{8,9},{9,8},{10,11... | collective-permute-start | bytes 202760 | tf_op jit(solution)/shard_map/ppermute | solution.py:452
  28.0 1.3 %collective-permute-start.7 = (bf16[264,128]{1,0:T(8,128)(2,1)S(1)}, bf16[264,128]{1,0:T(8,128)(2,1)S(1)}, u32[]{:S(2)}, u32[]{:S(2)}) collective-permute-start(bf16[264,128]{1,0:T(8,128)(2,1)S(1)} %get-tuple-element.56), channel_id=1, source_target_pairs={{0,2},{1,3},{2,0},{3,1},{4,6},{5,7},{6,4},{7,5},{8,10},{9,11},{10,... | collective-permute-start | bytes 202760 | tf_op jit(solution)/shard_map/ppermute | solution.py:452
  29.6 1.7 %collective-permute-start.6 = (bf16[264,128]{1,0:T(8,128)(2,1)S(1)}, bf16[264,128]{1,0:T(8,128)(2,1)S(1)}, u32[]{:S(2)}, u32[]{:S(2)}) collective-permute-start(bf16[264,128]{1,0:T(8,128)(2,1)S(1)} %get-tuple-element.57), channel_id=1, source_target_pairs={{0,6},{1,7},{2,4},{3,5},{4,2},{5,3},{6,0},{7,1},{8,14},{9,15},{10,... | collective-permute-start | bytes 202760 | tf_op jit(solution)/shard_map/ppermute | solution.py:452
  31.4 0.5 %out_m0_o0.1.refs_12_ = bf16[2,128,256]{2,1,0:T(8,128)(2,1)S(1)} custom-call(bf16[128,4096]{1,0:T(8,128)(2,1)S(1)} %copy-done, f32[16,4,128]{2,1,0:T(4,128)S(1)} %cum.1.cum_ref.refs_1_, f32[1,4096]{1,0:T(1,128)S(1)} %bitcast.27, bf16[264,128]{1,0:T(8,128)(2,1)S(1)} %get-tuple-element.51.refs_3_, f32[17,128,128]{2,1,0:T(8,128)S(1)} %intra_mine.1.refs_4_.refs_7_.refs_10_, ...), custom_call_target="tpu_custom_call" | custom-call | flops 1 | bytes 1 | tf_op jit(solution)/shard_map/out_m0_o0/pallas_call | solution.py:46
  32.0 1.6 %collective-permute-start.18 = (bf16[264,128]{1,0:T(8,128)(2,1)S(1)}, bf16[264,128]{1,0:T(8,128)(2,1)S(1)}, u32[]{:S(2)}, u32[]{:S(2)}) collective-permute-start(bf16[264,128]{1,0:T(8,128)(2,1)S(1)} %collective-permute-done.11.refs_3_), channel_id=1, source_target_pairs={{0,1},{1,0},{2,3},{3,2},{4,5},{5,4},{6,7},{7,6},{8,9},{9,8},{10,11... | collective-permute-start | bytes 202760 | tf_op jit(solution)/shard_map/ppermute | solution.py:452
  33.6 0.5 %out_m4_o4.1.refs_15_ = bf16[2,128,256]{2,1,0:T(8,128)(2,1)S(1)} custom-call(bf16[128,4096]{1,0:T(8,128)(2,1)S(1)} %copy-done, f32[16,4,128]{2,1,0:T(4,128)S(1)} %cum.1.cum_ref.refs_1_, f32[1,4096]{1,0:T(1,128)S(1)} %bitcast.28, bf16[264,128]{1,0:T(8,128)(2,1)S(1)} %get-tuple-element.55.refs_3_, f32[17,128,128]{2,1,0:T(8,128)S(1)} %intra_mine.1.refs_4_.refs_7_.refs_10_, ...), custom_call_target="tpu_custom_call" | custom-call | flops 1 | bytes 1 | tf_op jit(solution)/shard_map/out_m4_o4/pallas_call | solution.py:46
  34.2 0.6 %out_m2_m3_m1.1.refs_14_ = bf16[3,128,256]{2,1,0:T(8,128)(2,1)S(1)} custom-call(bf16[128,4096]{1,0:T(8,128)(2,1)S(1)} %copy-done, f32[16,4,128]{2,1,0:T(4,128)S(1)} %cum.1.cum_ref.refs_1_, f32[1,4096]{1,0:T(1,128)S(1)} %bitcast.29, bf16[264,128]{1,0:T(8,128)(2,1)S(1)} %collective-permute-done.11.refs_3_, ...), custom_call_target="tpu_custom_call" | custom-call | flops 1 | bytes 1 | tf_op jit(solution)/shard_map/out_m2_m3_m1/pallas_call | solution.py:46
  35.3 1.9 %collective-permute-start.15 = (bf16[264,128]{1,0:T(8,128)(2,1)S(1)}, bf16[264,128]{1,0:T(8,128)(2,1)S(1)}, u32[]{:S(2)}, u32[]{:S(2)}) collective-permute-start(bf16[264,128]{1,0:T(8,128)(2,1)S(1)} %collective-permute-done.5.refs_3_), channel_id=1, source_target_pairs={{0,1},{1,0},{2,3},{3,2},{4,5},{5,4},{6,7},{7,6},{8,9},{9,8},{10,11... | collective-permute-start | bytes 202760 | tf_op jit(solution)/shard_map/ppermute | solution.py:452
  37.7 0.6 %out_m6_m7_m5.1.refs_16_ = bf16[3,128,256]{2,1,0:T(8,128)(2,1)S(1)} custom-call(bf16[128,4096]{1,0:T(8,128)(2,1)S(1)} %copy-done, f32[16,4,128]{2,1,0:T(4,128)S(1)} %cum.1.cum_ref.refs_1_, f32[1,4096]{1,0:T(1,128)S(1)} %bitcast.30, bf16[264,128]{1,0:T(8,128)(2,1)S(1)} %collective-permute-done.5.refs_3_, ...), custom_call_target="tpu_custom_call" | custom-call | flops 1 | bytes 1 | tf_op jit(solution)/shard_map/out_m6_m7_m5/pallas_call | solution.py:46
  38.4 0.6 %out_o2_o3_o1.1.refs_13_ = bf16[3,128,256]{2,1,0:T(8,128)(2,1)S(1)} custom-call(bf16[128,4096]{1,0:T(8,128)(2,1)S(1)} %copy-done, f32[16,4,128]{2,1,0:T(4,128)S(1)} %cum.1.cum_ref.refs_1_, f32[1,4096]{1,0:T(1,128)S(1)} %bitcast.31, bf16[264,128]{1,0:T(8,128)(2,1)S(1)} %collective-permute-done.18.refs_3_, ...), custom_call_target="tpu_custom_call" | custom-call | flops 1 | bytes 1 | tf_op jit(solution)/shard_map/out_o2_o3_o1/pallas_call | solution.py:46
  39.1 1.5 %out_o6_o7_o5.1 = bf16[128,4096]{1,0:T(8,128)(2,1)} custom-call(bf16[128,4096]{1,0:T(8,128)(2,1)S(1)} %copy-done, f32[16,4,128]{2,1,0:T(4,128)S(1)} %cum.1.cum_ref.refs_1_, f32[1,4096]{1,0:T(1,128)S(1)} %bitcast.32, bf16[264,128]{1,0:T(8,128)(2,1)S(1)} %collective-permute-done.15.refs_3_, f32[17,128,128]{2,1,0:T(8,128)S(1)} %intra_other.1.refs_7_.refs_4_.refs_10_, ...), custom_call_target="tpu_custom_call" | custom-call | flops 1 | bytes 1 | tf_op jit(solution)/shard_map/out_o6_o7_o5/pallas_call | solution.py:46
  (49 shorter events, 4.6 us)
Async XLA Ops:
  0.0 3.0 %copy-start.3 = (f32[4,4096]{1,0:T(4,128)S(1)}, f32[4,4096]{1,0:T(4,128)}, u32[]{:S(2)}) copy-start(f32[4,4096]{1,0:T(4,128)} %w_ref.5) | copy-start | bytes 196612
  2.9 2.0 %collective-permute-start = (bf16[8,280,128]{2,1,0:T(8,128)(2,1)S(1)}, bf16[8,280,128]{2,1,0:T(8,128)(2,1)S(1)}, u32[]{:S(2)}, u32[]{:S(2)}) collective-permute-start(bf16[8,280,128]{2,1,0:T(8,128)(2,1)S(1)} %states_other.1), channel_id=1, source_target_pairs={{0,1},{1,0},{2,3},{3,2},{4,5},{5,4},{6,7},{7,6},{8,9},{9,8},{10,11... | collective-permute-start | bytes 1720328 | tf_op jit(solution)/shard_map/ppermute | solution.py:452
  4.5 5.7 %copy-start = (bf16[128,4096]{1,0:T(8,128)(2,1)S(1)}, bf16[128,4096]{1,0:T(8,128)(2,1)}, u32[]{:S(2)}) copy-start(bf16[128,4096]{1,0:T(8,128)(2,1)} %refs_0_.11) | copy-start | bytes 3145732
  5.3 8.4 %collective-permute-start.3 = (bf16[2,280,128]{2,1,0:T(8,128)(2,1)S(1)}, bf16[2,280,128]{2,1,0:T(8,128)(2,1)S(1)}, u32[]{:S(2)}, u32[]{:S(2)}) collective-permute-start(bf16[2,280,128]{2,1,0:T(8,128)(2,1)S(1)} %get-tuple-element.47), channel_id=1, source_target_pairs={{0,2},{1,3},{2,0},{3,1},{4,6},{5,7},{6,4},{7,5},{8,10},{9,11},{10,... | collective-permute-start | bytes 430088 | tf_op jit(solution)/shard_map/ppermute | solution.py:452
  7.8 6.0 %collective-permute-start.2 = (bf16[2,280,128]{2,1,0:T(8,128)(2,1)S(1)}, bf16[2,280,128]{2,1,0:T(8,128)(2,1)S(1)}, u32[]{:S(2)}, u32[]{:S(2)}) collective-permute-start(bf16[2,280,128]{2,1,0:T(8,128)(2,1)S(1)} %get-tuple-element.48), channel_id=1, source_target_pairs={{0,6},{1,7},{2,4},{3,5},{4,2},{5,3},{6,0},{7,1},{8,14},{9,15},{10,... | collective-permute-start | bytes 430088 | tf_op jit(solution)/shard_map/ppermute | solution.py:452
  9.0 6.7 %collective-permute-start.1 = (bf16[2,280,128]{2,1,0:T(8,128)(2,1)S(1)}, bf16[2,280,128]{2,1,0:T(8,128)(2,1)S(1)}, u32[]{:S(2)}, u32[]{:S(2)}) collective-permute-start(bf16[2,280,128]{2,1,0:T(8,128)(2,1)S(1)} %get-tuple-element.49), channel_id=1, source_target_pairs={{0,4},{1,5},{2,6},{3,7},{4,0},{5,1},{6,2},{7,3},{8,12},{9,13},{10,... | collective-permute-start | bytes 430088 | tf_op jit(solution)/shard_map/ppermute | solution.py:452
  9.1 19.0 %collective-permute-start.9 = (bf16[8,280,128]{2,1,0:T(8,128)(2,1)S(1)}, bf16[8,280,128]{2,1,0:T(8,128)(2,1)S(1)}, u32[]{:S(2)}, u32[]{:S(2)}) collective-permute-start(bf16[8,280,128]{2,1,0:T(8,128)(2,1)S(1)} %states_mine.1.own_ref), channel_id=1, source_target_pairs={{0,1},{1,0},{2,3},{3,2},{4,5},{5,4},{6,7},{7,6},{8,9},{9,8},{10,11... | collective-permute-start | bytes 1720328 | tf_op jit(solution)/shard_map/ppermute | solution.py:452
  16.0 4.1 %collective-permute-start.10 = (bf16[1,264,128]{2,1,0:T(8,128)(2,1)S(1)}, bf16[1,264,128]{2,1,0:T(8,128)(2,1)S(1)}, u32[]{:S(2)}, u32[]{:S(2)}) collective-permute-start(bf16[1,264,128]{2,1,0:T(8,128)(2,1)S(1)} %span_state.2), channel_id=1, source_target_pairs={{0,8},{1,9},{2,10},{3,11},{4,12},{5,13},{6,14},{7,15},{8,0},{9,1},... | collective-permute-start | bytes 202760 | tf_op jit(solution)/shard_map/ppermute | solution.py:452
  19.6 4.1 %collective-permute-start.4 = (bf16[1,264,128]{2,1,0:T(8,128)(2,1)S(1)}, bf16[1,264,128]{2,1,0:T(8,128)(2,1)S(1)}, u32[]{:S(2)}, u32[]{:S(2)}) collective-permute-start(bf16[1,264,128]{2,1,0:T(8,128)(2,1)S(1)} %span_state.3), channel_id=1, source_target_pairs={{0,8},{1,9},{2,10},{3,11},{4,12},{5,13},{6,14},{7,15},{8,0},{9,1},... | collective-permute-start | bytes 202760 | tf_op jit(solution)/shard_map/ppermute | solution.py:452
  20.4 11.0 %copy-start.4 = (f32[4096]{0:T(1024)S(1)}, f32[4096]{0:T(1024)}, u32[]{:S(2)}) copy-start(f32[4096]{0:T(1024)} %param.11) | copy-start | bytes 49156
  20.4 8.9 %collective-permute-start.13 = (bf16[264,128]{1,0:T(8,128)(2,1)S(1)}, bf16[264,128]{1,0:T(8,128)(2,1)S(1)}, u32[]{:S(2)}, u32[]{:S(2)}) collective-permute-start(bf16[264,128]{1,0:T(8,128)(2,1)S(1)} %get-tuple-element.52), channel_id=1, source_target_pairs={{0,2},{1,3},{2,0},{3,1},{4,6},{5,7},{6,4},{7,5},{8,10},{9,11},{10,... | collective-permute-start | bytes 202760 | tf_op jit(solution)/shard_map/ppermute | solution.py:452
  21.6 8.0 %collective-permute-start.12 = (bf16[264,128]{1,0:T(8,128)(2,1)S(1)}, bf16[264,128]{1,0:T(8,128)(2,1)S(1)}, u32[]{:S(2)}, u32[]{:S(2)}) collective-permute-start(bf16[264,128]{1,0:T(8,128)(2,1)S(1)} %get-tuple-element.53), channel_id=1, source_target_pairs={{0,6},{1,7},{2,4},{3,5},{4,2},{5,3},{6,0},{7,1},{8,14},{9,15},{10,... | collective-permute-start | bytes 202760 | tf_op jit(solution)/shard_map/ppermute | solution.py:452
  22.9 9.0 %collective-permute-start.11 = (bf16[264,128]{1,0:T(8,128)(2,1)S(1)}, bf16[264,128]{1,0:T(8,128)(2,1)S(1)}, u32[]{:S(2)}, u32[]{:S(2)}) collective-permute-start(bf16[264,128]{1,0:T(8,128)(2,1)S(1)} %get-tuple-element.54), channel_id=1, source_target_pairs={{0,4},{1,5},{2,6},{3,7},{4,0},{5,1},{6,2},{7,3},{8,12},{9,13},{10,... | collective-permute-start | bytes 202760 | tf_op jit(solution)/shard_map/ppermute | solution.py:452
  23.7 7.6 %collective-permute-start.14 = (bf16[264,128]{1,0:T(8,128)(2,1)S(1)}, bf16[264,128]{1,0:T(8,128)(2,1)S(1)}, u32[]{:S(2)}, u32[]{:S(2)}) collective-permute-start(bf16[264,128]{1,0:T(8,128)(2,1)S(1)} %get-tuple-element.51.refs_3_), channel_id=1, source_target_pairs={{0,1},{1,0},{2,3},{3,2},{4,5},{5,4},{6,7},{7,6},{8,9},{9,8},{10,11... | collective-permute-start | bytes 202760 | tf_op jit(solution)/shard_map/ppermute | solution.py:452
  28.0 6.8 %collective-permute-start.7 = (bf16[264,128]{1,0:T(8,128)(2,1)S(1)}, bf16[264,128]{1,0:T(8,128)(2,1)S(1)}, u32[]{:S(2)}, u32[]{:S(2)}) collective-permute-start(bf16[264,128]{1,0:T(8,128)(2,1)S(1)} %get-tuple-element.56), channel_id=1, source_target_pairs={{0,2},{1,3},{2,0},{3,1},{4,6},{5,7},{6,4},{7,5},{8,10},{9,11},{10,... | collective-permute-start | bytes 202760 | tf_op jit(solution)/shard_map/ppermute | solution.py:452
  29.3 4.2 %collective-permute-start.8 = (bf16[264,128]{1,0:T(8,128)(2,1)S(1)}, bf16[264,128]{1,0:T(8,128)(2,1)S(1)}, u32[]{:S(2)}, u32[]{:S(2)}) collective-permute-start(bf16[264,128]{1,0:T(8,128)(2,1)S(1)} %get-tuple-element.55.refs_3_), channel_id=1, source_target_pairs={{0,1},{1,0},{2,3},{3,2},{4,5},{5,4},{6,7},{7,6},{8,9},{9,8},{10,11... | collective-permute-start | bytes 202760 | tf_op jit(solution)/shard_map/ppermute | solution.py:452
  29.6 5.7 %collective-permute-start.6 = (bf16[264,128]{1,0:T(8,128)(2,1)S(1)}, bf16[264,128]{1,0:T(8,128)(2,1)S(1)}, u32[]{:S(2)}, u32[]{:S(2)}) collective-permute-start(bf16[264,128]{1,0:T(8,128)(2,1)S(1)} %get-tuple-element.57), channel_id=1, source_target_pairs={{0,6},{1,7},{2,4},{3,5},{4,2},{5,3},{6,0},{7,1},{8,14},{9,15},{10,... | collective-permute-start | bytes 202760 | tf_op jit(solution)/shard_map/ppermute | solution.py:452
  31.3 4.0 %collective-permute-start.5 = (bf16[264,128]{1,0:T(8,128)(2,1)S(1)}, bf16[264,128]{1,0:T(8,128)(2,1)S(1)}, u32[]{:S(2)}, u32[]{:S(2)}) collective-permute-start(bf16[264,128]{1,0:T(8,128)(2,1)S(1)} %get-tuple-element.58), channel_id=1, source_target_pairs={{0,4},{1,5},{2,6},{3,7},{4,0},{5,1},{6,2},{7,3},{8,12},{9,13},{10,... | collective-permute-start | bytes 202760 | tf_op jit(solution)/shard_map/ppermute | solution.py:452
  32.0 5.2 %collective-permute-start.18 = (bf16[264,128]{1,0:T(8,128)(2,1)S(1)}, bf16[264,128]{1,0:T(8,128)(2,1)S(1)}, u32[]{:S(2)}, u32[]{:S(2)}) collective-permute-start(bf16[264,128]{1,0:T(8,128)(2,1)S(1)} %collective-permute-done.11.refs_3_), channel_id=1, source_target_pairs={{0,1},{1,0},{2,3},{3,2},{4,5},{5,4},{6,7},{7,6},{8,9},{9,8},{10,11... | collective-permute-start | bytes 202760 | tf_op jit(solution)/shard_map/ppermute | solution.py:452
  33.5 4.8 %collective-permute-start.19 = (bf16[264,128]{1,0:T(8,128)(2,1)S(1)}, bf16[264,128]{1,0:T(8,128)(2,1)S(1)}, u32[]{:S(2)}, u32[]{:S(2)}) collective-permute-start(bf16[264,128]{1,0:T(8,128)(2,1)S(1)} %collective-permute-done.12.refs_6_), channel_id=1, source_target_pairs={{0,1},{1,0},{2,3},{3,2},{4,5},{5,4},{6,7},{7,6},{8,9},{9,8},{10,11... | collective-permute-start | bytes 202760 | tf_op jit(solution)/shard_map/ppermute | solution.py:452
  34.8 3.5 %collective-permute-start.20 = (bf16[264,128]{1,0:T(8,128)(2,1)S(1)}, bf16[264,128]{1,0:T(8,128)(2,1)S(1)}, u32[]{:S(2)}, u32[]{:S(2)}) collective-permute-start(bf16[264,128]{1,0:T(8,128)(2,1)S(1)} %collective-permute-done.13.refs_9_), channel_id=1, source_target_pairs={{0,1},{1,0},{2,3},{3,2},{4,5},{5,4},{6,7},{7,6},{8,9},{9,8},{10,11... | collective-permute-start | bytes 202760 | tf_op jit(solution)/shard_map/ppermute | solution.py:452
  35.3 3.7 %collective-permute-start.15 = (bf16[264,128]{1,0:T(8,128)(2,1)S(1)}, bf16[264,128]{1,0:T(8,128)(2,1)S(1)}, u32[]{:S(2)}, u32[]{:S(2)}) collective-permute-start(bf16[264,128]{1,0:T(8,128)(2,1)S(1)} %collective-permute-done.5.refs_3_), channel_id=1, source_target_pairs={{0,1},{1,0},{2,3},{3,2},{4,5},{5,4},{6,7},{7,6},{8,9},{9,8},{10,11... | collective-permute-start | bytes 202760 | tf_op jit(solution)/shard_map/ppermute | solution.py:452
  37.2 1.8 %collective-permute-start.16 = (bf16[264,128]{1,0:T(8,128)(2,1)S(1)}, bf16[264,128]{1,0:T(8,128)(2,1)S(1)}, u32[]{:S(2)}, u32[]{:S(2)}) collective-permute-start(bf16[264,128]{1,0:T(8,128)(2,1)S(1)} %collective-permute-done.6.refs_6_), channel_id=1, source_target_pairs={{0,1},{1,0},{2,3},{3,2},{4,5},{5,4},{6,7},{7,6},{8,9},{9,8},{10,11... | collective-permute-start | bytes 202760 | tf_op jit(solution)/shard_map/ppermute | solution.py:452
  37.2 1.9 %collective-permute-start.17 = (bf16[264,128]{1,0:T(8,128)(2,1)S(1)}, bf16[264,128]{1,0:T(8,128)(2,1)S(1)}, u32[]{:S(2)}, u32[]{:S(2)}) collective-permute-start(bf16[264,128]{1,0:T(8,128)(2,1)S(1)} %collective-permute-done.7.refs_9_), channel_id=1, source_target_pairs={{0,1},{1,0},{2,3},{3,2},{4,5},{5,4},{6,7},{7,6},{8,9},{9,8},{10,11... | collective-permute-start | bytes 202760 | tf_op jit(solution)/shard_map/ppermute | solution.py:452
  (3 other events, 9.0 us)

commit v14 on v12

--- a/solution.py
+++ b/solution.py
@@ -13,10 +13,10 @@
 SPAN = 2 * CHIPS
 HALO = 8
 EXCHANGE = (2, 3, 1)
-CHUNKS = 2
+CHUNKS = 1
 UNITS = CHUNKS * CHIPS
-SHIFTS = ((0,), (1,))
-PARTS = 8
+SHIFTS = ((0,),)
+PARTS = 16
 VMEM = pl.BlockSpec(memory_space=pltpu.VMEM)
 HBM = pl.BlockSpec(memory_space=pltpu.HBM)
 
@@ -601,24 +601,21 @@
             **hints,
         )
 
-    earlier = []
-    for part in range(CHUNKS):
-        first = part * CHIPS
-        units = [first + g for g in EXCHANGE]
-        items = [(True, first), (False, first)]
-        made = [output(items)] + [x for _, x in earlier[-1:]]
-        late, made = lax.optimization_barrier(([own[u] for u in units], made))
-        earlier = earlier[:-1] + [(there, x) for (there, _), x in zip(earlier[-1:], made[1:])]
-        earlier.append((items, made[0]))
-        own.update(zip(units, late))
-        other.update({u: swap(own[u], 1) for u in units})
-        items = [(True, u) for u in units]
-        if part < CHUNKS - 1:
-            others = [(False, u) for u in units]
-            earlier += [(others, output(others)), (items, output(items))]
-        else:
-            earlier.append((items, output(items)))
-    return output([(False, u) for u in units], earlier)
+    final, *early = EXCHANGE
+    items = [(True, 0), (False, 0)]
+    made = output(items)
+    *late, made = lax.optimization_barrier((*[own[u] for u in early], made))
+    earlier = [(items, made)]
+    own.update(zip(early, late))
+    other.update({u: swap(own[u], 1) for u in early})
+    items = [(True, u) for u in early]
+    made = output(items)
+    own[final], made = lax.optimization_barrier((own[final], made))
+    earlier.append((items, made))
+    other[final] = swap(own[final], 1)
+    items = [(True, final)] + [(False, u) for u in early]
+    earlier.append((items, output(items)))
+    return output([(False, final)], earlier)
 
 
 def solution(mesh):

time: 40.4 us -> 39.3 us (0.973)
  waiting for transfers between devices: 5.07 us -> 14.7 us
  starting transfers between devices: 22 us -> 12.9 us
  Pallas kernels: 12.8 us -> 11 us
    ppermute x21 -> x13, waiting for transfers between devices: 5.07 us -> 14.7 us  [swap(): return lax.ppermute(x, 'ctx', [(i, i ^ mask) for i in range(n)])]
    ppermute x21 -> x13, starting transfers between devices: 22 us -> 12.9 us  [swap(): return lax.ppermute(x, 'ctx', [(i, i ^ mask) for i in range(n)])]
    pallas_call x16 -> x12, Pallas kernels: 12.8 us -> 11 us  [call(): pl.pallas_call(kernel, out_shape=out_shape, in_specs=in_specs, out_specs=...]
  transfers between devices with their start and end apart: 21 -> 13, of which waited for: 5 -> 6; matrix products, arithmetic and copies ran while one was open for 0% -> 0% of each run, Pallas kernels for 20% -> 17%
where the time goes in v14:
time: 39.3 us; the launch traced here: 38.9 us
  waiting for transfers between devices  14.7 us (37%)
  starting transfers between devices  12.9 us (33%)
  Pallas kernels  11 us (28%)
    ppermute x13, waiting for transfers between devices, swap(): return lax.ppermute(x, 'ctx', [(i, i ^ mask) for i in range(n)])  14.7 us
    ppermute x13, starting transfers between devices, swap(): return lax.ppermute(x, 'ctx', [(i, i ^ mask) for i in range(n)])  12.9 us
    pallas_call x12, Pallas kernels, call(): pl.pallas_call(kernel, out_shape=out_shape, in_specs=in_specs, out_specs=...  11 us
  transfers between devices with their start and end apart: 13, of which 6 were waited for; matrix products, arithmetic and copies ran while one was open for 0% of the time, Pallas kernels for 17%

profile of v14, /device:TPU:1, one launch (start us, length us, event | category | flops | bytes accessed | tf_op | source)
XLA Modules:
  0.0 38.9 jit_solution(13568466791807361877)
XLA Ops:
  0.0 2.7 %states_other.1 = bf16[4,560,128]{2,1,0:T(8,128)(2,1)S(1)} custom-call(bf16[128,4096]{1,0:T(8,128)(2,1)} %k_ref.5, bf16[128,4096]{1,0:T(8,128)(2,1)} %v_ref.5, f32[4,4096]{1,0:T(4,128)} %w_ref.5, f32[32,128]{1,0:T(8,128)} %bitcast.23), custom_call_target="tpu_custom_call" | custom-call | tf_op jit(solution)/shard_map/states_other/pallas_call | solution.py:46
  2.8 1.2 %states_mine.1.own_ref = bf16[4,560,128]{2,1,0:T(8,128)(2,1)S(1)} custom-call(bf16[128,4096]{1,0:T(8,128)(2,1)S(1)} %copy-done.1, bf16[128,4096]{1,0:T(8,128)(2,1)S(1)} %copy-done.2, f32[4,4096]{1,0:T(4,128)S(1)} %copy-done.3, f32[32,128]{1,0:T(8,128)S(1)} %bitcast.24), custom_call_target="tpu_custom_call" | custom-call | tf_op jit(solution)/shard_map/states_mine/pallas_call | solution.py:46
  4.0 0.7 %collective-permute-done.got_ref.refs_5_.refs_8_ = bf16[4,560,128]{2,1,0:T(8,128)(2,1)S(1)} collective-permute-done((bf16[4,560,128]{2,1,0:T(8,128)(2,1)S(1)}, bf16[4,560,128]{2,1,0:T(8,128)(2,1)S(1)}, u32[]{:S(2)}, u32[]{:S(2)}) %collective-permute-start) | collective-permute-done | bytes 573472 | tf_op jit(solution)/shard_map/ppermute | solution.py:452
  4.7 0.4 chip_states.1
  5.2 2.4 %collective-permute-start.3 = (bf16[1,560,128]{2,1,0:T(8,128)(2,1)S(1)}, bf16[1,560,128]{2,1,0:T(8,128)(2,1)S(1)}, u32[]{:S(2)}, u32[]{:S(2)}) collective-permute-start(bf16[1,560,128]{2,1,0:T(8,128)(2,1)S(1)} %get-tuple-element.33), channel_id=1, source_target_pairs={{0,2},{1,3},{2,0},{3,1},{4,6},{5,7},{6,4},{7,5},{8,10},{9,11},{10,... | collective-permute-start | bytes 430088 | tf_op jit(solution)/shard_map/ppermute | solution.py:452
  7.6 1.2 %collective-permute-start.2 = (bf16[1,560,128]{2,1,0:T(8,128)(2,1)S(1)}, bf16[1,560,128]{2,1,0:T(8,128)(2,1)S(1)}, u32[]{:S(2)}, u32[]{:S(2)}) collective-permute-start(bf16[1,560,128]{2,1,0:T(8,128)(2,1)S(1)} %get-tuple-element.34), channel_id=1, source_target_pairs={{0,6},{1,7},{2,4},{3,5},{4,2},{5,3},{6,0},{7,1},{8,14},{9,15},{10,... | collective-permute-start | bytes 430088 | tf_op jit(solution)/shard_map/ppermute | solution.py:452
  8.9 0.9 %collective-permute-start.9 = (bf16[4,560,128]{2,1,0:T(8,128)(2,1)S(1)}, bf16[4,560,128]{2,1,0:T(8,128)(2,1)S(1)}, u32[]{:S(2)}, u32[]{:S(2)}) collective-permute-start(bf16[4,560,128]{2,1,0:T(8,128)(2,1)S(1)} %states_mine.1.own_ref), channel_id=1, source_target_pairs={{0,1},{1,0},{2,3},{3,2},{4,5},{5,4},{6,7},{7,6},{8,9},{9,8},{10,11... | collective-permute-start | bytes 1720328 | tf_op jit(solution)/shard_map/ppermute | solution.py:452
  10.0 1.1 %intra_mine.1.refs_4_.refs_7_ = f32[17,128,128]{2,1,0:T(8,128)S(1)} custom-call(bf16[128,4096]{1,0:T(8,128)(2,1)S(1)} %copy-done, bf16[128,4096]{1,0:T(8,128)(2,1)S(1)} %copy-done.1, bf16[128,4096]{1,0:T(8,128)(2,1)S(1)} %copy-done.2, f32[4,4096]{1,0:T(4,128)S(1)} %copy-done.3, f32[8,8,128]{2,1,0:T(8,128)S(1)} %cum.1.cum_ref.refs_1_), custom_call_target="tpu_custom_call" | custom-call | tf_op jit(solution)/shard_map/intra_mine/pallas_call | solution.py:46
  11.1 2.5 %collective-permute-done.3.refs_1_ = bf16[1,560,128]{2,1,0:T(8,128)(2,1)S(1)} collective-permute-done((bf16[1,560,128]{2,1,0:T(8,128)(2,1)S(1)}, bf16[1,560,128]{2,1,0:T(8,128)(2,1)S(1)}, u32[]{:S(2)}, u32[]{:S(2)}) %collective-permute-start.3) | collective-permute-done | bytes 143392 | tf_op jit(solution)/shard_map/ppermute | solution.py:452
  13.6 1.9 %collective-permute-done.1.refs_2_ = bf16[1,560,128]{2,1,0:T(8,128)(2,1)S(1)} collective-permute-done((bf16[1,560,128]{2,1,0:T(8,128)(2,1)S(1)}, bf16[1,560,128]{2,1,0:T(8,128)(2,1)S(1)}, u32[]{:S(2)}, u32[]{:S(2)}) %collective-permute-start.1) | collective-permute-done | bytes 143392 | tf_op jit(solution)/shard_map/ppermute | solution.py:452
  15.9 2.2 %collective-permute-start.4 = (bf16[1,528,128]{2,1,0:T(8,128)(2,1)S(1)}, bf16[1,528,128]{2,1,0:T(8,128)(2,1)S(1)}, u32[]{:S(2)}, u32[]{:S(2)}) collective-permute-start(bf16[1,528,128]{2,1,0:T(8,128)(2,1)S(1)} %span_state.1), channel_id=1, source_target_pairs={{0,8},{1,9},{2,10},{3,11},{4,12},{5,13},{6,14},{7,15},{8,0},{9,1},... | collective-permute-start | bytes 405512 | tf_op jit(solution)/shard_map/ppermute | solution.py:452
  18.1 1.1 %intra_other.1.refs_7_.refs_10_.refs_4_ = f32[17,128,128]{2,1,0:T(8,128)S(1)} custom-call(bf16[128,4096]{1,0:T(8,128)(2,1)S(1)} %copy-done, bf16[128,4096]{1,0:T(8,128)(2,1)S(1)} %copy-done.1, bf16[128,4096]{1,0:T(8,128)(2,1)S(1)} %copy-done.2, f32[4,4096]{1,0:T(4,128)S(1)} %copy-done.3, f32[8,8,128]{2,1,0:T(8,128)S(1)} %cum.1.cum_ref.refs_1_), custom_call_target="tpu_custom_call" | custom-call | tf_op jit(solution)/shard_map/intra_other/pallas_call | solution.py:46
  19.2 5.2 %collective-permute-done.4.refs_4_ = bf16[1,528,128]{2,1,0:T(8,128)(2,1)S(1)} collective-permute-done((bf16[1,528,128]{2,1,0:T(8,128)(2,1)S(1)}, bf16[1,528,128]{2,1,0:T(8,128)(2,1)S(1)}, u32[]{:S(2)}, u32[]{:S(2)}) %collective-permute-start.4) | collective-permute-done | bytes 135200 | tf_op jit(solution)/shard_map/ppermute | solution.py:452
  24.3 0.4 chip_prefix.1
  24.8 1.5 %collective-permute-start.8 = (bf16[528,128]{1,0:T(8,128)(2,1)S(1)}, bf16[528,128]{1,0:T(8,128)(2,1)S(1)}, u32[]{:S(2)}, u32[]{:S(2)}) collective-permute-start(bf16[528,128]{1,0:T(8,128)(2,1)S(1)} %get-tuple-element.37.refs_3_), channel_id=1, source_target_pairs={{0,1},{1,0},{2,3},{3,2},{4,5},{5,4},{6,7},{7,6},{8,9},{9,8},{10,11... | collective-permute-start | bytes 405512 | tf_op jit(solution)/shard_map/ppermute | solution.py:452
  26.2 1.1 %collective-permute-start.7 = (bf16[528,128]{1,0:T(8,128)(2,1)S(1)}, bf16[528,128]{1,0:T(8,128)(2,1)S(1)}, u32[]{:S(2)}, u32[]{:S(2)}) collective-permute-start(bf16[528,128]{1,0:T(8,128)(2,1)S(1)} %get-tuple-element.38), channel_id=1, source_target_pairs={{0,2},{1,3},{2,0},{3,1},{4,6},{5,7},{6,4},{7,5},{8,10},{9,11},{10,... | collective-permute-start | bytes 405512 | tf_op jit(solution)/shard_map/ppermute | solution.py:452
  27.7 1.2 %collective-permute-start.5 = (bf16[528,128]{1,0:T(8,128)(2,1)S(1)}, bf16[528,128]{1,0:T(8,128)(2,1)S(1)}, u32[]{:S(2)}, u32[]{:S(2)}) collective-permute-start(bf16[528,128]{1,0:T(8,128)(2,1)S(1)} %get-tuple-element.40), channel_id=1, source_target_pairs={{0,4},{1,5},{2,6},{3,7},{4,0},{5,1},{6,2},{7,3},{8,12},{9,13},{10,... | collective-permute-start | bytes 405512 | tf_op jit(solution)/shard_map/ppermute | solution.py:452
  28.9 0.7 %out_m0_o0.1.refs_6_ = bf16[2,128,512]{2,1,0:T(8,128)(2,1)S(1)} custom-call(bf16[128,4096]{1,0:T(8,128)(2,1)S(1)} %copy-done, f32[8,8,128]{2,1,0:T(8,128)S(1)} %cum.1.cum_ref.refs_1_, f32[1,4096]{1,0:T(1,128)S(1)} %bitcast.19, bf16[528,128]{1,0:T(8,128)(2,1)S(1)} %get-tuple-element.37.refs_3_, f32[17,128,128]{2,1,0:T(8,128)S(1)} %intra_mine.1.refs_4_.refs_7_, ...), custom_call_target="tpu_custom_call" | custom-call | flops 1 | bytes 1 | tf_op jit(solution)/shard_map/out_m0_o0/pallas_call | solution.py:46
  29.6 4.3 %collective-permute-done.7.refs_6_ = bf16[528,128]{1,0:T(8,128)(2,1)S(1)} collective-permute-done((bf16[528,128]{1,0:T(8,128)(2,1)S(1)}, bf16[528,128]{1,0:T(8,128)(2,1)S(1)}, u32[]{:S(2)}, u32[]{:S(2)}) %collective-permute-start.7) | collective-permute-done | bytes 135200 | tf_op jit(solution)/shard_map/ppermute | solution.py:452
  33.9 1.2 %collective-permute-start.11 = (bf16[528,128]{1,0:T(8,128)(2,1)S(1)}, bf16[528,128]{1,0:T(8,128)(2,1)S(1)}, u32[]{:S(2)}, u32[]{:S(2)}) collective-permute-start(bf16[528,128]{1,0:T(8,128)(2,1)S(1)} %collective-permute-done.6.refs_3_), channel_id=1, source_target_pairs={{0,1},{1,0},{2,3},{3,2},{4,5},{5,4},{6,7},{7,6},{8,9},{9,8},{10,11... | collective-permute-start | bytes 405512 | tf_op jit(solution)/shard_map/ppermute | solution.py:452
  35.2 0.7 %out_m3_m1.1.refs_7_ = bf16[2,128,512]{2,1,0:T(8,128)(2,1)S(1)} custom-call(bf16[128,4096]{1,0:T(8,128)(2,1)S(1)} %copy-done, f32[8,8,128]{2,1,0:T(8,128)S(1)} %cum.1.cum_ref.refs_1_, f32[1,4096]{1,0:T(1,128)S(1)} %bitcast.20, bf16[528,128]{1,0:T(8,128)(2,1)S(1)} %collective-permute-done.6.refs_3_, f32[17,128,128]{2,1,0:T(8,128)S(1)} %intra_mine.1.refs_4_.refs_7_, ...), custom_call_target="tpu_custom_call" | custom-call | flops 1 | bytes 1 | tf_op jit(solution)/shard_map/out_m3_m1/pallas_call | solution.py:46
  35.9 0.6 %collective-permute-start.10 = (bf16[528,128]{1,0:T(8,128)(2,1)S(1)}, bf16[528,128]{1,0:T(8,128)(2,1)S(1)}, u32[]{:S(2)}, u32[]{:S(2)}) collective-permute-start(bf16[528,128]{1,0:T(8,128)(2,1)S(1)} %collective-permute-done.5.refs_3_), channel_id=1, source_target_pairs={{0,1},{1,0},{2,3},{3,2},{4,5},{5,4},{6,7},{7,6},{8,9},{9,8},{10,11... | collective-permute-start | bytes 405512 | tf_op jit(solution)/shard_map/ppermute | solution.py:452
  36.5 0.9 %out_m2_o3_o1.1.refs_8_ = bf16[3,128,512]{2,1,0:T(8,128)(2,1)S(1)} custom-call(bf16[128,4096]{1,0:T(8,128)(2,1)S(1)} %copy-done, f32[8,8,128]{2,1,0:T(8,128)S(1)} %cum.1.cum_ref.refs_1_, f32[1,4096]{1,0:T(1,128)S(1)} %bitcast.21, bf16[528,128]{1,0:T(8,128)(2,1)S(1)} %collective-permute-done.5.refs_3_, f32[17,128,128]{2,1,0:T(8,128)S(1)} %intra_mine.1.refs_4_.refs_7_, ...), custom_call_target="tpu_custom_call" | custom-call | flops 1 | bytes 1 | tf_op jit(solution)/shard_map/out_m2_o3_o1/pallas_call | solution.py:46
  37.4 1.4 %out_o2.1 = bf16[128,4096]{1,0:T(8,128)(2,1)} custom-call(bf16[128,4096]{1,0:T(8,128)(2,1)S(1)} %copy-done, f32[8,8,128]{2,1,0:T(8,128)S(1)} %cum.1.cum_ref.refs_1_, f32[1,4096]{1,0:T(1,128)S(1)} %bitcast.22, bf16[528,128]{1,0:T(8,128)(2,1)S(1)} %collective-permute-done.10.refs_3_, f32[17,128,128]{2,1,0:T(8,128)S(1)} %intra_other.1.refs_7_.refs_10_.refs_4_, ...), custom_call_target="tpu_custom_call" | custom-call | flops 1 | bytes 1 | tf_op jit(solution)/shard_map/out_o2/pallas_call | solution.py:46
  (28 shorter events, 1.3 us)
Async XLA Ops:
  0.0 2.8 %copy-start.1 = (bf16[128,4096]{1,0:T(8,128)(2,1)S(1)}, bf16[128,4096]{1,0:T(8,128)(2,1)}, u32[]{:S(2)}) copy-start(bf16[128,4096]{1,0:T(8,128)(2,1)} %k_ref.5) | copy-start | bytes 3145732
  0.0 2.8 %copy-start.2 = (bf16[128,4096]{1,0:T(8,128)(2,1)S(1)}, bf16[128,4096]{1,0:T(8,128)(2,1)}, u32[]{:S(2)}) copy-start(bf16[128,4096]{1,0:T(8,128)(2,1)} %v_ref.5) | copy-start | bytes 3145732
  0.0 2.8 %copy-start.3 = (f32[4,4096]{1,0:T(4,128)S(1)}, f32[4,4096]{1,0:T(4,128)}, u32[]{:S(2)}) copy-start(f32[4,4096]{1,0:T(4,128)} %w_ref.5) | copy-start | bytes 196612
  0.0 2.8 %copy-start.5 = (f32[128,32]{0,1:T(8,128)S(1)}, f32[128,32]{0,1:T(8,128)}, u32[]{:S(2)}) copy-start(f32[128,32]{0,1:T(8,128)} %param.9) | copy-start | bytes 49156
  2.7 2.0 %collective-permute-start = (bf16[4,560,128]{2,1,0:T(8,128)(2,1)S(1)}, bf16[4,560,128]{2,1,0:T(8,128)(2,1)S(1)}, u32[]{:S(2)}, u32[]{:S(2)}) collective-permute-start(bf16[4,560,128]{2,1,0:T(8,128)(2,1)S(1)} %states_other.1), channel_id=1, source_target_pairs={{0,1},{1,0},{2,3},{3,2},{4,5},{5,4},{6,7},{7,6},{8,9},{9,8},{10,11... | collective-permute-start | bytes 1720328 | tf_op jit(solution)/shard_map/ppermute | solution.py:452
  4.0 6.0 %copy-start = (bf16[128,4096]{1,0:T(8,128)(2,1)S(1)}, bf16[128,4096]{1,0:T(8,128)(2,1)}, u32[]{:S(2)}) copy-start(bf16[128,4096]{1,0:T(8,128)(2,1)} %refs_0_.7) | copy-start | bytes 3145732
  5.2 8.4 %collective-permute-start.3 = (bf16[1,560,128]{2,1,0:T(8,128)(2,1)S(1)}, bf16[1,560,128]{2,1,0:T(8,128)(2,1)S(1)}, u32[]{:S(2)}, u32[]{:S(2)}) collective-permute-start(bf16[1,560,128]{2,1,0:T(8,128)(2,1)S(1)} %get-tuple-element.33), channel_id=1, source_target_pairs={{0,2},{1,3},{2,0},{3,1},{4,6},{5,7},{6,4},{7,5},{8,10},{9,11},{10,... | collective-permute-start | bytes 430088 | tf_op jit(solution)/shard_map/ppermute | solution.py:452
  7.6 6.0 %collective-permute-start.2 = (bf16[1,560,128]{2,1,0:T(8,128)(2,1)S(1)}, bf16[1,560,128]{2,1,0:T(8,128)(2,1)S(1)}, u32[]{:S(2)}, u32[]{:S(2)}) collective-permute-start(bf16[1,560,128]{2,1,0:T(8,128)(2,1)S(1)} %get-tuple-element.34), channel_id=1, source_target_pairs={{0,6},{1,7},{2,4},{3,5},{4,2},{5,3},{6,0},{7,1},{8,14},{9,15},{10,... | collective-permute-start | bytes 430088 | tf_op jit(solution)/shard_map/ppermute | solution.py:452
  8.8 6.7 %collective-permute-start.1 = (bf16[1,560,128]{2,1,0:T(8,128)(2,1)S(1)}, bf16[1,560,128]{2,1,0:T(8,128)(2,1)S(1)}, u32[]{:S(2)}, u32[]{:S(2)}) collective-permute-start(bf16[1,560,128]{2,1,0:T(8,128)(2,1)S(1)} %get-tuple-element.35), channel_id=1, source_target_pairs={{0,4},{1,5},{2,6},{3,7},{4,0},{5,1},{6,2},{7,3},{8,12},{9,13},{10,... | collective-permute-start | bytes 430088 | tf_op jit(solution)/shard_map/ppermute | solution.py:452
  8.9 20.0 %collective-permute-start.9 = (bf16[4,560,128]{2,1,0:T(8,128)(2,1)S(1)}, bf16[4,560,128]{2,1,0:T(8,128)(2,1)S(1)}, u32[]{:S(2)}, u32[]{:S(2)}) collective-permute-start(bf16[4,560,128]{2,1,0:T(8,128)(2,1)S(1)} %states_mine.1.own_ref), channel_id=1, source_target_pairs={{0,1},{1,0},{2,3},{3,2},{4,5},{5,4},{6,7},{7,6},{8,9},{9,8},{10,11... | collective-permute-start | bytes 1720328 | tf_op jit(solution)/shard_map/ppermute | solution.py:452
  15.9 8.5 %collective-permute-start.4 = (bf16[1,528,128]{2,1,0:T(8,128)(2,1)S(1)}, bf16[1,528,128]{2,1,0:T(8,128)(2,1)S(1)}, u32[]{:S(2)}, u32[]{:S(2)}) collective-permute-start(bf16[1,528,128]{2,1,0:T(8,128)(2,1)S(1)} %span_state.1), channel_id=1, source_target_pairs={{0,8},{1,9},{2,10},{3,11},{4,12},{5,13},{6,14},{7,15},{8,0},{9,1},... | collective-permute-start | bytes 405512 | tf_op jit(solution)/shard_map/ppermute | solution.py:452
  19.2 9.7 %copy-start.4 = (f32[4096]{0:T(1024)S(1)}, f32[4096]{0:T(1024)}, u32[]{:S(2)}) copy-start(f32[4096]{0:T(1024)} %param.11) | copy-start | bytes 49156
  24.8 4.1 %collective-permute-start.8 = (bf16[528,128]{1,0:T(8,128)(2,1)S(1)}, bf16[528,128]{1,0:T(8,128)(2,1)S(1)}, u32[]{:S(2)}, u32[]{:S(2)}) collective-permute-start(bf16[528,128]{1,0:T(8,128)(2,1)S(1)} %get-tuple-element.37.refs_3_), channel_id=1, source_target_pairs={{0,1},{1,0},{2,3},{3,2},{4,5},{5,4},{6,7},{7,6},{8,9},{9,8},{10,11... | collective-permute-start | bytes 405512 | tf_op jit(solution)/shard_map/ppermute | solution.py:452
  26.2 7.7 %collective-permute-start.7 = (bf16[528,128]{1,0:T(8,128)(2,1)S(1)}, bf16[528,128]{1,0:T(8,128)(2,1)S(1)}, u32[]{:S(2)}, u32[]{:S(2)}) collective-permute-start(bf16[528,128]{1,0:T(8,128)(2,1)S(1)} %get-tuple-element.38), channel_id=1, source_target_pairs={{0,2},{1,3},{2,0},{3,1},{4,6},{5,7},{6,4},{7,5},{8,10},{9,11},{10,... | collective-permute-start | bytes 405512 | tf_op jit(solution)/shard_map/ppermute | solution.py:452
  27.3 6.6 %collective-permute-start.6 = (bf16[528,128]{1,0:T(8,128)(2,1)S(1)}, bf16[528,128]{1,0:T(8,128)(2,1)S(1)}, u32[]{:S(2)}, u32[]{:S(2)}) collective-permute-start(bf16[528,128]{1,0:T(8,128)(2,1)S(1)} %get-tuple-element.39), channel_id=1, source_target_pairs={{0,6},{1,7},{2,4},{3,5},{4,2},{5,3},{6,0},{7,1},{8,14},{9,15},{10,... | collective-permute-start | bytes 405512 | tf_op jit(solution)/shard_map/ppermute | solution.py:452
  27.7 8.2 %collective-permute-start.5 = (bf16[528,128]{1,0:T(8,128)(2,1)S(1)}, bf16[528,128]{1,0:T(8,128)(2,1)S(1)}, u32[]{:S(2)}, u32[]{:S(2)}) collective-permute-start(bf16[528,128]{1,0:T(8,128)(2,1)S(1)} %get-tuple-element.40), channel_id=1, source_target_pairs={{0,4},{1,5},{2,6},{3,7},{4,0},{5,1},{6,2},{7,3},{8,12},{9,13},{10,... | collective-permute-start | bytes 405512 | tf_op jit(solution)/shard_map/ppermute | solution.py:452
  33.9 2.5 %collective-permute-start.11 = (bf16[528,128]{1,0:T(8,128)(2,1)S(1)}, bf16[528,128]{1,0:T(8,128)(2,1)S(1)}, u32[]{:S(2)}, u32[]{:S(2)}) collective-permute-start(bf16[528,128]{1,0:T(8,128)(2,1)S(1)} %collective-permute-done.6.refs_3_), channel_id=1, source_target_pairs={{0,1},{1,0},{2,3},{3,2},{4,5},{5,4},{6,7},{7,6},{8,9},{9,8},{10,11... | collective-permute-start | bytes 405512 | tf_op jit(solution)/shard_map/ppermute | solution.py:452
  35.1 1.4 %collective-permute-start.12 = (bf16[528,128]{1,0:T(8,128)(2,1)S(1)}, bf16[528,128]{1,0:T(8,128)(2,1)S(1)}, u32[]{:S(2)}, u32[]{:S(2)}) collective-permute-start(bf16[528,128]{1,0:T(8,128)(2,1)S(1)} %collective-permute-done.7.refs_6_), channel_id=1, source_target_pairs={{0,1},{1,0},{2,3},{3,2},{4,5},{5,4},{6,7},{7,6},{8,9},{9,8},{10,11... | collective-permute-start | bytes 405512 | tf_op jit(solution)/shard_map/ppermute | solution.py:452
  35.9 1.6 %collective-permute-start.10 = (bf16[528,128]{1,0:T(8,128)(2,1)S(1)}, bf16[528,128]{1,0:T(8,128)(2,1)S(1)}, u32[]{:S(2)}, u32[]{:S(2)}) collective-permute-start(bf16[528,128]{1,0:T(8,128)(2,1)S(1)} %collective-permute-done.5.refs_3_), channel_id=1, source_target_pairs={{0,1},{1,0},{2,3},{3,2},{4,5},{5,4},{6,7},{7,6},{8,9},{9,8},{10,11... | collective-permute-start | bytes 405512 | tf_op jit(solution)/shard_map/ppermute | solution.py:452

commit v15 on v14

--- a/solution.py
+++ b/solution.py
@@ -601,21 +601,15 @@
             **hints,
         )
 
-    final, *early = EXCHANGE
     items = [(True, 0), (False, 0)]
     made = output(items)
-    *late, made = lax.optimization_barrier((*[own[u] for u in early], made))
+    *late, made = lax.optimization_barrier((*[own[u] for u in EXCHANGE], made))
     earlier = [(items, made)]
-    own.update(zip(early, late))
-    other.update({u: swap(own[u], 1) for u in early})
-    items = [(True, u) for u in early]
-    made = output(items)
-    own[final], made = lax.optimization_barrier((own[final], made))
-    earlier.append((items, made))
-    other[final] = swap(own[final], 1)
-    items = [(True, final)] + [(False, u) for u in early]
+    own.update(zip(EXCHANGE, late))
+    other.update({u: swap(own[u], 1) for u in EXCHANGE})
+    items = [(True, u) for u in EXCHANGE]
     earlier.append((items, output(items)))
-    return output([(False, final)], earlier)
+    return output([(False, u) for u in EXCHANGE], earlier)
 
 
 def solution(mesh):

time: 39.3 us -> 40 us (1.018)
  waiting for transfers between devices: 14.7 us -> 16 us
  Pallas kernels: 11 us -> 10.6 us
    ppermute x13, waiting for transfers between devices: 14.7 us -> 16 us  [swap(): return lax.ppermute(x, 'ctx', [(i, i ^ mask) for i in range(n)])]
    pallas_call x12 -> x11, Pallas kernels: 11 us -> 10.6 us  [call(): pl.pallas_call(kernel, out_shape=out_shape, in_specs=in_specs, out_specs=...]
  transfers between devices with their start and end apart: 13 -> 13, of which waited for: 6 -> 7; matrix products, arithmetic and copies ran while one was open for 0% -> 0% of each run, Pallas kernels for 17% -> 15%
where the time goes in v15:
time: 40 us; the launch traced here: 39.6 us
  waiting for transfers between devices  16 us (40%)
  starting transfers between devices  12.8 us (32%)
  Pallas kernels  10.6 us (26%)
    ppermute x13, waiting for transfers between devices, swap(): return lax.ppermute(x, 'ctx', [(i, i ^ mask) for i in range(n)])  16 us
    ppermute x13, starting transfers between devices, swap(): return lax.ppermute(x, 'ctx', [(i, i ^ mask) for i in range(n)])  12.8 us
    pallas_call x11, Pallas kernels, call(): pl.pallas_call(kernel, out_shape=out_shape, in_specs=in_specs, out_specs=...  10.6 us
  transfers between devices with their start and end apart: 13, of which 7 were waited for; matrix products, arithmetic and copies ran while one was open for 0% of the time, Pallas kernels for 15%

profile of v15, /device:TPU:1, one launch (start us, length us, event | category | flops | bytes accessed | tf_op | source)
XLA Modules:
  0.0 39.6 jit_solution(9804600556949021499)
XLA Ops:
  0.0 2.7 %states_other.1 = bf16[4,560,128]{2,1,0:T(8,128)(2,1)S(1)} custom-call(bf16[128,4096]{1,0:T(8,128)(2,1)} %k_ref.5, bf16[128,4096]{1,0:T(8,128)(2,1)} %v_ref.5, f32[4,4096]{1,0:T(4,128)} %w_ref.5, f32[32,128]{1,0:T(8,128)} %bitcast.22), custom_call_target="tpu_custom_call" | custom-call | tf_op jit(solution)/shard_map/states_other/pallas_call | solution.py:46
  2.8 1.2 %states_mine.1.own_ref = bf16[4,560,128]{2,1,0:T(8,128)(2,1)S(1)} custom-call(bf16[128,4096]{1,0:T(8,128)(2,1)S(1)} %copy-done.1, bf16[128,4096]{1,0:T(8,128)(2,1)S(1)} %copy-done.2, f32[4,4096]{1,0:T(4,128)S(1)} %copy-done.3, f32[32,128]{1,0:T(8,128)S(1)} %bitcast.23), custom_call_target="tpu_custom_call" | custom-call | tf_op jit(solution)/shard_map/states_mine/pallas_call | solution.py:46
  4.0 0.7 %collective-permute-done.got_ref.refs_5_.refs_8_.refs_11_ = bf16[4,560,128]{2,1,0:T(8,128)(2,1)S(1)} collective-permute-done((bf16[4,560,128]{2,1,0:T(8,128)(2,1)S(1)}, bf16[4,560,128]{2,1,0:T(8,128)(2,1)S(1)}, u32[]{:S(2)}, u32[]{:S(2)}) %collective-permute-start) | collective-permute-done | bytes 573472 | tf_op jit(solution)/shard_map/ppermute | solution.py:452
  4.7 0.4 chip_states.1
  5.2 2.4 %collective-permute-start.3 = (bf16[1,560,128]{2,1,0:T(8,128)(2,1)S(1)}, bf16[1,560,128]{2,1,0:T(8,128)(2,1)S(1)}, u32[]{:S(2)}, u32[]{:S(2)}) collective-permute-start(bf16[1,560,128]{2,1,0:T(8,128)(2,1)S(1)} %get-tuple-element.31), channel_id=1, source_target_pairs={{0,2},{1,3},{2,0},{3,1},{4,6},{5,7},{6,4},{7,5},{8,10},{9,11},{10,... | collective-permute-start | bytes 430088 | tf_op jit(solution)/shard_map/ppermute | solution.py:452
  7.6 1.2 %collective-permute-start.2 = (bf16[1,560,128]{2,1,0:T(8,128)(2,1)S(1)}, bf16[1,560,128]{2,1,0:T(8,128)(2,1)S(1)}, u32[]{:S(2)}, u32[]{:S(2)}) collective-permute-start(bf16[1,560,128]{2,1,0:T(8,128)(2,1)S(1)} %get-tuple-element.32), channel_id=1, source_target_pairs={{0,6},{1,7},{2,4},{3,5},{4,2},{5,3},{6,0},{7,1},{8,14},{9,15},{10,... | collective-permute-start | bytes 430088 | tf_op jit(solution)/shard_map/ppermute | solution.py:452
  8.9 0.9 %collective-permute-start.9 = (bf16[4,560,128]{2,1,0:T(8,128)(2,1)S(1)}, bf16[4,560,128]{2,1,0:T(8,128)(2,1)S(1)}, u32[]{:S(2)}, u32[]{:S(2)}) collective-permute-start(bf16[4,560,128]{2,1,0:T(8,128)(2,1)S(1)} %states_mine.1.own_ref), channel_id=1, source_target_pairs={{0,1},{1,0},{2,3},{3,2},{4,5},{5,4},{6,7},{7,6},{8,9},{9,8},{10,11... | collective-permute-start | bytes 1720328 | tf_op jit(solution)/shard_map/ppermute | solution.py:452
  10.0 1.1 %intra_mine.1.refs_4_.refs_7_.refs_10_ = f32[17,128,128]{2,1,0:T(8,128)S(1)} custom-call(bf16[128,4096]{1,0:T(8,128)(2,1)S(1)} %copy-done, bf16[128,4096]{1,0:T(8,128)(2,1)S(1)} %copy-done.1, bf16[128,4096]{1,0:T(8,128)(2,1)S(1)} %copy-done.2, f32[4,4096]{1,0:T(4,128)S(1)} %copy-done.3, f32[8,8,128]{2,1,0:T(8,128)S(1)} %cum.1.cum_ref.refs_1_), custom_call_target="tpu_custom_call" | custom-call | tf_op jit(solution)/shard_map/intra_mine/pallas_call | solution.py:46
  11.1 2.5 %collective-permute-done.3.refs_1_ = bf16[1,560,128]{2,1,0:T(8,128)(2,1)S(1)} collective-permute-done((bf16[1,560,128]{2,1,0:T(8,128)(2,1)S(1)}, bf16[1,560,128]{2,1,0:T(8,128)(2,1)S(1)}, u32[]{:S(2)}, u32[]{:S(2)}) %collective-permute-start.3) | collective-permute-done | bytes 143392 | tf_op jit(solution)/shard_map/ppermute | solution.py:452
  13.6 1.9 %collective-permute-done.1.refs_2_ = bf16[1,560,128]{2,1,0:T(8,128)(2,1)S(1)} collective-permute-done((bf16[1,560,128]{2,1,0:T(8,128)(2,1)S(1)}, bf16[1,560,128]{2,1,0:T(8,128)(2,1)S(1)}, u32[]{:S(2)}, u32[]{:S(2)}) %collective-permute-start.1) | collective-permute-done | bytes 143392 | tf_op jit(solution)/shard_map/ppermute | solution.py:452
  15.9 2.2 %collective-permute-start.4 = (bf16[1,528,128]{2,1,0:T(8,128)(2,1)S(1)}, bf16[1,528,128]{2,1,0:T(8,128)(2,1)S(1)}, u32[]{:S(2)}, u32[]{:S(2)}) collective-permute-start(bf16[1,528,128]{2,1,0:T(8,128)(2,1)S(1)} %span_state.1), channel_id=1, source_target_pairs={{0,8},{1,9},{2,10},{3,11},{4,12},{5,13},{6,14},{7,15},{8,0},{9,1},... | collective-permute-start | bytes 405512 | tf_op jit(solution)/shard_map/ppermute | solution.py:452
  18.1 1.1 %intra_other.1.refs_7_.refs_4_.refs_10_ = f32[17,128,128]{2,1,0:T(8,128)S(1)} custom-call(bf16[128,4096]{1,0:T(8,128)(2,1)S(1)} %copy-done, bf16[128,4096]{1,0:T(8,128)(2,1)S(1)} %copy-done.1, bf16[128,4096]{1,0:T(8,128)(2,1)S(1)} %copy-done.2, f32[4,4096]{1,0:T(4,128)S(1)} %copy-done.3, f32[8,8,128]{2,1,0:T(8,128)S(1)} %cum.1.cum_ref.refs_1_), custom_call_target="tpu_custom_call" | custom-call | tf_op jit(solution)/shard_map/intra_other/pallas_call | solution.py:46
  19.2 5.2 %collective-permute-done.4.refs_4_ = bf16[1,528,128]{2,1,0:T(8,128)(2,1)S(1)} collective-permute-done((bf16[1,528,128]{2,1,0:T(8,128)(2,1)S(1)}, bf16[1,528,128]{2,1,0:T(8,128)(2,1)S(1)}, u32[]{:S(2)}, u32[]{:S(2)}) %collective-permute-start.4) | collective-permute-done | bytes 135200 | tf_op jit(solution)/shard_map/ppermute | solution.py:452
  24.3 0.4 chip_prefix.1
  24.8 1.5 %collective-permute-start.8 = (bf16[528,128]{1,0:T(8,128)(2,1)S(1)}, bf16[528,128]{1,0:T(8,128)(2,1)S(1)}, u32[]{:S(2)}, u32[]{:S(2)}) collective-permute-start(bf16[528,128]{1,0:T(8,128)(2,1)S(1)} %get-tuple-element.35.refs_3_), channel_id=1, source_target_pairs={{0,1},{1,0},{2,3},{3,2},{4,5},{5,4},{6,7},{7,6},{8,9},{9,8},{10,11... | collective-permute-start | bytes 405512 | tf_op jit(solution)/shard_map/ppermute | solution.py:452
  26.2 1.1 %collective-permute-start.7 = (bf16[528,128]{1,0:T(8,128)(2,1)S(1)}, bf16[528,128]{1,0:T(8,128)(2,1)S(1)}, u32[]{:S(2)}, u32[]{:S(2)}) collective-permute-start(bf16[528,128]{1,0:T(8,128)(2,1)S(1)} %get-tuple-element.36), channel_id=1, source_target_pairs={{0,2},{1,3},{2,0},{3,1},{4,6},{5,7},{6,4},{7,5},{8,10},{9,11},{10,... | collective-permute-start | bytes 405512 | tf_op jit(solution)/shard_map/ppermute | solution.py:452
  27.7 1.2 %collective-permute-start.5 = (bf16[528,128]{1,0:T(8,128)(2,1)S(1)}, bf16[528,128]{1,0:T(8,128)(2,1)S(1)}, u32[]{:S(2)}, u32[]{:S(2)}) collective-permute-start(bf16[528,128]{1,0:T(8,128)(2,1)S(1)} %get-tuple-element.38), channel_id=1, source_target_pairs={{0,4},{1,5},{2,6},{3,7},{4,0},{5,1},{6,2},{7,3},{8,12},{9,13},{10,... | collective-permute-start | bytes 405512 | tf_op jit(solution)/shard_map/ppermute | solution.py:452
  28.9 0.7 %out_m0_o0.1.refs_12_ = bf16[2,128,512]{2,1,0:T(8,128)(2,1)S(1)} custom-call(bf16[128,4096]{1,0:T(8,128)(2,1)S(1)} %copy-done, f32[8,8,128]{2,1,0:T(8,128)S(1)} %cum.1.cum_ref.refs_1_, f32[1,4096]{1,0:T(1,128)S(1)} %bitcast.19, bf16[528,128]{1,0:T(8,128)(2,1)S(1)} %get-tuple-element.35.refs_3_, f32[17,128,128]{2,1,0:T(8,128)S(1)} %intra_mine.1.refs_4_.refs_7_.refs_10_, ...), custom_call_target="tpu_custom_call" | custom-call | flops 1 | bytes 1 | tf_op jit(solution)/shard_map/out_m0_o0/pallas_call | solution.py:46
  29.6 4.3 %collective-permute-done.7.refs_9_ = bf16[528,128]{1,0:T(8,128)(2,1)S(1)} collective-permute-done((bf16[528,128]{1,0:T(8,128)(2,1)S(1)}, bf16[528,128]{1,0:T(8,128)(2,1)S(1)}, u32[]{:S(2)}, u32[]{:S(2)}) %collective-permute-start.7) | collective-permute-done | bytes 135200 | tf_op jit(solution)/shard_map/ppermute | solution.py:452
  33.9 1.3 %collective-permute-done.5.refs_3_ = bf16[528,128]{1,0:T(8,128)(2,1)S(1)} collective-permute-done((bf16[528,128]{1,0:T(8,128)(2,1)S(1)}, bf16[528,128]{1,0:T(8,128)(2,1)S(1)}, u32[]{:S(2)}, u32[]{:S(2)}) %collective-permute-start.5) | collective-permute-done | bytes 135200 | tf_op jit(solution)/shard_map/ppermute | solution.py:452
  35.2 1.2 %collective-permute-start.10 = (bf16[528,128]{1,0:T(8,128)(2,1)S(1)}, bf16[528,128]{1,0:T(8,128)(2,1)S(1)}, u32[]{:S(2)}, u32[]{:S(2)}) collective-permute-start(bf16[528,128]{1,0:T(8,128)(2,1)S(1)} %collective-permute-done.5.refs_3_), channel_id=1, source_target_pairs={{0,1},{1,0},{2,3},{3,2},{4,5},{5,4},{6,7},{7,6},{8,9},{9,8},{10,11... | collective-permute-start | bytes 405512 | tf_op jit(solution)/shard_map/ppermute | solution.py:452
  36.4 0.5 %collective-permute-start.12 = (bf16[528,128]{1,0:T(8,128)(2,1)S(1)}, bf16[528,128]{1,0:T(8,128)(2,1)S(1)}, u32[]{:S(2)}, u32[]{:S(2)}) collective-permute-start(bf16[528,128]{1,0:T(8,128)(2,1)S(1)} %collective-permute-done.7.refs_9_), channel_id=1, source_target_pairs={{0,1},{1,0},{2,3},{3,2},{4,5},{5,4},{6,7},{7,6},{8,9},{9,8},{10,11... | collective-permute-start | bytes 405512 | tf_op jit(solution)/shard_map/ppermute | solution.py:452
  36.9 0.9 %out_m2_m3_m1.1.refs_13_ = bf16[3,128,512]{2,1,0:T(8,128)(2,1)S(1)} custom-call(bf16[128,4096]{1,0:T(8,128)(2,1)S(1)} %copy-done, f32[8,8,128]{2,1,0:T(8,128)S(1)} %cum.1.cum_ref.refs_1_, f32[1,4096]{1,0:T(1,128)S(1)} %bitcast.20, bf16[528,128]{1,0:T(8,128)(2,1)S(1)} %collective-permute-done.5.refs_3_, ...), custom_call_target="tpu_custom_call" | custom-call | flops 1 | bytes 1 | tf_op jit(solution)/shard_map/out_m2_m3_m1/pallas_call | solution.py:46
  37.9 1.7 %out_o2_o3_o1.1 = bf16[128,4096]{1,0:T(8,128)(2,1)} custom-call(bf16[128,4096]{1,0:T(8,128)(2,1)S(1)} %copy-done, f32[8,8,128]{2,1,0:T(8,128)S(1)} %cum.1.cum_ref.refs_1_, f32[1,4096]{1,0:T(1,128)S(1)} %bitcast.21, bf16[528,128]{1,0:T(8,128)(2,1)S(1)} %collective-permute-done.10.refs_3_, f32[17,128,128]{2,1,0:T(8,128)S(1)} %intra_other.1.refs_7_.refs_4_.refs_10_, ...), custom_call_target="tpu_custom_call" | custom-call | flops 1 | bytes 1 | tf_op jit(solution)/shard_map/out_o2_o3_o1/pallas_call | solution.py:46
  (27 shorter events, 1.3 us)
Async XLA Ops:
  0.0 2.8 %copy-start.1 = (bf16[128,4096]{1,0:T(8,128)(2,1)S(1)}, bf16[128,4096]{1,0:T(8,128)(2,1)}, u32[]{:S(2)}) copy-start(bf16[128,4096]{1,0:T(8,128)(2,1)} %k_ref.5) | copy-start | bytes 3145732
  0.0 2.8 %copy-start.2 = (bf16[128,4096]{1,0:T(8,128)(2,1)S(1)}, bf16[128,4096]{1,0:T(8,128)(2,1)}, u32[]{:S(2)}) copy-start(bf16[128,4096]{1,0:T(8,128)(2,1)} %v_ref.5) | copy-start | bytes 3145732
  0.0 2.8 %copy-start.3 = (f32[4,4096]{1,0:T(4,128)S(1)}, f32[4,4096]{1,0:T(4,128)}, u32[]{:S(2)}) copy-start(f32[4,4096]{1,0:T(4,128)} %w_ref.5) | copy-start | bytes 196612
  0.0 2.8 %copy-start.5 = (f32[128,32]{0,1:T(8,128)S(1)}, f32[128,32]{0,1:T(8,128)}, u32[]{:S(2)}) copy-start(f32[128,32]{0,1:T(8,128)} %param.9) | copy-start | bytes 49156
  2.7 2.0 %collective-permute-start = (bf16[4,560,128]{2,1,0:T(8,128)(2,1)S(1)}, bf16[4,560,128]{2,1,0:T(8,128)(2,1)S(1)}, u32[]{:S(2)}, u32[]{:S(2)}) collective-permute-start(bf16[4,560,128]{2,1,0:T(8,128)(2,1)S(1)} %states_other.1), channel_id=1, source_target_pairs={{0,1},{1,0},{2,3},{3,2},{4,5},{5,4},{6,7},{7,6},{8,9},{9,8},{10,11... | collective-permute-start | bytes 1720328 | tf_op jit(solution)/shard_map/ppermute | solution.py:452
  4.0 6.0 %copy-start = (bf16[128,4096]{1,0:T(8,128)(2,1)S(1)}, bf16[128,4096]{1,0:T(8,128)(2,1)}, u32[]{:S(2)}) copy-start(bf16[128,4096]{1,0:T(8,128)(2,1)} %refs_0_.5) | copy-start | bytes 3145732
  5.2 8.4 %collective-permute-start.3 = (bf16[1,560,128]{2,1,0:T(8,128)(2,1)S(1)}, bf16[1,560,128]{2,1,0:T(8,128)(2,1)S(1)}, u32[]{:S(2)}, u32[]{:S(2)}) collective-permute-start(bf16[1,560,128]{2,1,0:T(8,128)(2,1)S(1)} %get-tuple-element.31), channel_id=1, source_target_pairs={{0,2},{1,3},{2,0},{3,1},{4,6},{5,7},{6,4},{7,5},{8,10},{9,11},{10,... | collective-permute-start | bytes 430088 | tf_op jit(solution)/shard_map/ppermute | solution.py:452
  7.6 6.0 %collective-permute-start.2 = (bf16[1,560,128]{2,1,0:T(8,128)(2,1)S(1)}, bf16[1,560,128]{2,1,0:T(8,128)(2,1)S(1)}, u32[]{:S(2)}, u32[]{:S(2)}) collective-permute-start(bf16[1,560,128]{2,1,0:T(8,128)(2,1)S(1)} %get-tuple-element.32), channel_id=1, source_target_pairs={{0,6},{1,7},{2,4},{3,5},{4,2},{5,3},{6,0},{7,1},{8,14},{9,15},{10,... | collective-permute-start | bytes 430088 | tf_op jit(solution)/shard_map/ppermute | solution.py:452
  8.8 6.7 %collective-permute-start.1 = (bf16[1,560,128]{2,1,0:T(8,128)(2,1)S(1)}, bf16[1,560,128]{2,1,0:T(8,128)(2,1)S(1)}, u32[]{:S(2)}, u32[]{:S(2)}) collective-permute-start(bf16[1,560,128]{2,1,0:T(8,128)(2,1)S(1)} %get-tuple-element.33), channel_id=1, source_target_pairs={{0,4},{1,5},{2,6},{3,7},{4,0},{5,1},{6,2},{7,3},{8,12},{9,13},{10,... | collective-permute-start | bytes 430088 | tf_op jit(solution)/shard_map/ppermute | solution.py:452
  8.9 20.0 %collective-permute-start.9 = (bf16[4,560,128]{2,1,0:T(8,128)(2,1)S(1)}, bf16[4,560,128]{2,1,0:T(8,128)(2,1)S(1)}, u32[]{:S(2)}, u32[]{:S(2)}) collective-permute-start(bf16[4,560,128]{2,1,0:T(8,128)(2,1)S(1)} %states_mine.1.own_ref), channel_id=1, source_target_pairs={{0,1},{1,0},{2,3},{3,2},{4,5},{5,4},{6,7},{7,6},{8,9},{9,8},{10,11... | collective-permute-start | bytes 1720328 | tf_op jit(solution)/shard_map/ppermute | solution.py:452
  15.9 8.5 %collective-permute-start.4 = (bf16[1,528,128]{2,1,0:T(8,128)(2,1)S(1)}, bf16[1,528,128]{2,1,0:T(8,128)(2,1)S(1)}, u32[]{:S(2)}, u32[]{:S(2)}) collective-permute-start(bf16[1,528,128]{2,1,0:T(8,128)(2,1)S(1)} %span_state.1), channel_id=1, source_target_pairs={{0,8},{1,9},{2,10},{3,11},{4,12},{5,13},{6,14},{7,15},{8,0},{9,1},... | collective-permute-start | bytes 405512 | tf_op jit(solution)/shard_map/ppermute | solution.py:452
  19.2 9.7 %copy-start.4 = (f32[4096]{0:T(1024)S(1)}, f32[4096]{0:T(1024)}, u32[]{:S(2)}) copy-start(f32[4096]{0:T(1024)} %param.11) | copy-start | bytes 49156
  24.8 4.1 %collective-permute-start.8 = (bf16[528,128]{1,0:T(8,128)(2,1)S(1)}, bf16[528,128]{1,0:T(8,128)(2,1)S(1)}, u32[]{:S(2)}, u32[]{:S(2)}) collective-permute-start(bf16[528,128]{1,0:T(8,128)(2,1)S(1)} %get-tuple-element.35.refs_3_), channel_id=1, source_target_pairs={{0,1},{1,0},{2,3},{3,2},{4,5},{5,4},{6,7},{7,6},{8,9},{9,8},{10,11... | collective-permute-start | bytes 405512 | tf_op jit(solution)/shard_map/ppermute | solution.py:452
  26.2 7.7 %collective-permute-start.7 = (bf16[528,128]{1,0:T(8,128)(2,1)S(1)}, bf16[528,128]{1,0:T(8,128)(2,1)S(1)}, u32[]{:S(2)}, u32[]{:S(2)}) collective-permute-start(bf16[528,128]{1,0:T(8,128)(2,1)S(1)} %get-tuple-element.36), channel_id=1, source_target_pairs={{0,2},{1,3},{2,0},{3,1},{4,6},{5,7},{6,4},{7,5},{8,10},{9,11},{10,... | collective-permute-start | bytes 405512 | tf_op jit(solution)/shard_map/ppermute | solution.py:452
  27.3 6.6 %collective-permute-start.6 = (bf16[528,128]{1,0:T(8,128)(2,1)S(1)}, bf16[528,128]{1,0:T(8,128)(2,1)S(1)}, u32[]{:S(2)}, u32[]{:S(2)}) collective-permute-start(bf16[528,128]{1,0:T(8,128)(2,1)S(1)} %get-tuple-element.37), channel_id=1, source_target_pairs={{0,6},{1,7},{2,4},{3,5},{4,2},{5,3},{6,0},{7,1},{8,14},{9,15},{10,... | collective-permute-start | bytes 405512 | tf_op jit(solution)/shard_map/ppermute | solution.py:452
  27.7 7.5 %collective-permute-start.5 = (bf16[528,128]{1,0:T(8,128)(2,1)S(1)}, bf16[528,128]{1,0:T(8,128)(2,1)S(1)}, u32[]{:S(2)}, u32[]{:S(2)}) collective-permute-start(bf16[528,128]{1,0:T(8,128)(2,1)S(1)} %get-tuple-element.38), channel_id=1, source_target_pairs={{0,4},{1,5},{2,6},{3,7},{4,0},{5,1},{6,2},{7,3},{8,12},{9,13},{10,... | collective-permute-start | bytes 405512 | tf_op jit(solution)/shard_map/ppermute | solution.py:452
  35.2 2.6 %collective-permute-start.10 = (bf16[528,128]{1,0:T(8,128)(2,1)S(1)}, bf16[528,128]{1,0:T(8,128)(2,1)S(1)}, u32[]{:S(2)}, u32[]{:S(2)}) collective-permute-start(bf16[528,128]{1,0:T(8,128)(2,1)S(1)} %collective-permute-done.5.refs_3_), channel_id=1, source_target_pairs={{0,1},{1,0},{2,3},{3,2},{4,5},{5,4},{6,7},{7,6},{8,9},{9,8},{10,11... | collective-permute-start | bytes 405512 | tf_op jit(solution)/shard_map/ppermute | solution.py:452
  36.4 1.4 %collective-permute-start.11 = (bf16[528,128]{1,0:T(8,128)(2,1)S(1)}, bf16[528,128]{1,0:T(8,128)(2,1)S(1)}, u32[]{:S(2)}, u32[]{:S(2)}) collective-permute-start(bf16[528,128]{1,0:T(8,128)(2,1)S(1)} %collective-permute-done.6.refs_6_), channel_id=1, source_target_pairs={{0,1},{1,0},{2,3},{3,2},{4,5},{5,4},{6,7},{7,6},{8,9},{9,8},{10,11... | collective-permute-start | bytes 405512 | tf_op jit(solution)/shard_map/ppermute | solution.py:452
  36.4 1.5 %collective-permute-start.12 = (bf16[528,128]{1,0:T(8,128)(2,1)S(1)}, bf16[528,128]{1,0:T(8,128)(2,1)S(1)}, u32[]{:S(2)}, u32[]{:S(2)}) collective-permute-start(bf16[528,128]{1,0:T(8,128)(2,1)S(1)} %collective-permute-done.7.refs_9_), channel_id=1, source_target_pairs={{0,1},{1,0},{2,3},{3,2},{4,5},{5,4},{6,7},{7,6},{8,9},{9,8},{10,11... | collective-permute-start | bytes 405512 | tf_op jit(solution)/shard_map/ppermute | solution.py:452

commit v16 on v14

--- a/solution.py
+++ b/solution.py
@@ -28,8 +28,14 @@
 
 def head_group(mine, unit):
     core, chip = position()
-    group = (core if mine else 1 - core) * CHIPS + (chip ^ (unit % CHIPS))
+    core = core if mine else 1 - core
+    group = core * CHIPS + (chip ^ distance(unit % CHIPS, core))
     return group * CHUNKS + unit // CHIPS
+
+
+def distance(slot, core):
+    turned = ((slot & 1) << 1) | (slot >> 1)
+    return slot + core * (turned - slot)
 
 
 def columns(block, offset, size):
@@ -267,9 +273,9 @@
 
 
 def in_order(packets, part, held):
-    _, chip = position()
+    core, chip = position()
     for g in range(CHIPS):
-        held[chip ^ g] = packets[g][part]
+        held[chip ^ distance(g, core)] = packets[g][part]
 
 
 def chip_fixes(held, b, edges, heads, size):
@@ -316,7 +322,8 @@
 
 def spread_kernel(part, place, heads, size, *refs):
     packets, before, known, (out_ref, held) = refs[:CHIPS], refs[CHIPS], refs[CHIPS + 1 : -2], refs[-2:]
-    _, chip = position()
+    core, chip = position()
+    slots = [distance(chip ^ b, core) for b in range(CHIPS)]
     later = lax.axis_index("ctx") >= SPAN
     in_order(packets, part, held)
     decays = [get_decay(held.at[b], heads, size) for b in range(CHIPS)]
@@ -327,14 +334,14 @@
     for j in range(heads):
         rows = slice(j * size, (j + 1) * size)
         acc = jnp.where(later, before[place, rows, :].astype(F32), 0.0)
-        out_ref[chip, rows, :] = acc.astype(BF16)
+        out_ref[slots[0], rows, :] = acc.astype(BF16)
         for b in range(1, CHIPS):
             acc = acc * decays[b - 1][j : j + 1] + (
                 held[b - 1, rows, :].astype(F32) + fixes[b - 1][j]
             )
-            out_ref[chip ^ b, rows, :] = acc.astype(BF16)
+            out_ref[slots[b], rows, :] = acc.astype(BF16)
     for b in range(CHIPS):
-        out_ref[chip ^ b, heads * size : heads * size + PARTS, :] = edges[b]
+        out_ref[slots[b], heads * size : heads * size + PARTS, :] = edges[b]
 
 
 def last_out_kernel(items, earlier, heads, size, *refs):
@@ -451,6 +458,9 @@
     def swap(x, mask):
         return lax.ppermute(x, "ctx", [(i, i ^ mask) for i in range(n)])
 
+    def exchange(x, slot):
+        return lax.ppermute(x, "ctx", [(i, i ^ (2 * distance(slot, i & 1))) for i in range(n)])
+
     def shift(x, by):
         return lax.ppermute(x, "ctx", [(i, i + by) for i in range(n - by)])
 
@@ -505,7 +515,7 @@
 
     packets = {0: chip_states[0]}
     for g in EXCHANGE:
-        packets[g] = swap(chip_states[g], 2 * g)
+        packets[g] = exchange(chip_states[g], g)
     q_after, decay_after, chip_states = lax.optimization_barrier(
         (queries, log_decay, chip_states)
     )
@@ -571,7 +581,7 @@
         first = part * CHIPS
         own[first] = chip_prefix[0]
         for g in EXCHANGE:
-            own[first + g] = swap(chip_prefix[g], 2 * g)
+            own[first + g] = exchange(chip_prefix[g], g)
         other[first] = swap(own[first], 1)
 
     def output(items, earlier=None):

time: 39.3 us -> 39.2 us (level)
    ppermute x0 -> x6, waiting for transfers between devices: none -> 8.61 us  [exchange(): lax.ppermute(x, 'ctx', [(i, i ^ 2 * distance(slot, i & 1)) for i in range...]
    ppermute x13 -> x7, waiting for transfers between devices: 14.7 us -> 6.23 us  [swap(): return lax.ppermute(x, 'ctx', [(i, i ^ mask) for i in range(n)])]
    ppermute x13 -> x7, starting transfers between devices: 12.9 us -> 6.19 us  [swap(): return lax.ppermute(x, 'ctx', [(i, i ^ mask) for i in range(n)])]
    ppermute x0 -> x6, starting transfers between devices: none -> 6.4 us  [exchange(): lax.ppermute(x, 'ctx', [(i, i ^ 2 * distance(slot, i & 1)) for i in range...]
  transfers between devices with their start and end apart: 13 -> 13, of which waited for: 6 -> 7; matrix products, arithmetic and copies ran while one was open for 0% -> 0% of each run, Pallas kernels for 17% -> 17%
where the time goes in v16:
time: 39.2 us; the launch traced here: 38.8 us
  waiting for transfers between devices  14.8 us (38%)
  starting transfers between devices  12.6 us (32%)
  Pallas kernels  11.1 us (28%)
    pallas_call x12, Pallas kernels, call(): pl.pallas_call(kernel, out_shape=out_shape, in_specs=in_specs, out_specs=...  11.1 us
    ppermute x6, waiting for transfers between devices, exchange(): lax.ppermute(x, 'ctx', [(i, i ^ 2 * distance(slot, i & 1)) for i in range...  8.61 us
    ppermute x6, starting transfers between devices, exchange(): lax.ppermute(x, 'ctx', [(i, i ^ 2 * distance(slot, i & 1)) for i in range...  6.4 us
    ppermute x7, waiting for transfers between devices, swap(): return lax.ppermute(x, 'ctx', [(i, i ^ mask) for i in range(n)])  6.23 us
    ppermute x7, starting transfers between devices, swap(): return lax.ppermute(x, 'ctx', [(i, i ^ mask) for i in range(n)])  6.19 us
  transfers between devices with their start and end apart: 13, of which 7 were waited for; matrix products, arithmetic and copies ran while one was open for 0% of the time, Pallas kernels for 17%

profile of v16, /device:TPU:1, one launch (start us, length us, event | category | flops | bytes accessed | tf_op | source)
XLA Modules:
  0.0 38.8 jit_solution(9501393091363858274)
XLA Ops:
  0.0 2.7 %states_other.1 = bf16[4,560,128]{2,1,0:T(8,128)(2,1)S(1)} custom-call(bf16[128,4096]{1,0:T(8,128)(2,1)} %k_ref.5, bf16[128,4096]{1,0:T(8,128)(2,1)} %v_ref.5, f32[4,4096]{1,0:T(4,128)} %w_ref.5, f32[32,128]{1,0:T(8,128)} %bitcast.23), custom_call_target="tpu_custom_call" | custom-call | tf_op jit(solution)/shard_map/states_other/pallas_call | solution.py:52
  2.8 1.2 %states_mine.1.own_ref = bf16[4,560,128]{2,1,0:T(8,128)(2,1)S(1)} custom-call(bf16[128,4096]{1,0:T(8,128)(2,1)S(1)} %copy-done.1, bf16[128,4096]{1,0:T(8,128)(2,1)S(1)} %copy-done.2, f32[4,4096]{1,0:T(4,128)S(1)} %copy-done.3, f32[32,128]{1,0:T(8,128)S(1)} %bitcast.24), custom_call_target="tpu_custom_call" | custom-call | tf_op jit(solution)/shard_map/states_mine/pallas_call | solution.py:52
  4.0 0.7 %collective-permute-done.got_ref.refs_5_.refs_8_ = bf16[4,560,128]{2,1,0:T(8,128)(2,1)S(1)} collective-permute-done((bf16[4,560,128]{2,1,0:T(8,128)(2,1)S(1)}, bf16[4,560,128]{2,1,0:T(8,128)(2,1)S(1)}, u32[]{:S(2)}, u32[]{:S(2)}) %collective-permute-start) | collective-permute-done | bytes 573472 | tf_op jit(solution)/shard_map/ppermute | solution.py:459
  5.2 2.5 %collective-permute-start.3 = (bf16[1,560,128]{2,1,0:T(8,128)(2,1)S(1)}, bf16[1,560,128]{2,1,0:T(8,128)(2,1)S(1)}, u32[]{:S(2)}, u32[]{:S(2)}) collective-permute-start(bf16[1,560,128]{2,1,0:T(8,128)(2,1)S(1)} %get-tuple-element.33), channel_id=1, source_target_pairs={{0,2},{1,5},{2,0},{3,7},{4,6},{5,1},{6,4},{7,3},{8,10},{9,13},{10,... | collective-permute-start | bytes 430088 | tf_op jit(solution)/shard_map/ppermute | solution.py:462
  7.6 1.1 %collective-permute-start.2 = (bf16[1,560,128]{2,1,0:T(8,128)(2,1)S(1)}, bf16[1,560,128]{2,1,0:T(8,128)(2,1)S(1)}, u32[]{:S(2)}, u32[]{:S(2)}) collective-permute-start(bf16[1,560,128]{2,1,0:T(8,128)(2,1)S(1)} %get-tuple-element.34), channel_id=1, source_target_pairs={{0,6},{1,7},{2,4},{3,5},{4,2},{5,3},{6,0},{7,1},{8,14},{9,15},{10,... | collective-permute-start | bytes 430088 | tf_op jit(solution)/shard_map/ppermute | solution.py:462
  8.9 0.9 %collective-permute-start.9 = (bf16[4,560,128]{2,1,0:T(8,128)(2,1)S(1)}, bf16[4,560,128]{2,1,0:T(8,128)(2,1)S(1)}, u32[]{:S(2)}, u32[]{:S(2)}) collective-permute-start(bf16[4,560,128]{2,1,0:T(8,128)(2,1)S(1)} %states_mine.1.own_ref), channel_id=1, source_target_pairs={{0,1},{1,0},{2,3},{3,2},{4,5},{5,4},{6,7},{7,6},{8,9},{9,8},{10,11... | collective-permute-start | bytes 1720328 | tf_op jit(solution)/shard_map/ppermute | solution.py:459
  10.0 1.1 %intra_mine.1.refs_4_.refs_7_ = f32[17,128,128]{2,1,0:T(8,128)S(1)} custom-call(bf16[128,4096]{1,0:T(8,128)(2,1)S(1)} %copy-done, bf16[128,4096]{1,0:T(8,128)(2,1)S(1)} %copy-done.1, bf16[128,4096]{1,0:T(8,128)(2,1)S(1)} %copy-done.2, f32[4,4096]{1,0:T(4,128)S(1)} %copy-done.3, f32[8,8,128]{2,1,0:T(8,128)S(1)} %cum.1.cum_ref.refs_1_), custom_call_target="tpu_custom_call" | custom-call | tf_op jit(solution)/shard_map/intra_mine/pallas_call | solution.py:52
  11.1 2.7 %collective-permute-done.2.refs_3_ = bf16[1,560,128]{2,1,0:T(8,128)(2,1)S(1)} collective-permute-done((bf16[1,560,128]{2,1,0:T(8,128)(2,1)S(1)}, bf16[1,560,128]{2,1,0:T(8,128)(2,1)S(1)}, u32[]{:S(2)}, u32[]{:S(2)}) %collective-permute-start.2) | collective-permute-done | bytes 143392 | tf_op jit(solution)/shard_map/ppermute | solution.py:462
  13.8 2.0 %collective-permute-done.1.refs_2_ = bf16[1,560,128]{2,1,0:T(8,128)(2,1)S(1)} collective-permute-done((bf16[1,560,128]{2,1,0:T(8,128)(2,1)S(1)}, bf16[1,560,128]{2,1,0:T(8,128)(2,1)S(1)}, u32[]{:S(2)}, u32[]{:S(2)}) %collective-permute-start.1) | collective-permute-done | bytes 143392 | tf_op jit(solution)/shard_map/ppermute | solution.py:462
  16.2 2.5 %collective-permute-start.4 = (bf16[1,528,128]{2,1,0:T(8,128)(2,1)S(1)}, bf16[1,528,128]{2,1,0:T(8,128)(2,1)S(1)}, u32[]{:S(2)}, u32[]{:S(2)}) collective-permute-start(bf16[1,528,128]{2,1,0:T(8,128)(2,1)S(1)} %span_state.1), channel_id=1, source_target_pairs={{0,8},{1,9},{2,10},{3,11},{4,12},{5,13},{6,14},{7,15},{8,0},{9,1},... | collective-permute-start | bytes 405512 | tf_op jit(solution)/shard_map/ppermute | solution.py:459
  18.7 1.1 %intra_other.1.refs_7_.refs_10_.refs_4_ = f32[17,128,128]{2,1,0:T(8,128)S(1)} custom-call(bf16[128,4096]{1,0:T(8,128)(2,1)S(1)} %copy-done, bf16[128,4096]{1,0:T(8,128)(2,1)S(1)} %copy-done.1, bf16[128,4096]{1,0:T(8,128)(2,1)S(1)} %copy-done.2, f32[4,4096]{1,0:T(4,128)S(1)} %copy-done.3, f32[8,8,128]{2,1,0:T(8,128)S(1)} %cum.1.cum_ref.refs_1_), custom_call_target="tpu_custom_call" | custom-call | tf_op jit(solution)/shard_map/intra_other/pallas_call | solution.py:52
  19.8 5.4 %collective-permute-done.4.refs_4_ = bf16[1,528,128]{2,1,0:T(8,128)(2,1)S(1)} collective-permute-done((bf16[1,528,128]{2,1,0:T(8,128)(2,1)S(1)}, bf16[1,528,128]{2,1,0:T(8,128)(2,1)S(1)}, u32[]{:S(2)}, u32[]{:S(2)}) %collective-permute-start.4) | collective-permute-done | bytes 135200 | tf_op jit(solution)/shard_map/ppermute | solution.py:459
  25.6 1.0 %collective-permute-start.8 = (bf16[528,128]{1,0:T(8,128)(2,1)S(1)}, bf16[528,128]{1,0:T(8,128)(2,1)S(1)}, u32[]{:S(2)}, u32[]{:S(2)}) collective-permute-start(bf16[528,128]{1,0:T(8,128)(2,1)S(1)} %get-tuple-element.37.refs_3_), channel_id=1, source_target_pairs={{0,1},{1,0},{2,3},{3,2},{4,5},{5,4},{6,7},{7,6},{8,9},{9,8},{10,11... | collective-permute-start | bytes 405512 | tf_op jit(solution)/shard_map/ppermute | solution.py:459
  26.6 0.4 %collective-permute-start.7 = (bf16[528,128]{1,0:T(8,128)(2,1)S(1)}, bf16[528,128]{1,0:T(8,128)(2,1)S(1)}, u32[]{:S(2)}, u32[]{:S(2)}) collective-permute-start(bf16[528,128]{1,0:T(8,128)(2,1)S(1)} %get-tuple-element.38), channel_id=1, source_target_pairs={{0,2},{1,5},{2,0},{3,7},{4,6},{5,1},{6,4},{7,3},{8,10},{9,13},{10,... | collective-permute-start | bytes 405512 | tf_op jit(solution)/shard_map/ppermute | solution.py:462
  27.0 1.9 %collective-permute-start.6 = (bf16[528,128]{1,0:T(8,128)(2,1)S(1)}, bf16[528,128]{1,0:T(8,128)(2,1)S(1)}, u32[]{:S(2)}, u32[]{:S(2)}) collective-permute-start(bf16[528,128]{1,0:T(8,128)(2,1)S(1)} %get-tuple-element.39), channel_id=1, source_target_pairs={{0,6},{1,7},{2,4},{3,5},{4,2},{5,3},{6,0},{7,1},{8,14},{9,15},{10,... | collective-permute-start | bytes 405512 | tf_op jit(solution)/shard_map/ppermute | solution.py:462
  28.9 0.4 %collective-permute-start.5 = (bf16[528,128]{1,0:T(8,128)(2,1)S(1)}, bf16[528,128]{1,0:T(8,128)(2,1)S(1)}, u32[]{:S(2)}, u32[]{:S(2)}) collective-permute-start(bf16[528,128]{1,0:T(8,128)(2,1)S(1)} %get-tuple-element.40), channel_id=1, source_target_pairs={{0,4},{1,3},{2,6},{3,1},{4,0},{5,7},{6,2},{7,5},{8,12},{9,11},{10,... | collective-permute-start | bytes 405512 | tf_op jit(solution)/shard_map/ppermute | solution.py:462
  29.3 0.7 %out_m0_o0.1.refs_6_ = bf16[2,128,512]{2,1,0:T(8,128)(2,1)S(1)} custom-call(bf16[128,4096]{1,0:T(8,128)(2,1)S(1)} %copy-done, f32[8,8,128]{2,1,0:T(8,128)S(1)} %cum.1.cum_ref.refs_1_, f32[1,4096]{1,0:T(1,128)S(1)} %bitcast.19, bf16[528,128]{1,0:T(8,128)(2,1)S(1)} %get-tuple-element.37.refs_3_, f32[17,128,128]{2,1,0:T(8,128)S(1)} %intra_mine.1.refs_4_.refs_7_, ...), custom_call_target="tpu_custom_call" | custom-call | flops 1 | bytes 1 | tf_op jit(solution)/shard_map/out_m0_o0/pallas_call | solution.py:52
  30.0 0.8 %collective-permute-done.7.refs_6_ = bf16[528,128]{1,0:T(8,128)(2,1)S(1)} collective-permute-done((bf16[528,128]{1,0:T(8,128)(2,1)S(1)}, bf16[528,128]{1,0:T(8,128)(2,1)S(1)}, u32[]{:S(2)}, u32[]{:S(2)}) %collective-permute-start.7) | collective-permute-done | bytes 135200 | tf_op jit(solution)/shard_map/ppermute | solution.py:462
  30.8 3.1 %collective-permute-done.6.refs_3_ = bf16[528,128]{1,0:T(8,128)(2,1)S(1)} collective-permute-done((bf16[528,128]{1,0:T(8,128)(2,1)S(1)}, bf16[528,128]{1,0:T(8,128)(2,1)S(1)}, u32[]{:S(2)}, u32[]{:S(2)}) %collective-permute-start.6) | collective-permute-done | bytes 135200 | tf_op jit(solution)/shard_map/ppermute | solution.py:462
  33.9 1.1 %collective-permute-start.11 = (bf16[528,128]{1,0:T(8,128)(2,1)S(1)}, bf16[528,128]{1,0:T(8,128)(2,1)S(1)}, u32[]{:S(2)}, u32[]{:S(2)}) collective-permute-start(bf16[528,128]{1,0:T(8,128)(2,1)S(1)} %collective-permute-done.6.refs_3_), channel_id=1, source_target_pairs={{0,1},{1,0},{2,3},{3,2},{4,5},{5,4},{6,7},{7,6},{8,9},{9,8},{10,11... | collective-permute-start | bytes 405512 | tf_op jit(solution)/shard_map/ppermute | solution.py:459
  35.0 0.7 %out_m3_m1.1.refs_7_ = bf16[2,128,512]{2,1,0:T(8,128)(2,1)S(1)} custom-call(bf16[128,4096]{1,0:T(8,128)(2,1)S(1)} %copy-done, f32[8,8,128]{2,1,0:T(8,128)S(1)} %cum.1.cum_ref.refs_1_, f32[1,4096]{1,0:T(1,128)S(1)} %bitcast.20, bf16[528,128]{1,0:T(8,128)(2,1)S(1)} %collective-permute-done.6.refs_3_, f32[17,128,128]{2,1,0:T(8,128)S(1)} %intra_mine.1.refs_4_.refs_7_, ...), custom_call_target="tpu_custom_call" | custom-call | flops 1 | bytes 1 | tf_op jit(solution)/shard_map/out_m3_m1/pallas_call | solution.py:52
  35.7 0.6 %collective-permute-start.10 = (bf16[528,128]{1,0:T(8,128)(2,1)S(1)}, bf16[528,128]{1,0:T(8,128)(2,1)S(1)}, u32[]{:S(2)}, u32[]{:S(2)}) collective-permute-start(bf16[528,128]{1,0:T(8,128)(2,1)S(1)} %collective-permute-done.5.refs_3_), channel_id=1, source_target_pairs={{0,1},{1,0},{2,3},{3,2},{4,5},{5,4},{6,7},{7,6},{8,9},{9,8},{10,11... | collective-permute-start | bytes 405512 | tf_op jit(solution)/shard_map/ppermute | solution.py:459
  36.3 0.9 %out_m2_o3_o1.1.refs_8_ = bf16[3,128,512]{2,1,0:T(8,128)(2,1)S(1)} custom-call(bf16[128,4096]{1,0:T(8,128)(2,1)S(1)} %copy-done, f32[8,8,128]{2,1,0:T(8,128)S(1)} %cum.1.cum_ref.refs_1_, f32[1,4096]{1,0:T(1,128)S(1)} %bitcast.21, bf16[528,128]{1,0:T(8,128)(2,1)S(1)} %collective-permute-done.5.refs_3_, f32[17,128,128]{2,1,0:T(8,128)S(1)} %intra_mine.1.refs_4_.refs_7_, ...), custom_call_target="tpu_custom_call" | custom-call | flops 1 | bytes 1 | tf_op jit(solution)/shard_map/out_m2_o3_o1/pallas_call | solution.py:52
  37.2 1.5 %out_o2.1 = bf16[128,4096]{1,0:T(8,128)(2,1)} custom-call(bf16[128,4096]{1,0:T(8,128)(2,1)S(1)} %copy-done, f32[8,8,128]{2,1,0:T(8,128)S(1)} %cum.1.cum_ref.refs_1_, f32[1,4096]{1,0:T(1,128)S(1)} %bitcast.22, bf16[528,128]{1,0:T(8,128)(2,1)S(1)} %collective-permute-done.10.refs_3_, f32[17,128,128]{2,1,0:T(8,128)S(1)} %intra_other.1.refs_7_.refs_10_.refs_4_, ...), custom_call_target="tpu_custom_call" | custom-call | flops 1 | bytes 1 | tf_op jit(solution)/shard_map/out_o2/pallas_call | solution.py:52
  (28 shorter events, 1.7 us)
Async XLA Ops:
  0.0 2.8 %copy-start.1 = (bf16[128,4096]{1,0:T(8,128)(2,1)S(1)}, bf16[128,4096]{1,0:T(8,128)(2,1)}, u32[]{:S(2)}) copy-start(bf16[128,4096]{1,0:T(8,128)(2,1)} %k_ref.5) | copy-start | bytes 3145732
  0.0 2.8 %copy-start.2 = (bf16[128,4096]{1,0:T(8,128)(2,1)S(1)}, bf16[128,4096]{1,0:T(8,128)(2,1)}, u32[]{:S(2)}) copy-start(bf16[128,4096]{1,0:T(8,128)(2,1)} %v_ref.5) | copy-start | bytes 3145732
  0.0 2.8 %copy-start.3 = (f32[4,4096]{1,0:T(4,128)S(1)}, f32[4,4096]{1,0:T(4,128)}, u32[]{:S(2)}) copy-start(f32[4,4096]{1,0:T(4,128)} %w_ref.5) | copy-start | bytes 196612
  0.0 2.8 %copy-start.5 = (f32[128,32]{0,1:T(8,128)S(1)}, f32[128,32]{0,1:T(8,128)}, u32[]{:S(2)}) copy-start(f32[128,32]{0,1:T(8,128)} %param.9) | copy-start | bytes 49156
  2.7 2.0 %collective-permute-start = (bf16[4,560,128]{2,1,0:T(8,128)(2,1)S(1)}, bf16[4,560,128]{2,1,0:T(8,128)(2,1)S(1)}, u32[]{:S(2)}, u32[]{:S(2)}) collective-permute-start(bf16[4,560,128]{2,1,0:T(8,128)(2,1)S(1)} %states_other.1), channel_id=1, source_target_pairs={{0,1},{1,0},{2,3},{3,2},{4,5},{5,4},{6,7},{7,6},{8,9},{9,8},{10,11... | collective-permute-start | bytes 1720328 | tf_op jit(solution)/shard_map/ppermute | solution.py:459
  4.0 6.0 %copy-start = (bf16[128,4096]{1,0:T(8,128)(2,1)S(1)}, bf16[128,4096]{1,0:T(8,128)(2,1)}, u32[]{:S(2)}) copy-start(bf16[128,4096]{1,0:T(8,128)(2,1)} %refs_0_.7) | copy-start | bytes 3145732
  5.2 5.9 %collective-permute-start.3 = (bf16[1,560,128]{2,1,0:T(8,128)(2,1)S(1)}, bf16[1,560,128]{2,1,0:T(8,128)(2,1)S(1)}, u32[]{:S(2)}, u32[]{:S(2)}) collective-permute-start(bf16[1,560,128]{2,1,0:T(8,128)(2,1)S(1)} %get-tuple-element.33), channel_id=1, source_target_pairs={{0,2},{1,5},{2,0},{3,7},{4,6},{5,1},{6,4},{7,3},{8,10},{9,13},{10,... | collective-permute-start | bytes 430088 | tf_op jit(solution)/shard_map/ppermute | solution.py:462
  7.6 6.2 %collective-permute-start.2 = (bf16[1,560,128]{2,1,0:T(8,128)(2,1)S(1)}, bf16[1,560,128]{2,1,0:T(8,128)(2,1)S(1)}, u32[]{:S(2)}, u32[]{:S(2)}) collective-permute-start(bf16[1,560,128]{2,1,0:T(8,128)(2,1)S(1)} %get-tuple-element.34), channel_id=1, source_target_pairs={{0,6},{1,7},{2,4},{3,5},{4,2},{5,3},{6,0},{7,1},{8,14},{9,15},{10,... | collective-permute-start | bytes 430088 | tf_op jit(solution)/shard_map/ppermute | solution.py:462
  8.8 7.0 %collective-permute-start.1 = (bf16[1,560,128]{2,1,0:T(8,128)(2,1)S(1)}, bf16[1,560,128]{2,1,0:T(8,128)(2,1)S(1)}, u32[]{:S(2)}, u32[]{:S(2)}) collective-permute-start(bf16[1,560,128]{2,1,0:T(8,128)(2,1)S(1)} %get-tuple-element.35), channel_id=1, source_target_pairs={{0,4},{1,3},{2,6},{3,1},{4,0},{5,7},{6,2},{7,5},{8,12},{9,11},{10,... | collective-permute-start | bytes 430088 | tf_op jit(solution)/shard_map/ppermute | solution.py:462
  8.9 20.4 %collective-permute-start.9 = (bf16[4,560,128]{2,1,0:T(8,128)(2,1)S(1)}, bf16[4,560,128]{2,1,0:T(8,128)(2,1)S(1)}, u32[]{:S(2)}, u32[]{:S(2)}) collective-permute-start(bf16[4,560,128]{2,1,0:T(8,128)(2,1)S(1)} %states_mine.1.own_ref), channel_id=1, source_target_pairs={{0,1},{1,0},{2,3},{3,2},{4,5},{5,4},{6,7},{7,6},{8,9},{9,8},{10,11... | collective-permute-start | bytes 1720328 | tf_op jit(solution)/shard_map/ppermute | solution.py:459
  16.2 9.1 %collective-permute-start.4 = (bf16[1,528,128]{2,1,0:T(8,128)(2,1)S(1)}, bf16[1,528,128]{2,1,0:T(8,128)(2,1)S(1)}, u32[]{:S(2)}, u32[]{:S(2)}) collective-permute-start(bf16[1,528,128]{2,1,0:T(8,128)(2,1)S(1)} %span_state.1), channel_id=1, source_target_pairs={{0,8},{1,9},{2,10},{3,11},{4,12},{5,13},{6,14},{7,15},{8,0},{9,1},... | collective-permute-start | bytes 405512 | tf_op jit(solution)/shard_map/ppermute | solution.py:459
  19.8 9.5 %copy-start.4 = (f32[4096]{0:T(1024)S(1)}, f32[4096]{0:T(1024)}, u32[]{:S(2)}) copy-start(f32[4096]{0:T(1024)} %param.11) | copy-start | bytes 49156
  25.6 3.6 %collective-permute-start.8 = (bf16[528,128]{1,0:T(8,128)(2,1)S(1)}, bf16[528,128]{1,0:T(8,128)(2,1)S(1)}, u32[]{:S(2)}, u32[]{:S(2)}) collective-permute-start(bf16[528,128]{1,0:T(8,128)(2,1)S(1)} %get-tuple-element.37.refs_3_), channel_id=1, source_target_pairs={{0,1},{1,0},{2,3},{3,2},{4,5},{5,4},{6,7},{7,6},{8,9},{9,8},{10,11... | collective-permute-start | bytes 405512 | tf_op jit(solution)/shard_map/ppermute | solution.py:459
  26.6 4.2 %collective-permute-start.7 = (bf16[528,128]{1,0:T(8,128)(2,1)S(1)}, bf16[528,128]{1,0:T(8,128)(2,1)S(1)}, u32[]{:S(2)}, u32[]{:S(2)}) collective-permute-start(bf16[528,128]{1,0:T(8,128)(2,1)S(1)} %get-tuple-element.38), channel_id=1, source_target_pairs={{0,2},{1,5},{2,0},{3,7},{4,6},{5,1},{6,4},{7,3},{8,10},{9,13},{10,... | collective-permute-start | bytes 405512 | tf_op jit(solution)/shard_map/ppermute | solution.py:462
  27.0 6.9 %collective-permute-start.6 = (bf16[528,128]{1,0:T(8,128)(2,1)S(1)}, bf16[528,128]{1,0:T(8,128)(2,1)S(1)}, u32[]{:S(2)}, u32[]{:S(2)}) collective-permute-start(bf16[528,128]{1,0:T(8,128)(2,1)S(1)} %get-tuple-element.39), channel_id=1, source_target_pairs={{0,6},{1,7},{2,4},{3,5},{4,2},{5,3},{6,0},{7,1},{8,14},{9,15},{10,... | collective-permute-start | bytes 405512 | tf_op jit(solution)/shard_map/ppermute | solution.py:462
  28.9 6.8 %collective-permute-start.5 = (bf16[528,128]{1,0:T(8,128)(2,1)S(1)}, bf16[528,128]{1,0:T(8,128)(2,1)S(1)}, u32[]{:S(2)}, u32[]{:S(2)}) collective-permute-start(bf16[528,128]{1,0:T(8,128)(2,1)S(1)} %get-tuple-element.40), channel_id=1, source_target_pairs={{0,4},{1,3},{2,6},{3,1},{4,0},{5,7},{6,2},{7,5},{8,12},{9,11},{10,... | collective-permute-start | bytes 405512 | tf_op jit(solution)/shard_map/ppermute | solution.py:462
  33.9 2.4 %collective-permute-start.11 = (bf16[528,128]{1,0:T(8,128)(2,1)S(1)}, bf16[528,128]{1,0:T(8,128)(2,1)S(1)}, u32[]{:S(2)}, u32[]{:S(2)}) collective-permute-start(bf16[528,128]{1,0:T(8,128)(2,1)S(1)} %collective-permute-done.6.refs_3_), channel_id=1, source_target_pairs={{0,1},{1,0},{2,3},{3,2},{4,5},{5,4},{6,7},{7,6},{8,9},{9,8},{10,11... | collective-permute-start | bytes 405512 | tf_op jit(solution)/shard_map/ppermute | solution.py:459
  35.0 1.4 %collective-permute-start.12 = (bf16[528,128]{1,0:T(8,128)(2,1)S(1)}, bf16[528,128]{1,0:T(8,128)(2,1)S(1)}, u32[]{:S(2)}, u32[]{:S(2)}) collective-permute-start(bf16[528,128]{1,0:T(8,128)(2,1)S(1)} %collective-permute-done.7.refs_6_), channel_id=1, source_target_pairs={{0,1},{1,0},{2,3},{3,2},{4,5},{5,4},{6,7},{7,6},{8,9},{9,8},{10,11... | collective-permute-start | bytes 405512 | tf_op jit(solution)/shard_map/ppermute | solution.py:459
  35.7 1.6 %collective-permute-start.10 = (bf16[528,128]{1,0:T(8,128)(2,1)S(1)}, bf16[528,128]{1,0:T(8,128)(2,1)S(1)}, u32[]{:S(2)}, u32[]{:S(2)}) collective-permute-start(bf16[528,128]{1,0:T(8,128)(2,1)S(1)} %collective-permute-done.5.refs_3_), channel_id=1, source_target_pairs={{0,1},{1,0},{2,3},{3,2},{4,5},{5,4},{6,7},{7,6},{8,9},{9,8},{10,11... | collective-permute-start | bytes 405512 | tf_op jit(solution)/shard_map/ppermute | solution.py:459

commit v17 on v16

--- a/solution.py
+++ b/solution.py
@@ -611,21 +611,21 @@
             **hints,
         )
 
-    final, *early = EXCHANGE
+    *late, soon = EXCHANGE[1], EXCHANGE[0], EXCHANGE[2]
     items = [(True, 0), (False, 0)]
     made = output(items)
-    *late, made = lax.optimization_barrier((*[own[u] for u in early], made))
+    own[soon], made = lax.optimization_barrier((own[soon], made))
     earlier = [(items, made)]
-    own.update(zip(early, late))
-    other.update({u: swap(own[u], 1) for u in early})
-    items = [(True, u) for u in early]
+    other[soon] = swap(own[soon], 1)
+    items = [(True, soon)]
     made = output(items)
-    own[final], made = lax.optimization_barrier((own[final], made))
+    *arrived, made = lax.optimization_barrier((*[own[u] for u in late], made))
     earlier.append((items, made))
-    other[final] = swap(own[final], 1)
-    items = [(True, final)] + [(False, u) for u in early]
+    own.update(zip(late, arrived))
+    other.update({u: swap(own[u], 1) for u in late})
+    items = [(True, u) for u in late] + [(False, soon)]
     earlier.append((items, output(items)))
-    return output([(False, final)], earlier)
+    return output([(False, u) for u in late], earlier)
 
 
 def solution(mesh):

time: 39.2 us -> 39.2 us (level)
  starting transfers between devices: 12.6 us -> 15.3 us
  waiting for transfers between devices: 14.8 us -> 12.2 us
    ppermute x7, starting transfers between devices: 6.19 us -> 8.89 us  [swap(): return lax.ppermute(x, 'ctx', [(i, i ^ mask) for i in range(n)])]
    ppermute x6, waiting for transfers between devices: 8.61 us -> 6.63 us  [exchange(): lax.ppermute(x, 'ctx', [(i, i ^ 2 * distance(slot, i & 1)) for i in range...]
    ppermute x7, waiting for transfers between devices: 6.23 us -> 5.56 us  [swap(): return lax.ppermute(x, 'ctx', [(i, i ^ mask) for i in range(n)])]
where the time goes in v17:
time: 39.2 us; the launch traced here: 38.7 us
  starting transfers between devices  15.3 us (39%)
  waiting for transfers between devices  12.2 us (31%)
  Pallas kernels  11 us (28%)
    pallas_call x12, Pallas kernels, call(): pl.pallas_call(kernel, out_shape=out_shape, in_specs=in_specs, out_specs=...  11 us
    ppermute x7, starting transfers between devices, swap(): return lax.ppermute(x, 'ctx', [(i, i ^ mask) for i in range(n)])  8.89 us
    ppermute x6, waiting for transfers between devices, exchange(): lax.ppermute(x, 'ctx', [(i, i ^ 2 * distance(slot, i & 1)) for i in range...  6.63 us
    ppermute x6, starting transfers between devices, exchange(): lax.ppermute(x, 'ctx', [(i, i ^ 2 * distance(slot, i & 1)) for i in range...  6.38 us
    ppermute x7, waiting for transfers between devices, swap(): return lax.ppermute(x, 'ctx', [(i, i ^ mask) for i in range(n)])  5.56 us
  transfers between devices with their start and end apart: 13, of which 7 were waited for; matrix products, arithmetic and copies ran while one was open for 0% of the time, Pallas kernels for 17%

profile of v17, /device:TPU:1, one launch (start us, length us, event | category | flops | bytes accessed | tf_op | source)
XLA Modules:
  0.0 38.7 jit_solution(8672340638017511834)
XLA Ops:
  0.0 2.7 %states_other.1 = bf16[4,560,128]{2,1,0:T(8,128)(2,1)S(1)} custom-call(bf16[128,4096]{1,0:T(8,128)(2,1)} %k_ref.5, bf16[128,4096]{1,0:T(8,128)(2,1)} %v_ref.5, f32[4,4096]{1,0:T(4,128)} %w_ref.5, f32[32,128]{1,0:T(8,128)} %bitcast.23), custom_call_target="tpu_custom_call" | custom-call | tf_op jit(solution)/shard_map/states_other/pallas_call | solution.py:52
  2.8 1.2 %states_mine.1.own_ref = bf16[4,560,128]{2,1,0:T(8,128)(2,1)S(1)} custom-call(bf16[128,4096]{1,0:T(8,128)(2,1)S(1)} %copy-done.1, bf16[128,4096]{1,0:T(8,128)(2,1)S(1)} %copy-done.2, f32[4,4096]{1,0:T(4,128)S(1)} %copy-done.3, f32[32,128]{1,0:T(8,128)S(1)} %bitcast.24), custom_call_target="tpu_custom_call" | custom-call | tf_op jit(solution)/shard_map/states_mine/pallas_call | solution.py:52
  4.0 0.7 %collective-permute-done.got_ref.refs_5_.refs_8_ = bf16[4,560,128]{2,1,0:T(8,128)(2,1)S(1)} collective-permute-done((bf16[4,560,128]{2,1,0:T(8,128)(2,1)S(1)}, bf16[4,560,128]{2,1,0:T(8,128)(2,1)S(1)}, u32[]{:S(2)}, u32[]{:S(2)}) %collective-permute-start) | collective-permute-done | bytes 573472 | tf_op jit(solution)/shard_map/ppermute | solution.py:459
  5.2 2.4 %collective-permute-start.1 = (bf16[1,560,128]{2,1,0:T(8,128)(2,1)S(1)}, bf16[1,560,128]{2,1,0:T(8,128)(2,1)S(1)}, u32[]{:S(2)}, u32[]{:S(2)}) collective-permute-start(bf16[1,560,128]{2,1,0:T(8,128)(2,1)S(1)} %get-tuple-element.35), channel_id=1, source_target_pairs={{0,4},{1,3},{2,6},{3,1},{4,0},{5,7},{6,2},{7,5},{8,12},{9,11},{10,... | collective-permute-start | bytes 430088 | tf_op jit(solution)/shard_map/ppermute | solution.py:462
  7.6 1.2 %collective-permute-start.2 = (bf16[1,560,128]{2,1,0:T(8,128)(2,1)S(1)}, bf16[1,560,128]{2,1,0:T(8,128)(2,1)S(1)}, u32[]{:S(2)}, u32[]{:S(2)}) collective-permute-start(bf16[1,560,128]{2,1,0:T(8,128)(2,1)S(1)} %get-tuple-element.34), channel_id=1, source_target_pairs={{0,6},{1,7},{2,4},{3,5},{4,2},{5,3},{6,0},{7,1},{8,14},{9,15},{10,... | collective-permute-start | bytes 430088 | tf_op jit(solution)/shard_map/ppermute | solution.py:462
  8.9 0.9 %collective-permute-start.9 = (bf16[4,560,128]{2,1,0:T(8,128)(2,1)S(1)}, bf16[4,560,128]{2,1,0:T(8,128)(2,1)S(1)}, u32[]{:S(2)}, u32[]{:S(2)}) collective-permute-start(bf16[4,560,128]{2,1,0:T(8,128)(2,1)S(1)} %states_mine.1.own_ref), channel_id=1, source_target_pairs={{0,1},{1,0},{2,3},{3,2},{4,5},{5,4},{6,7},{7,6},{8,9},{9,8},{10,11... | collective-permute-start | bytes 1720328 | tf_op jit(solution)/shard_map/ppermute | solution.py:459
  10.0 1.1 %intra_mine.1.refs_4_.refs_7_ = f32[17,128,128]{2,1,0:T(8,128)S(1)} custom-call(bf16[128,4096]{1,0:T(8,128)(2,1)S(1)} %copy-done, bf16[128,4096]{1,0:T(8,128)(2,1)S(1)} %copy-done.1, bf16[128,4096]{1,0:T(8,128)(2,1)S(1)} %copy-done.2, f32[4,4096]{1,0:T(4,128)S(1)} %copy-done.3, f32[8,8,128]{2,1,0:T(8,128)S(1)} %cum.1.cum_ref.refs_1_), custom_call_target="tpu_custom_call" | custom-call | tf_op jit(solution)/shard_map/intra_mine/pallas_call | solution.py:52
  11.1 3.0 %collective-permute-done.2.refs_3_ = bf16[1,560,128]{2,1,0:T(8,128)(2,1)S(1)} collective-permute-done((bf16[1,560,128]{2,1,0:T(8,128)(2,1)S(1)}, bf16[1,560,128]{2,1,0:T(8,128)(2,1)S(1)}, u32[]{:S(2)}, u32[]{:S(2)}) %collective-permute-start.2) | collective-permute-done | bytes 143392 | tf_op jit(solution)/shard_map/ppermute | solution.py:462
  14.2 1.4 %collective-permute-done.3.refs_1_ = bf16[1,560,128]{2,1,0:T(8,128)(2,1)S(1)} collective-permute-done((bf16[1,560,128]{2,1,0:T(8,128)(2,1)S(1)}, bf16[1,560,128]{2,1,0:T(8,128)(2,1)S(1)}, u32[]{:S(2)}, u32[]{:S(2)}) %collective-permute-start.3) | collective-permute-done | bytes 143392 | tf_op jit(solution)/shard_map/ppermute | solution.py:462
  16.0 2.8 %collective-permute-start.4 = (bf16[1,528,128]{2,1,0:T(8,128)(2,1)S(1)}, bf16[1,528,128]{2,1,0:T(8,128)(2,1)S(1)}, u32[]{:S(2)}, u32[]{:S(2)}) collective-permute-start(bf16[1,528,128]{2,1,0:T(8,128)(2,1)S(1)} %span_state.1), channel_id=1, source_target_pairs={{0,8},{1,9},{2,10},{3,11},{4,12},{5,13},{6,14},{7,15},{8,0},{9,1},... | collective-permute-start | bytes 405512 | tf_op jit(solution)/shard_map/ppermute | solution.py:459
  18.8 1.1 %intra_other.1.refs_7_.refs_10_.refs_4_ = f32[17,128,128]{2,1,0:T(8,128)S(1)} custom-call(bf16[128,4096]{1,0:T(8,128)(2,1)S(1)} %copy-done, bf16[128,4096]{1,0:T(8,128)(2,1)S(1)} %copy-done.1, bf16[128,4096]{1,0:T(8,128)(2,1)S(1)} %copy-done.2, f32[4,4096]{1,0:T(4,128)S(1)} %copy-done.3, f32[8,8,128]{2,1,0:T(8,128)S(1)} %cum.1.cum_ref.refs_1_), custom_call_target="tpu_custom_call" | custom-call | tf_op jit(solution)/shard_map/intra_other/pallas_call | solution.py:52
  19.9 4.7 %collective-permute-done.4.refs_4_ = bf16[1,528,128]{2,1,0:T(8,128)(2,1)S(1)} collective-permute-done((bf16[1,528,128]{2,1,0:T(8,128)(2,1)S(1)}, bf16[1,528,128]{2,1,0:T(8,128)(2,1)S(1)}, u32[]{:S(2)}, u32[]{:S(2)}) %collective-permute-start.4) | collective-permute-done | bytes 135200 | tf_op jit(solution)/shard_map/ppermute | solution.py:459
  25.0 1.7 %collective-permute-start.8 = (bf16[528,128]{1,0:T(8,128)(2,1)S(1)}, bf16[528,128]{1,0:T(8,128)(2,1)S(1)}, u32[]{:S(2)}, u32[]{:S(2)}) collective-permute-start(bf16[528,128]{1,0:T(8,128)(2,1)S(1)} %get-tuple-element.37.refs_3_), channel_id=1, source_target_pairs={{0,1},{1,0},{2,3},{3,2},{4,5},{5,4},{6,7},{7,6},{8,9},{9,8},{10,11... | collective-permute-start | bytes 405512 | tf_op jit(solution)/shard_map/ppermute | solution.py:459
  26.7 0.4 %collective-permute-start.7 = (bf16[528,128]{1,0:T(8,128)(2,1)S(1)}, bf16[528,128]{1,0:T(8,128)(2,1)S(1)}, u32[]{:S(2)}, u32[]{:S(2)}) collective-permute-start(bf16[528,128]{1,0:T(8,128)(2,1)S(1)} %get-tuple-element.38), channel_id=1, source_target_pairs={{0,2},{1,5},{2,0},{3,7},{4,6},{5,1},{6,4},{7,3},{8,10},{9,13},{10,... | collective-permute-start | bytes 405512 | tf_op jit(solution)/shard_map/ppermute | solution.py:462
  27.1 1.7 %collective-permute-start.5 = (bf16[528,128]{1,0:T(8,128)(2,1)S(1)}, bf16[528,128]{1,0:T(8,128)(2,1)S(1)}, u32[]{:S(2)}, u32[]{:S(2)}) collective-permute-start(bf16[528,128]{1,0:T(8,128)(2,1)S(1)} %get-tuple-element.40), channel_id=1, source_target_pairs={{0,6},{1,7},{2,4},{3,5},{4,2},{5,3},{6,0},{7,1},{8,14},{9,15},{10,... | collective-permute-start | bytes 405512 | tf_op jit(solution)/shard_map/ppermute | solution.py:462
  28.9 0.5 %collective-permute-start.6 = (bf16[528,128]{1,0:T(8,128)(2,1)S(1)}, bf16[528,128]{1,0:T(8,128)(2,1)S(1)}, u32[]{:S(2)}, u32[]{:S(2)}) collective-permute-start(bf16[528,128]{1,0:T(8,128)(2,1)S(1)} %get-tuple-element.39), channel_id=1, source_target_pairs={{0,4},{1,3},{2,6},{3,1},{4,0},{5,7},{6,2},{7,5},{8,12},{9,11},{10,... | collective-permute-start | bytes 405512 | tf_op jit(solution)/shard_map/ppermute | solution.py:462
  29.4 0.7 %out_m0_o0.1.refs_9_ = bf16[2,128,512]{2,1,0:T(8,128)(2,1)S(1)} custom-call(bf16[128,4096]{1,0:T(8,128)(2,1)S(1)} %copy-done, f32[8,8,128]{2,1,0:T(8,128)S(1)} %cum.1.cum_ref.refs_1_, f32[1,4096]{1,0:T(1,128)S(1)} %bitcast.19, bf16[528,128]{1,0:T(8,128)(2,1)S(1)} %get-tuple-element.37.refs_3_, f32[17,128,128]{2,1,0:T(8,128)S(1)} %intra_mine.1.refs_4_.refs_7_, ...), custom_call_target="tpu_custom_call" | custom-call | flops 1 | bytes 1 | tf_op jit(solution)/shard_map/out_m0_o0/pallas_call | solution.py:52
  30.0 0.8 %collective-permute-done.7.refs_3_ = bf16[528,128]{1,0:T(8,128)(2,1)S(1)} collective-permute-done((bf16[528,128]{1,0:T(8,128)(2,1)S(1)}, bf16[528,128]{1,0:T(8,128)(2,1)S(1)}, u32[]{:S(2)}, u32[]{:S(2)}) %collective-permute-start.7) | collective-permute-done | bytes 135200 | tf_op jit(solution)/shard_map/ppermute | solution.py:462
  30.9 2.8 %collective-permute-start.12 = (bf16[528,128]{1,0:T(8,128)(2,1)S(1)}, bf16[528,128]{1,0:T(8,128)(2,1)S(1)}, u32[]{:S(2)}, u32[]{:S(2)}) collective-permute-start(bf16[528,128]{1,0:T(8,128)(2,1)S(1)} %collective-permute-done.7.refs_3_), channel_id=1, source_target_pairs={{0,1},{1,0},{2,3},{3,2},{4,5},{5,4},{6,7},{7,6},{8,9},{9,8},{10,11... | collective-permute-start | bytes 405512 | tf_op jit(solution)/shard_map/ppermute | solution.py:459
  33.7 0.6 %out_m1.1.refs_10_ = bf16[1,128,512]{2,1,0:T(8,128)(2,1)S(1)} custom-call(bf16[128,4096]{1,0:T(8,128)(2,1)S(1)} %copy-done, f32[8,8,128]{2,1,0:T(8,128)S(1)} %cum.1.cum_ref.refs_1_, f32[1,4096]{1,0:T(1,128)S(1)} %bitcast.20, bf16[528,128]{1,0:T(8,128)(2,1)S(1)} %collective-permute-done.7.refs_3_, f32[17,128,128]{2,1,0:T(8,128)S(1)} %intra_mine.1.refs_4_.refs_7_, ...), custom_call_target="tpu_custom_call" | custom-call | flops 1 | bytes 1 | tf_op jit(solution)/shard_map/out_m1/pallas_call | solution.py:52
  34.3 1.4 %collective-permute-done.6.refs_6_ = bf16[528,128]{1,0:T(8,128)(2,1)S(1)} collective-permute-done((bf16[528,128]{1,0:T(8,128)(2,1)S(1)}, bf16[528,128]{1,0:T(8,128)(2,1)S(1)}, u32[]{:S(2)}, u32[]{:S(2)}) %collective-permute-start.6) | collective-permute-done | bytes 135200 | tf_op jit(solution)/shard_map/ppermute | solution.py:462
  35.6 0.5 %collective-permute-start.11 = (bf16[528,128]{1,0:T(8,128)(2,1)S(1)}, bf16[528,128]{1,0:T(8,128)(2,1)S(1)}, u32[]{:S(2)}, u32[]{:S(2)}) collective-permute-start(bf16[528,128]{1,0:T(8,128)(2,1)S(1)} %collective-permute-done.6.refs_6_), channel_id=1, source_target_pairs={{0,1},{1,0},{2,3},{3,2},{4,5},{5,4},{6,7},{7,6},{8,9},{9,8},{10,11... | collective-permute-start | bytes 405512 | tf_op jit(solution)/shard_map/ppermute | solution.py:459
  36.1 0.9 %out_m3_m2_o1.1.refs_11_ = bf16[3,128,512]{2,1,0:T(8,128)(2,1)S(1)} custom-call(bf16[128,4096]{1,0:T(8,128)(2,1)S(1)} %copy-done, f32[8,8,128]{2,1,0:T(8,128)S(1)} %cum.1.cum_ref.refs_1_, f32[1,4096]{1,0:T(1,128)S(1)} %bitcast.21, bf16[528,128]{1,0:T(8,128)(2,1)S(1)} %collective-permute-done.5.refs_3_, f32[17,128,128]{2,1,0:T(8,128)S(1)} %intra_mine.1.refs_4_.refs_7_, ...), custom_call_target="tpu_custom_call" | custom-call | flops 1 | bytes 1 | tf_op jit(solution)/shard_map/out_m3_m2_o1/pallas_call | solution.py:52
  37.2 1.6 %out_o3_o2.1 = bf16[128,4096]{1,0:T(8,128)(2,1)} custom-call(bf16[128,4096]{1,0:T(8,128)(2,1)S(1)} %copy-done, f32[8,8,128]{2,1,0:T(8,128)S(1)} %cum.1.cum_ref.refs_1_, f32[1,4096]{1,0:T(1,128)S(1)} %bitcast.22, bf16[528,128]{1,0:T(8,128)(2,1)S(1)} %collective-permute-done.10.refs_3_, f32[17,128,128]{2,1,0:T(8,128)S(1)} %intra_other.1.refs_7_.refs_10_.refs_4_, ...), custom_call_target="tpu_custom_call" | custom-call | flops 1 | bytes 1 | tf_op jit(solution)/shard_map/out_o3_o2/pallas_call | solution.py:52
  (28 shorter events, 1.7 us)
Async XLA Ops:
  0.0 2.8 %copy-start.1 = (bf16[128,4096]{1,0:T(8,128)(2,1)S(1)}, bf16[128,4096]{1,0:T(8,128)(2,1)}, u32[]{:S(2)}) copy-start(bf16[128,4096]{1,0:T(8,128)(2,1)} %k_ref.5) | copy-start | bytes 3145732
  0.0 2.8 %copy-start.2 = (bf16[128,4096]{1,0:T(8,128)(2,1)S(1)}, bf16[128,4096]{1,0:T(8,128)(2,1)}, u32[]{:S(2)}) copy-start(bf16[128,4096]{1,0:T(8,128)(2,1)} %v_ref.5) | copy-start | bytes 3145732
  0.0 2.8 %copy-start.3 = (f32[4,4096]{1,0:T(4,128)S(1)}, f32[4,4096]{1,0:T(4,128)}, u32[]{:S(2)}) copy-start(f32[4,4096]{1,0:T(4,128)} %w_ref.5) | copy-start | bytes 196612
  0.0 2.8 %copy-start.5 = (f32[128,32]{0,1:T(8,128)S(1)}, f32[128,32]{0,1:T(8,128)}, u32[]{:S(2)}) copy-start(f32[128,32]{0,1:T(8,128)} %param.9) | copy-start | bytes 49156
  2.7 2.0 %collective-permute-start = (bf16[4,560,128]{2,1,0:T(8,128)(2,1)S(1)}, bf16[4,560,128]{2,1,0:T(8,128)(2,1)S(1)}, u32[]{:S(2)}, u32[]{:S(2)}) collective-permute-start(bf16[4,560,128]{2,1,0:T(8,128)(2,1)S(1)} %states_other.1), channel_id=1, source_target_pairs={{0,1},{1,0},{2,3},{3,2},{4,5},{5,4},{6,7},{7,6},{8,9},{9,8},{10,11... | collective-permute-start | bytes 1720328 | tf_op jit(solution)/shard_map/ppermute | solution.py:459
  4.0 6.0 %copy-start = (bf16[128,4096]{1,0:T(8,128)(2,1)S(1)}, bf16[128,4096]{1,0:T(8,128)(2,1)}, u32[]{:S(2)}) copy-start(bf16[128,4096]{1,0:T(8,128)(2,1)} %refs_0_.7) | copy-start | bytes 3145732
  5.2 6.0 %collective-permute-start.1 = (bf16[1,560,128]{2,1,0:T(8,128)(2,1)S(1)}, bf16[1,560,128]{2,1,0:T(8,128)(2,1)S(1)}, u32[]{:S(2)}, u32[]{:S(2)}) collective-permute-start(bf16[1,560,128]{2,1,0:T(8,128)(2,1)S(1)} %get-tuple-element.35), channel_id=1, source_target_pairs={{0,4},{1,3},{2,6},{3,1},{4,0},{5,7},{6,2},{7,5},{8,12},{9,11},{10,... | collective-permute-start | bytes 430088 | tf_op jit(solution)/shard_map/ppermute | solution.py:462
  7.6 6.6 %collective-permute-start.2 = (bf16[1,560,128]{2,1,0:T(8,128)(2,1)S(1)}, bf16[1,560,128]{2,1,0:T(8,128)(2,1)S(1)}, u32[]{:S(2)}, u32[]{:S(2)}) collective-permute-start(bf16[1,560,128]{2,1,0:T(8,128)(2,1)S(1)} %get-tuple-element.34), channel_id=1, source_target_pairs={{0,6},{1,7},{2,4},{3,5},{4,2},{5,3},{6,0},{7,1},{8,14},{9,15},{10,... | collective-permute-start | bytes 430088 | tf_op jit(solution)/shard_map/ppermute | solution.py:462
  8.8 6.8 %collective-permute-start.3 = (bf16[1,560,128]{2,1,0:T(8,128)(2,1)S(1)}, bf16[1,560,128]{2,1,0:T(8,128)(2,1)S(1)}, u32[]{:S(2)}, u32[]{:S(2)}) collective-permute-start(bf16[1,560,128]{2,1,0:T(8,128)(2,1)S(1)} %get-tuple-element.33), channel_id=1, source_target_pairs={{0,2},{1,5},{2,0},{3,7},{4,6},{5,1},{6,4},{7,3},{8,10},{9,13},{10,... | collective-permute-start | bytes 430088 | tf_op jit(solution)/shard_map/ppermute | solution.py:462
  8.9 20.5 %collective-permute-start.9 = (bf16[4,560,128]{2,1,0:T(8,128)(2,1)S(1)}, bf16[4,560,128]{2,1,0:T(8,128)(2,1)S(1)}, u32[]{:S(2)}, u32[]{:S(2)}) collective-permute-start(bf16[4,560,128]{2,1,0:T(8,128)(2,1)S(1)} %states_mine.1.own_ref), channel_id=1, source_target_pairs={{0,1},{1,0},{2,3},{3,2},{4,5},{5,4},{6,7},{7,6},{8,9},{9,8},{10,11... | collective-permute-start | bytes 1720328 | tf_op jit(solution)/shard_map/ppermute | solution.py:459
  16.0 8.6 %collective-permute-start.4 = (bf16[1,528,128]{2,1,0:T(8,128)(2,1)S(1)}, bf16[1,528,128]{2,1,0:T(8,128)(2,1)S(1)}, u32[]{:S(2)}, u32[]{:S(2)}) collective-permute-start(bf16[1,528,128]{2,1,0:T(8,128)(2,1)S(1)} %span_state.1), channel_id=1, source_target_pairs={{0,8},{1,9},{2,10},{3,11},{4,12},{5,13},{6,14},{7,15},{8,0},{9,1},... | collective-permute-start | bytes 405512 | tf_op jit(solution)/shard_map/ppermute | solution.py:459
  19.9 9.5 %copy-start.4 = (f32[4096]{0:T(1024)S(1)}, f32[4096]{0:T(1024)}, u32[]{:S(2)}) copy-start(f32[4096]{0:T(1024)} %param.11) | copy-start | bytes 49156
  25.0 4.3 %collective-permute-start.8 = (bf16[528,128]{1,0:T(8,128)(2,1)S(1)}, bf16[528,128]{1,0:T(8,128)(2,1)S(1)}, u32[]{:S(2)}, u32[]{:S(2)}) collective-permute-start(bf16[528,128]{1,0:T(8,128)(2,1)S(1)} %get-tuple-element.37.refs_3_), channel_id=1, source_target_pairs={{0,1},{1,0},{2,3},{3,2},{4,5},{5,4},{6,7},{7,6},{8,9},{9,8},{10,11... | collective-permute-start | bytes 405512 | tf_op jit(solution)/shard_map/ppermute | solution.py:459
  26.7 4.2 %collective-permute-start.7 = (bf16[528,128]{1,0:T(8,128)(2,1)S(1)}, bf16[528,128]{1,0:T(8,128)(2,1)S(1)}, u32[]{:S(2)}, u32[]{:S(2)}) collective-permute-start(bf16[528,128]{1,0:T(8,128)(2,1)S(1)} %get-tuple-element.38), channel_id=1, source_target_pairs={{0,2},{1,5},{2,0},{3,7},{4,6},{5,1},{6,4},{7,3},{8,10},{9,13},{10,... | collective-permute-start | bytes 405512 | tf_op jit(solution)/shard_map/ppermute | solution.py:462
  27.1 7.1 %collective-permute-start.5 = (bf16[528,128]{1,0:T(8,128)(2,1)S(1)}, bf16[528,128]{1,0:T(8,128)(2,1)S(1)}, u32[]{:S(2)}, u32[]{:S(2)}) collective-permute-start(bf16[528,128]{1,0:T(8,128)(2,1)S(1)} %get-tuple-element.40), channel_id=1, source_target_pairs={{0,6},{1,7},{2,4},{3,5},{4,2},{5,3},{6,0},{7,1},{8,14},{9,15},{10,... | collective-permute-start | bytes 405512 | tf_op jit(solution)/shard_map/ppermute | solution.py:462
  28.9 6.7 %collective-permute-start.6 = (bf16[528,128]{1,0:T(8,128)(2,1)S(1)}, bf16[528,128]{1,0:T(8,128)(2,1)S(1)}, u32[]{:S(2)}, u32[]{:S(2)}) collective-permute-start(bf16[528,128]{1,0:T(8,128)(2,1)S(1)} %get-tuple-element.39), channel_id=1, source_target_pairs={{0,4},{1,3},{2,6},{3,1},{4,0},{5,7},{6,2},{7,5},{8,12},{9,11},{10,... | collective-permute-start | bytes 405512 | tf_op jit(solution)/shard_map/ppermute | solution.py:462
  30.9 5.3 %collective-permute-start.12 = (bf16[528,128]{1,0:T(8,128)(2,1)S(1)}, bf16[528,128]{1,0:T(8,128)(2,1)S(1)}, u32[]{:S(2)}, u32[]{:S(2)}) collective-permute-start(bf16[528,128]{1,0:T(8,128)(2,1)S(1)} %collective-permute-done.7.refs_3_), channel_id=1, source_target_pairs={{0,1},{1,0},{2,3},{3,2},{4,5},{5,4},{6,7},{7,6},{8,9},{9,8},{10,11... | collective-permute-start | bytes 405512 | tf_op jit(solution)/shard_map/ppermute | solution.py:459
  35.6 1.4 %collective-permute-start.10 = (bf16[528,128]{1,0:T(8,128)(2,1)S(1)}, bf16[528,128]{1,0:T(8,128)(2,1)S(1)}, u32[]{:S(2)}, u32[]{:S(2)}) collective-permute-start(bf16[528,128]{1,0:T(8,128)(2,1)S(1)} %collective-permute-done.5.refs_3_), channel_id=1, source_target_pairs={{0,1},{1,0},{2,3},{3,2},{4,5},{5,4},{6,7},{7,6},{8,9},{9,8},{10,11... | collective-permute-start | bytes 405512 | tf_op jit(solution)/shard_map/ppermute | solution.py:459
  35.6 1.5 %collective-permute-start.11 = (bf16[528,128]{1,0:T(8,128)(2,1)S(1)}, bf16[528,128]{1,0:T(8,128)(2,1)S(1)}, u32[]{:S(2)}, u32[]{:S(2)}) collective-permute-start(bf16[528,128]{1,0:T(8,128)(2,1)S(1)} %collective-permute-done.6.refs_6_), channel_id=1, source_target_pairs={{0,1},{1,0},{2,3},{3,2},{4,5},{5,4},{6,7},{7,6},{8,9},{9,8},{10,11... | collective-permute-start | bytes 405512 | tf_op jit(solution)/shard_map/ppermute | solution.py:459

commit v18 on v17

--- a/solution.py
+++ b/solution.py
@@ -514,7 +514,7 @@
     order = pltpu.VMEM((CHIPS, packet, size), BF16)
 
     packets = {0: chip_states[0]}
-    for g in EXCHANGE:
+    for g in EXCHANGE[::-1]:
         packets[g] = exchange(chip_states[g], g)
     q_after, decay_after, chip_states = lax.optimization_barrier(
         (queries, log_decay, chip_states)
@@ -526,8 +526,10 @@
         decay_after.T,
     )
     intra_mine = intra_part(True, q_after)
-    *late, intra_mine = lax.optimization_barrier((*[packets[g] for g in EXCHANGE], intra_mine))
-    packets.update(zip(EXCHANGE, late))
+    *late, intra_mine = lax.optimization_barrier(
+        (*[packets[g] for g in EXCHANGE[::-1]], intra_mine)
+    )
+    packets.update(zip(EXCHANGE[::-1], late))
     packets = [packets[g] for g in range(CHIPS)]
 
     known = []

time: 39.2 us -> 39.2 us (level)
  starting transfers between devices: 15.3 us -> 14.4 us
  waiting for transfers between devices: 12.2 us -> 13 us
    ppermute x7, starting transfers between devices: 8.89 us -> 8.02 us  [swap(): return lax.ppermute(x, 'ctx', [(i, i ^ mask) for i in range(n)])]
    ppermute x7, waiting for transfers between devices: 5.56 us -> 6.27 us  [swap(): return lax.ppermute(x, 'ctx', [(i, i ^ mask) for i in range(n)])]
where the time goes in v18:
time: 39.2 us; the launch traced here: 38.7 us
  starting transfers between devices  14.4 us (37%)
  waiting for transfers between devices  13 us (33%)
  Pallas kernels  11 us (28%)
    pallas_call x12, Pallas kernels, call(): pl.pallas_call(kernel, out_shape=out_shape, in_specs=in_specs, out_specs=...  11 us
    ppermute x7, starting transfers between devices, swap(): return lax.ppermute(x, 'ctx', [(i, i ^ mask) for i in range(n)])  8.02 us
    ppermute x6, waiting for transfers between devices, exchange(): lax.ppermute(x, 'ctx', [(i, i ^ 2 * distance(slot, i & 1)) for i in range...  6.76 us
    ppermute x6, starting transfers between devices, exchange(): lax.ppermute(x, 'ctx', [(i, i ^ 2 * distance(slot, i & 1)) for i in range...  6.4 us
    ppermute x7, waiting for transfers between devices, swap(): return lax.ppermute(x, 'ctx', [(i, i ^ mask) for i in range(n)])  6.27 us
  transfers between devices with their start and end apart: 13, of which 7 were waited for; matrix products, arithmetic and copies ran while one was open for 0% of the time, Pallas kernels for 17%

profile of v18, /device:TPU:1, one launch (start us, length us, event | category | flops | bytes accessed | tf_op | source)
XLA Modules:
  0.0 38.7 jit_solution(3925906855625566444)
XLA Ops:
  0.0 2.7 %states_other.1 = bf16[4,560,128]{2,1,0:T(8,128)(2,1)S(1)} custom-call(bf16[128,4096]{1,0:T(8,128)(2,1)} %k_ref.5, bf16[128,4096]{1,0:T(8,128)(2,1)} %v_ref.5, f32[4,4096]{1,0:T(4,128)} %w_ref.5, f32[32,128]{1,0:T(8,128)} %bitcast.23), custom_call_target="tpu_custom_call" | custom-call | tf_op jit(solution)/shard_map/states_other/pallas_call | solution.py:52
  2.8 1.2 %states_mine.1.own_ref = bf16[4,560,128]{2,1,0:T(8,128)(2,1)S(1)} custom-call(bf16[128,4096]{1,0:T(8,128)(2,1)S(1)} %copy-done.1, bf16[128,4096]{1,0:T(8,128)(2,1)S(1)} %copy-done.2, f32[4,4096]{1,0:T(4,128)S(1)} %copy-done.3, f32[32,128]{1,0:T(8,128)S(1)} %bitcast.24), custom_call_target="tpu_custom_call" | custom-call | tf_op jit(solution)/shard_map/states_mine/pallas_call | solution.py:52
  4.0 0.7 %collective-permute-done.got_ref.refs_5_.refs_8_ = bf16[4,560,128]{2,1,0:T(8,128)(2,1)S(1)} collective-permute-done((bf16[4,560,128]{2,1,0:T(8,128)(2,1)S(1)}, bf16[4,560,128]{2,1,0:T(8,128)(2,1)S(1)}, u32[]{:S(2)}, u32[]{:S(2)}) %collective-permute-start) | collective-permute-done | bytes 573472 | tf_op jit(solution)/shard_map/ppermute | solution.py:459
  5.2 2.5 %collective-permute-start.1 = (bf16[1,560,128]{2,1,0:T(8,128)(2,1)S(1)}, bf16[1,560,128]{2,1,0:T(8,128)(2,1)S(1)}, u32[]{:S(2)}, u32[]{:S(2)}) collective-permute-start(bf16[1,560,128]{2,1,0:T(8,128)(2,1)S(1)} %get-tuple-element.35), channel_id=1, source_target_pairs={{0,2},{1,5},{2,0},{3,7},{4,6},{5,1},{6,4},{7,3},{8,10},{9,13},{10,... | collective-permute-start | bytes 430088 | tf_op jit(solution)/shard_map/ppermute | solution.py:462
  7.6 1.1 %collective-permute-start.2 = (bf16[1,560,128]{2,1,0:T(8,128)(2,1)S(1)}, bf16[1,560,128]{2,1,0:T(8,128)(2,1)S(1)}, u32[]{:S(2)}, u32[]{:S(2)}) collective-permute-start(bf16[1,560,128]{2,1,0:T(8,128)(2,1)S(1)} %get-tuple-element.34), channel_id=1, source_target_pairs={{0,6},{1,7},{2,4},{3,5},{4,2},{5,3},{6,0},{7,1},{8,14},{9,15},{10,... | collective-permute-start | bytes 430088 | tf_op jit(solution)/shard_map/ppermute | solution.py:462
  8.9 0.9 %collective-permute-start.9 = (bf16[4,560,128]{2,1,0:T(8,128)(2,1)S(1)}, bf16[4,560,128]{2,1,0:T(8,128)(2,1)S(1)}, u32[]{:S(2)}, u32[]{:S(2)}) collective-permute-start(bf16[4,560,128]{2,1,0:T(8,128)(2,1)S(1)} %states_mine.1.own_ref), channel_id=1, source_target_pairs={{0,1},{1,0},{2,3},{3,2},{4,5},{5,4},{6,7},{7,6},{8,9},{9,8},{10,11... | collective-permute-start | bytes 1720328 | tf_op jit(solution)/shard_map/ppermute | solution.py:459
  10.0 1.1 %intra_mine.1.refs_4_.refs_7_ = f32[17,128,128]{2,1,0:T(8,128)S(1)} custom-call(bf16[128,4096]{1,0:T(8,128)(2,1)S(1)} %copy-done, bf16[128,4096]{1,0:T(8,128)(2,1)S(1)} %copy-done.1, bf16[128,4096]{1,0:T(8,128)(2,1)S(1)} %copy-done.2, f32[4,4096]{1,0:T(4,128)S(1)} %copy-done.3, f32[8,8,128]{2,1,0:T(8,128)S(1)} %cum.1.cum_ref.refs_1_), custom_call_target="tpu_custom_call" | custom-call | tf_op jit(solution)/shard_map/intra_mine/pallas_call | solution.py:52
  11.1 2.7 %collective-permute-done.2.refs_3_ = bf16[1,560,128]{2,1,0:T(8,128)(2,1)S(1)} collective-permute-done((bf16[1,560,128]{2,1,0:T(8,128)(2,1)S(1)}, bf16[1,560,128]{2,1,0:T(8,128)(2,1)S(1)}, u32[]{:S(2)}, u32[]{:S(2)}) %collective-permute-start.2) | collective-permute-done | bytes 143392 | tf_op jit(solution)/shard_map/ppermute | solution.py:462
  13.8 2.0 %collective-permute-done.3.refs_2_ = bf16[1,560,128]{2,1,0:T(8,128)(2,1)S(1)} collective-permute-done((bf16[1,560,128]{2,1,0:T(8,128)(2,1)S(1)}, bf16[1,560,128]{2,1,0:T(8,128)(2,1)S(1)}, u32[]{:S(2)}, u32[]{:S(2)}) %collective-permute-start.3) | collective-permute-done | bytes 143392 | tf_op jit(solution)/shard_map/ppermute | solution.py:462
  16.2 2.5 %collective-permute-start.4 = (bf16[1,528,128]{2,1,0:T(8,128)(2,1)S(1)}, bf16[1,528,128]{2,1,0:T(8,128)(2,1)S(1)}, u32[]{:S(2)}, u32[]{:S(2)}) collective-permute-start(bf16[1,528,128]{2,1,0:T(8,128)(2,1)S(1)} %span_state.1), channel_id=1, source_target_pairs={{0,8},{1,9},{2,10},{3,11},{4,12},{5,13},{6,14},{7,15},{8,0},{9,1},... | collective-permute-start | bytes 405512 | tf_op jit(solution)/shard_map/ppermute | solution.py:459
  18.7 1.1 %intra_other.1.refs_7_.refs_10_.refs_4_ = f32[17,128,128]{2,1,0:T(8,128)S(1)} custom-call(bf16[128,4096]{1,0:T(8,128)(2,1)S(1)} %copy-done, bf16[128,4096]{1,0:T(8,128)(2,1)S(1)} %copy-done.1, bf16[128,4096]{1,0:T(8,128)(2,1)S(1)} %copy-done.2, f32[4,4096]{1,0:T(4,128)S(1)} %copy-done.3, f32[8,8,128]{2,1,0:T(8,128)S(1)} %cum.1.cum_ref.refs_1_), custom_call_target="tpu_custom_call" | custom-call | tf_op jit(solution)/shard_map/intra_other/pallas_call | solution.py:52
  19.8 5.4 %collective-permute-done.4.refs_4_ = bf16[1,528,128]{2,1,0:T(8,128)(2,1)S(1)} collective-permute-done((bf16[1,528,128]{2,1,0:T(8,128)(2,1)S(1)}, bf16[1,528,128]{2,1,0:T(8,128)(2,1)S(1)}, u32[]{:S(2)}, u32[]{:S(2)}) %collective-permute-start.4) | collective-permute-done | bytes 135200 | tf_op jit(solution)/shard_map/ppermute | solution.py:459
  25.6 1.0 %collective-permute-start.8 = (bf16[528,128]{1,0:T(8,128)(2,1)S(1)}, bf16[528,128]{1,0:T(8,128)(2,1)S(1)}, u32[]{:S(2)}, u32[]{:S(2)}) collective-permute-start(bf16[528,128]{1,0:T(8,128)(2,1)S(1)} %get-tuple-element.37.refs_3_), channel_id=1, source_target_pairs={{0,1},{1,0},{2,3},{3,2},{4,5},{5,4},{6,7},{7,6},{8,9},{9,8},{10,11... | collective-permute-start | bytes 405512 | tf_op jit(solution)/shard_map/ppermute | solution.py:459
  26.6 0.4 %collective-permute-start.7 = (bf16[528,128]{1,0:T(8,128)(2,1)S(1)}, bf16[528,128]{1,0:T(8,128)(2,1)S(1)}, u32[]{:S(2)}, u32[]{:S(2)}) collective-permute-start(bf16[528,128]{1,0:T(8,128)(2,1)S(1)} %get-tuple-element.38), channel_id=1, source_target_pairs={{0,2},{1,5},{2,0},{3,7},{4,6},{5,1},{6,4},{7,3},{8,10},{9,13},{10,... | collective-permute-start | bytes 405512 | tf_op jit(solution)/shard_map/ppermute | solution.py:462
  27.0 1.9 %collective-permute-start.5 = (bf16[528,128]{1,0:T(8,128)(2,1)S(1)}, bf16[528,128]{1,0:T(8,128)(2,1)S(1)}, u32[]{:S(2)}, u32[]{:S(2)}) collective-permute-start(bf16[528,128]{1,0:T(8,128)(2,1)S(1)} %get-tuple-element.40), channel_id=1, source_target_pairs={{0,6},{1,7},{2,4},{3,5},{4,2},{5,3},{6,0},{7,1},{8,14},{9,15},{10,... | collective-permute-start | bytes 405512 | tf_op jit(solution)/shard_map/ppermute | solution.py:462
  28.9 0.4 %collective-permute-start.6 = (bf16[528,128]{1,0:T(8,128)(2,1)S(1)}, bf16[528,128]{1,0:T(8,128)(2,1)S(1)}, u32[]{:S(2)}, u32[]{:S(2)}) collective-permute-start(bf16[528,128]{1,0:T(8,128)(2,1)S(1)} %get-tuple-element.39), channel_id=1, source_target_pairs={{0,4},{1,3},{2,6},{3,1},{4,0},{5,7},{6,2},{7,5},{8,12},{9,11},{10,... | collective-permute-start | bytes 405512 | tf_op jit(solution)/shard_map/ppermute | solution.py:462
  29.3 0.7 %out_m0_o0.1.refs_9_ = bf16[2,128,512]{2,1,0:T(8,128)(2,1)S(1)} custom-call(bf16[128,4096]{1,0:T(8,128)(2,1)S(1)} %copy-done, f32[8,8,128]{2,1,0:T(8,128)S(1)} %cum.1.cum_ref.refs_1_, f32[1,4096]{1,0:T(1,128)S(1)} %bitcast.19, bf16[528,128]{1,0:T(8,128)(2,1)S(1)} %get-tuple-element.37.refs_3_, f32[17,128,128]{2,1,0:T(8,128)S(1)} %intra_mine.1.refs_4_.refs_7_, ...), custom_call_target="tpu_custom_call" | custom-call | flops 1 | bytes 1 | tf_op jit(solution)/shard_map/out_m0_o0/pallas_call | solution.py:52
  30.0 0.8 %collective-permute-done.7.refs_3_ = bf16[528,128]{1,0:T(8,128)(2,1)S(1)} collective-permute-done((bf16[528,128]{1,0:T(8,128)(2,1)S(1)}, bf16[528,128]{1,0:T(8,128)(2,1)S(1)}, u32[]{:S(2)}, u32[]{:S(2)}) %collective-permute-start.7) | collective-permute-done | bytes 135200 | tf_op jit(solution)/shard_map/ppermute | solution.py:462
  30.8 3.0 %collective-permute-start.12 = (bf16[528,128]{1,0:T(8,128)(2,1)S(1)}, bf16[528,128]{1,0:T(8,128)(2,1)S(1)}, u32[]{:S(2)}, u32[]{:S(2)}) collective-permute-start(bf16[528,128]{1,0:T(8,128)(2,1)S(1)} %collective-permute-done.7.refs_3_), channel_id=1, source_target_pairs={{0,1},{1,0},{2,3},{3,2},{4,5},{5,4},{6,7},{7,6},{8,9},{9,8},{10,11... | collective-permute-start | bytes 405512 | tf_op jit(solution)/shard_map/ppermute | solution.py:459
  33.7 0.6 %out_m1.1.refs_10_ = bf16[1,128,512]{2,1,0:T(8,128)(2,1)S(1)} custom-call(bf16[128,4096]{1,0:T(8,128)(2,1)S(1)} %copy-done, f32[8,8,128]{2,1,0:T(8,128)S(1)} %cum.1.cum_ref.refs_1_, f32[1,4096]{1,0:T(1,128)S(1)} %bitcast.20, bf16[528,128]{1,0:T(8,128)(2,1)S(1)} %collective-permute-done.7.refs_3_, f32[17,128,128]{2,1,0:T(8,128)S(1)} %intra_mine.1.refs_4_.refs_7_, ...), custom_call_target="tpu_custom_call" | custom-call | flops 1 | bytes 1 | tf_op jit(solution)/shard_map/out_m1/pallas_call | solution.py:52
  34.4 1.3 %collective-permute-done.6.refs_6_ = bf16[528,128]{1,0:T(8,128)(2,1)S(1)} collective-permute-done((bf16[528,128]{1,0:T(8,128)(2,1)S(1)}, bf16[528,128]{1,0:T(8,128)(2,1)S(1)}, u32[]{:S(2)}, u32[]{:S(2)}) %collective-permute-start.6) | collective-permute-done | bytes 135200 | tf_op jit(solution)/shard_map/ppermute | solution.py:462
  35.6 0.5 %collective-permute-start.11 = (bf16[528,128]{1,0:T(8,128)(2,1)S(1)}, bf16[528,128]{1,0:T(8,128)(2,1)S(1)}, u32[]{:S(2)}, u32[]{:S(2)}) collective-permute-start(bf16[528,128]{1,0:T(8,128)(2,1)S(1)} %collective-permute-done.6.refs_6_), channel_id=1, source_target_pairs={{0,1},{1,0},{2,3},{3,2},{4,5},{5,4},{6,7},{7,6},{8,9},{9,8},{10,11... | collective-permute-start | bytes 405512 | tf_op jit(solution)/shard_map/ppermute | solution.py:459
  36.1 0.9 %out_m3_m2_o1.1.refs_11_ = bf16[3,128,512]{2,1,0:T(8,128)(2,1)S(1)} custom-call(bf16[128,4096]{1,0:T(8,128)(2,1)S(1)} %copy-done, f32[8,8,128]{2,1,0:T(8,128)S(1)} %cum.1.cum_ref.refs_1_, f32[1,4096]{1,0:T(1,128)S(1)} %bitcast.21, bf16[528,128]{1,0:T(8,128)(2,1)S(1)} %collective-permute-done.5.refs_3_, f32[17,128,128]{2,1,0:T(8,128)S(1)} %intra_mine.1.refs_4_.refs_7_, ...), custom_call_target="tpu_custom_call" | custom-call | flops 1 | bytes 1 | tf_op jit(solution)/shard_map/out_m3_m2_o1/pallas_call | solution.py:52
  37.2 1.6 %out_o3_o2.1 = bf16[128,4096]{1,0:T(8,128)(2,1)} custom-call(bf16[128,4096]{1,0:T(8,128)(2,1)S(1)} %copy-done, f32[8,8,128]{2,1,0:T(8,128)S(1)} %cum.1.cum_ref.refs_1_, f32[1,4096]{1,0:T(1,128)S(1)} %bitcast.22, bf16[528,128]{1,0:T(8,128)(2,1)S(1)} %collective-permute-done.10.refs_3_, f32[17,128,128]{2,1,0:T(8,128)S(1)} %intra_other.1.refs_7_.refs_10_.refs_4_, ...), custom_call_target="tpu_custom_call" | custom-call | flops 1 | bytes 1 | tf_op jit(solution)/shard_map/out_o3_o2/pallas_call | solution.py:52
  (28 shorter events, 1.8 us)
Async XLA Ops:
  0.0 2.8 %copy-start.1 = (bf16[128,4096]{1,0:T(8,128)(2,1)S(1)}, bf16[128,4096]{1,0:T(8,128)(2,1)}, u32[]{:S(2)}) copy-start(bf16[128,4096]{1,0:T(8,128)(2,1)} %k_ref.5) | copy-start | bytes 3145732
  0.0 2.8 %copy-start.2 = (bf16[128,4096]{1,0:T(8,128)(2,1)S(1)}, bf16[128,4096]{1,0:T(8,128)(2,1)}, u32[]{:S(2)}) copy-start(bf16[128,4096]{1,0:T(8,128)(2,1)} %v_ref.5) | copy-start | bytes 3145732
  0.0 2.8 %copy-start.3 = (f32[4,4096]{1,0:T(4,128)S(1)}, f32[4,4096]{1,0:T(4,128)}, u32[]{:S(2)}) copy-start(f32[4,4096]{1,0:T(4,128)} %w_ref.5) | copy-start | bytes 196612
  0.0 2.8 %copy-start.5 = (f32[128,32]{0,1:T(8,128)S(1)}, f32[128,32]{0,1:T(8,128)}, u32[]{:S(2)}) copy-start(f32[128,32]{0,1:T(8,128)} %param.9) | copy-start | bytes 49156
  2.7 2.0 %collective-permute-start = (bf16[4,560,128]{2,1,0:T(8,128)(2,1)S(1)}, bf16[4,560,128]{2,1,0:T(8,128)(2,1)S(1)}, u32[]{:S(2)}, u32[]{:S(2)}) collective-permute-start(bf16[4,560,128]{2,1,0:T(8,128)(2,1)S(1)} %states_other.1), channel_id=1, source_target_pairs={{0,1},{1,0},{2,3},{3,2},{4,5},{5,4},{6,7},{7,6},{8,9},{9,8},{10,11... | collective-permute-start | bytes 1720328 | tf_op jit(solution)/shard_map/ppermute | solution.py:459
  4.0 6.0 %copy-start = (bf16[128,4096]{1,0:T(8,128)(2,1)S(1)}, bf16[128,4096]{1,0:T(8,128)(2,1)}, u32[]{:S(2)}) copy-start(bf16[128,4096]{1,0:T(8,128)(2,1)} %refs_0_.7) | copy-start | bytes 3145732
  5.2 5.9 %collective-permute-start.1 = (bf16[1,560,128]{2,1,0:T(8,128)(2,1)S(1)}, bf16[1,560,128]{2,1,0:T(8,128)(2,1)S(1)}, u32[]{:S(2)}, u32[]{:S(2)}) collective-permute-start(bf16[1,560,128]{2,1,0:T(8,128)(2,1)S(1)} %get-tuple-element.35), channel_id=1, source_target_pairs={{0,2},{1,5},{2,0},{3,7},{4,6},{5,1},{6,4},{7,3},{8,10},{9,13},{10,... | collective-permute-start | bytes 430088 | tf_op jit(solution)/shard_map/ppermute | solution.py:462
  7.6 6.2 %collective-permute-start.2 = (bf16[1,560,128]{2,1,0:T(8,128)(2,1)S(1)}, bf16[1,560,128]{2,1,0:T(8,128)(2,1)S(1)}, u32[]{:S(2)}, u32[]{:S(2)}) collective-permute-start(bf16[1,560,128]{2,1,0:T(8,128)(2,1)S(1)} %get-tuple-element.34), channel_id=1, source_target_pairs={{0,6},{1,7},{2,4},{3,5},{4,2},{5,3},{6,0},{7,1},{8,14},{9,15},{10,... | collective-permute-start | bytes 430088 | tf_op jit(solution)/shard_map/ppermute | solution.py:462
  8.8 7.0 %collective-permute-start.3 = (bf16[1,560,128]{2,1,0:T(8,128)(2,1)S(1)}, bf16[1,560,128]{2,1,0:T(8,128)(2,1)S(1)}, u32[]{:S(2)}, u32[]{:S(2)}) collective-permute-start(bf16[1,560,128]{2,1,0:T(8,128)(2,1)S(1)} %get-tuple-element.33), channel_id=1, source_target_pairs={{0,4},{1,3},{2,6},{3,1},{4,0},{5,7},{6,2},{7,5},{8,12},{9,11},{10,... | collective-permute-start | bytes 430088 | tf_op jit(solution)/shard_map/ppermute | solution.py:462
  8.9 20.4 %collective-permute-start.9 = (bf16[4,560,128]{2,1,0:T(8,128)(2,1)S(1)}, bf16[4,560,128]{2,1,0:T(8,128)(2,1)S(1)}, u32[]{:S(2)}, u32[]{:S(2)}) collective-permute-start(bf16[4,560,128]{2,1,0:T(8,128)(2,1)S(1)} %states_mine.1.own_ref), channel_id=1, source_target_pairs={{0,1},{1,0},{2,3},{3,2},{4,5},{5,4},{6,7},{7,6},{8,9},{9,8},{10,11... | collective-permute-start | bytes 1720328 | tf_op jit(solution)/shard_map/ppermute | solution.py:459
  16.2 9.1 %collective-permute-start.4 = (bf16[1,528,128]{2,1,0:T(8,128)(2,1)S(1)}, bf16[1,528,128]{2,1,0:T(8,128)(2,1)S(1)}, u32[]{:S(2)}, u32[]{:S(2)}) collective-permute-start(bf16[1,528,128]{2,1,0:T(8,128)(2,1)S(1)} %span_state.1), channel_id=1, source_target_pairs={{0,8},{1,9},{2,10},{3,11},{4,12},{5,13},{6,14},{7,15},{8,0},{9,1},... | collective-permute-start | bytes 405512 | tf_op jit(solution)/shard_map/ppermute | solution.py:459
  19.8 9.5 %copy-start.4 = (f32[4096]{0:T(1024)S(1)}, f32[4096]{0:T(1024)}, u32[]{:S(2)}) copy-start(f32[4096]{0:T(1024)} %param.11) | copy-start | bytes 49156
  25.6 3.6 %collective-permute-start.8 = (bf16[528,128]{1,0:T(8,128)(2,1)S(1)}, bf16[528,128]{1,0:T(8,128)(2,1)S(1)}, u32[]{:S(2)}, u32[]{:S(2)}) collective-permute-start(bf16[528,128]{1,0:T(8,128)(2,1)S(1)} %get-tuple-element.37.refs_3_), channel_id=1, source_target_pairs={{0,1},{1,0},{2,3},{3,2},{4,5},{5,4},{6,7},{7,6},{8,9},{9,8},{10,11... | collective-permute-start | bytes 405512 | tf_op jit(solution)/shard_map/ppermute | solution.py:459
  26.6 4.2 %collective-permute-start.7 = (bf16[528,128]{1,0:T(8,128)(2,1)S(1)}, bf16[528,128]{1,0:T(8,128)(2,1)S(1)}, u32[]{:S(2)}, u32[]{:S(2)}) collective-permute-start(bf16[528,128]{1,0:T(8,128)(2,1)S(1)} %get-tuple-element.38), channel_id=1, source_target_pairs={{0,2},{1,5},{2,0},{3,7},{4,6},{5,1},{6,4},{7,3},{8,10},{9,13},{10,... | collective-permute-start | bytes 405512 | tf_op jit(solution)/shard_map/ppermute | solution.py:462
  27.0 7.3 %collective-permute-start.5 = (bf16[528,128]{1,0:T(8,128)(2,1)S(1)}, bf16[528,128]{1,0:T(8,128)(2,1)S(1)}, u32[]{:S(2)}, u32[]{:S(2)}) collective-permute-start(bf16[528,128]{1,0:T(8,128)(2,1)S(1)} %get-tuple-element.40), channel_id=1, source_target_pairs={{0,6},{1,7},{2,4},{3,5},{4,2},{5,3},{6,0},{7,1},{8,14},{9,15},{10,... | collective-permute-start | bytes 405512 | tf_op jit(solution)/shard_map/ppermute | solution.py:462
  28.9 6.7 %collective-permute-start.6 = (bf16[528,128]{1,0:T(8,128)(2,1)S(1)}, bf16[528,128]{1,0:T(8,128)(2,1)S(1)}, u32[]{:S(2)}, u32[]{:S(2)}) collective-permute-start(bf16[528,128]{1,0:T(8,128)(2,1)S(1)} %get-tuple-element.39), channel_id=1, source_target_pairs={{0,4},{1,3},{2,6},{3,1},{4,0},{5,7},{6,2},{7,5},{8,12},{9,11},{10,... | collective-permute-start | bytes 405512 | tf_op jit(solution)/shard_map/ppermute | solution.py:462
  30.8 5.4 %collective-permute-start.12 = (bf16[528,128]{1,0:T(8,128)(2,1)S(1)}, bf16[528,128]{1,0:T(8,128)(2,1)S(1)}, u32[]{:S(2)}, u32[]{:S(2)}) collective-permute-start(bf16[528,128]{1,0:T(8,128)(2,1)S(1)} %collective-permute-done.7.refs_3_), channel_id=1, source_target_pairs={{0,1},{1,0},{2,3},{3,2},{4,5},{5,4},{6,7},{7,6},{8,9},{9,8},{10,11... | collective-permute-start | bytes 405512 | tf_op jit(solution)/shard_map/ppermute | solution.py:459
  35.6 1.4 %collective-permute-start.10 = (bf16[528,128]{1,0:T(8,128)(2,1)S(1)}, bf16[528,128]{1,0:T(8,128)(2,1)S(1)}, u32[]{:S(2)}, u32[]{:S(2)}) collective-permute-start(bf16[528,128]{1,0:T(8,128)(2,1)S(1)} %collective-permute-done.5.refs_3_), channel_id=1, source_target_pairs={{0,1},{1,0},{2,3},{3,2},{4,5},{5,4},{6,7},{7,6},{8,9},{9,8},{10,11... | collective-permute-start | bytes 405512 | tf_op jit(solution)/shard_map/ppermute | solution.py:459
  35.6 1.5 %collective-permute-start.11 = (bf16[528,128]{1,0:T(8,128)(2,1)S(1)}, bf16[528,128]{1,0:T(8,128)(2,1)S(1)}, u32[]{:S(2)}, u32[]{:S(2)}) collective-permute-start(bf16[528,128]{1,0:T(8,128)(2,1)S(1)} %collective-permute-done.6.refs_6_), channel_id=1, source_target_pairs={{0,1},{1,0},{2,3},{3,2},{4,5},{5,4},{6,7},{7,6},{8,9},{9,8},{10,11... | collective-permute-start | bytes 405512 | tf_op jit(solution)/shard_map/ppermute | solution.py:459

commit v19 on v18

--- a/solution.py
+++ b/solution.py
@@ -584,7 +584,6 @@
         own[first] = chip_prefix[0]
         for g in EXCHANGE:
             own[first + g] = exchange(chip_prefix[g], g)
-        other[first] = swap(own[first], 1)
 
     def output(items, earlier=None):
         args = [queries, cum, gain]
@@ -614,18 +613,16 @@
         )
 
     *late, soon = EXCHANGE[1], EXCHANGE[0], EXCHANGE[2]
-    items = [(True, 0), (False, 0)]
-    made = output(items)
-    own[soon], made = lax.optimization_barrier((own[soon], made))
-    earlier = [(items, made)]
-    other[soon] = swap(own[soon], 1)
-    items = [(True, soon)]
+    own[0], own[soon] = lax.optimization_barrier((own[0], own[soon]))
+    other.update({u: swap(own[u], 1) for u in (0, soon)})
+    earlier = []
+    items = [(True, 0), (True, soon)]
     made = output(items)
     *arrived, made = lax.optimization_barrier((*[own[u] for u in late], made))
     earlier.append((items, made))
     own.update(zip(late, arrived))
     other.update({u: swap(own[u], 1) for u in late})
-    items = [(True, u) for u in late] + [(False, soon)]
+    items = [(True, u) for u in late] + [(False, 0), (False, soon)]
     earlier.append((items, output(items)))
     return output([(False, u) for u in late], earlier)
 

time: 39.2 us -> 39.3 us (level)
  starting transfers between devices: 14.4 us -> 17.2 us
  waiting for transfers between devices: 13 us -> 10.8 us
    ppermute x7, starting transfers between devices: 8.02 us -> 10.5 us  [swap(): return lax.ppermute(x, 'ctx', [(i, i ^ mask) for i in range(n)])]
    ppermute x7, waiting for transfers between devices: 6.27 us -> 4.2 us  [swap(): return lax.ppermute(x, 'ctx', [(i, i ^ mask) for i in range(n)])]
    pallas_call x12 -> x11, Pallas kernels: 11 us -> 10.7 us  [call(): pl.pallas_call(kernel, out_shape=out_shape, in_specs=in_specs, out_specs=...]
  transfers between devices with their start and end apart: 13 -> 13, of which waited for: 7 -> 7; matrix products, arithmetic and copies ran while one was open for 0% -> 0% of each run, Pallas kernels for 17% -> 15%
where the time goes in v19:
time: 39.3 us; the launch traced here: 38.8 us
  starting transfers between devices  17.2 us (44%)
  waiting for transfers between devices  10.8 us (27%)
  Pallas kernels  10.7 us (27%)
    pallas_call x11, Pallas kernels, call(): pl.pallas_call(kernel, out_shape=out_shape, in_specs=in_specs, out_specs=...  10.7 us
    ppermute x7, starting transfers between devices, swap(): return lax.ppermute(x, 'ctx', [(i, i ^ mask) for i in range(n)])  10.5 us
    ppermute x6, starting transfers between devices, exchange(): lax.ppermute(x, 'ctx', [(i, i ^ 2 * distance(slot, i & 1)) for i in range...  6.63 us
    ppermute x6, waiting for transfers between devices, exchange(): lax.ppermute(x, 'ctx', [(i, i ^ 2 * distance(slot, i & 1)) for i in range...  6.56 us
    ppermute x7, waiting for transfers between devices, swap(): return lax.ppermute(x, 'ctx', [(i, i ^ mask) for i in range(n)])  4.2 us
  transfers between devices with their start and end apart: 13, of which 7 were waited for; matrix products, arithmetic and copies ran while one was open for 0% of the time, Pallas kernels for 15%

profile of v19, /device:TPU:1, one launch (start us, length us, event | category | flops | bytes accessed | tf_op | source)
XLA Modules:
  0.0 38.8 jit_solution(18112244636639670265)
XLA Ops:
  0.0 2.7 %states_other.1 = bf16[4,560,128]{2,1,0:T(8,128)(2,1)S(1)} custom-call(bf16[128,4096]{1,0:T(8,128)(2,1)} %k_ref.5, bf16[128,4096]{1,0:T(8,128)(2,1)} %v_ref.5, f32[4,4096]{1,0:T(4,128)} %w_ref.5, f32[32,128]{1,0:T(8,128)} %bitcast.22), custom_call_target="tpu_custom_call" | custom-call | tf_op jit(solution)/shard_map/states_other/pallas_call | solution.py:52
  2.8 1.2 %states_mine.1.own_ref = bf16[4,560,128]{2,1,0:T(8,128)(2,1)S(1)} custom-call(bf16[128,4096]{1,0:T(8,128)(2,1)S(1)} %copy-done.1, bf16[128,4096]{1,0:T(8,128)(2,1)S(1)} %copy-done.2, f32[4,4096]{1,0:T(4,128)S(1)} %copy-done.3, f32[32,128]{1,0:T(8,128)S(1)} %bitcast.23), custom_call_target="tpu_custom_call" | custom-call | tf_op jit(solution)/shard_map/states_mine/pallas_call | solution.py:52
  4.0 0.7 %collective-permute-done.got_ref.refs_5_.refs_8_ = bf16[4,560,128]{2,1,0:T(8,128)(2,1)S(1)} collective-permute-done((bf16[4,560,128]{2,1,0:T(8,128)(2,1)S(1)}, bf16[4,560,128]{2,1,0:T(8,128)(2,1)S(1)}, u32[]{:S(2)}, u32[]{:S(2)}) %collective-permute-start) | collective-permute-done | bytes 573472 | tf_op jit(solution)/shard_map/ppermute | solution.py:459
  4.7 0.4 chip_states.1
  5.2 2.4 %collective-permute-start.3 = (bf16[1,560,128]{2,1,0:T(8,128)(2,1)S(1)}, bf16[1,560,128]{2,1,0:T(8,128)(2,1)S(1)}, u32[]{:S(2)}, u32[]{:S(2)}) collective-permute-start(bf16[1,560,128]{2,1,0:T(8,128)(2,1)S(1)} %get-tuple-element.33), channel_id=1, source_target_pairs={{0,4},{1,3},{2,6},{3,1},{4,0},{5,7},{6,2},{7,5},{8,12},{9,11},{10,... | collective-permute-start | bytes 430088 | tf_op jit(solution)/shard_map/ppermute | solution.py:462
  7.6 1.2 %collective-permute-start.2 = (bf16[1,560,128]{2,1,0:T(8,128)(2,1)S(1)}, bf16[1,560,128]{2,1,0:T(8,128)(2,1)S(1)}, u32[]{:S(2)}, u32[]{:S(2)}) collective-permute-start(bf16[1,560,128]{2,1,0:T(8,128)(2,1)S(1)} %get-tuple-element.34), channel_id=1, source_target_pairs={{0,6},{1,7},{2,4},{3,5},{4,2},{5,3},{6,0},{7,1},{8,14},{9,15},{10,... | collective-permute-start | bytes 430088 | tf_op jit(solution)/shard_map/ppermute | solution.py:462
  9.1 1.1 %intra_mine.1.refs_4_.refs_7_ = f32[17,128,128]{2,1,0:T(8,128)S(1)} custom-call(bf16[128,4096]{1,0:T(8,128)(2,1)S(1)} %copy-done, bf16[128,4096]{1,0:T(8,128)(2,1)S(1)} %copy-done.1, bf16[128,4096]{1,0:T(8,128)(2,1)S(1)} %copy-done.2, f32[4,4096]{1,0:T(4,128)S(1)} %copy-done.3, f32[8,8,128]{2,1,0:T(8,128)S(1)} %cum.1.cum_ref.refs_1_), custom_call_target="tpu_custom_call" | custom-call | tf_op jit(solution)/shard_map/intra_mine/pallas_call | solution.py:52
  10.4 3.8 %collective-permute-done.2.refs_3_ = bf16[1,560,128]{2,1,0:T(8,128)(2,1)S(1)} collective-permute-done((bf16[1,560,128]{2,1,0:T(8,128)(2,1)S(1)}, bf16[1,560,128]{2,1,0:T(8,128)(2,1)S(1)}, u32[]{:S(2)}, u32[]{:S(2)}) %collective-permute-start.2) | collective-permute-done | bytes 143392 | tf_op jit(solution)/shard_map/ppermute | solution.py:462
  14.2 1.4 %collective-permute-done.1.refs_1_ = bf16[1,560,128]{2,1,0:T(8,128)(2,1)S(1)} collective-permute-done((bf16[1,560,128]{2,1,0:T(8,128)(2,1)S(1)}, bf16[1,560,128]{2,1,0:T(8,128)(2,1)S(1)}, u32[]{:S(2)}, u32[]{:S(2)}) %collective-permute-start.1) | collective-permute-done | bytes 143392 | tf_op jit(solution)/shard_map/ppermute | solution.py:462
  15.6 0.4 span_state.1
  16.0 2.8 %collective-permute-start.4 = (bf16[1,528,128]{2,1,0:T(8,128)(2,1)S(1)}, bf16[1,528,128]{2,1,0:T(8,128)(2,1)S(1)}, u32[]{:S(2)}, u32[]{:S(2)}) collective-permute-start(bf16[1,528,128]{2,1,0:T(8,128)(2,1)S(1)} %span_state.1), channel_id=1, source_target_pairs={{0,8},{1,9},{2,10},{3,11},{4,12},{5,13},{6,14},{7,15},{8,0},{9,1},... | collective-permute-start | bytes 405512 | tf_op jit(solution)/shard_map/ppermute | solution.py:459
  18.8 1.4 %collective-permute-start.9 = (bf16[4,560,128]{2,1,0:T(8,128)(2,1)S(1)}, bf16[4,560,128]{2,1,0:T(8,128)(2,1)S(1)}, u32[]{:S(2)}, u32[]{:S(2)}) collective-permute-start(bf16[4,560,128]{2,1,0:T(8,128)(2,1)S(1)} %states_mine.1.own_ref), channel_id=1, source_target_pairs={{0,1},{1,0},{2,3},{3,2},{4,5},{5,4},{6,7},{7,6},{8,9},{9,8},{10,11... | collective-permute-start | bytes 1720328 | tf_op jit(solution)/shard_map/ppermute | solution.py:459
  20.1 1.1 %intra_other.1.refs_10_.refs_13_.refs_4_.refs_7_ = f32[17,128,128]{2,1,0:T(8,128)S(1)} custom-call(bf16[128,4096]{1,0:T(8,128)(2,1)S(1)} %copy-done, bf16[128,4096]{1,0:T(8,128)(2,1)S(1)} %copy-done.1, bf16[128,4096]{1,0:T(8,128)(2,1)S(1)} %copy-done.2, f32[4,4096]{1,0:T(4,128)S(1)} %copy-done.3, f32[8,8,128]{2,1,0:T(8,128)S(1)} %cum.1.cum_ref.refs_1_), custom_call_target="tpu_custom_call" | custom-call | tf_op jit(solution)/shard_map/intra_other/pallas_call | solution.py:52
  21.2 3.3 %collective-permute-done.4.refs_4_ = bf16[1,528,128]{2,1,0:T(8,128)(2,1)S(1)} collective-permute-done((bf16[1,528,128]{2,1,0:T(8,128)(2,1)S(1)}, bf16[1,528,128]{2,1,0:T(8,128)(2,1)S(1)}, u32[]{:S(2)}, u32[]{:S(2)}) %collective-permute-start.4) | collective-permute-done | bytes 135200 | tf_op jit(solution)/shard_map/ppermute | solution.py:459
  24.6 0.4 chip_prefix.1
  25.0 1.6 %collective-permute-start.7 = (bf16[528,128]{1,0:T(8,128)(2,1)S(1)}, bf16[528,128]{1,0:T(8,128)(2,1)S(1)}, u32[]{:S(2)}, u32[]{:S(2)}) collective-permute-start(bf16[528,128]{1,0:T(8,128)(2,1)S(1)} %get-tuple-element.37), channel_id=1, source_target_pairs={{0,2},{1,5},{2,0},{3,7},{4,6},{5,1},{6,4},{7,3},{8,10},{9,13},{10,... | collective-permute-start | bytes 405512 | tf_op jit(solution)/shard_map/ppermute | solution.py:462
  26.6 1.0 %collective-permute-start.6 = (bf16[528,128]{1,0:T(8,128)(2,1)S(1)}, bf16[528,128]{1,0:T(8,128)(2,1)S(1)}, u32[]{:S(2)}, u32[]{:S(2)}) collective-permute-start(bf16[528,128]{1,0:T(8,128)(2,1)S(1)} %get-tuple-element.39), channel_id=1, source_target_pairs={{0,4},{1,3},{2,6},{3,1},{4,0},{5,7},{6,2},{7,5},{8,12},{9,11},{10,... | collective-permute-start | bytes 405512 | tf_op jit(solution)/shard_map/ppermute | solution.py:462
  27.6 0.3 collective-permute-start.5
  27.9 1.1 %collective-permute-done.7.refs_6_ = bf16[528,128]{1,0:T(8,128)(2,1)S(1)} collective-permute-done((bf16[528,128]{1,0:T(8,128)(2,1)S(1)}, bf16[528,128]{1,0:T(8,128)(2,1)S(1)}, u32[]{:S(2)}, u32[]{:S(2)}) %collective-permute-start.7) | collective-permute-done | bytes 135200 | tf_op jit(solution)/shard_map/ppermute | solution.py:462
  29.0 4.7 %collective-permute-start.11 = (bf16[528,128]{1,0:T(8,128)(2,1)S(1)}, bf16[528,128]{1,0:T(8,128)(2,1)S(1)}, u32[]{:S(2)}, u32[]{:S(2)}) collective-permute-start(bf16[528,128]{1,0:T(8,128)(2,1)S(1)} %get-tuple-element.26.refs_3_), channel_id=1, source_target_pairs={{0,1},{1,0},{2,3},{3,2},{4,5},{5,4},{6,7},{7,6},{8,9},{9,8},{10,11... | collective-permute-start | bytes 405512 | tf_op jit(solution)/shard_map/ppermute | solution.py:459
  33.8 0.7 %out_m0_m1.1.refs_9_ = bf16[2,128,512]{2,1,0:T(8,128)(2,1)S(1)} custom-call(bf16[128,4096]{1,0:T(8,128)(2,1)S(1)} %copy-done, f32[8,8,128]{2,1,0:T(8,128)S(1)} %cum.1.cum_ref.refs_1_, f32[1,4096]{1,0:T(1,128)S(1)} %bitcast.19, bf16[528,128]{1,0:T(8,128)(2,1)S(1)} %get-tuple-element.26.refs_3_, f32[17,128,128]{2,1,0:T(8,128)S(1)} %intra_mine.1.refs_4_.refs_7_, ...), custom_call_target="tpu_custom_call" | custom-call | flops 1 | bytes 1 | tf_op jit(solution)/shard_map/out_m0_m1/pallas_call | solution.py:52
  34.5 1.5 %collective-permute-start.8 = (bf16[528,128]{1,0:T(8,128)(2,1)S(1)}, bf16[528,128]{1,0:T(8,128)(2,1)S(1)}, u32[]{:S(2)}, u32[]{:S(2)}) collective-permute-start(bf16[528,128]{1,0:T(8,128)(2,1)S(1)} %collective-permute-done.5.refs_3_), channel_id=1, source_target_pairs={{0,1},{1,0},{2,3},{3,2},{4,5},{5,4},{6,7},{7,6},{8,9},{9,8},{10,11... | collective-permute-start | bytes 405512 | tf_op jit(solution)/shard_map/ppermute | solution.py:459
  36.0 1.2 %out_m3_m2_o0_o1.1.refs_10_ = bf16[4,128,512]{2,1,0:T(8,128)(2,1)S(1)} custom-call(bf16[128,4096]{1,0:T(8,128)(2,1)S(1)} %copy-done, f32[8,8,128]{2,1,0:T(8,128)S(1)} %cum.1.cum_ref.refs_1_, f32[1,4096]{1,0:T(1,128)S(1)} %bitcast.20, bf16[528,128]{1,0:T(8,128)(2,1)S(1)} %collective-permute-done.5.refs_3_, f32[17,128,128]{2,1,0:T(8,128)S(1)} %intra_mine.1.refs_4_.refs_7_, ...), custom_call_target="tpu_custom_call" | custom-call | flops 1 | bytes 1 | tf_op jit(solution)/shard_map/out_m3_m2_o0_o1/pallas_call | solution.py:52
  37.3 1.5 %out_o3_o2.1 = bf16[128,4096]{1,0:T(8,128)(2,1)} custom-call(bf16[128,4096]{1,0:T(8,128)(2,1)S(1)} %copy-done, f32[8,8,128]{2,1,0:T(8,128)S(1)} %cum.1.cum_ref.refs_1_, f32[1,4096]{1,0:T(1,128)S(1)} %bitcast.21, bf16[528,128]{1,0:T(8,128)(2,1)S(1)} %collective-permute-done.8.refs_3_, f32[17,128,128]{2,1,0:T(8,128)S(1)} %intra_other.1.refs_10_.refs_13_.refs_4_.refs_7_, ...), custom_call_target="tpu_custom_call" | custom-call | flops 1 | bytes 1 | tf_op jit(solution)/shard_map/out_o3_o2/pallas_call | solution.py:52
  (27 shorter events, 0.8 us)
Async XLA Ops:
  0.0 2.8 %copy-start.1 = (bf16[128,4096]{1,0:T(8,128)(2,1)S(1)}, bf16[128,4096]{1,0:T(8,128)(2,1)}, u32[]{:S(2)}) copy-start(bf16[128,4096]{1,0:T(8,128)(2,1)} %k_ref.5) | copy-start | bytes 3145732
  0.0 2.8 %copy-start.2 = (bf16[128,4096]{1,0:T(8,128)(2,1)S(1)}, bf16[128,4096]{1,0:T(8,128)(2,1)}, u32[]{:S(2)}) copy-start(bf16[128,4096]{1,0:T(8,128)(2,1)} %v_ref.5) | copy-start | bytes 3145732
  0.0 2.8 %copy-start.3 = (f32[4,4096]{1,0:T(4,128)S(1)}, f32[4,4096]{1,0:T(4,128)}, u32[]{:S(2)}) copy-start(f32[4,4096]{1,0:T(4,128)} %w_ref.5) | copy-start | bytes 196612
  0.0 2.8 %copy-start.5 = (f32[128,32]{0,1:T(8,128)S(1)}, f32[128,32]{0,1:T(8,128)}, u32[]{:S(2)}) copy-start(f32[128,32]{0,1:T(8,128)} %param.9) | copy-start | bytes 49156
  2.7 2.0 %collective-permute-start = (bf16[4,560,128]{2,1,0:T(8,128)(2,1)S(1)}, bf16[4,560,128]{2,1,0:T(8,128)(2,1)S(1)}, u32[]{:S(2)}, u32[]{:S(2)}) collective-permute-start(bf16[4,560,128]{2,1,0:T(8,128)(2,1)S(1)} %states_other.1), channel_id=1, source_target_pairs={{0,1},{1,0},{2,3},{3,2},{4,5},{5,4},{6,7},{7,6},{8,9},{9,8},{10,11... | collective-permute-start | bytes 1720328 | tf_op jit(solution)/shard_map/ppermute | solution.py:459
  4.0 5.1 %copy-start = (bf16[128,4096]{1,0:T(8,128)(2,1)S(1)}, bf16[128,4096]{1,0:T(8,128)(2,1)}, u32[]{:S(2)}) copy-start(bf16[128,4096]{1,0:T(8,128)(2,1)} %refs_0_.5) | copy-start | bytes 3145732
  5.2 5.2 %collective-permute-start.3 = (bf16[1,560,128]{2,1,0:T(8,128)(2,1)S(1)}, bf16[1,560,128]{2,1,0:T(8,128)(2,1)S(1)}, u32[]{:S(2)}, u32[]{:S(2)}) collective-permute-start(bf16[1,560,128]{2,1,0:T(8,128)(2,1)S(1)} %get-tuple-element.33), channel_id=1, source_target_pairs={{0,4},{1,3},{2,6},{3,1},{4,0},{5,7},{6,2},{7,5},{8,12},{9,11},{10,... | collective-permute-start | bytes 430088 | tf_op jit(solution)/shard_map/ppermute | solution.py:462
  7.6 6.6 %collective-permute-start.2 = (bf16[1,560,128]{2,1,0:T(8,128)(2,1)S(1)}, bf16[1,560,128]{2,1,0:T(8,128)(2,1)S(1)}, u32[]{:S(2)}, u32[]{:S(2)}) collective-permute-start(bf16[1,560,128]{2,1,0:T(8,128)(2,1)S(1)} %get-tuple-element.34), channel_id=1, source_target_pairs={{0,6},{1,7},{2,4},{3,5},{4,2},{5,3},{6,0},{7,1},{8,14},{9,15},{10,... | collective-permute-start | bytes 430088 | tf_op jit(solution)/shard_map/ppermute | solution.py:462
  8.8 6.8 %collective-permute-start.1 = (bf16[1,560,128]{2,1,0:T(8,128)(2,1)S(1)}, bf16[1,560,128]{2,1,0:T(8,128)(2,1)S(1)}, u32[]{:S(2)}, u32[]{:S(2)}) collective-permute-start(bf16[1,560,128]{2,1,0:T(8,128)(2,1)S(1)} %get-tuple-element.35), channel_id=1, source_target_pairs={{0,2},{1,5},{2,0},{3,7},{4,6},{5,1},{6,4},{7,3},{8,10},{9,13},{10,... | collective-permute-start | bytes 430088 | tf_op jit(solution)/shard_map/ppermute | solution.py:462
  16.0 8.6 %collective-permute-start.4 = (bf16[1,528,128]{2,1,0:T(8,128)(2,1)S(1)}, bf16[1,528,128]{2,1,0:T(8,128)(2,1)S(1)}, u32[]{:S(2)}, u32[]{:S(2)}) collective-permute-start(bf16[1,528,128]{2,1,0:T(8,128)(2,1)S(1)} %span_state.1), channel_id=1, source_target_pairs={{0,8},{1,9},{2,10},{3,11},{4,12},{5,13},{6,14},{7,15},{8,0},{9,1},... | collective-permute-start | bytes 405512 | tf_op jit(solution)/shard_map/ppermute | solution.py:459
  18.8 17.2 %collective-permute-start.9 = (bf16[4,560,128]{2,1,0:T(8,128)(2,1)S(1)}, bf16[4,560,128]{2,1,0:T(8,128)(2,1)S(1)}, u32[]{:S(2)}, u32[]{:S(2)}) collective-permute-start(bf16[4,560,128]{2,1,0:T(8,128)(2,1)S(1)} %states_mine.1.own_ref), channel_id=1, source_target_pairs={{0,1},{1,0},{2,3},{3,2},{4,5},{5,4},{6,7},{7,6},{8,9},{9,8},{10,11... | collective-permute-start | bytes 1720328 | tf_op jit(solution)/shard_map/ppermute | solution.py:459
  21.2 12.5 %copy-start.4 = (f32[4096]{0:T(1024)S(1)}, f32[4096]{0:T(1024)}, u32[]{:S(2)}) copy-start(f32[4096]{0:T(1024)} %param.11) | copy-start | bytes 49156
  25.0 4.0 %collective-permute-start.7 = (bf16[528,128]{1,0:T(8,128)(2,1)S(1)}, bf16[528,128]{1,0:T(8,128)(2,1)S(1)}, u32[]{:S(2)}, u32[]{:S(2)}) collective-permute-start(bf16[528,128]{1,0:T(8,128)(2,1)S(1)} %get-tuple-element.37), channel_id=1, source_target_pairs={{0,2},{1,5},{2,0},{3,7},{4,6},{5,1},{6,4},{7,3},{8,10},{9,13},{10,... | collective-permute-start | bytes 405512 | tf_op jit(solution)/shard_map/ppermute | solution.py:462
  26.6 7.8 %collective-permute-start.6 = (bf16[528,128]{1,0:T(8,128)(2,1)S(1)}, bf16[528,128]{1,0:T(8,128)(2,1)S(1)}, u32[]{:S(2)}, u32[]{:S(2)}) collective-permute-start(bf16[528,128]{1,0:T(8,128)(2,1)S(1)} %get-tuple-element.39), channel_id=1, source_target_pairs={{0,4},{1,3},{2,6},{3,1},{4,0},{5,7},{6,2},{7,5},{8,12},{9,11},{10,... | collective-permute-start | bytes 405512 | tf_op jit(solution)/shard_map/ppermute | solution.py:462
  27.6 6.8 %collective-permute-start.5 = (bf16[528,128]{1,0:T(8,128)(2,1)S(1)}, bf16[528,128]{1,0:T(8,128)(2,1)S(1)}, u32[]{:S(2)}, u32[]{:S(2)}) collective-permute-start(bf16[528,128]{1,0:T(8,128)(2,1)S(1)} %get-tuple-element.40), channel_id=1, source_target_pairs={{0,6},{1,7},{2,4},{3,5},{4,2},{5,3},{6,0},{7,1},{8,14},{9,15},{10,... | collective-permute-start | bytes 405512 | tf_op jit(solution)/shard_map/ppermute | solution.py:462
  29.0 6.9 %collective-permute-start.11 = (bf16[528,128]{1,0:T(8,128)(2,1)S(1)}, bf16[528,128]{1,0:T(8,128)(2,1)S(1)}, u32[]{:S(2)}, u32[]{:S(2)}) collective-permute-start(bf16[528,128]{1,0:T(8,128)(2,1)S(1)} %get-tuple-element.26.refs_3_), channel_id=1, source_target_pairs={{0,1},{1,0},{2,3},{3,2},{4,5},{5,4},{6,7},{7,6},{8,9},{9,8},{10,11... | collective-permute-start | bytes 405512 | tf_op jit(solution)/shard_map/ppermute | solution.py:459
  33.8 2.2 %collective-permute-start.12 = (bf16[528,128]{1,0:T(8,128)(2,1)S(1)}, bf16[528,128]{1,0:T(8,128)(2,1)S(1)}, u32[]{:S(2)}, u32[]{:S(2)}) collective-permute-start(bf16[528,128]{1,0:T(8,128)(2,1)S(1)} %collective-permute-done.7.refs_6_), channel_id=1, source_target_pairs={{0,1},{1,0},{2,3},{3,2},{4,5},{5,4},{6,7},{7,6},{8,9},{9,8},{10,11... | collective-permute-start | bytes 405512 | tf_op jit(solution)/shard_map/ppermute | solution.py:459
  34.5 2.7 %collective-permute-start.8 = (bf16[528,128]{1,0:T(8,128)(2,1)S(1)}, bf16[528,128]{1,0:T(8,128)(2,1)S(1)}, u32[]{:S(2)}, u32[]{:S(2)}) collective-permute-start(bf16[528,128]{1,0:T(8,128)(2,1)S(1)} %collective-permute-done.5.refs_3_), channel_id=1, source_target_pairs={{0,1},{1,0},{2,3},{3,2},{4,5},{5,4},{6,7},{7,6},{8,9},{9,8},{10,11... | collective-permute-start | bytes 405512 | tf_op jit(solution)/shard_map/ppermute | solution.py:459
  36.0 1.4 %collective-permute-start.10 = (bf16[528,128]{1,0:T(8,128)(2,1)S(1)}, bf16[528,128]{1,0:T(8,128)(2,1)S(1)}, u32[]{:S(2)}, u32[]{:S(2)}) collective-permute-start(bf16[528,128]{1,0:T(8,128)(2,1)S(1)} %collective-permute-done.6.refs_6_), channel_id=1, source_target_pairs={{0,1},{1,0},{2,3},{3,2},{4,5},{5,4},{6,7},{7,6},{8,9},{9,8},{10,11... | collective-permute-start | bytes 405512 | tf_op jit(solution)/shard_map/ppermute | solution.py:459
